TPU v7x, 32 devices: a whole 2x2x4 slice. The times are simulated.
32 devices in a mesh: dp: 16 (over z, y, x), head: 2 (over core).
Axes of the slice: x: 2, y: 2, z: 4, core: 2. Of those that a mesh axis runs over, the one named last changes fastest.
Arguments:
- tokens: bfloat16 [49152, 384], P(('dp', 'head')), may hold values from -6 to 6
- cotangent: bfloat16 [49152, 384], P(('dp', 'head')), may hold values from -6 to 6
- token_counts: int32 [192], P('dp'), may hold values from 64 to 256, as said below
- head_mask: int32 [192, 6], P('dp', 'head'), may hold values 0 or 1
- norm_params: float32 [4, 384], replicated, may hold values from -2 to 2
- norm_state: float32 [4, 384], replicated, may hold values from 0.1 to 1
- weights: float32 [2, 3, 128, 48, 48], P('head', None, 'dp'), may hold values from -1 to 1
- stat_left: float32 [2, 3, 128, 48, 48], P('head', None, 'dp'), may hold values from 0 to 2, as said below
- stat_right: float32 [2, 3, 128, 48, 48], P('head', None, 'dp'), may hold values from 0 to 2, as said below
Outputs:
- block_out: float32 [49152, 384], P(('dp', 'head'))
- input_grad: float32 [49152, 384], P(('dp', 'head'))
- weight_grads: float32 [2, 3, 128, 48, 48], P('head', None, 'dp')
- left_new: float32 [2, 3, 128, 48, 48], P('head', None, 'dp')
- right_new: float32 [2, 3, 128, 48, 48], P('head', None, 'dp')
- new_weights: float32 [2, 3, 128, 48, 48], P('head', None, 'dp')
- norm_grads: float32 [4, 384], replicated
- state_new: float32 [4, 384], replicated
- norm_new: float32 [4, 384], replicated
Inputs may be any that keep to these rules, and one draw needn't show every extreme that they name: `token_counts`: some image has all 256 tokens valid and some has a quarter of 256. `stat_left`: diagonal and positive. `stat_right`: diagonal and positive.
All inputs are finite; a program needn't handle non-finite values. No bound on the sum of `head_mask` on one device may be relied on, other than what follows from the above.
Results may differ from a plain program's by a relative error of at most 0.0092.
Values may be sent and summed in bfloat16 or wider, within the bound.
No kernel may reach another device: no remote copies, remote signals or barrier semaphores. Data moves between devices by JAX's collectives and lax.ppermute only.
A program may use at most 128 MiB of HBM per device.

v0:
```python
import math

import jax
import jax.numpy as jnp
from jax import lax
from jax.sharding import PartitionSpec as P

D = 384
HEAD_DIM = 64
MLP = 1536
S = 256
ITERS = 8


ROOT_HALF = 0.7071067811865476
DENSITY_FACTOR = 0.3989422804014327


def unpack(blocks, row_count, col_count):
    edge = blocks.shape[-1]
    shaped = blocks.reshape(row_count // edge, col_count // edge, edge, edge)
    return shaped.transpose(0, 2, 1, 3).reshape(row_count, col_count)


def pack(matrix, edge):
    row_count, col_count = matrix.shape
    shaped = matrix.reshape(row_count // edge, edge, col_count // edge, edge)
    return shaped.transpose(0, 2, 1, 3).reshape(-1, edge, edge)


def batched(left, right):
    return jnp.einsum("...ij,...jk->...ik", left, right, precision=lax.Precision.HIGHEST)


def left_product(left, right):
    return lax.dot_general(
        left, right, (((0,), (0,)), ((), ())), preferred_element_type=jnp.float32
    )


def right_product(left, right):
    return lax.dot_general(
        left, right, (((1,), (1,)), ((), ())), preferred_element_type=jnp.float32
    )


def inverse_root(matrix):
    identity = jnp.eye(matrix.shape[-1], dtype=matrix.dtype)
    frobenius = jnp.sqrt(jnp.sum(matrix * matrix, axis=(-2, -1), keepdims=True))
    factor = 2.5 / frobenius
    result = jnp.sqrt(jnp.sqrt(factor)) * identity
    current = factor * matrix
    for iteration in range(ITERS):
        middle = (5.0 * identity - current) * 0.25
        result = batched(result, middle)
        square = batched(middle, middle)
        current = batched(batched(square, square), current)
    return result


def norm_forward(values, gain, shift):
    centered = values - jnp.mean(values, axis=-1, keepdims=True)
    variance = jnp.mean(centered * centered, axis=-1, keepdims=True)
    inverse_std = lax.rsqrt(variance + 1e-06)
    normed = centered * inverse_std
    return (normed * gain + shift, normed, inverse_std)


def norm_backward(grad_out, normed, inverse_std, gain):
    grad_normed = grad_out * gain
    mean_first = jnp.mean(grad_normed, axis=-1, keepdims=True)
    mean_second = jnp.mean(grad_normed * normed, axis=-1, keepdims=True)
    grad_in = inverse_std * (grad_normed - mean_first - normed * mean_second)
    return (grad_in, jnp.sum(grad_out * normed, axis=0), jnp.sum(grad_out, axis=0))


def masked_scores(queries, keys_all, key_valid):
    scores = 0.125 * jnp.einsum(
        "gqhd,gkhd->ghqk", queries, keys_all, preferred_element_type=jnp.float32
    )
    return jnp.where(key_valid[:, None, None, :], scores, -1e30)


def split_matrices(blocks):
    return (
        unpack(blocks[0, :96], D, 3 * D // 2),
        unpack(blocks[0, 96:], D // 2, D),
        unpack(blocks[1], D, MLP // 2),
        unpack(blocks[2], MLP // 2, D),
    )


def attention_forward(first_rows, qkv_weight, counts, heads_low):
    image_count = counts.shape[0]
    local_heads = heads_low.shape[2]
    projected = jnp.dot(first_rows, qkv_weight, preferred_element_type=jnp.float32).astype(
        jnp.bfloat16
    )
    split_heads = projected.reshape(image_count, S, 3, local_heads, HEAD_DIM)
    queries = split_heads[:, :, 0]
    keys_all = split_heads[:, :, 1]
    values_all = split_heads[:, :, 2]
    key_valid = lax.broadcasted_iota(jnp.int32, (image_count, S), 1) < counts[:, None]
    scores = masked_scores(queries, keys_all, key_valid)
    row_max = jnp.max(scores, axis=-1, keepdims=True)
    exp_scores = jnp.exp(scores - row_max)
    totals = jnp.sum(exp_scores, axis=-1, keepdims=True)
    log_total = row_max + jnp.log(totals)
    prob_low = (exp_scores / totals).astype(jnp.bfloat16)
    head_out = jnp.einsum(
        "ghqk,gkhd->gqhd", prob_low, values_all, preferred_element_type=jnp.float32
    )
    head_out = (head_out * heads_low.astype(jnp.float32)).astype(jnp.bfloat16)
    attn_rows = head_out.reshape(image_count * S, local_heads * HEAD_DIM)
    return (attn_rows, (queries, keys_all, values_all, key_valid, log_total))


def attention_backward(saved, head_grad):
    queries, keys_all, values_all, key_valid, log_total = saved
    scores = masked_scores(queries, keys_all, key_valid)
    probabilities = jnp.exp(scores - log_total)
    prob_low = probabilities.astype(jnp.bfloat16)
    prob_grad = jnp.einsum(
        "gqhd,gkhd->ghqk", head_grad, values_all, preferred_element_type=jnp.float32
    )
    row_dot = jnp.sum(probabilities * prob_grad, axis=-1, keepdims=True)
    score_grad = (probabilities * (prob_grad - row_dot)).astype(jnp.bfloat16)
    query_grad = 0.125 * jnp.einsum(
        "ghqk,gkhd->gqhd", score_grad, keys_all, preferred_element_type=jnp.float32
    )
    key_grad = 0.125 * jnp.einsum(
        "ghqk,gqhd->gkhd", score_grad, queries, preferred_element_type=jnp.float32
    )
    value_grad = jnp.einsum(
        "ghqk,gqhd->gkhd", prob_low, head_grad, preferred_element_type=jnp.float32
    )
    qkv_grad = jnp.stack([query_grad, key_grad, value_grad], axis=2).astype(jnp.bfloat16)
    return qkv_grad.reshape(queries.shape[0] * S, 3 * queries.shape[2] * HEAD_DIM)


def feed_forward(second_rows, up_weight):
    pre_act = jnp.dot(second_rows, up_weight, preferred_element_type=jnp.float32)
    activated = jax.nn.gelu(pre_act, approximate=False).astype(jnp.bfloat16)
    return (pre_act, activated)


def feed_back(branch_rows, pre_act, second_rows, activated, down_weight):
    down_grad = left_product(activated, branch_rows)
    act_grad = right_product(branch_rows, down_weight)
    cumulative = 0.5 * (1.0 + jax.scipy.special.erf(pre_act * ROOT_HALF))
    density = jnp.exp(-0.5 * pre_act * pre_act) * DENSITY_FACTOR
    pre_grad = (act_grad * (cumulative + pre_act * density)).astype(jnp.bfloat16)
    up_grad = left_product(second_rows, pre_grad)
    return (pre_grad, up_grad, down_grad)


def per_device(
    tokens,
    cotangent,
    token_counts,
    head_mask,
    norm_params,
    norm_state,
    weights,
    stat_left,
    stat_right,
):
    edge = weights.shape[-1]
    local_rows = tokens.shape[0]
    image_count = token_counts.shape[0]
    inputs = tokens.astype(jnp.float32)
    grad_out = cotangent.astype(jnp.float32)
    gain_one, shift_one, gain_two, shift_two = (
        norm_params[0],
        norm_params[1],
        norm_params[2],
        norm_params[3],
    )
    normed_in, normed_one, inverse_one = norm_forward(inputs, gain_one, shift_one)
    local_heads = head_mask.shape[1]
    gathered = lax.all_gather(weights.astype(jnp.bfloat16), "dp", axis=2, tiled=True)[0]
    qkv_weight, out_weight, up_weight, down_weight = split_matrices(gathered)
    first_rows = lax.all_gather(normed_in.astype(jnp.bfloat16), "head", axis=0, tiled=True)
    heads_low = head_mask.astype(jnp.bfloat16)[:, None, :, None]
    attn_rows, saved = attention_forward(first_rows, qkv_weight, token_counts, heads_low)
    part_rows = attn_rows
    middle = inputs + lax.psum_scatter(
        jnp.dot(part_rows, out_weight, preferred_element_type=jnp.float32),
        "head",
        scatter_dimension=0,
        tiled=True,
    )
    normed_mid, normed_two, inverse_two = norm_forward(middle, gain_two, shift_two)
    second_rows = lax.all_gather(normed_mid.astype(jnp.bfloat16), "head", axis=0, tiled=True)
    pre_act, activated = feed_forward(second_rows, up_weight)
    part_rows = activated
    block_out = middle + lax.psum_scatter(
        jnp.dot(part_rows, down_weight, preferred_element_type=jnp.float32).astype(jnp.bfloat16),
        "head",
        scatter_dimension=0,
        tiled=True,
    ).astype(jnp.float32)
    branch_rows = lax.all_gather(cotangent, "head", axis=0, tiled=True)
    pre_grad, up_grad, down_grad = feed_back(
        branch_rows, pre_act, second_rows, activated, down_weight
    )
    later_pack = jnp.stack([pack(up_grad, edge), pack(down_grad, edge)])[None]
    part_rows = pre_grad
    mid_normed_grad = lax.psum_scatter(
        right_product(part_rows, up_weight), "head", scatter_dimension=0, tiled=True
    )
    mid_in_grad, gain_two_grad, shift_two_grad = norm_backward(
        mid_normed_grad, normed_two, inverse_two, gain_two
    )
    middle_grad = grad_out + mid_in_grad
    residual_rows = lax.all_gather(middle_grad.astype(jnp.bfloat16), "head", axis=0, tiled=True)
    out_grad = left_product(attn_rows, residual_rows)
    head_grad = right_product(residual_rows, out_weight).astype(jnp.bfloat16)
    head_grad = head_grad.reshape(image_count, S, local_heads, HEAD_DIM) * heads_low
    qkv_grad = attention_backward(saved, head_grad)
    qkv_weight_grad = left_product(first_rows, qkv_grad)
    part_rows = qkv_grad
    in_normed_grad = lax.psum_scatter(
        right_product(part_rows, qkv_weight).astype(jnp.bfloat16),
        "head",
        scatter_dimension=0,
        tiled=True,
    ).astype(jnp.float32)
    in_grad, gain_one_grad, shift_one_grad = norm_backward(
        in_normed_grad, normed_one, inverse_one, gain_one
    )
    input_grad = middle_grad + in_grad
    early_pack = jnp.concatenate([pack(qkv_weight_grad, edge), pack(out_grad, edge)])[None, None]
    owned = lax.psum_scatter(
        jnp.concatenate([early_pack, later_pack], axis=1), "dp", scatter_dimension=2, tiled=True
    )
    norm_local = jnp.stack([gain_one_grad, shift_one_grad, gain_two_grad, shift_two_grad])
    norm_total = lax.psum(norm_local, ("dp", "head"))
    token_total = local_rows * lax.axis_size("dp") * lax.axis_size("head")
    scale = 1.0 / math.sqrt(token_total)
    grads = owned * scale
    left_new = 0.5 * stat_left + 0.5 * batched(grads, jnp.swapaxes(grads, -1, -2))
    right_new = 0.5 * stat_right + 0.5 * batched(jnp.swapaxes(grads, -1, -2), grads)
    direction = batched(batched(inverse_root(left_new), grads), inverse_root(right_new))
    new_weights = weights - 0.25 * direction
    norm_grads = norm_total * scale
    state_new = 0.5 * norm_state + 0.5 * norm_grads * norm_grads
    norm_new = norm_params - 0.2 * norm_grads / jnp.sqrt(state_new)
    return (
        block_out,
        input_grad,
        grads,
        left_new,
        right_new,
        new_weights,
        norm_grads,
        state_new,
        norm_new,
    )


def solution(mesh):
    placed = (
        P(("dp", "head"), None),
        P(("dp", "head"), None),
        P("dp"),
        P("dp", "head"),
        P(),
        P(),
        P("head", None, "dp", None, None),
        P("head", None, "dp", None, None),
        P("head", None, "dp", None, None),
    )
    return jax.shard_map(
        per_device,
        mesh=mesh,
        in_specs=placed,
        out_specs=(
            P(("dp", "head"), None),
            P(("dp", "head"), None),
            P("head", None, "dp", None, None),
            P("head", None, "dp", None, None),
            P("head", None, "dp", None, None),
            P("head", None, "dp", None, None),
            P(),
            P(),
            P(),
        ),
        check_vma=False,
    )
```

profile of v0, /device:TPU:0, one launch (start us, length us, event | category | flops | bytes accessed | tf_op | source)
XLA Modules:
  0.0 549.3 jit_solution(17342946108123096912)
XLA Ops:
  15.4 79.0 %all-gather.8.cloned.1.call-done = bf16[1,3,128,48,48]{4,3,2,1,0:T(8,128)(2,1)} async-done(((bf16[1,3,8,48,48]{4,3,2,1,0:T(8,128)(2,1)}), bf16[1,3,128,48,48]{4,3,2,1,0:T(8,128)(2,1)}) %all-gather.8.cloned.1.call-update) | async-done | bytes 1769488 | tf_op jit(solution)/shard_map/all_gather | solution.py:181
  99.5 6.7 %all-gather.6.cloned.1.call-done = bf16[3072,384]{1,0:T(8,128)(2,1)} async-done(((bf16[1536,384]{1,0:T(8,128)(2,1)}), bf16[3072,384]{1,0:T(8,128)(2,1)}) %all-gather.6.cloned.1.call-update) | async-done | bytes 2359312 | tf_op jit(solution)/shard_map/all_gather | solution.py:183
  106.2 5.5 convolution_convert_fusion
  111.7 7.3 %reshape.534 = bf16[12,256,3,3,64]{1,0,4,3,2:T(8,128)(2,1)} reshape(bf16[3072,576]{0,1:T(8,128)(2,1)} %convolution_convert_fusion) | data formatting | bytes 7077888 | tf_op jit(solution)/shard_map/reshape | solution.py:99
  137.7 13.9 %reduce-scatter.8.cloned.1.call-done = f32[1536,384]{1,0:T(8,128)} async-done(((f32[3072,384]{1,0:T(8,128)}), f32[1536,384]{1,0:T(8,128)}) %reduce-scatter.8.cloned.1.call-update) | async-done | bytes 2359312 | tf_op jit(solution)/shard_map/reduce_scatter | solution.py:187
  170.6 23.7 %fusion.2 = (bf16[3072,768]{1,0:T(8,128)(2,1)}, f32[3072,768]{1,0:T(8,128)}) fusion(bf16[3072,384]{1,0:T(8,128)(2,1)} %all-gather.10.cloned.1.call-done, bf16[384,768]{1,0:T(8,128)(2,1)S(1)} %reshape.537), kind=kOutput, calls=%fused_computation.4 | convolution fusion | flops 1965293568 | bytes 17104896 | tf_op jit(solution)/shard_map/dot_general | solution.py:142
  194.3 9.3 %fusion.8 = bf16[3072,768]{1,0:T(8,128)(2,1)S(1)} fusion(f32[3072,768]{1,0:T(8,128)} %get-tuple-element.45, bf16[3072,384]{1,0:T(8,128)(2,1)} %all-gather.12.cloned.1.call-done, bf16[768,384]{1,0:T(8,128)(2,1)S(1)} %reshape.538), kind=kOutput, calls=%fused_computation.10 | convolution fusion | flops 1835532288 | bytes 17104896 | tf_op jit(solution)/shard_map/dot_general | solution.py:42
  205.8 4.3 fusion.203
  210.2 6.4 %convolution_convert_fusion.2 = bf16[3072,384]{1,0:T(8,128)(2,1)} fusion(bf16[3072,768]{1,0:T(8,128)(2,1)} %get-tuple-element.44, bf16[768,384]{1,0:T(8,128)(2,1)S(1)} %reshape.538), kind=kOutput, calls=%fused_computation.40 | convolution fusion | flops 1813118976 | bytes 7667712 | tf_op jit(solution)/shard_map/dot_general | solution.py:198
  216.8 7.3 %reduce-scatter.12.cloned.1.call-done = f32[1536,384]{1,0:T(8,128)} async-done(((f32[3072,384]{1,0:T(8,128)}), f32[1536,384]{1,0:T(8,128)}) %reduce-scatter.12.cloned.1.call-update) | async-done | bytes 2359312 | tf_op jit(solution)/shard_map/reduce_scatter | solution.py:209
  228.0 10.0 %reduce-scatter.10.cloned.1.call-done = bf16[1536,384]{1,0:T(8,128)(2,1)} async-done(((bf16[3072,384]{1,0:T(8,128)(2,1)}), bf16[1536,384]{1,0:T(8,128)(2,1)}) %reduce-scatter.10.cloned.1.call-update) | async-done | bytes 1179664 | tf_op jit(solution)/shard_map/reduce_scatter | solution.py:197
  238.0 5.0 fusion.198
  243.9 11.4 %all-gather.14.cloned.1.call-done = bf16[3072,384]{1,0:T(8,128)(2,1)} async-done(((bf16[1536,384]{1,0:T(8,128)(2,1)}), bf16[3072,384]{1,0:T(8,128)(2,1)}) %all-gather.14.cloned.1.call-update) | async-done | bytes 2359312 | tf_op jit(solution)/shard_map/all_gather | solution.py:216
  259.0 5.6 %fusion.38 = bf16[12,256,1,3,64]{1,4,3,0,2:T(8,128)(2,1)S(1)} fusion(f32[12,3,256]{2,1,0:T(4,128)S(1)} %log_add_fusion, f32[12,3,256,256]{2,3,1,0:T(8,128)} %copy-done, pred[12,256]{1,0:T(8,128)(4,1)S(1)} %copy-done.34, bf16[12,256,3,64]{1,0,3,2:T(8,128)(2,1)S(1)} %broadcast_multiply_fusion), kind=kOutput, calls=%fused_computation.77 | convolution fusion | flops 311427072 | bytes 11836416 | tf_op jit(solution)/shard_map/ghqk,gqhd->gkhd/dot_general | solution.py:134
  264.7 6.9 %multiply_reduce_fusion = (f32[12,3,256]{2,1,0:T(4,128)S(1)}, f32[12,3,256,256]{2,3,1,0:T(8,128)S(1)}) fusion(f32[12,3,256]{2,1,0:T(4,128)S(1)} %log_add_fusion, f32[12,3,256,256]{2,3,1,0:T(8,128)} %copy-done, pred[12,256]{1,0:T(8,128)(4,1)S(1)} %copy-done.34, bf16[12,256,1,3,64]{1,0,4,3,2:T(8,128)(2,1)S(1)} %copy-done.15, ...), kind=kOutput, calls=%fused_computation.12 | convolution fusion | flops 313777152 | bytes 21310464 | tf_op jit(solution)/shard_map/gqhd,gkhd->ghqk/dot_general | solution.py:123
  284.1 3.7 convolution_convert_fusion.1
  287.9 4.9 copy.94
  292.8 5.5 %fusion.206 = f32[384,768]{1,0:T(8,128)} fusion(bf16[3072,384]{1,0:T(8,128)(2,1)S(1)} %copy-done.13, bf16[3072,768]{1,0:T(8,128)(2,1)} %copy-done.4), kind=kOutput, calls=%fused_computation.298 | convolution fusion | flops 1811939328 | bytes 8257536 | tf_op jit(solution)/shard_map/dot_general | solution.py:36
  307.0 6.0 %fusion.207 = f32[768,384]{1,0:T(8,128)} fusion(bf16[3072,768]{1,0:T(8,128)(2,1)} %get-tuple-element.44, bf16[3072,384]{1,0:T(8,128)(2,1)S(1)} %copy-done.21), kind=kOutput, calls=%fused_computation.299 | convolution fusion | flops 1811939328 | bytes 8257536 | tf_op jit(solution)/shard_map/dot_general | solution.py:36
  330.0 7.3 %fusion.204 = f32[8,48,12,48]{3,1,2,0:T(8,128)} fusion(bf16[8,48,3072,1]{2,1,3,0:T(8,128)(2,1)} %bitcast.277, bf16[12,48,3072,1]{2,1,0,3:T(8,128)(2,1)} %bitcast.275), kind=kOutput, calls=%fused_computation.296 | convolution fusion | flops 1358954496 | bytes 6782976 | tf_op jit(solution)/shard_map/dot_general | solution.py:36
  341.1 5.8 %copy.111 = f32[1,3,128,48,48]{4,3,1,0,2:T(8,128)} copy(f32[1,3,128,48,48]{2,4,3,1,0:T(8,128)S(1)} %pad_maximum_fusion) | data formatting | bytes 7077888
  346.9 8.2 %reshape.553 = f32[128,6912]{1,0:T(8,128)} reshape(f32[128,1,3,48,48]{4,3,2,1,0:T(8,128)} %bitcast.258) | data formatting | bytes 7077888
  359.2 40.8 %psum.7 = f32[4,384]{1,0:T(4,128)S(1)} all-reduce(f32[4,384]{1,0:T(4,128)S(1)} %pad_maximum_fusion.1), channel_id=1, replica_groups=mesh['dp'=16,'head'=2] {'dp','head'}, use_global_device_ids=true, to_apply=%region_22.23 | all-reduce | flops 1536 | bytes 12288 | tf_op jit(solution)/shard_map/psum | solution.py:238
  404.3 86.6 %reduce-scatter.16.cloned.1.call-done = f32[8,6912]{1,0:T(8,128)} async-done(((f32[128,6912]{1,0:T(8,128)}), f32[8,6912]{1,0:T(8,128)}) %reduce-scatter.16.cloned.1.call-update) | async-done | bytes 221200
  (260 shorter events, 162.5 us)
Async XLA Ops:
  7.2 87.3 %all-gather.8.cloned.1.call-start = ((), (), s32[]{:S(2)}) async-start(), calls=%async_computation.6 | async-start | bytes 5013504 | tf_op jit(solution)/shard_map/all_gather | solution.py:181
  9.2 97.1 %all-gather.6.cloned.1.call-start = ((), (), s32[]{:S(2)}) async-start(), calls=%async_computation.5 | async-start | bytes 3538944 | tf_op jit(solution)/shard_map/all_gather | solution.py:183
  15.2 136.4 %reduce-scatter.8.cloned.1.call-start = ((), (), s32[]{:S(2)}) async-start(), calls=%async_computation.7 | async-start | bytes 7077888 | tf_op jit(solution)/shard_map/reduce_scatter | solution.py:187
  15.2 79.2 %copy-start.39 = (bf16[12,3]{0,1:T(4,128)(2,1)}, bf16[12,3]{0,1:T(4,128)(2,1)S(1)}, u32[]{:S(2)}) copy-start(bf16[12,3]{0,1:T(4,128)(2,1)S(1)} %convert_element_type.93) | copy-start | bytes 220
  15.4 111.7 %copy-start.33 = (pred[12,256]{1,0:T(8,128)(4,1)}, pred[12,256]{1,0:T(8,128)(4,1)S(1)}, u32[]{:S(2)}) copy-start(pred[12,256]{1,0:T(8,128)(4,1)S(1)} %iota_compare_fusion.1) | copy-start | bytes 9220
  99.5 12.1 %copy-start.26 = (bf16[384,576]{0,1:T(8,128)(2,1)}, bf16[384,576]{0,1:T(8,128)(2,1)S(1)}, u32[]{:S(2)}) copy-start(bf16[384,576]{0,1:T(8,128)(2,1)S(1)} %reshape.533) | copy-start | bytes 1327108
  121.6 5.6 %copy-start.14 = (bf16[12,256,1,3,64]{1,0,4,3,2:T(8,128)(2,1)}, bf16[12,256,1,3,64]{1,0,4,3,2:T(8,128)(2,1)S(1)}, u32[]{:S(2)}) copy-start(bf16[12,256,1,3,64]{1,0,4,3,2:T(8,128)(2,1)S(1)} %get-tuple-element.34) | copy-start | bytes 3538948
  137.7 32.9 %all-gather.10.cloned.1.call-start = ((), (), s32[]{:S(2)}) async-start(), calls=%async_computation.8 | async-start | bytes 3538944 | tf_op jit(solution)/shard_map/all_gather | solution.py:194
  155.8 38.5 %all-gather.12.cloned.1.call-start = ((), (), s32[]{:S(2)}) async-start(), calls=%async_computation.10 | async-start | bytes 3538944 | tf_op jit(solution)/shard_map/all_gather | solution.py:203
  156.4 67.6 %reduce-scatter.12.cloned.1.call-start = ((), (), s32[]{:S(2)}) async-start(), calls=%async_computation.11 | async-start | bytes 7077888 | tf_op jit(solution)/shard_map/reduce_scatter | solution.py:209
  210.1 27.9 %reduce-scatter.10.cloned.1.call-start = ((), (), s32[]{:S(2)}) async-start(), calls=%async_computation.9 | async-start | bytes 3538944 | tf_op jit(solution)/shard_map/reduce_scatter | solution.py:197
  216.5 21.5 %copy-start.16 = (bf16[1536,384]{1,0:T(8,128)(2,1)S(1)}, bf16[1536,384]{1,0:T(8,128)(2,1)}, u32[]{:S(2)}) copy-start(bf16[1536,384]{1,0:T(8,128)(2,1)} %param.10) | copy-start | bytes 3538948
  216.6 38.7 %all-gather.14.cloned.1.call-start = ((), (), s32[]{:S(2)}) async-start(), calls=%async_computation.12 | async-start | bytes 3538944 | tf_op jit(solution)/shard_map/all_gather | solution.py:216
  243.0 112.9 %reduce-scatter.14.cloned.1.call-start = ((), (), s32[]{:S(2)}) async-start(), calls=%async_computation.13 | async-start | bytes 3538944 | tf_op jit(solution)/shard_map/reduce_scatter | solution.py:223
  259.0 5.7 %copy-start.15 = (bf16[12,256,1,3,64]{1,0,4,3,2:T(8,128)(2,1)S(1)}, bf16[12,256,1,3,64]{1,0,4,3,2:T(8,128)(2,1)}, u32[]{:S(2)}) copy-start(bf16[12,256,1,3,64]{1,0,4,3,2:T(8,128)(2,1)} %copy-done.14) | copy-start | bytes 3538948
  259.0 12.6 %slice-start = ((s8[9437184]{0:T(1024)(128)(4,1)}), s8[4194304]{0:T(1024)(128)(4,1)S(1)}, s32[]{:S(2)}) async-start(s8[9437184]{0:T(1024)(128)(4,1)} %bitcast.256), calls=%async_computation.15 | async-start | bytes 8388608
  259.0 12.6 %slice-start.1 = ((s8[9437184]{0:T(1024)(128)(4,1)}), s8[4194304]{0:T(1024)(128)(4,1)S(1)}, s32[]{:S(2)}) async-start(s8[9437184]{0:T(1024)(128)(4,1)} %bitcast.256), calls=%async_computation.16 | async-start | bytes 8388608
  264.7 6.9 %slice-start.2 = ((s8[9437184]{0:T(1024)(128)(4,1)}), s8[1048576]{0:T(1024)(128)(4,1)S(1)}, s32[]{:S(2)}) async-start(s8[9437184]{0:T(1024)(128)(4,1)} %bitcast.256), calls=%async_computation.17 | async-start | bytes 2097152
  287.9 203.1 %reduce-scatter.16.cloned.1.call-start = ((), (), s32[]{:S(2)}) async-start(), calls=%async_computation.14 | async-start | bytes 3760128
  355.2 44.8 %copy-start.38 = (f32[4,384]{1,0:T(4,128)S(1)}, f32[4,384]{1,0:T(4,128)}, u32[]{:S(2)}) copy-start(f32[4,384]{1,0:T(4,128)} %param.13) | copy-start | bytes 18436
  355.2 44.8 %copy-start.44 = (f32[4,384]{1,0:T(4,128)S(1)}, f32[4,384]{1,0:T(4,128)}, u32[]{:S(2)}) copy-start(f32[4,384]{1,0:T(4,128)} %param.14) | copy-start | bytes 18436
  356.5 44.1 %copy-start.17 = (bf16[1536,384]{1,0:T(8,128)(2,1)S(1)}, bf16[1536,384]{1,0:T(8,128)(2,1)}, u32[]{:S(2)}) copy-start(bf16[1536,384]{1,0:T(8,128)(2,1)} %reduce-scatter.14.cloned.1.call-done) | copy-start | bytes 3538948
  404.3 88.0 %copy-start.23 = (f32[1,3,8,48,48]{4,3,2,1,0:T(8,128)S(1)}, f32[1,3,8,48,48]{4,3,2,1,0:T(8,128)}, u32[]{:S(2)}) copy-start(f32[1,3,8,48,48]{4,3,2,1,0:T(8,128)} %param.17) | copy-start | bytes 663556
  492.3 46.9 %copy-start.12 = (f32[1,3,8,48,48]{4,3,2,1,0:T(8,128)}, f32[1,3,8,48,48]{4,3,2,1,0:T(8,128)S(1)}, u32[]{:S(2)}) copy-start(f32[1,3,8,48,48]{4,3,2,1,0:T(8,128)S(1)} %copy_multiply_fusion) | copy-start | bytes 663556
  (36 other events, 82.3 us)
Sparse Core Ops, SparseCore 0:
  11.3 83.1 all-gather.7
  96.6 9.5 all-gather.5
  137.8 13.7 reduce-scatter.7
  156.0 12.1 all-gather.9
  169.6 12.1 all-gather.11
  210.2 13.7 reduce-scatter.11
  226.9 11.0 reduce-scatter.9
  243.1 12.1 all-gather.13
  288.0 11.0 reduce-scatter.13
  355.4 135.5 reduce-scatter.15
where the time goes:
time: 559 us; the launch traced here: 549 us
  waiting for transfers between devices  216 us (39%)
  matrix products  152 us (27%)
  local copies, waits for them, and re-layouts  88.5 us (16%)
  blocking collectives  40.8 us (7%)
  other arithmetic  35.9 us (6%)
  between operations  15.7 us (3%)
    unnamed x11, waiting for transfers between devices  87.3 us
    all_gather x1, waiting for transfers between devices, per_device(): lax.all_gather(weights.astype(jnp.bfloat16), 'dp', axis=2, tiled=True)[0]  79 us
    dot_general x62, matrix products, batched(): jnp.einsum('...ij,...jk->...ik', left, right, precision=lax.Precision.HIG...  49.4 us
    psum x1, blocking collectives, per_device(): norm_total = lax.psum(norm_local, ('dp', 'head'))  40.8 us
    unnamed x105, local copies, waits for them, and re-layouts  27.9 us
    dot_general x1, matrix products, feed_forward(): jnp.dot(second_rows, up_weight, preferred_element_type=jnp.float32)  23.7 us
    dot_general x4, matrix products, left_product(): lax.dot_general(left, right, (((0,), (0,)), ((), ())), preferred_element_...  21.8 us
    dot_general x4, matrix products, right_product(): lax.dot_general(left, right, (((1,), (1,)), ((), ())), preferred_element_...  20 us
  transfers between devices with their start and end apart: 10, of which 7 were waited for; matrix products, arithmetic and copies ran while one was open for 24% of the time, Pallas kernels for 0%

commit v1 on v0

v1 whole, which is shorter than its diff:
```python
import math

import jax
import jax.numpy as jnp
from jax import lax
from jax.experimental import pallas as pl
from jax.experimental.pallas import tpu as pltpu
from jax.sharding import PartitionSpec as P

D = 384
HEAD_DIM = 64
MLP = 1536
S = 256
ITERS = 8
PAIR = 2 * HEAD_DIM
PAIRS = D // PAIR
HALF = D // 2
SLABS = 16
ROOT_HALF = 0.7071067811865476
DENSITY_FACTOR = 0.3989422804014327
BF = jnp.bfloat16
F32 = jnp.float32
VMEM_LIMIT = 56 << 20


def nn(left, right):
    return jnp.dot(left, right, preferred_element_type=F32)


def nt(left, right):
    return lax.dot_general(left, right, (((1,), (1,)), ((), ())), preferred_element_type=F32)


def tn(left, right):
    return lax.dot_general(left, right, (((0,), (0,)), ((), ())), preferred_element_type=F32)


def normalize(values):
    centered = values - jnp.mean(values, axis=-1, keepdims=True)
    variance = jnp.mean(centered * centered, axis=-1, keepdims=True)
    inverse_std = lax.rsqrt(variance + 1e-06)
    return centered * inverse_std, inverse_std


def norm_backward(grad_out, normed, inverse_std, gain):
    grad_normed = grad_out * gain
    mean_first = jnp.mean(grad_normed, axis=-1, keepdims=True)
    mean_second = jnp.mean(grad_normed * normed, axis=-1, keepdims=True)
    grad_in = inverse_std * (grad_normed - mean_first - normed * mean_second)
    gain_grad = jnp.sum(grad_out * normed, axis=0, keepdims=True)
    shift_grad = jnp.sum(grad_out, axis=0, keepdims=True)
    return grad_in, jnp.concatenate([gain_grad, shift_grad], axis=0)


def lane_halves():
    lane = lax.broadcasted_iota(jnp.int32, (1, PAIR), 1)
    first = (lane < HEAD_DIM).astype(BF)
    return first, (1 - first).astype(BF)


def stacked(values, first, second):
    return jnp.concatenate([values * first, values * second], axis=0)


def attn_forward_kernel(
    counts_ref, x_ref, mask_ref, norm_ref, own_ref, other_ref,
    prob_ref, qkv_ref, out_ref, middle_ref, wqkv_ref, wo_ref,
):
    step = pl.program_id(0)

    @pl.when(step == 0)
    def _():
        slabs = (own_ref, other_ref)
        for row in range(D // 48):
            for part in range(3):
                pieces = []
                for ref in slabs:
                    slab, side = divmod(3 * row + part, 2)
                    pieces.append(ref[slab][:, side * HALF : (side + 1) * HALF])
                joined = jnp.concatenate(pieces, axis=1)
                if part == 0:
                    joined = joined * 0.125
                wqkv_ref[48 * row : 48 * row + 48, D * part : D * part + D] = joined
        for side, ref in enumerate(slabs):
            for row in range(HALF // 48):
                start = side * HALF + 48 * row
                wo_ref[start : start + 48, :] = ref[12 + row]

    x = x_ref[...].astype(F32)
    normed, _ = normalize(x)
    rows = (normed * norm_ref[0:1, :] + norm_ref[1:2, :]).astype(BF)
    qkv_ref[...] = nn(rows, wqkv_ref[...]).astype(BF)
    first, second = lane_halves()
    count = counts_ref[step]
    column = lax.broadcasted_iota(jnp.int32, (1, S), 1)
    valid = column < count
    for pair in range(PAIRS):
        lanes = slice(PAIR * pair, PAIR * (pair + 1))
        queries = qkv_ref[:, lanes]
        keys = qkv_ref[:, D + PAIR * pair : D + PAIR * (pair + 1)]
        values = qkv_ref[:, 2 * D + PAIR * pair : 2 * D + PAIR * (pair + 1)]
        scores = nt(stacked(queries, first, second), keys)
        scores = jnp.where(valid, scores, -1e30)
        top = jnp.max(scores, axis=-1, keepdims=True)
        exp_scores = jnp.exp(scores - top)
        total = jnp.sum(exp_scores, axis=-1, keepdims=True)
        prob = (exp_scores * (1.0 / total)).astype(BF)
        prob_ref[0, pair] = prob
        head_out = nn(prob[:S], values * first) + nn(prob[S:], values * second)
        out_ref[:, lanes] = (head_out * mask_ref[0, :, lanes]).astype(BF)
    middle_ref[...] = x + nn(out_ref[...], wo_ref[...])


def attn_forward(counts, tokens, mask_lanes, norm_params, own, other):
    rows = tokens.shape[0]
    images = rows // S
    return pl.pallas_call(
        attn_forward_kernel,
        grid=(images,),
        in_specs=[
            pl.BlockSpec(memory_space=pltpu.SMEM),
            pl.BlockSpec((S, D), lambda i: (i, 0)),
            pl.BlockSpec((1, 1, D), lambda i: (i, 0, 0)),
            pl.BlockSpec((4, D), lambda i: (0, 0)),
            pl.BlockSpec((SLABS, 48, D), lambda i: (0, 0, 0)),
            pl.BlockSpec((SLABS, 48, D), lambda i: (0, 0, 0)),
        ],
        out_specs=[
            pl.BlockSpec((1, PAIRS, 2 * S, S), lambda i: (i, 0, 0, 0)),
            pl.BlockSpec((S, 3 * D), lambda i: (i, 0)),
            pl.BlockSpec((S, D), lambda i: (i, 0)),
            pl.BlockSpec((S, D), lambda i: (i, 0)),
            pl.BlockSpec((D, 3 * D), lambda i: (0, 0)),
            pl.BlockSpec((D, D), lambda i: (0, 0)),
        ],
        out_shape=[
            jax.ShapeDtypeStruct((images, PAIRS, 2 * S, S), BF),
            jax.ShapeDtypeStruct((rows, 3 * D), BF),
            jax.ShapeDtypeStruct((rows, D), BF),
            jax.ShapeDtypeStruct((rows, D), F32),
            jax.ShapeDtypeStruct((D, 3 * D), BF),
            jax.ShapeDtypeStruct((D, D), BF),
        ],
        compiler_params=pltpu.CompilerParams(vmem_limit_bytes=VMEM_LIMIT),
        name="attn_forward",
    )(counts, tokens, mask_lanes, norm_params, own, other)


def mlp_kernel(
    middle_ref, cot_ref, norm_ref, up_own_ref, up_other_ref, down_own_ref, down_other_ref,
    out_ref, grad_ref, up_grad_ref, down_grad_ref, norm_grad_ref,
):
    step = pl.program_id(0)

    @pl.when(step == 0)
    def _():
        up_grad_ref[...] = jnp.zeros_like(up_grad_ref)
        down_grad_ref[...] = jnp.zeros_like(down_grad_ref)
        norm_grad_ref[...] = jnp.zeros_like(norm_grad_ref)

    middle = middle_ref[...]
    normed, inverse_std = normalize(middle)
    rows = (normed * norm_ref[2:3, :] + norm_ref[3:4, :]).astype(BF)
    cot = cot_ref[...]
    total = middle
    back = None
    for side, (up_ref, down_ref) in enumerate(
        ((up_own_ref, down_own_ref), (up_other_ref, down_other_ref))
    ):
        for part in range(2):
            up = jnp.concatenate([up_ref[2 * r + part] for r in range(8)], axis=0)
            down = jnp.concatenate([down_ref[8 * part + r] for r in range(8)], axis=0)
            pre = nn(rows, up)
            cumulative = 0.5 * (1.0 + lax.erf(pre * ROOT_HALF))
            density = jnp.exp(-0.5 * pre * pre) * DENSITY_FACTOR
            act = (pre * cumulative).astype(BF)
            total = total + nn(act, down)
            act_grad = nt(cot, down)
            pre_grad = (act_grad * (cumulative + pre * density)).astype(BF)
            down_part = tn(act, cot)
            up_part = tn(rows, pre_grad)
            for r in range(8):
                down_grad_ref[side, 8 * part + r] += down_part[48 * r : 48 * r + 48]
                up_grad_ref[side, 2 * r + part] += up_part[48 * r : 48 * r + 48]
            term = nt(pre_grad, up)
            back = term if back is None else back + term
    out_ref[...] = total
    grad_in, norm_part = norm_backward(back, normed, inverse_std, norm_ref[2:3, :])
    norm_grad_ref[...] += norm_part
    grad_ref[...] = cot.astype(F32) + grad_in


def mlp(middle, cotangent, norm_params, up_own, up_other, down_own, down_other):
    rows = middle.shape[0]
    slab = pl.BlockSpec((SLABS, 48, D), lambda i: (0, 0, 0))
    tile = pl.BlockSpec((S, D), lambda i: (i, 0))
    grad = pl.BlockSpec((2, SLABS, 48, D), lambda i: (0, 0, 0, 0))
    return pl.pallas_call(
        mlp_kernel,
        grid=(rows // S,),
        in_specs=[tile, tile, pl.BlockSpec((4, D), lambda i: (0, 0)), slab, slab, slab, slab],
        out_specs=[tile, tile, grad, grad, pl.BlockSpec((2, D), lambda i: (0, 0))],
        out_shape=[
            jax.ShapeDtypeStruct((rows, D), F32),
            jax.ShapeDtypeStruct((rows, D), F32),
            jax.ShapeDtypeStruct((2, SLABS, 48, D), F32),
            jax.ShapeDtypeStruct((2, SLABS, 48, D), F32),
            jax.ShapeDtypeStruct((2, D), F32),
        ],
        compiler_params=pltpu.CompilerParams(vmem_limit_bytes=VMEM_LIMIT),
        name="mlp",
    )(middle, cotangent, norm_params, up_own, up_other, down_own, down_other)


def attn_backward_kernel(
    x_ref, grad_ref, prob_ref, qkv_ref, out_ref, mask_ref, norm_ref, wqkv_ref, wo_ref,
    in_grad_ref, slab_grad_ref, norm_grad_ref, dqkv_ref, wqkv_grad_ref, wo_grad_ref,
):
    step = pl.program_id(0)

    @pl.when(step == 0)
    def _():
        wqkv_grad_ref[...] = jnp.zeros_like(wqkv_grad_ref)
        wo_grad_ref[...] = jnp.zeros_like(wo_grad_ref)
        norm_grad_ref[...] = jnp.zeros_like(norm_grad_ref)

    x = x_ref[...].astype(F32)
    normed, inverse_std = normalize(x)
    rows = (normed * norm_ref[0:1, :] + norm_ref[1:2, :]).astype(BF)
    grad = grad_ref[...]
    low_grad = grad.astype(BF)
    head_out = out_ref[...]
    wo_grad_ref[...] += tn(head_out, low_grad)
    out_grad = (nt(low_grad, wo_ref[...]).astype(BF) * mask_ref[0].astype(BF))
    first, second = lane_halves()
    for pair in range(PAIRS):
        lanes = slice(PAIR * pair, PAIR * (pair + 1))
        key_lanes = slice(D + PAIR * pair, D + PAIR * (pair + 1))
        value_lanes = slice(2 * D + PAIR * pair, 2 * D + PAIR * (pair + 1))
        queries = qkv_ref[:, lanes]
        keys = qkv_ref[:, key_lanes]
        values = qkv_ref[:, value_lanes]
        prob = prob_ref[0, pair]
        pair_grad = stacked(out_grad[:, lanes], first, second)
        dots = out_grad[:, lanes].astype(F32) * head_out[:, lanes].astype(F32)
        row_dot = jnp.concatenate(
            [
                jnp.sum(dots * first.astype(F32), axis=-1, keepdims=True),
                jnp.sum(dots * second.astype(F32), axis=-1, keepdims=True),
            ],
            axis=0,
        )
        prob_grad = nt(pair_grad, values)
        score_grad = (prob.astype(F32) * (prob_grad - row_dot)).astype(BF)
        dqkv_ref[:, lanes] = (
            nn(score_grad[:S], keys * first) + nn(score_grad[S:], keys * second)
        ).astype(BF)
        dqkv_ref[:, key_lanes] = tn(score_grad, stacked(queries, first, second)).astype(BF)
        dqkv_ref[:, value_lanes] = tn(prob, pair_grad).astype(BF)
    dqkv = dqkv_ref[...]
    wqkv_grad_ref[...] += tn(rows, dqkv)
    back = nt(dqkv, wqkv_ref[...])
    grad_in, norm_part = norm_backward(back, normed, inverse_std, norm_ref[0:1, :])
    norm_grad_ref[...] += norm_part
    in_grad_ref[...] = grad + grad_in

    @pl.when(step == pl.num_programs(0) - 1)
    def _():
        for side in range(2):
            for slab in range(12):
                pieces = []
                for unit in (2 * slab, 2 * slab + 1):
                    row, part = divmod(unit, 3)
                    start = D * part + HALF * side
                    piece = wqkv_grad_ref[48 * row : 48 * row + 48, D * part : D * part + D]
                    piece = piece[:, HALF * side : HALF * side + HALF]
                    pieces.append(piece * 0.125 if part == 0 else piece)
                slab_grad_ref[side, slab] = jnp.concatenate(pieces, axis=1)
            for row in range(HALF // 48):
                start = HALF * side + 48 * row
                slab_grad_ref[side, 12 + row] = wo_grad_ref[start : start + 48, :]


def attn_backward(tokens, grad, prob, qkv, out, mask_lanes, norm_params, wqkv, wo):
    rows = tokens.shape[0]
    images = rows // S
    tile = pl.BlockSpec((S, D), lambda i: (i, 0))
    return pl.pallas_call(
        attn_backward_kernel,
        grid=(images,),
        in_specs=[
            tile,
            tile,
            pl.BlockSpec((1, PAIRS, 2 * S, S), lambda i: (i, 0, 0, 0)),
            pl.BlockSpec((S, 3 * D), lambda i: (i, 0)),
            tile,
            pl.BlockSpec((1, 1, D), lambda i: (i, 0, 0)),
            pl.BlockSpec((4, D), lambda i: (0, 0)),
            pl.BlockSpec((D, 3 * D), lambda i: (0, 0)),
            pl.BlockSpec((D, D), lambda i: (0, 0)),
        ],
        out_specs=[
            tile,
            pl.BlockSpec((2, SLABS, 48, D), lambda i: (0, 0, 0, 0)),
            pl.BlockSpec((2, D), lambda i: (0, 0)),
        ],
        out_shape=[
            jax.ShapeDtypeStruct((rows, D), F32),
            jax.ShapeDtypeStruct((2, SLABS, 48, D), F32),
            jax.ShapeDtypeStruct((2, D), F32),
        ],
        scratch_shapes=[
            pltpu.VMEM((S, 3 * D), BF),
            pltpu.VMEM((D, 3 * D), F32),
            pltpu.VMEM((D, D), F32),
        ],
        compiler_params=pltpu.CompilerParams(vmem_limit_bytes=VMEM_LIMIT),
        name="attn_backward",
    )(tokens, grad, prob, qkv, out, mask_lanes, norm_params, wqkv, wo)


def split(values):
    high = values.astype(BF)
    return high, (values - high.astype(F32)).astype(BF)


def product(left, right):
    left_high, left_low = left
    right_high, right_low = right
    return nn(left_high, right_high) + (nn(left_high, right_low) + nn(left_low, right_high))


def shampoo_kernel(
    scale, grad_ref, weight_ref, left_ref, right_ref,
    out_grad_ref, left_new_ref, right_new_ref, new_weight_ref, root_ref, power_ref,
):
    count, edge = weight_ref.shape[1], weight_ref.shape[2]
    row = lax.broadcasted_iota(jnp.int32, (edge, edge), 0)
    column = lax.broadcasted_iota(jnp.int32, (edge, edge), 1)
    identity = (row == column).astype(F32)
    whole = grad_ref[0] * scale
    for block in range(count):
        grad = whole[:, edge * block : edge * block + edge]
        out_grad_ref[0, block] = grad
        high, low = split(grad)
        high_t, low_t = split(jnp.transpose(grad))
        for kind, (old_ref, new_ref, one, two) in enumerate(
            (
                (left_ref, left_new_ref, (high, low), (high_t, low_t)),
                (right_ref, right_new_ref, (high_t, low_t), (high, low)),
            )
        ):
            new = 0.5 * old_ref[0, block] + 0.5 * product(one, two)
            new_ref[0, block] = new
            squares = jnp.sum(jnp.sum(new * new, axis=1, keepdims=True), axis=0, keepdims=True)
            factor = 2.5 * lax.rsqrt(squares)
            root_ref[2 * block + kind] = jnp.sqrt(jnp.sqrt(factor)) * identity
            power_ref[2 * block + kind] = factor * new

    def iteration(_, carry):
        for index in range(2 * count):
            power = power_ref[index]
            middle = split((5.0 * identity - power) * 0.25)
            root_ref[index] = product(split(root_ref[index]), middle)
            square = split(product(middle, middle))
            fourth = split(product(square, square))
            power_ref[index] = product(fourth, split(power))
        return carry

    lax.fori_loop(0, ITERS, iteration, 0)
    for block in range(count):
        grad = split(out_grad_ref[0, block])
        step = product(split(root_ref[2 * block]), grad)
        step = product(split(step), split(root_ref[2 * block + 1]))
        new_weight_ref[0, block] = weight_ref[0, block] - 0.25 * step


def shampoo(grads, weights, stat_left, stat_right, scale):
    groups, count, edge, _ = weights.shape
    block = pl.BlockSpec((1, count, edge, edge), lambda i: (i, 0, 0, 0))
    shape = jax.ShapeDtypeStruct(weights.shape, F32)
    return pl.pallas_call(
        lambda *refs: shampoo_kernel(scale, *refs),
        grid=(groups,),
        in_specs=[pl.BlockSpec((1, edge, count * edge), lambda i: (i, 0, 0)), block, block, block],
        out_specs=[block] * 4,
        out_shape=[shape] * 4,
        scratch_shapes=[
            pltpu.VMEM((2 * count, edge, edge), F32),
            pltpu.VMEM((2 * count, edge, edge), F32),
        ],
        compiler_params=pltpu.CompilerParams(vmem_limit_bytes=VMEM_LIMIT),
        name="shampoo",
    )(grads, weights, stat_left, stat_right)


def swap_heads(values):
    return lax.ppermute(values, "head", [(0, 1), (1, 0)])


def gather_slabs(weights):
    groups, count, edge, _ = weights.shape
    local = weights.astype(BF)
    if count * lax.axis_size("dp") != SLABS * (D // edge):
        raise ValueError("block count")
    if count * edge == D:
        local = local.transpose(0, 2, 1, 3).reshape(groups, edge, D)
        return lax.all_gather(local, "dp", axis=1)
    blocks = lax.all_gather(local, "dp", axis=1, tiled=True)
    blocks = blocks.reshape(groups, SLABS, D // edge, edge, edge)
    return blocks.transpose(0, 1, 3, 2, 4).reshape(groups, SLABS, edge, D)


def scatter_slabs(slabs, count, edge):
    groups = slabs.shape[0]
    if count * edge == D:
        return lax.psum_scatter(slabs, "dp", scatter_dimension=1)
    blocks = slabs.reshape(groups, SLABS, edge, D // edge, edge).transpose(0, 1, 3, 2, 4)
    blocks = blocks.reshape(groups, SLABS * (D // edge), edge, edge)
    owned = lax.psum_scatter(blocks, "dp", scatter_dimension=1, tiled=True)
    return owned.transpose(0, 2, 1, 3).reshape(groups, edge, count * edge)


def per_device(
    tokens,
    cotangent,
    token_counts,
    head_mask,
    norm_params,
    norm_state,
    weights,
    stat_left,
    stat_right,
):
    weights, stat_left, stat_right = weights[0], stat_left[0], stat_right[0]
    _, count, edge, _ = weights.shape
    images = tokens.shape[0] // S
    half = lax.axis_index("head")
    counts = lax.dynamic_slice_in_dim(token_counts, half * images, images)
    own_mask = lax.dynamic_slice_in_dim(head_mask, half * images, images)
    sent_mask = lax.dynamic_slice_in_dim(head_mask, (1 - half) * images, images)
    mask = jnp.concatenate([own_mask, swap_heads(sent_mask)], axis=1)
    mask_lanes = jnp.repeat(mask.astype(F32), HEAD_DIM, axis=1)[:, None, :]

    own = gather_slabs(weights)
    other = swap_heads(own)
    prob, qkv, out, middle, wqkv, wo = attn_forward(
        counts, tokens, mask_lanes, norm_params, own[0], other[0]
    )
    block_out, middle_grad, up_grad, down_grad, norm_two = mlp(
        middle, cotangent, norm_params, own[1], other[1], own[2], other[2]
    )
    input_grad, early_grad, norm_one = attn_backward(
        tokens, middle_grad, prob, qkv, out, mask_lanes, norm_params, wqkv, wo
    )
    all_grads = jnp.stack([early_grad, up_grad, down_grad])
    received = swap_heads(all_grads[:, 1].astype(BF))
    summed = (all_grads[:, 0] + received.astype(F32)).astype(BF)
    owned = scatter_slabs(summed, count, edge).astype(F32)
    norm_total = lax.psum(jnp.concatenate([norm_one, norm_two], axis=0), ("dp", "head"))
    token_total = tokens.shape[0] * lax.axis_size("dp") * lax.axis_size("head")
    scale = 1.0 / math.sqrt(token_total)
    grads, left_new, right_new, new_weights = shampoo(owned, weights, stat_left, stat_right, scale)
    norm_grads = norm_total * scale
    state_new = 0.5 * norm_state + 0.5 * norm_grads * norm_grads
    norm_new = norm_params - 0.2 * norm_grads / jnp.sqrt(state_new)
    return (
        block_out,
        input_grad,
        grads[None],
        left_new[None],
        right_new[None],
        new_weights[None],
        norm_grads,
        state_new,
        norm_new,
    )


def solution(mesh):
    blocks = P("head", None, "dp", None, None)
    rows = P(("dp", "head"), None)
    return jax.shard_map(
        per_device,
        mesh=mesh,
        in_specs=(rows, rows, P("dp"), P("dp", "head"), P(), P(), blocks, blocks, blocks),
        out_specs=(rows, rows, blocks, blocks, blocks, blocks, P(), P(), P()),
        check_vma=False,
    )
```

time: 559 us -> 432 us (0.77); the launches traced: 549 us -> 431 us
  Pallas kernels: 0 us -> 208 us
  matrix products: 152 us -> 0 us
  local copies, waits for them, and re-layouts: 88.5 us -> 8.02 us
  waiting for transfers between devices: 216 us -> 154 us
  other arithmetic: 35.9 us -> 7.19 us
    pallas_call x0 -> x4, Pallas kernels: none -> 208 us  [the longest x1 145 us: shampoo(): pl.pallas_call(lambda *refs: shampoo_kernel(scale, *refs), grid=(groups,)...]
    dot_general x80 -> x0, matrix products: 152 us -> none  [the longest x62 49.4 us: batched(): jnp.einsum('...ij,...jk->...ik', left, right, precision=lax.Precision.HIG...]
    unnamed x11 -> x2, waiting for transfers between devices: 87.3 us -> 0.03 us
    reduce_scatter x4 -> x1, waiting for transfers between devices: 31.2 us -> 85.4 us  [scatter_slabs(): return lax.psum_scatter(slabs, 'dp', scatter_dimension=1)]
    all_gather x5 -> x1, waiting for transfers between devices: 97.1 us -> 63.6 us  [gather_slabs(): return lax.all_gather(local, 'dp', axis=1)]
    unnamed x105 -> x12, local copies, waits for them, and re-layouts: 27.9 us -> 0.03 us
    reshape x12 -> x0, local copies, waits for them, and re-layouts: 27.6 us -> none  [the longest x4 9.91 us: pack(): shaped = matrix.reshape(row_count // edge, edge, col_count // edge, edge)]
    reduce_sum x7 -> x0, other arithmetic: 13 us -> none  [the longest x2 5.96 us: norm_backward(): jnp.sum(grad_out * normed, axis=0)]
  transfers between devices with their start and end apart: 10 -> 5, of which waited for: 7 -> 4; matrix products, arithmetic and copies ran while one was open for 24% -> 1% of each run, Pallas kernels for 0% -> 0%
where the time goes in v1:
time: 432 us; the launch traced here: 431 us
  Pallas kernels  208 us (48%)
  waiting for transfers between devices  154 us (36%)
  blocking collectives  39.3 us (9%)
  between operations  14.2 us (3%)
  local copies, waits for them, and re-layouts  8.02 us (2%)
  other arithmetic  7.19 us (2%)
    pallas_call x1, Pallas kernels, shampoo(): pl.pallas_call(lambda *refs: shampoo_kernel(scale, *refs), grid=(groups,)...  145 us
    reduce_scatter x1, waiting for transfers between devices, scatter_slabs(): return lax.psum_scatter(slabs, 'dp', scatter_dimension=1)  85.4 us
    all_gather x1, waiting for transfers between devices, gather_slabs(): return lax.all_gather(local, 'dp', axis=1)  63.6 us
    psum x1, blocking collectives, per_device(): lax.psum(jnp.concatenate([norm_one, norm_two], axis=0), ('dp', 'head'))  39.3 us
    pallas_call x1, Pallas kernels, mlp(): pl.pallas_call(mlp_kernel, grid=(rows // S,), in_specs=[tile, tile, pl.Bl...  27.5 us
    pallas_call x1, Pallas kernels, attn_backward(): pl.pallas_call(attn_backward_kernel, grid=(images,), in_specs=[tile, tile...  21.3 us
    pallas_call x1, Pallas kernels, attn_forward(): pl.pallas_call(attn_forward_kernel, grid=(images,), in_specs=[pl.BlockSpe...  14.7 us
  transfers between devices with their start and end apart: 5, of which 4 were waited for; matrix products, arithmetic and copies ran while one was open for 1% of the time, Pallas kernels for 0%

profile of v1, /device:TPU:0, one launch (start us, length us, event | category | flops | bytes accessed | tf_op | source)
XLA Modules:
  0.0 431.2 jit_solution(9520845083854734813)
XLA Ops:
  7.2 1.1 convert_bitcast_fusion
  8.4 0.9 all_gather_reshape.3
  9.3 63.6 %all-gather.2.cloned.1.call-done = bf16[3,16,48,384]{3,2,1,0:T(8,128)(2,1)} async-done(((bf16[3,1,48,384]{3,2,1,0:T(8,128)(2,1)}), bf16[3,16,48,384]{3,2,1,0:T(8,128)(2,1)}) %all-gather.2.cloned.1.call-update) | async-done | bytes 1769488 | tf_op jit(solution)/shard_map/all_gather | solution.py:408
  73.0 0.8 constant_dynamic-slice_fusion.1
  73.8 0.5 collective-permute-start
  74.3 1.2 dynamic_slice.9.counts_ref
  75.5 1.1 collective-permute-done
  76.7 0.1 copy.19
  76.8 0.7 broadcast_in_dim_reshape.3.mask_ref
  77.5 2.7 slice_bitcast_fusion.2
  80.2 1.3 slice_bitcast_fusion.1
  81.5 14.7 %attn_forward.1 = (bf16[6,3,512,256]{3,2,1,0:T(8,128)(2,1)}, bf16[1536,1152]{1,0:T(8,128)(2,1)}, bf16[1536,384]{1,0:T(8,128)(2,1)}, f32[1536,384]{1,0:T(8,128)},...) custom-call(s32[6]{0:T(128)} %dynamic_slice.9.counts_ref, bf16[1536,384]{1,0:T(8,128)(2,1)} %x_ref.3, ...), custom_call_target="tpu_custom_call" | custom-call | tf_op jit(solution)/shard_map/attn_forward/pallas_call | solution.py:117
  96.1 27.5 %mlp.1 = (f32[1536,384]{1,0:T(8,128)}, f32[1536,384]{1,0:T(8,128)}, f32[2,16,48,384]{3,2,1,0:T(8,128)}, f32[2,16,48,384]{3,2,1,0:T(8,128)}, f32[2,384]{1,0:T(2,128)}) custom-call(f32[1536,384]{1,0:T(8,128)} %get-tuple-element.27.middle_ref, bf16[1536,384]{1,0:T(8,128)(2,1)} %cot_ref.1, f32[4,384]{1,0:T(4,128)} %norm_ref.5, ...), custom_call_target="tpu_custom_call" | custom-call | tf_op jit(solution)/shard_map/mlp/pallas_call | solution.py:198
  123.6 21.3 %attn_backward.1 = (f32[1536,384]{1,0:T(8,128)}, f32[2,16,48,384]{3,2,1,0:T(8,128)}, f32[2,384]{1,0:T(2,128)}) custom-call(bf16[1536,384]{1,0:T(8,128)(2,1)} %x_ref.3, f32[1536,384]{1,0:T(8,128)} %get-tuple-element.29.grad_ref, bf16[6,3,512,256]{3,2,1,0:T(8,128)(2,1)} %get-tuple-element.30.prob_ref, bf16[1536,1152]{1,0:T(8,128)(2,1)} %get-tuple-element.31.qkv_ref, ...), custom_call_target="tpu_custom_call" | custom-call | tf_op jit(solution)/shard_map/attn_backward/pallas_call | solution.py:288
  144.9 2.1 pad_maximum_fusion
  147.0 0.2 fusion.2
  147.3 0.2 collective-permute-start.2
  147.5 3.5 collective-permute-done.2
  151.0 1.7 fusion.1
  152.8 39.3 %psum.7 = f32[4,384]{1,0:T(4,128)S(1)} all-reduce(f32[4,384]{1,0:T(4,128)S(1)} %pad_maximum_fusion.1), channel_id=1, replica_groups=mesh['dp'=16,'head'=2] {'dp','head'}, use_global_device_ids=true, to_apply=%region_1.0 | all-reduce | flops 1536 | bytes 12288 | tf_op jit(solution)/shard_map/psum | solution.py:460
  192.2 0.6 multiply_subtract_fusion
  192.8 85.4 %reduce-scatter.2.cloned.1.call-done = bf16[3,1,48,384]{3,2,0,1:T(8,128)(2,1)} async-done(((bf16[3,16,48,384]{3,2,0,1:T(8,128)(2,1)}), bf16[3,1,48,384]{3,2,0,1:T(8,128)(2,1)}) %reduce-scatter.2.cloned.1.call-update) | async-done | bytes 110608 | tf_op jit(solution)/shard_map/reduce_scatter | solution.py:417
  278.2 1.6 bitcast_convert_fusion.refs_0_
  279.8 144.6 %shampoo.1 = (f32[3,8,48,48]{3,2,1,0:T(8,128)}, f32[3,8,48,48]{3,2,1,0:T(8,128)}, f32[3,8,48,48]{3,2,1,0:T(8,128)}, f32[3,8,48,48]{3,2,1,0:T(8,128)}) custom-call(f32[3,48,384]{2,1,0:T(8,128)} %bitcast_convert_fusion.refs_0_, f32[3,8,48,48]{3,2,1,0:T(8,128)} %bitcast.42, f32[3,8,48,48]{3,2,1,0:T(8,128)} %bitcast.43, f32[3,8,48,48]{3,2,1,0:T(8,128)} %bitcast.44), custom_call_target="tpu_custom_call" | custom-call | tf_op jit(solution)/shard_map/shampoo/pallas_call | solution.py:382
  (22 shorter events, 0.3 us)
Async XLA Ops:
  7.2 65.8 %all-gather.2.cloned.1.call-start = ((), (), s32[]{:S(2)}) async-start(), calls=%async_computation.1 | async-start | bytes 1880064 | tf_op jit(solution)/shard_map/all_gather | solution.py:408
  9.3 268.9 %reduce-scatter.2.cloned.1.call-start = ((), (), s32[]{:S(2)}) async-start(), calls=%async_computation.2 | async-start | bytes 1880064 | tf_op jit(solution)/shard_map/reduce_scatter | solution.py:417
  73.0 7.2 %collective-permute-start.1 = (bf16[3,16,48,384]{3,2,1,0:T(8,128)(2,1)}, bf16[3,16,48,384]{3,2,1,0:T(8,128)(2,1)S(1)}, u32[]{:S(2)}, u32[]{:S(2)}) collective-permute-start(bf16[3,16,48,384]{3,2,1,0:T(8,128)(2,1)} %all-gather.2.cloned.1.call-done), channel_id=1, source_target_pairs={{0,1},{1,0},{2,3},{3,2},{4,5},{5,4},{6,7},{7,6},{8,9},{9,8},{10,11... | collective-permute-start | bytes 5308424 | tf_op jit(solution)/shard_map/ppermute | solution.py:398
  73.8 2.9 collective-permute-start
  123.6 21.3 %copy-start = (f32[2,16,48,384]{3,2,1,0:T(8,128)S(1)}, f32[2,16,48,384]{3,2,1,0:T(8,128)}, u32[]{:S(2)}) copy-start(f32[2,16,48,384]{3,2,1,0:T(8,128)} %get-tuple-element.37) | copy-start | bytes 7077892
  123.6 21.3 %copy-start.1 = (f32[2,16,48,384]{3,2,1,0:T(8,128)S(1)}, f32[2,16,48,384]{3,2,1,0:T(8,128)}, u32[]{:S(2)}) copy-start(f32[2,16,48,384]{3,2,1,0:T(8,128)} %get-tuple-element.38) | copy-start | bytes 7077892
  147.2 5.6 %copy-start.4 = (f32[2,384]{1,0:T(2,128)S(1)}, f32[2,384]{1,0:T(2,128)}, u32[]{:S(2)}) copy-start(f32[2,384]{1,0:T(2,128)} %get-tuple-element.44) | copy-start | bytes 9220
  147.2 5.6 %copy-start.5 = (f32[2,384]{1,0:T(2,128)S(1)}, f32[2,384]{1,0:T(2,128)}, u32[]{:S(2)}) copy-start(f32[2,384]{1,0:T(2,128)} %get-tuple-element.43) | copy-start | bytes 9220
  147.2 44.9 %copy-start.2 = (f32[4,384]{1,0:T(4,128)S(1)}, f32[4,384]{1,0:T(4,128)}, u32[]{:S(2)}) copy-start(f32[4,384]{1,0:T(4,128)} %norm_ref.5) | copy-start | bytes 18436
  147.3 44.9 %copy-start.3 = (f32[4,384]{1,0:T(4,128)S(1)}, f32[4,384]{1,0:T(4,128)}, u32[]{:S(2)}) copy-start(f32[4,384]{1,0:T(4,128)} %param.14) | copy-start | bytes 18436
  147.3 3.8 collective-permute-start.2
Sparse Core Ops, SparseCore 0:
  11.3 61.6 all-gather.1
  152.9 125.2 reduce-scatter.1

commit v2 on v1

--- a/solution.py
+++ b/solution.py
@@ -5,7 +5,7 @@
 from jax import lax
 from jax.experimental import pallas as pl
 from jax.experimental.pallas import tpu as pltpu
-from jax.sharding import PartitionSpec as P
+from jax.sharding import Mesh, PartitionSpec as P
 
 D = 384
 HEAD_DIM = 64
@@ -16,6 +16,9 @@
 PAIRS = D // PAIR
 HALF = D // 2
 SLABS = 16
+INNER = 4
+PACK = 4
+WIDE = 64
 ROOT_HALF = 0.7071067811865476
 DENSITY_FACTOR = 0.3989422804014327
 BF = jnp.bfloat16
@@ -52,6 +55,10 @@
     return grad_in, jnp.concatenate([gain_grad, shift_grad], axis=0)
 
 
+def slab_at(owner):
+    return (owner % INNER) * (SLABS // INNER) + owner // INNER
+
+
 def lane_halves():
     lane = lax.broadcasted_iota(jnp.int32, (1, PAIR), 1)
     first = (lane < HEAD_DIM).astype(BF)
@@ -76,7 +83,7 @@
                 pieces = []
                 for ref in slabs:
                     slab, side = divmod(3 * row + part, 2)
-                    pieces.append(ref[slab][:, side * HALF : (side + 1) * HALF])
+                    pieces.append(ref[slab_at(slab)][:, side * HALF : (side + 1) * HALF])
                 joined = jnp.concatenate(pieces, axis=1)
                 if part == 0:
                     joined = joined * 0.125
@@ -84,7 +91,7 @@
         for side, ref in enumerate(slabs):
             for row in range(HALF // 48):
                 start = side * HALF + 48 * row
-                wo_ref[start : start + 48, :] = ref[12 + row]
+                wo_ref[start : start + 48, :] = ref[slab_at(12 + row)]
 
     x = x_ref[...].astype(F32)
     normed, _ = normalize(x)
@@ -142,20 +149,23 @@
             jax.ShapeDtypeStruct((D, D), BF),
         ],
         compiler_params=pltpu.CompilerParams(vmem_limit_bytes=VMEM_LIMIT),
+        cost_estimate=pl.CostEstimate(
+            flops=rows * D * (8 * D + 16 * S), bytes_accessed=16 << 20, transcendentals=rows * 6 * S
+        ),
         name="attn_forward",
     )(counts, tokens, mask_lanes, norm_params, own, other)
 
 
 def mlp_kernel(
-    middle_ref, cot_ref, norm_ref, up_own_ref, up_other_ref, down_own_ref, down_other_ref,
-    out_ref, grad_ref, up_grad_ref, down_grad_ref, norm_grad_ref,
+    middle_ref, cot_ref, norm_ref, own_ref, other_ref,
+    out_ref, grad_ref, own_grad_ref, sent_grad_ref, norm_grad_ref, other_grad_ref,
 ):
     step = pl.program_id(0)
 
     @pl.when(step == 0)
     def _():
-        up_grad_ref[...] = jnp.zeros_like(up_grad_ref)
-        down_grad_ref[...] = jnp.zeros_like(down_grad_ref)
+        own_grad_ref[...] = jnp.zeros_like(own_grad_ref)
+        other_grad_ref[...] = jnp.zeros_like(other_grad_ref)
         norm_grad_ref[...] = jnp.zeros_like(norm_grad_ref)
 
     middle = middle_ref[...]
@@ -164,12 +174,12 @@
     cot = cot_ref[...]
     total = middle
     back = None
-    for side, (up_ref, down_ref) in enumerate(
-        ((up_own_ref, down_own_ref), (up_other_ref, down_other_ref))
-    ):
+    for ref, grads in ((own_ref, own_grad_ref), (other_ref, other_grad_ref)):
         for part in range(2):
-            up = jnp.concatenate([up_ref[2 * r + part] for r in range(8)], axis=0)
-            down = jnp.concatenate([down_ref[8 * part + r] for r in range(8)], axis=0)
+            up_at = [slab_at(2 * r + part) for r in range(8)]
+            down_at = [slab_at(8 * part + r) for r in range(8)]
+            up = jnp.concatenate([ref[at, 0] for at in up_at], axis=0)
+            down = jnp.concatenate([ref[at, 1] for at in down_at], axis=0)
             pre = nn(rows, up)
             cumulative = 0.5 * (1.0 + lax.erf(pre * ROOT_HALF))
             density = jnp.exp(-0.5 * pre * pre) * DENSITY_FACTOR
@@ -180,8 +190,8 @@
             down_part = tn(act, cot)
             up_part = tn(rows, pre_grad)
             for r in range(8):
-                down_grad_ref[side, 8 * part + r] += down_part[48 * r : 48 * r + 48]
-                up_grad_ref[side, 2 * r + part] += up_part[48 * r : 48 * r + 48]
+                grads[up_at[r], 0] += up_part[48 * r : 48 * r + 48]
+                grads[down_at[r], 1] += down_part[48 * r : 48 * r + 48]
             term = nt(pre_grad, up)
             back = term if back is None else back + term
     out_ref[...] = total
@@ -189,32 +199,40 @@
     norm_grad_ref[...] += norm_part
     grad_ref[...] = cot.astype(F32) + grad_in
 
-
-def mlp(middle, cotangent, norm_params, up_own, up_other, down_own, down_other):
+    @pl.when(step == pl.num_programs(0) - 1)
+    def _():
+        sent_grad_ref[...] = other_grad_ref[...].astype(BF)
+
+
+def mlp(middle, cotangent, norm_params, own, other):
     rows = middle.shape[0]
-    slab = pl.BlockSpec((SLABS, 48, D), lambda i: (0, 0, 0))
+    slabs = (SLABS, 2, 48, D)
+    slab = pl.BlockSpec(slabs, lambda i: (0, 0, 0, 0))
     tile = pl.BlockSpec((S, D), lambda i: (i, 0))
-    grad = pl.BlockSpec((2, SLABS, 48, D), lambda i: (0, 0, 0, 0))
     return pl.pallas_call(
         mlp_kernel,
         grid=(rows // S,),
-        in_specs=[tile, tile, pl.BlockSpec((4, D), lambda i: (0, 0)), slab, slab, slab, slab],
-        out_specs=[tile, tile, grad, grad, pl.BlockSpec((2, D), lambda i: (0, 0))],
+        in_specs=[tile, tile, pl.BlockSpec((4, D), lambda i: (0, 0)), slab, slab],
+        out_specs=[tile, tile, slab, slab, pl.BlockSpec((2, D), lambda i: (0, 0))],
         out_shape=[
             jax.ShapeDtypeStruct((rows, D), F32),
             jax.ShapeDtypeStruct((rows, D), F32),
-            jax.ShapeDtypeStruct((2, SLABS, 48, D), F32),
-            jax.ShapeDtypeStruct((2, SLABS, 48, D), F32),
+            jax.ShapeDtypeStruct(slabs, F32),
+            jax.ShapeDtypeStruct(slabs, BF),
             jax.ShapeDtypeStruct((2, D), F32),
         ],
+        scratch_shapes=[pltpu.VMEM(slabs, F32)],
         compiler_params=pltpu.CompilerParams(vmem_limit_bytes=VMEM_LIMIT),
+        cost_estimate=pl.CostEstimate(
+            flops=12 * rows * D * MLP, bytes_accessed=20 << 20, transcendentals=2 * rows * MLP
+        ),
         name="mlp",
-    )(middle, cotangent, norm_params, up_own, up_other, down_own, down_other)
+    )(middle, cotangent, norm_params, own, other)
 
 
 def attn_backward_kernel(
     x_ref, grad_ref, prob_ref, qkv_ref, out_ref, mask_ref, norm_ref, wqkv_ref, wo_ref,
-    in_grad_ref, slab_grad_ref, norm_grad_ref, dqkv_ref, wqkv_grad_ref, wo_grad_ref,
+    in_grad_ref, own_grad_ref, sent_grad_ref, norm_grad_ref, dqkv_ref, wqkv_grad_ref, wo_grad_ref,
 ):
     step = pl.program_id(0)
 
@@ -266,25 +284,27 @@
 
     @pl.when(step == pl.num_programs(0) - 1)
     def _():
-        for side in range(2):
+        for side, slab_grads in enumerate((own_grad_ref, sent_grad_ref)):
             for slab in range(12):
                 pieces = []
                 for unit in (2 * slab, 2 * slab + 1):
                     row, part = divmod(unit, 3)
-                    start = D * part + HALF * side
                     piece = wqkv_grad_ref[48 * row : 48 * row + 48, D * part : D * part + D]
                     piece = piece[:, HALF * side : HALF * side + HALF]
                     pieces.append(piece * 0.125 if part == 0 else piece)
-                slab_grad_ref[side, slab] = jnp.concatenate(pieces, axis=1)
+                joined = jnp.concatenate(pieces, axis=1)
+                slab_grads[slab_at(slab)] = joined.astype(slab_grads.dtype)
             for row in range(HALF // 48):
                 start = HALF * side + 48 * row
-                slab_grad_ref[side, 12 + row] = wo_grad_ref[start : start + 48, :]
+                joined = wo_grad_ref[start : start + 48, :]
+                slab_grads[slab_at(12 + row)] = joined.astype(slab_grads.dtype)
 
 
 def attn_backward(tokens, grad, prob, qkv, out, mask_lanes, norm_params, wqkv, wo):
     rows = tokens.shape[0]
     images = rows // S
     tile = pl.BlockSpec((S, D), lambda i: (i, 0))
+    slab = pl.BlockSpec((SLABS, 48, D), lambda i: (0, 0, 0))
     return pl.pallas_call(
         attn_backward_kernel,
         grid=(images,),
@@ -301,12 +321,14 @@
         ],
         out_specs=[
             tile,
-            pl.BlockSpec((2, SLABS, 48, D), lambda i: (0, 0, 0, 0)),
+            slab,
+            slab,
             pl.BlockSpec((2, D), lambda i: (0, 0)),
         ],
         out_shape=[
             jax.ShapeDtypeStruct((rows, D), F32),
-            jax.ShapeDtypeStruct((2, SLABS, 48, D), F32),
+            jax.ShapeDtypeStruct((SLABS, 48, D), F32),
+            jax.ShapeDtypeStruct((SLABS, 48, D), BF),
             jax.ShapeDtypeStruct((2, D), F32),
         ],
         scratch_shapes=[
@@ -315,6 +337,9 @@
             pltpu.VMEM((D, D), F32),
         ],
         compiler_params=pltpu.CompilerParams(vmem_limit_bytes=VMEM_LIMIT),
+        cost_estimate=pl.CostEstimate(
+            flops=rows * D * (16 * D + 32 * S), bytes_accessed=20 << 20, transcendentals=0
+        ),
         name="attn_backward",
     )(tokens, grad, prob, qkv, out, mask_lanes, norm_params, wqkv, wo)
 
@@ -327,98 +352,180 @@
 def product(left, right):
     left_high, left_low = left
     right_high, right_low = right
-    return nn(left_high, right_high) + (nn(left_high, right_low) + nn(left_low, right_high))
+    both = nn(jnp.concatenate([left_high, left_low], axis=0), right_high)
+    edge = left_high.shape[0]
+    return both[:edge] + (both[edge:] + nn(left_high, right_low))
 
 
 def shampoo_kernel(
-    scale, grad_ref, weight_ref, left_ref, right_ref,
-    out_grad_ref, left_new_ref, right_new_ref, new_weight_ref, root_ref, power_ref,
+    scale, grad_ref, weight_ref, left_ref, right_ref, *refs
 ):
+    out_grad_ref, left_new_ref, right_new_ref, new_weight_ref, root_ref, power_ref = refs[-6:]
     count, edge = weight_ref.shape[1], weight_ref.shape[2]
-    row = lax.broadcasted_iota(jnp.int32, (edge, edge), 0)
-    column = lax.broadcasted_iota(jnp.int32, (edge, edge), 1)
-    identity = (row == column).astype(F32)
+    pack = min(PACK, count)
+    width = pack * WIDE
+    row = lax.broadcasted_iota(jnp.int32, (WIDE, width), 0)
+    lane = lax.broadcasted_iota(jnp.int32, (WIDE, width), 1)
+    identity = (lane % WIDE == row).astype(F32)
+    row = lax.broadcasted_iota(jnp.int32, (width, width), 0)
+    lane = lax.broadcasted_iota(jnp.int32, (width, width), 1)
+    same = (row // WIDE == lane // WIDE).astype(BF)
+    lane = lax.broadcasted_iota(jnp.int32, (1, width), 1)
+
+    def wide(block):
+        block = jnp.concatenate([block, jnp.zeros((edge, WIDE - edge), block.dtype)], axis=1)
+        return jnp.concatenate([block, jnp.zeros((WIDE - edge, WIDE), block.dtype)], axis=0)
+
+    def spread(pieces):
+        return tuple(jnp.concatenate([piece] * pack, axis=0) * same for piece in pieces)
+
+    def cut(packed, index):
+        return packed[:edge, WIDE * index : WIDE * index + edge]
+
     whole = grad_ref[0] * scale
-    for block in range(count):
-        grad = whole[:, edge * block : edge * block + edge]
-        out_grad_ref[0, block] = grad
-        high, low = split(grad)
-        high_t, low_t = split(jnp.transpose(grad))
-        for kind, (old_ref, new_ref, one, two) in enumerate(
+    packs = count // pack
+    grads = []
+    for number in range(packs):
+        blocks = []
+        for index in range(pack):
+            block = pack * number + index
+            grad = whole[:, edge * block : edge * block + edge]
+            out_grad_ref[0, block] = grad
+            blocks.append(wide(grad))
+        grad = jnp.concatenate(blocks, axis=1)
+        grad_t = jnp.concatenate([jnp.transpose(block) for block in blocks], axis=1)
+        one, two = split(grad), split(grad_t)
+        one_diagonal, two_diagonal = spread(one), spread(two)
+        grads.append(one_diagonal)
+        for kind, (old_ref, new_ref, gram) in enumerate(
             (
-                (left_ref, left_new_ref, (high, low), (high_t, low_t)),
-                (right_ref, right_new_ref, (high_t, low_t), (high, low)),
+                (left_ref, left_new_ref, product(one, two_diagonal)),
+                (right_ref, right_new_ref, product(two, one_diagonal)),
             )
         ):
-            new = 0.5 * old_ref[0, block] + 0.5 * product(one, two)
-            new_ref[0, block] = new
-            squares = jnp.sum(jnp.sum(new * new, axis=1, keepdims=True), axis=0, keepdims=True)
-            factor = 2.5 * lax.rsqrt(squares)
-            root_ref[2 * block + kind] = jnp.sqrt(jnp.sqrt(factor)) * identity
-            power_ref[2 * block + kind] = factor * new
+            old = jnp.concatenate([wide(old_ref[0, pack * number + i]) for i in range(pack)], axis=1)
+            new = 0.5 * old + 0.5 * gram
+            for index in range(pack):
+                new_ref[0, pack * number + index] = cut(new, index)
+            columns = jnp.sum(new * new, axis=0, keepdims=True)
+            squares = jnp.zeros((1, width), F32)
+            for index in range(pack):
+                inside = lane // WIDE == index
+                part = jnp.sum(jnp.where(inside, columns, 0.0), axis=1, keepdims=True)
+                squares = jnp.where(inside, part, squares)
+            factor = 2.5 / jnp.sqrt(squares)
+            root_ref[2 * number + kind] = jnp.sqrt(jnp.sqrt(factor)) * identity
+            power_ref[2 * number + kind] = factor * new
 
     def iteration(_, carry):
-        for index in range(2 * count):
+        for index in range(2 * packs):
             power = power_ref[index]
             middle = split((5.0 * identity - power) * 0.25)
-            root_ref[index] = product(split(root_ref[index]), middle)
-            square = split(product(middle, middle))
-            fourth = split(product(square, square))
-            power_ref[index] = product(fourth, split(power))
+            right = spread(middle)
+            root_ref[index] = product(split(root_ref[index]), right)
+            square = split(product(middle, right))
+            fourth = split(product(square, spread(square)))
+            power_ref[index] = product(fourth, spread(split(power)))
         return carry
 
     lax.fori_loop(0, ITERS, iteration, 0)
-    for block in range(count):
-        grad = split(out_grad_ref[0, block])
-        step = product(split(root_ref[2 * block]), grad)
-        step = product(split(step), split(root_ref[2 * block + 1]))
-        new_weight_ref[0, block] = weight_ref[0, block] - 0.25 * step
-
-
-def shampoo(grads, weights, stat_left, stat_right, scale):
-    groups, count, edge, _ = weights.shape
-    block = pl.BlockSpec((1, count, edge, edge), lambda i: (i, 0, 0, 0))
+    for number in range(packs):
+        step = product(split(root_ref[2 * number]), grads[number])
+        step = product(split(step), spread(split(root_ref[2 * number + 1])))
+        for index in range(pack):
+            block = pack * number + index
+            new_weight_ref[0, block] = weight_ref[0, block] - 0.25 * cut(step, index)
+
+
+def shampoo(grads, weights, stat_left, stat_right, scale, first, earlier=()):
+    groups, edge, _ = grads.shape
+    _, count, _, _ = weights.shape
+    packs = count // min(PACK, count)
+    width = min(PACK, count) * WIDE
+    block = pl.BlockSpec((1, count, edge, edge), lambda i: (i + first, 0, 0, 0))
     shape = jax.ShapeDtypeStruct(weights.shape, F32)
     return pl.pallas_call(
         lambda *refs: shampoo_kernel(scale, *refs),
         grid=(groups,),
-        in_specs=[pl.BlockSpec((1, edge, count * edge), lambda i: (i, 0, 0)), block, block, block],
+        in_specs=[
+            pl.BlockSpec((1, edge, count * edge), lambda i: (i, 0, 0)), block, block, block,
+            *[pl.BlockSpec(memory_space=pl.ANY) for _ in earlier],
+        ],
         out_specs=[block] * 4,
         out_shape=[shape] * 4,
         scratch_shapes=[
-            pltpu.VMEM((2 * count, edge, edge), F32),
-            pltpu.VMEM((2 * count, edge, edge), F32),
-        ],
+            pltpu.VMEM((2 * packs, WIDE, width), F32),
+            pltpu.VMEM((2 * packs, WIDE, width), F32),
+        ],
+        input_output_aliases={4 + i: i for i in range(len(earlier))},
         compiler_params=pltpu.CompilerParams(vmem_limit_bytes=VMEM_LIMIT),
+        cost_estimate=pl.CostEstimate(
+            flops=groups * (3 << 30), bytes_accessed=4 << 20, transcendentals=0
+        ),
         name="shampoo",
-    )(grads, weights, stat_left, stat_right)
+    )(grads, weights, stat_left, stat_right, *earlier)
 
 
 def swap_heads(values):
     return lax.ppermute(values, "head", [(0, 1), (1, 0)])
 
 
-def gather_slabs(weights):
-    groups, count, edge, _ = weights.shape
-    local = weights.astype(BF)
-    if count * lax.axis_size("dp") != SLABS * (D // edge):
-        raise ValueError("block count")
-    if count * edge == D:
-        local = local.transpose(0, 2, 1, 3).reshape(groups, edge, D)
-        return lax.all_gather(local, "dp", axis=1)
-    blocks = lax.all_gather(local, "dp", axis=1, tiled=True)
-    blocks = blocks.reshape(groups, SLABS, D // edge, edge, edge)
-    return blocks.transpose(0, 1, 3, 2, 4).reshape(groups, SLABS, edge, D)
-
-
-def scatter_slabs(slabs, count, edge):
-    groups = slabs.shape[0]
-    if count * edge == D:
-        return lax.psum_scatter(slabs, "dp", scatter_dimension=1)
-    blocks = slabs.reshape(groups, SLABS, edge, D // edge, edge).transpose(0, 1, 3, 2, 4)
-    blocks = blocks.reshape(groups, SLABS * (D // edge), edge, edge)
-    owned = lax.psum_scatter(blocks, "dp", scatter_dimension=1, tiled=True)
+def to_all(values, axis):
+    return lax.all_to_all(values, axis, 0, 0)
+
+
+def copies(values, number):
+    return jnp.broadcast_to(values[None], (number,) + values.shape)
+
+
+def gather_slabs(local):
+    groups, edge, _ = local.shape
+    slabs = local if groups > 1 else local[0]
+    slabs = to_all(copies(slabs, lax.axis_size("outer")), "outer")
+    slabs = to_all(copies(slabs, lax.axis_size("inner")), "inner")
+    return slabs.reshape((SLABS,) + slabs.shape[2:])
+
+
+def gather_blocks(local):
+    groups, _, edge, _ = local.shape
+    blocks = lax.all_gather(local, ("outer", "inner"), axis=1, tiled=True)
+    blocks = blocks.reshape(groups, SLABS // INNER, INNER, D // edge, edge, edge)
+    slabs = blocks.transpose(2, 1, 0, 4, 3, 5).reshape(SLABS, groups, edge, D)
+    return slabs if groups > 1 else slabs[:, 0]
+
+
+def scatter_blocks(slabs, count, edge):
+    groups = slabs.shape[1]
+    blocks = slabs.reshape(INNER, SLABS // INNER, groups, edge, D // edge, edge)
+    blocks = blocks.transpose(2, 1, 0, 4, 3, 5).reshape(groups, SLABS * (D // edge), edge, edge)
+    owned = lax.psum_scatter(blocks, ("outer", "inner"), scatter_dimension=1, tiled=True)
     return owned.transpose(0, 2, 1, 3).reshape(groups, edge, count * edge)
+
+
+def scatter_slabs(slabs):
+    groups = slabs.shape[1]
+    inner, outer = lax.axis_size("inner"), lax.axis_size("outer")
+    shape = (outer, groups, 48, D)
+    received = to_all(slabs.reshape((inner,) + shape), "inner")
+    partial = jnp.sum(received.astype(F32), axis=0).astype(BF)
+    return jnp.sum(to_all(partial, "outer").astype(F32), axis=0)
+
+
+def with_norms(slabs, norms):
+    high, low = split(norms)
+    rows = jnp.concatenate([high, low, jnp.zeros_like(high), jnp.zeros_like(high)], axis=0)
+    return jnp.concatenate([slabs, copies(rows, slabs.shape[0])], axis=1)
+
+
+def scatter_with_norms(slabs, norms):
+    inner, outer = lax.axis_size("inner"), lax.axis_size("outer")
+    sent = with_norms(slabs.reshape(inner, outer * 48, D), norms)
+    received = jnp.sum(to_all(sent, "inner").astype(F32), axis=0)
+    edge = outer * 48
+    norms = received[edge : edge + 4] + received[edge + 4 : edge + 8]
+    sent = with_norms(received[:edge].reshape(outer, 48, D).astype(BF), norms)
+    received = jnp.sum(to_all(sent, "outer").astype(F32), axis=0)
+    return received[None, :48], received[48:52] + received[52:56]
 
 
 def per_device(
@@ -434,6 +541,7 @@
 ):
     weights, stat_left, stat_right = weights[0], stat_left[0], stat_right[0]
     _, count, edge, _ = weights.shape
+    whole_slabs = count * edge == D
     images = tokens.shape[0] // S
     half = lax.axis_index("head")
     counts = lax.dynamic_slice_in_dim(token_counts, half * images, images)
@@ -442,25 +550,36 @@
     mask = jnp.concatenate([own_mask, swap_heads(sent_mask)], axis=1)
     mask_lanes = jnp.repeat(mask.astype(F32), HEAD_DIM, axis=1)[:, None, :]
 
-    own = gather_slabs(weights)
-    other = swap_heads(own)
+    local = weights.astype(BF)
+    if whole_slabs:
+        local = local.transpose(0, 2, 1, 3).reshape(-1, edge, D)
+        early, late = gather_slabs(local[:1]), gather_slabs(local[1:])
+    else:
+        early, late = gather_blocks(local[:1]), gather_blocks(local[1:])
     prob, qkv, out, middle, wqkv, wo = attn_forward(
-        counts, tokens, mask_lanes, norm_params, own[0], other[0]
+        counts, tokens, mask_lanes, norm_params, early, swap_heads(early)
     )
-    block_out, middle_grad, up_grad, down_grad, norm_two = mlp(
-        middle, cotangent, norm_params, own[1], other[1], own[2], other[2]
+    block_out, middle_grad, own_late, sent_late, norm_two = mlp(
+        middle, cotangent, norm_params, late, swap_heads(late)
     )
-    input_grad, early_grad, norm_one = attn_backward(
+    late_slabs = (own_late + swap_heads(sent_late).astype(F32)).astype(BF)
+    input_grad, own_early, sent_early, norm_one = attn_backward(
         tokens, middle_grad, prob, qkv, out, mask_lanes, norm_params, wqkv, wo
     )
-    all_grads = jnp.stack([early_grad, up_grad, down_grad])
-    received = swap_heads(all_grads[:, 1].astype(BF))
-    summed = (all_grads[:, 0] + received.astype(F32)).astype(BF)
-    owned = scatter_slabs(summed, count, edge).astype(F32)
-    norm_total = lax.psum(jnp.concatenate([norm_one, norm_two], axis=0), ("dp", "head"))
-    token_total = tokens.shape[0] * lax.axis_size("dp") * lax.axis_size("head")
-    scale = 1.0 / math.sqrt(token_total)
-    grads, left_new, right_new, new_weights = shampoo(owned, weights, stat_left, stat_right, scale)
+    early_slabs = (own_early + swap_heads(sent_early).astype(F32)).astype(BF)
+    norms = jnp.concatenate([norm_one, norm_two], axis=0)
+    if whole_slabs:
+        late_owned = scatter_slabs(late_slabs)
+        early_owned, norm_total = scatter_with_norms(early_slabs, norms + swap_heads(norms))
+    else:
+        late_owned = scatter_blocks(late_slabs, count, edge).astype(F32)
+        early_owned = scatter_blocks(early_slabs[:, None], count, edge).astype(F32)
+        norm_total = lax.psum(norms, ("outer", "inner", "head"))
+    devices = lax.axis_size("outer") * lax.axis_size("inner") * lax.axis_size("head")
+    scale = 1.0 / math.sqrt(tokens.shape[0] * devices)
+    state = (weights, stat_left, stat_right, scale)
+    results = shampoo(late_owned, *state, 1)
+    grads, left_new, right_new, new_weights = shampoo(early_owned, *state, 0, results)
     norm_grads = norm_total * scale
     state_new = 0.5 * norm_state + 0.5 * norm_grads * norm_grads
     norm_new = norm_params - 0.2 * norm_grads / jnp.sqrt(state_new)
@@ -478,12 +597,15 @@
 
 
 def solution(mesh):
-    blocks = P("head", None, "dp", None, None)
-    rows = P(("dp", "head"), None)
+    shape = (mesh.shape["dp"] // INNER, INNER, mesh.shape["head"])
+    split_mesh = Mesh(mesh.devices.reshape(shape), ("outer", "inner", "head"))
+    group = ("outer", "inner")
+    blocks = P("head", None, group, None, None)
+    rows = P(group + ("head",), None)
     return jax.shard_map(
         per_device,
-        mesh=mesh,
-        in_specs=(rows, rows, P("dp"), P("dp", "head"), P(), P(), blocks, blocks, blocks),
+        mesh=split_mesh,
+        in_specs=(rows, rows, P(group), P(group, "head"), P(), P(), blocks, blocks, blocks),
         out_specs=(rows, rows, blocks, blocks, blocks, blocks, P(), P(), P()),
         check_vma=False,
     )

time: 432 us -> 238 us (0.55)
  waiting for transfers between devices: 154 us -> 48.5 us
  Pallas kernels: 208 us -> 116 us
  starting transfers between devices: 0.8 us -> 27.6 us
  between operations: 14.2 us -> 0.84 us
  blocking collectives: 39.3 us -> 28.3 us
    pallas_call x1 -> x2, Pallas kernels: 145 us -> 52.2 us  [shampoo(): pl.pallas_call(lambda *refs: shampoo_kernel(scale, *refs), grid=(groups,)...]
    reduce_scatter x1 -> x0, waiting for transfers between devices: 85.4 us -> none  [scatter_slabs(): return lax.psum_scatter(slabs, 'dp', scatter_dimension=1)]
    all_gather x1 -> x0, waiting for transfers between devices: 63.6 us -> none  [gather_slabs(): return lax.all_gather(local, 'dp', axis=1)]
    all_to_all x0 -> x6, waiting for transfers between devices: none -> 46.9 us  [to_all(): return lax.all_to_all(values, axis, 0, 0)]
    psum x1 -> x0, blocking collectives: 39.3 us -> none  [per_device(): lax.psum(jnp.concatenate([norm_one, norm_two], axis=0), ('dp', 'head'))]
    all_to_all x0 -> x2, blocking collectives: none -> 28.3 us  [to_all(): return lax.all_to_all(values, axis, 0, 0)]
    all_to_all x0 -> x6, starting transfers between devices: none -> 26.1 us  [to_all(): return lax.all_to_all(values, axis, 0, 0)]
  transfers between devices with their start and end apart: 5 -> 12, of which waited for: 4 -> 8; matrix products, arithmetic and copies ran while one was open for 1% -> 3% of each run, Pallas kernels for 0% -> 6%
where the time goes in v2:
time: 238 us; the launch traced here: 237 us
  Pallas kernels  116 us (49%)
  waiting for transfers between devices  48.5 us (20%)
  blocking collectives  28.3 us (12%)
  starting transfers between devices  27.6 us (12%)
  other arithmetic  10.7 us (4%)
  local copies, waits for them, and re-layouts  5.39 us (2%)
    pallas_call x2, Pallas kernels, shampoo(): pl.pallas_call(lambda *refs: shampoo_kernel(scale, *refs), grid=(groups,)...  52.2 us
    all_to_all x6, waiting for transfers between devices, to_all(): return lax.all_to_all(values, axis, 0, 0)  46.9 us
    all_to_all x2, blocking collectives, to_all(): return lax.all_to_all(values, axis, 0, 0)  28.3 us
    pallas_call x1, Pallas kernels, mlp(): pl.pallas_call(mlp_kernel, grid=(rows // S,), in_specs=[tile, tile, pl.Bl...  27.8 us
    all_to_all x6, starting transfers between devices, to_all(): return lax.all_to_all(values, axis, 0, 0)  26.1 us
    pallas_call x1, Pallas kernels, attn_backward(): pl.pallas_call(attn_backward_kernel, grid=(images,), in_specs=[tile, tile...  21 us
    pallas_call x1, Pallas kernels, attn_forward(): pl.pallas_call(attn_forward_kernel, grid=(images,), in_specs=[pl.BlockSpe...  14.7 us
  transfers between devices with their start and end apart: 12, of which 8 were waited for; matrix products, arithmetic and copies ran while one was open for 3% of the time, Pallas kernels for 6%

profile of v2, /device:TPU:0, one launch (start us, length us, event | category | flops | bytes accessed | tf_op | source)
XLA Modules:
  0.0 237.0 jit_solution(9466175263392183407)
XLA Ops:
  0.6 1.1 convert_bitcast_fusion
  2.6 6.3 %all-to-all-start = ((bf16[4,48,384]{2,1,0:T(8,128)(2,1)}), bf16[4,48,384]{2,1,0:T(8,128)(2,1)S(1)}, u32[]{:S(2)}, u32[]{:S(2)}) async-start(bf16[4,48,384]{2,1,0:T(8,128)(2,1)} %broadcast_in_dim.59), calls=%async_computation | async-start | bytes 294912 | tf_op jit(solution)/shard_map/all_to_all | solution.py:474
  9.2 6.0 %all-to-all-done = bf16[4,48,384]{2,1,0:T(8,128)(2,1)S(1)} async-done(((bf16[4,48,384]{2,1,0:T(8,128)(2,1)}), bf16[4,48,384]{2,1,0:T(8,128)(2,1)S(1)}, u32[]{:S(2)}, u32[]{:S(2)}) %all-to-all-start) | async-done | bytes 147488 | tf_op jit(solution)/shard_map/all_to_all | solution.py:474
  15.2 11.7 %all_to_all.40 = bf16[4,2,48,384]{3,2,1,0:T(8,128)(2,1)S(1)} all-to-all(bf16[4,2,48,384]{3,2,1,0:T(8,128)(2,1)S(1)} %broadcast_in_dim.62), channel_id=1, replica_groups=mesh['outer'=4,'inner'=4,'head'=2] {'outer'}, dimensions={0} | all-to-all | bytes 589824 | tf_op jit(solution)/shard_map/all_to_all | solution.py:474
  27.0 16.6 %all_to_all.41 = bf16[4,4,2,48,384]{4,3,2,1,0:T(8,128)(2,1)S(1)} all-to-all(bf16[4,4,2,48,384]{4,3,2,1,0:T(8,128)(2,1)S(1)} %broadcast_in_dim.63), channel_id=1, replica_groups=mesh['outer'=4,'inner'=4,'head'=2] {'inner'}, dimensions={0} | all-to-all | bytes 2359296 | tf_op jit(solution)/shard_map/all_to_all | solution.py:474
  44.5 3.5 %all-to-all-start.1 = ((bf16[4,4,48,384]{3,2,1,0:T(8,128)(2,1)}), bf16[4,4,48,384]{3,2,1,0:T(8,128)(2,1)S(1)}, u32[]{:S(2)}, u32[]{:S(2)}) async-start(bf16[4,4,48,384]{3,2,1,0:T(8,128)(2,1)} %broadcast_in_dim.60), calls=%async_computation.1 | async-start | bytes 1179648 | tf_op jit(solution)/shard_map/all_to_all | solution.py:474
  48.1 6.9 %all-to-all-done.1 = bf16[4,4,48,384]{3,2,1,0:T(8,128)(2,1)S(1)} async-done(((bf16[4,4,48,384]{3,2,1,0:T(8,128)(2,1)}), bf16[4,4,48,384]{3,2,1,0:T(8,128)(2,1)S(1)}, u32[]{:S(2)}, u32[]{:S(2)}) %all-to-all-start.1) | async-done | bytes 589856 | tf_op jit(solution)/shard_map/all_to_all | solution.py:474
  57.8 14.7 %attn_forward.1 = (bf16[6,3,512,256]{3,2,1,0:T(8,128)(2,1)}, bf16[1536,1152]{1,0:T(8,128)(2,1)}, bf16[1536,384]{1,0:T(8,128)(2,1)}, f32[1536,384]{1,0:T(8,128)},...) custom-call(s32[6]{0:T(128)} %dynamic_slice.9.counts_ref, bf16[1536,384]{1,0:T(8,128)(2,1)} %x_ref.3, ...), custom_call_target="tpu_custom_call" | custom-call | flops 4227858432 | bytes 16777216 | tf_op jit(solution)/shard_map/attn_forward/pallas_call | solution.py:124
  72.5 1.0 copy-done.7
  73.5 27.8 %mlp.1 = (f32[1536,384]{1,0:T(8,128)}, f32[1536,384]{1,0:T(8,128)}, f32[16,2,48,384]{3,2,1,0:T(8,128)}, bf16[16,2,48,384]{3,2,1,0:T(8,128)(2,1)}, f32[2,384]{1,0:T(2,128)}) custom-call(f32[1536,384]{1,0:T(8,128)} %get-tuple-element.32.middle_ref, bf16[1536,384]{1,0:T(8,128)(2,1)} %cot_ref.1, f32[4,384]{1,0:T(4,128)} %norm_ref.5, ...), custom_call_target="tpu_custom_call" | custom-call | flops 10871635968 | bytes 20971520 | tf_op jit(solution)/shard_map/mlp/pallas_call | solution.py:212
  101.3 21.0 %attn_backward.1 = (f32[1536,384]{1,0:T(8,128)}, f32[16,48,384]{2,1,0:T(8,128)}, bf16[16,48,384]{2,1,0:T(8,128)(2,1)}, f32[2,384]{1,0:T(2,128)}) custom-call(bf16[1536,384]{1,0:T(8,128)(2,1)} %x_ref.3, f32[1536,384]{1,0:T(8,128)} %get-tuple-element.34.grad_ref, bf16[6,3,512,256]{3,2,1,0:T(8,128)(2,1)} %get-tuple-element.35.prob_ref, ...), custom_call_target="tpu_custom_call" | custom-call | flops 8455716864 | bytes 20971520 | tf_op jit(solution)/shard_map/attn_backward/pallas_call | solution.py:308
  125.2 1.4 add_convert_fusion.1
  127.5 3.6 %all-to-all-start.4 = ((bf16[4,208,384]{2,1,0:T(8,128)(2,1)}), bf16[4,208,384]{2,1,0:T(8,128)(2,1)S(1)}, u32[]{:S(2)}, u32[]{:S(2)}) async-start(bf16[4,208,384]{2,1,0:T(8,128)(2,1)} %pad_maximum_fusion), calls=%async_computation.4 | async-start | bytes 1277952 | tf_op jit(solution)/shard_map/all_to_all | solution.py:474
  131.5 9.6 %all-to-all-done.4 = bf16[4,208,384]{2,1,0:T(8,128)(2,1)S(1)} async-done(((bf16[4,208,384]{2,1,0:T(8,128)(2,1)}), bf16[4,208,384]{2,1,0:T(8,128)(2,1)S(1)}, u32[]{:S(2)}, u32[]{:S(2)}) %all-to-all-start.4) | async-done | bytes 639008 | tf_op jit(solution)/shard_map/all_to_all | solution.py:474
  142.0 4.4 %all-to-all-start.5 = ((bf16[4,64,384]{2,1,0:T(8,128)(2,1)}), bf16[4,64,384]{2,1,0:T(8,128)(2,1)S(1)}, u32[]{:S(2)}, u32[]{:S(2)}) async-start(bf16[4,64,384]{2,1,0:T(8,128)(2,1)} %pad_maximum_fusion.1), calls=%async_computation.5 | async-start | bytes 393216 | tf_op jit(solution)/shard_map/all_to_all | solution.py:474
  146.4 2.7 %add_convert_fusion = bf16[16,2,48,384]{3,2,1,0:T(8,128)(2,1)} fusion(f32[16,2,48,384]{3,2,1,0:T(8,128)S(1)} %copy-done, bf16[16,2,48,384]{3,2,1,0:T(8,128)(2,1)} %collective-permute-done.5), kind=kLoop, calls=%fused_computation | loop fusion | flops 1769472 | bytes 4718592 | tf_op jit(solution)/shard_map/convert_element_type | solution.py:565
  149.1 4.6 %all-to-all-done.5 = bf16[4,64,384]{2,1,0:T(8,128)(2,1)S(1)} async-done(((bf16[4,64,384]{2,1,0:T(8,128)(2,1)}), bf16[4,64,384]{2,1,0:T(8,128)(2,1)S(1)}, u32[]{:S(2)}, u32[]{:S(2)}) %all-to-all-start.5) | async-done | bytes 196640 | tf_op jit(solution)/shard_map/all_to_all | solution.py:474
  153.7 3.7 %all-to-all-start.6 = ((bf16[4,4,2,48,384]{4,3,2,1,0:T(8,128)(2,1)}), bf16[4,4,2,48,384]{4,3,2,1,0:T(8,128)(2,1)S(1)}, u32[]{:S(2)}, u32[]{:S(2)}) async-start(bf16[4,4,2,48,384]{4,3,2,1,0:T(8,128)(2,1)} %bitcast.9), calls=%async_computation.6 | async-start | bytes 2359296 | tf_op jit(solution)/shard_map/all_to_all | solution.py:474
  157.5 12.3 %all-to-all-done.6 = bf16[4,4,2,48,384]{4,3,2,1,0:T(8,128)(2,1)S(1)} async-done(((bf16[4,4,2,48,384]{4,3,2,1,0:T(8,128)(2,1)}), bf16[4,4,2,48,384]{4,3,2,1,0:T(8,128)(2,1)S(1)}, u32[]{:S(2)}, u32[]{:S(2)}) %all-to-all-start.6) | async-done | bytes 1179680 | tf_op jit(solution)/shard_map/all_to_all | solution.py:474
  169.9 0.9 reduce_sum.41
  170.8 4.6 %all-to-all-start.7 = ((bf16[4,2,48,384]{3,2,1,0:T(8,128)(2,1)}), bf16[4,2,48,384]{3,2,1,0:T(8,128)(2,1)S(1)}, u32[]{:S(2)}, u32[]{:S(2)}) async-start(bf16[4,2,48,384]{3,2,1,0:T(8,128)(2,1)} %reduce_sum.41), calls=%async_computation.7 | async-start | bytes 589824 | tf_op jit(solution)/shard_map/all_to_all | solution.py:474
  176.6 7.5 %all-to-all-done.7 = bf16[4,2,48,384]{3,2,1,0:T(8,128)(2,1)S(1)} async-done(((bf16[4,2,48,384]{3,2,1,0:T(8,128)(2,1)}), bf16[4,2,48,384]{3,2,1,0:T(8,128)(2,1)S(1)}, u32[]{:S(2)}, u32[]{:S(2)}) %all-to-all-start.7) | async-done | bytes 294944 | tf_op jit(solution)/shard_map/all_to_all | solution.py:474
  184.8 34.2 %shampoo.2 = (f32[3,8,48,48]{3,2,1,0:T(8,128)}, f32[3,8,48,48]{3,2,1,0:T(8,128)}, f32[3,8,48,48]{3,2,1,0:T(8,128)}, f32[3,8,48,48]{3,2,1,0:T(8,128)}) custom-call(f32[2,48,384]{2,1,0:T(8,128)} %convert_reduce_fusion.1.refs_0_, f32[3,8,48,48]{3,2,1,0:T(8,128)} %bitcast.25, f32[3,8,48,48]{3,2,1,0:T(8,128)} %bitcast.29, f32[3,8,48,48]{3,2,1,0:T(8,128)} %bitcast.31), custom_call_target="tpu_custom_call" | custom-call | flops 6442450944 | bytes 4194304 | tf_op jit(solution)/shard_map/shampoo/pallas_call | solution.py:447
  219.0 18.0 %shampoo.3 = (f32[3,8,48,48]{3,2,1,0:T(8,128)}, f32[3,8,48,48]{3,2,1,0:T(8,128)}, f32[3,8,48,48]{3,2,1,0:T(8,128)}, f32[3,8,48,48]{3,2,1,0:T(8,128)}) custom-call(f32[1,48,384]{2,1,0:T(8,128)} %slice_bitcast_fusion.refs_0_, f32[3,8,48,48]{3,2,1,0:T(8,128)} %bitcast.26, ...), custom_call_target="tpu_custom_call", output_to_operand_aliasing={{0}: (4, {}), {1}: (5, {}), {2}: (6, {}), {3}: (7, {})} | custom-call | flops 3221225472 | bytes 4194304 | tf_op jit(solution)/shard_map/shampoo/pallas_call | solution.py:447
  (62 shorter events, 12.1 us)
Async XLA Ops:
  2.6 12.6 %all-to-all-start = ((bf16[4,48,384]{2,1,0:T(8,128)(2,1)}), bf16[4,48,384]{2,1,0:T(8,128)(2,1)S(1)}, u32[]{:S(2)}, u32[]{:S(2)}) async-start(bf16[4,48,384]{2,1,0:T(8,128)(2,1)} %broadcast_in_dim.59), calls=%async_computation | async-start | bytes 294912 | tf_op jit(solution)/shard_map/all_to_all | solution.py:474
  43.6 28.8 %copy-start.1 = (bf16[4,4,2,48,384]{4,3,2,1,0:T(8,128)(2,1)}, bf16[4,4,2,48,384]{4,3,2,1,0:T(8,128)(2,1)S(1)}, u32[]{:S(2)}) copy-start(bf16[4,4,2,48,384]{4,3,2,1,0:T(8,128)(2,1)S(1)} %all_to_all.41) | copy-start | bytes 3538948
  43.6 11.3 %copy-start.4 = (s32[12,3]{0,1:T(4,128)S(1)}, s32[12,3]{0,1:T(4,128)}, u32[]{:S(2)}) copy-start(s32[12,3]{0,1:T(4,128)} %param.12) | copy-start | bytes 436
  43.7 11.9 %copy-start.8 = (s32[12]{0:T(128)S(1)}, s32[12]{0:T(128)}, u32[]{:S(2)}) copy-start(s32[12]{0:T(128)} %param.11) | copy-start | bytes 148
  44.5 10.4 %all-to-all-start.1 = ((bf16[4,4,48,384]{3,2,1,0:T(8,128)(2,1)}), bf16[4,4,48,384]{3,2,1,0:T(8,128)(2,1)S(1)}, u32[]{:S(2)}, u32[]{:S(2)}) async-start(bf16[4,4,48,384]{3,2,1,0:T(8,128)(2,1)} %broadcast_in_dim.60), calls=%async_computation.1 | async-start | bytes 1179648 | tf_op jit(solution)/shard_map/all_to_all | solution.py:474
  48.0 24.5 %collective-permute-start.2 = (bf16[16,2,48,384]{3,2,1,0:T(8,128)(2,1)S(1)}, bf16[16,2,48,384]{3,2,1,0:T(8,128)(2,1)S(1)}, u32[]{:S(2)}, u32[]{:S(2)}) collective-permute-start(bf16[16,2,48,384]{3,2,1,0:T(8,128)(2,1)S(1)} %bitcast.22), channel_id=1, source_target_pairs={{0,1},{1,0},{2,3},{3,2},{4,5},{5,4},{6,7},{7,6},{8,9},{9,8},{10,11... | collective-permute-start | bytes 3538952 | tf_op jit(solution)/shard_map/ppermute | solution.py:470
  54.9 2.9 %copy-start.2 = (bf16[4,4,48,384]{3,2,1,0:T(8,128)(2,1)}, bf16[4,4,48,384]{3,2,1,0:T(8,128)(2,1)S(1)}, u32[]{:S(2)}) copy-start(bf16[4,4,48,384]{3,2,1,0:T(8,128)(2,1)S(1)} %all-to-all-done.1) | copy-start | bytes 1769476
  54.9 2.9 %collective-permute-start.1 = (bf16[16,48,384]{2,1,0:T(8,128)(2,1)S(1)}, bf16[16,48,384]{2,1,0:T(8,128)(2,1)}, u32[]{:S(2)}, u32[]{:S(2)}) collective-permute-start(bf16[16,48,384]{2,1,0:T(8,128)(2,1)S(1)} %bitcast.27), channel_id=1, source_target_pairs={{0,1},{1,0},{2,3},{3,2},{4,5},{5,4},{6,7},{7,6},{8,9},{9,8},{10,11... | collective-permute-start | bytes 1769480 | tf_op jit(solution)/shard_map/ppermute | solution.py:470
  55.0 1.9 collective-permute-start
  72.5 1.0 copy-start.7
  101.3 21.2 %copy-start.3 = (f32[2,384]{1,0:T(2,128)S(1)}, f32[2,384]{1,0:T(2,128)}, u32[]{:S(2)}) copy-start(f32[2,384]{1,0:T(2,128)} %get-tuple-element.44) | copy-start | bytes 9220
  122.3 2.9 %collective-permute-start.3 = (bf16[16,48,384]{2,1,0:T(8,128)(2,1)}, bf16[16,48,384]{2,1,0:T(8,128)(2,1)S(1)}, u32[]{:S(2)}, u32[]{:S(2)}) collective-permute-start(bf16[16,48,384]{2,1,0:T(8,128)(2,1)} %get-tuple-element.42), channel_id=1, source_target_pairs={{0,1},{1,0},{2,3},{3,2},{4,5},{5,4},{6,7},{7,6},{8,9},{9,8},{10,11... | collective-permute-start | bytes 1769480 | tf_op jit(solution)/shard_map/ppermute | solution.py:470
  123.2 1.2 collective-permute-start.4
  127.5 18.9 %copy-start = (f32[16,2,48,384]{3,2,1,0:T(8,128)S(1)}, f32[16,2,48,384]{3,2,1,0:T(8,128)}, u32[]{:S(2)}) copy-start(f32[16,2,48,384]{3,2,1,0:T(8,128)} %get-tuple-element.45) | copy-start | bytes 7077892
  127.5 13.6 %all-to-all-start.4 = ((bf16[4,208,384]{2,1,0:T(8,128)(2,1)}), bf16[4,208,384]{2,1,0:T(8,128)(2,1)S(1)}, u32[]{:S(2)}, u32[]{:S(2)}) async-start(bf16[4,208,384]{2,1,0:T(8,128)(2,1)} %pad_maximum_fusion), calls=%async_computation.4 | async-start | bytes 1277952 | tf_op jit(solution)/shard_map/all_to_all | solution.py:474
  131.1 15.3 %collective-permute-start.5 = (bf16[16,2,48,384]{3,2,1,0:T(8,128)(2,1)}, bf16[16,2,48,384]{3,2,1,0:T(8,128)(2,1)}, u32[]{:S(2)}, u32[]{:S(2)}) collective-permute-start(bf16[16,2,48,384]{3,2,1,0:T(8,128)(2,1)} %get-tuple-element.46), channel_id=1, source_target_pairs={{0,1},{1,0},{2,3},{3,2},{4,5},{5,4},{6,7},{7,6},{8,9},{9,8},{10,11... | collective-permute-start | bytes 3538952 | tf_op jit(solution)/shard_map/ppermute | solution.py:470
  142.0 11.7 %all-to-all-start.5 = ((bf16[4,64,384]{2,1,0:T(8,128)(2,1)}), bf16[4,64,384]{2,1,0:T(8,128)(2,1)S(1)}, u32[]{:S(2)}, u32[]{:S(2)}) async-start(bf16[4,64,384]{2,1,0:T(8,128)(2,1)} %pad_maximum_fusion.1), calls=%async_computation.5 | async-start | bytes 393216 | tf_op jit(solution)/shard_map/all_to_all | solution.py:474
  153.7 16.1 %all-to-all-start.6 = ((bf16[4,4,2,48,384]{4,3,2,1,0:T(8,128)(2,1)}), bf16[4,4,2,48,384]{4,3,2,1,0:T(8,128)(2,1)S(1)}, u32[]{:S(2)}, u32[]{:S(2)}) async-start(bf16[4,4,2,48,384]{4,3,2,1,0:T(8,128)(2,1)} %bitcast.9), calls=%async_computation.6 | async-start | bytes 2359296 | tf_op jit(solution)/shard_map/all_to_all | solution.py:474
  157.4 17.9 %copy-start.5 = (f32[4,384]{1,0:T(4,128)S(1)}, f32[4,384]{1,0:T(4,128)}, u32[]{:S(2)}) copy-start(f32[4,384]{1,0:T(4,128)} %norm_ref.5) | copy-start | bytes 18436
  157.5 17.9 %copy-start.6 = (f32[4,384]{1,0:T(4,128)S(1)}, f32[4,384]{1,0:T(4,128)}, u32[]{:S(2)}) copy-start(f32[4,384]{1,0:T(4,128)} %param.14) | copy-start | bytes 18436
  170.8 13.3 %all-to-all-start.7 = ((bf16[4,2,48,384]{3,2,1,0:T(8,128)(2,1)}), bf16[4,2,48,384]{3,2,1,0:T(8,128)(2,1)S(1)}, u32[]{:S(2)}, u32[]{:S(2)}) async-start(bf16[4,2,48,384]{3,2,1,0:T(8,128)(2,1)} %reduce_sum.41), calls=%async_computation.7 | async-start | bytes 589824 | tf_op jit(solution)/shard_map/all_to_all | solution.py:474

commit v3 on v2

--- a/solution.py
+++ b/solution.py
@@ -17,8 +17,9 @@
 HALF = D // 2
 SLABS = 16
 INNER = 4
-PACK = 4
-WIDE = 64
+TILE = 512
+HIDDEN = 768
+PACK = 2
 ROOT_HALF = 0.7071067811865476
 DENSITY_FACTOR = 0.3989422804014327
 BF = jnp.bfloat16
@@ -158,15 +159,28 @@
 
 def mlp_kernel(
     middle_ref, cot_ref, norm_ref, own_ref, other_ref,
-    out_ref, grad_ref, own_grad_ref, sent_grad_ref, norm_grad_ref, other_grad_ref,
+    out_ref, grad_ref, own_grad_ref, sent_grad_ref, norm_grad_ref,
+    up_ref, down_ref, up_grad_ref, down_grad_ref,
 ):
     step = pl.program_id(0)
+    sides = ((own_ref, own_grad_ref), (other_ref, sent_grad_ref))
+    places = [
+        (side, part, MLP // 2 * side + D * part, row)
+        for side in range(2)
+        for part in range(2)
+        for row in range(8)
+    ]
 
     @pl.when(step == 0)
     def _():
-        own_grad_ref[...] = jnp.zeros_like(own_grad_ref)
-        other_grad_ref[...] = jnp.zeros_like(other_grad_ref)
+        up_grad_ref[...] = jnp.zeros_like(up_grad_ref)
+        down_grad_ref[...] = jnp.zeros_like(down_grad_ref)
         norm_grad_ref[...] = jnp.zeros_like(norm_grad_ref)
+        for side, part, start, row in places:
+            up = sides[side][0][slab_at(2 * row + part), 0]
+            up_ref[48 * row : 48 * row + 48, start : start + D] = up
+            down = sides[side][0][slab_at(8 * part + row), 1]
+            down_ref[start + 48 * row : start + 48 * row + 48, :] = down
 
     middle = middle_ref[...]
     normed, inverse_std = normalize(middle)
@@ -174,26 +188,20 @@
     cot = cot_ref[...]
     total = middle
     back = None
-    for ref, grads in ((own_ref, own_grad_ref), (other_ref, other_grad_ref)):
-        for part in range(2):
-            up_at = [slab_at(2 * r + part) for r in range(8)]
-            down_at = [slab_at(8 * part + r) for r in range(8)]
-            up = jnp.concatenate([ref[at, 0] for at in up_at], axis=0)
-            down = jnp.concatenate([ref[at, 1] for at in down_at], axis=0)
-            pre = nn(rows, up)
-            cumulative = 0.5 * (1.0 + lax.erf(pre * ROOT_HALF))
-            density = jnp.exp(-0.5 * pre * pre) * DENSITY_FACTOR
-            act = (pre * cumulative).astype(BF)
-            total = total + nn(act, down)
-            act_grad = nt(cot, down)
-            pre_grad = (act_grad * (cumulative + pre * density)).astype(BF)
-            down_part = tn(act, cot)
-            up_part = tn(rows, pre_grad)
-            for r in range(8):
-                grads[up_at[r], 0] += up_part[48 * r : 48 * r + 48]
-                grads[down_at[r], 1] += down_part[48 * r : 48 * r + 48]
-            term = nt(pre_grad, up)
-            back = term if back is None else back + term
+    for start in range(0, MLP, HIDDEN):
+        hidden = slice(start, start + HIDDEN)
+        up, down = up_ref[:, hidden], down_ref[hidden, :]
+        pre = nn(rows, up)
+        act_grad = nt(cot, down)
+        cumulative = 0.5 * (1.0 + lax.erf(pre * ROOT_HALF))
+        density = jnp.exp(-0.5 * pre * pre) * DENSITY_FACTOR
+        act = (pre * cumulative).astype(BF)
+        pre_grad = (act_grad * (cumulative + pre * density)).astype(BF)
+        total = total + nn(act, down)
+        term = nt(pre_grad, up)
+        back = term if back is None else back + term
+        down_grad_ref[hidden, :] += tn(act, cot)
+        up_grad_ref[:, hidden] += tn(rows, pre_grad)
     out_ref[...] = total
     grad_in, norm_part = norm_backward(back, normed, inverse_std, norm_ref[2:3, :])
     norm_grad_ref[...] += norm_part
@@ -201,17 +209,22 @@
 
     @pl.when(step == pl.num_programs(0) - 1)
     def _():
-        sent_grad_ref[...] = other_grad_ref[...].astype(BF)
+        for side, part, start, row in places:
+            ref = sides[side][1]
+            up = up_grad_ref[48 * row : 48 * row + 48, start : start + D]
+            ref[slab_at(2 * row + part), 0] = up.astype(ref.dtype)
+            down = down_grad_ref[start + 48 * row : start + 48 * row + 48, :]
+            ref[slab_at(8 * part + row), 1] = down.astype(ref.dtype)
 
 
 def mlp(middle, cotangent, norm_params, own, other):
     rows = middle.shape[0]
     slabs = (SLABS, 2, 48, D)
     slab = pl.BlockSpec(slabs, lambda i: (0, 0, 0, 0))
-    tile = pl.BlockSpec((S, D), lambda i: (i, 0))
+    tile = pl.BlockSpec((TILE, D), lambda i: (i, 0))
     return pl.pallas_call(
         mlp_kernel,
-        grid=(rows // S,),
+        grid=(rows // TILE,),
         in_specs=[tile, tile, pl.BlockSpec((4, D), lambda i: (0, 0)), slab, slab],
         out_specs=[tile, tile, slab, slab, pl.BlockSpec((2, D), lambda i: (0, 0))],
         out_shape=[
@@ -221,7 +234,12 @@
             jax.ShapeDtypeStruct(slabs, BF),
             jax.ShapeDtypeStruct((2, D), F32),
         ],
-        scratch_shapes=[pltpu.VMEM(slabs, F32)],
+        scratch_shapes=[
+            pltpu.VMEM((D, MLP), BF),
+            pltpu.VMEM((MLP, D), BF),
+            pltpu.VMEM((D, MLP), F32),
+            pltpu.VMEM((MLP, D), F32),
+        ],
         compiler_params=pltpu.CompilerParams(vmem_limit_bytes=VMEM_LIMIT),
         cost_estimate=pl.CostEstimate(
             flops=12 * rows * D * MLP, bytes_accessed=20 << 20, transcendentals=2 * rows * MLP
@@ -349,99 +367,121 @@
     return high, (values - high.astype(F32)).astype(BF)
 
 
+def stack(*pieces):
+    return jnp.concatenate(pieces, axis=0)
+
+
+def cut_rows(values, number):
+    edge = values.shape[0] // number
+    return [values[edge * i : edge * i + edge] for i in range(number)]
+
+
 def product(left, right):
-    left_high, left_low = left
+    high, low = left
     right_high, right_low = right
-    both = nn(jnp.concatenate([left_high, left_low], axis=0), right_high)
-    edge = left_high.shape[0]
-    return both[:edge] + (both[edge:] + nn(left_high, right_low))
-
-
-def shampoo_kernel(
-    scale, grad_ref, weight_ref, left_ref, right_ref, *refs
-):
+    one, two = cut_rows(nn(stack(high, low), right_high), 2)
+    return one + (two + nn(high, right_low))
+
+
+def two_products(left, middle, right):
+    right_high, right_low = right
+    both = cut_rows(nn(stack(left[0], middle[0], left[1], middle[1]), right_high), 4)
+    high = cut_rows(nn(stack(left[0], middle[0]), right_low), 2)
+    return both[0] + (both[2] + high[0]), both[1] + (both[3] + high[1])
+
+
+def shampoo_kernel(scale, grad_ref, weight_ref, left_ref, right_ref, *refs):
     out_grad_ref, left_new_ref, right_new_ref, new_weight_ref, root_ref, power_ref = refs[-6:]
     count, edge = weight_ref.shape[1], weight_ref.shape[2]
     pack = min(PACK, count)
-    width = pack * WIDE
-    row = lax.broadcasted_iota(jnp.int32, (WIDE, width), 0)
-    lane = lax.broadcasted_iota(jnp.int32, (WIDE, width), 1)
-    identity = (lane % WIDE == row).astype(F32)
-    row = lax.broadcasted_iota(jnp.int32, (width, width), 0)
-    lane = lax.broadcasted_iota(jnp.int32, (width, width), 1)
-    same = (row // WIDE == lane // WIDE).astype(BF)
-    lane = lax.broadcasted_iota(jnp.int32, (1, width), 1)
-
-    def wide(block):
-        block = jnp.concatenate([block, jnp.zeros((edge, WIDE - edge), block.dtype)], axis=1)
-        return jnp.concatenate([block, jnp.zeros((WIDE - edge, WIDE), block.dtype)], axis=0)
+    packs = count // pack
+    width = pack * edge
+
+    def block_of(shape, dim):
+        return lax.broadcasted_iota(jnp.int32, shape, dim) // edge
+
+    row = lax.broadcasted_iota(jnp.int32, (edge, width), 0)
+    lane = lax.broadcasted_iota(jnp.int32, (edge, width), 1)
+    identity = (lane % edge == row).astype(F32)
+    same = (block_of((width, width), 0) == block_of((width, width), 1)).astype(BF)
+    lane_block = block_of((1, width), 1)
 
     def spread(pieces):
-        return tuple(jnp.concatenate([piece] * pack, axis=0) * same for piece in pieces)
+        return tuple(stack(*[piece] * pack) * same for piece in pieces)
 
     def cut(packed, index):
-        return packed[:edge, WIDE * index : WIDE * index + edge]
-
-    whole = grad_ref[0] * scale
-    packs = count // pack
-    grads = []
+        return packed[:, edge * index : edge * index + edge]
+
+    def beside(ref, number):
+        return jnp.concatenate([ref[0, pack * number + i] for i in range(pack)], axis=1)
+
+    grads, parts = [], []
     for number in range(packs):
-        blocks = []
+        grad = grad_ref[0, :, width * number : width * number + width] * scale
+        blocks = [cut(grad, index) for index in range(pack)]
         for index in range(pack):
-            block = pack * number + index
-            grad = whole[:, edge * block : edge * block + edge]
-            out_grad_ref[0, block] = grad
-            blocks.append(wide(grad))
-        grad = jnp.concatenate(blocks, axis=1)
+            out_grad_ref[0, pack * number + index] = blocks[index]
         grad_t = jnp.concatenate([jnp.transpose(block) for block in blocks], axis=1)
         one, two = split(grad), split(grad_t)
         one_diagonal, two_diagonal = spread(one), spread(two)
         grads.append(one_diagonal)
-        for kind, (old_ref, new_ref, gram) in enumerate(
-            (
-                (left_ref, left_new_ref, product(one, two_diagonal)),
-                (right_ref, right_new_ref, product(two, one_diagonal)),
-            )
-        ):
-            old = jnp.concatenate([wide(old_ref[0, pack * number + i]) for i in range(pack)], axis=1)
-            new = 0.5 * old + 0.5 * gram
-            for index in range(pack):
-                new_ref[0, pack * number + index] = cut(new, index)
-            columns = jnp.sum(new * new, axis=0, keepdims=True)
-            squares = jnp.zeros((1, width), F32)
-            for index in range(pack):
-                inside = lane // WIDE == index
-                part = jnp.sum(jnp.where(inside, columns, 0.0), axis=1, keepdims=True)
-                squares = jnp.where(inside, part, squares)
-            factor = 2.5 / jnp.sqrt(squares)
-            root_ref[2 * number + kind] = jnp.sqrt(jnp.sqrt(factor)) * identity
-            power_ref[2 * number + kind] = factor * new
-
-    def iteration(_, carry):
-        for index in range(2 * packs):
-            power = power_ref[index]
-            middle = split((5.0 * identity - power) * 0.25)
-            right = spread(middle)
-            root_ref[index] = product(split(root_ref[index]), right)
-            square = split(product(middle, right))
-            fourth = split(product(square, spread(square)))
-            power_ref[index] = product(fourth, spread(split(power)))
-        return carry
-
-    lax.fori_loop(0, ITERS, iteration, 0)
+        parts.append((left_ref, left_new_ref, one, two_diagonal))
+        parts.append((right_ref, right_new_ref, two, one_diagonal))
+    grams = [product(left, right) for _, _, left, right in parts]
+    for slot, (old_ref, new_ref, _, _) in enumerate(parts):
+        new = 0.5 * beside(old_ref, slot // 2) + 0.5 * grams[slot]
+        for index in range(pack):
+            new_ref[0, pack * (slot // 2) + index] = cut(new, index)
+        columns = jnp.sum(new * new, axis=0, keepdims=True)
+        squares = jnp.zeros((1, width), F32)
+        for index in range(pack):
+            inside = lane_block == index
+            part = jnp.sum(jnp.where(inside, columns, 0.0), axis=1, keepdims=True)
+            squares = jnp.where(inside, part, squares)
+        factor = 2.5 / jnp.sqrt(squares)
+        root_ref[slot] = jnp.broadcast_to(jnp.sqrt(jnp.sqrt(factor)), (edge, width))
+        power_ref[slot] = factor * new
+    slots = range(2 * packs)
+
+    def advance(first):
+        powers = [power_ref[slot] for slot in slots]
+        middles = [split((5.0 * identity - power) * 0.25) for power in powers]
+        rights = [spread(middle) for middle in middles]
+        powers = [split(power) for power in powers]
+        if first:
+            squares = [product(middles[s], rights[s]) for s in slots]
+            for slot in slots:
+                root_ref[slot] *= (5.0 * identity - power_ref[slot]) * 0.25
+        else:
+            roots = [split(root_ref[slot]) for slot in slots]
+            both = [two_products(roots[s], middles[s], rights[s]) for s in slots]
+            squares = [pair[1] for pair in both]
+            for slot in slots:
+                root_ref[slot] = both[slot][0]
+        rights = [spread(split(square)) for square in squares]
+        powers = [split(product(powers[s], rights[s])) for s in slots]
+        for slot in slots:
+            power_ref[slot] = product(powers[slot], rights[slot])
+
+    advance(True)
+    lax.fori_loop(0, ITERS - 2, lambda _, carry: advance(False) or carry, 0)
+    rights = [spread(split((5.0 * identity - power_ref[slot]) * 0.25)) for slot in slots]
+    for slot in slots:
+        root_ref[slot] = product(split(root_ref[slot]), rights[slot])
+    steps = [product(split(root_ref[2 * n]), grads[n]) for n in range(packs)]
+    rights = [spread(split(root_ref[2 * n + 1])) for n in range(packs)]
+    steps = [product(split(steps[n]), rights[n]) for n in range(packs)]
     for number in range(packs):
-        step = product(split(root_ref[2 * number]), grads[number])
-        step = product(split(step), spread(split(root_ref[2 * number + 1])))
         for index in range(pack):
             block = pack * number + index
-            new_weight_ref[0, block] = weight_ref[0, block] - 0.25 * cut(step, index)
+            new_weight_ref[0, block] = weight_ref[0, block] - 0.25 * cut(steps[number], index)
 
 
 def shampoo(grads, weights, stat_left, stat_right, scale, first, earlier=()):
     groups, edge, _ = grads.shape
     _, count, _, _ = weights.shape
     packs = count // min(PACK, count)
-    width = min(PACK, count) * WIDE
+    width = min(PACK, count) * edge
     block = pl.BlockSpec((1, count, edge, edge), lambda i: (i + first, 0, 0, 0))
     shape = jax.ShapeDtypeStruct(weights.shape, F32)
     return pl.pallas_call(
@@ -454,8 +494,8 @@
         out_specs=[block] * 4,
         out_shape=[shape] * 4,
         scratch_shapes=[
-            pltpu.VMEM((2 * packs, WIDE, width), F32),
-            pltpu.VMEM((2 * packs, WIDE, width), F32),
+            pltpu.VMEM((2 * packs, edge, width), F32),
+            pltpu.VMEM((2 * packs, edge, width), F32),
         ],
         input_output_aliases={4 + i: i for i in range(len(earlier))},
         compiler_params=pltpu.CompilerParams(vmem_limit_bytes=VMEM_LIMIT),
@@ -479,11 +519,13 @@
 
 
 def gather_slabs(local):
-    groups, edge, _ = local.shape
-    slabs = local if groups > 1 else local[0]
-    slabs = to_all(copies(slabs, lax.axis_size("outer")), "outer")
-    slabs = to_all(copies(slabs, lax.axis_size("inner")), "inner")
-    return slabs.reshape((SLABS,) + slabs.shape[2:])
+    inner, outer = lax.axis_size("inner"), lax.axis_size("outer")
+    column = to_all(copies(local, outer), "outer")
+    early = to_all(copies(column[:, 0], inner), "inner")
+    early = early.reshape((SLABS,) + early.shape[2:])
+    column, early = lax.optimization_barrier((column, early))
+    late = to_all(copies(column[:, 1:], inner), "inner")
+    return early, late.reshape((SLABS,) + late.shape[2:])
 
 
 def gather_blocks(local):
@@ -502,30 +544,10 @@
     return owned.transpose(0, 2, 1, 3).reshape(groups, edge, count * edge)
 
 
-def scatter_slabs(slabs):
-    groups = slabs.shape[1]
-    inner, outer = lax.axis_size("inner"), lax.axis_size("outer")
-    shape = (outer, groups, 48, D)
-    received = to_all(slabs.reshape((inner,) + shape), "inner")
-    partial = jnp.sum(received.astype(F32), axis=0).astype(BF)
-    return jnp.sum(to_all(partial, "outer").astype(F32), axis=0)
-
-
 def with_norms(slabs, norms):
     high, low = split(norms)
     rows = jnp.concatenate([high, low, jnp.zeros_like(high), jnp.zeros_like(high)], axis=0)
-    return jnp.concatenate([slabs, copies(rows, slabs.shape[0])], axis=1)
-
-
-def scatter_with_norms(slabs, norms):
-    inner, outer = lax.axis_size("inner"), lax.axis_size("outer")
-    sent = with_norms(slabs.reshape(inner, outer * 48, D), norms)
-    received = jnp.sum(to_all(sent, "inner").astype(F32), axis=0)
-    edge = outer * 48
-    norms = received[edge : edge + 4] + received[edge + 4 : edge + 8]
-    sent = with_norms(received[:edge].reshape(outer, 48, D).astype(BF), norms)
-    received = jnp.sum(to_all(sent, "outer").astype(F32), axis=0)
-    return received[None, :48], received[48:52] + received[52:56]
+    return jnp.concatenate([slabs, copies(rows, SLABS)], axis=1)
 
 
 def per_device(
@@ -553,24 +575,30 @@
     local = weights.astype(BF)
     if whole_slabs:
         local = local.transpose(0, 2, 1, 3).reshape(-1, edge, D)
-        early, late = gather_slabs(local[:1]), gather_slabs(local[1:])
+        early, late = gather_slabs(local)
     else:
         early, late = gather_blocks(local[:1]), gather_blocks(local[1:])
     prob, qkv, out, middle, wqkv, wo = attn_forward(
         counts, tokens, mask_lanes, norm_params, early, swap_heads(early)
     )
+    late, middle = lax.optimization_barrier((late, middle))
     block_out, middle_grad, own_late, sent_late, norm_two = mlp(
         middle, cotangent, norm_params, late, swap_heads(late)
     )
     late_slabs = (own_late + swap_heads(sent_late).astype(F32)).astype(BF)
+    late_slabs, middle_grad = lax.optimization_barrier((late_slabs, middle_grad))
     input_grad, own_early, sent_early, norm_one = attn_backward(
         tokens, middle_grad, prob, qkv, out, mask_lanes, norm_params, wqkv, wo
     )
     early_slabs = (own_early + swap_heads(sent_early).astype(F32)).astype(BF)
     norms = jnp.concatenate([norm_one, norm_two], axis=0)
     if whole_slabs:
-        late_owned = scatter_slabs(late_slabs)
-        early_owned, norm_total = scatter_with_norms(early_slabs, norms + swap_heads(norms))
+        late_received = to_all(late_slabs, ("inner", "outer"))
+        sent = with_norms(early_slabs, norms + swap_heads(norms))
+        late_received, sent = lax.optimization_barrier((late_received, sent))
+        late_owned = jnp.sum(late_received.astype(F32), axis=0)
+        received = jnp.sum(to_all(sent, ("inner", "outer")).astype(F32), axis=0)
+        early_owned, norm_total = received[None, :48], received[48:52] + received[52:56]
     else:
         late_owned = scatter_blocks(late_slabs, count, edge).astype(F32)
         early_owned = scatter_blocks(early_slabs[:, None], count, edge).astype(F32)

time: 238 us -> 157 us (0.66)
  Pallas kernels: 116 us -> 78.2 us
  waiting for transfers between devices: 48.5 us -> 17.4 us
  starting transfers between devices: 27.6 us -> 14.2 us
  blocking collectives: 28.3 us -> 30.9 us
    all_to_all x6 -> x3, waiting for transfers between devices: 46.9 us -> 11.2 us  [to_all(): return lax.all_to_all(values, axis, 0, 0)]
    pallas_call x2, Pallas kernels: 52.2 us -> 21.4 us  [shampoo(): pl.pallas_call(lambda *refs: shampoo_kernel(scale, *refs), grid=(groups,)...]
    all_to_all x6 -> x3, starting transfers between devices: 26.1 us -> 12.4 us  [to_all(): return lax.all_to_all(values, axis, 0, 0)]
    pallas_call x1, Pallas kernels: 27.8 us -> 21.2 us  [mlp(): pl.pallas_call(mlp_kernel, grid=(rows // TILE,), in_specs=[tile, tile, pl...]
    ppermute x6, waiting for transfers between devices: 1.58 us -> 6.2 us  [swap_heads(): return lax.ppermute(values, 'head', [(0, 1), (1, 0)])]
    all_to_all x2, blocking collectives: 28.3 us -> 30.9 us  [to_all(): return lax.all_to_all(values, axis, 0, 0)]
  transfers between devices with their start and end apart: 12 -> 9, of which waited for: 8 -> 6; matrix products, arithmetic and copies ran while one was open for 3% -> 5% of each run, Pallas kernels for 6% -> 31%
where the time goes in v3:
time: 157 us
  Pallas kernels  78.2 us (50%)
  blocking collectives  30.9 us (20%)
  waiting for transfers between devices  17.4 us (11%)
  starting transfers between devices  14.2 us (9%)
  other arithmetic  9.48 us (6%)
  local copies, waits for them, and re-layouts  5.7 us (4%)
    all_to_all x2, blocking collectives, to_all(): return lax.all_to_all(values, axis, 0, 0)  30.9 us
    pallas_call x2, Pallas kernels, shampoo(): pl.pallas_call(lambda *refs: shampoo_kernel(scale, *refs), grid=(groups,)...  21.4 us
    pallas_call x1, Pallas kernels, mlp(): pl.pallas_call(mlp_kernel, grid=(rows // TILE,), in_specs=[tile, tile, pl...  21.2 us
    pallas_call x1, Pallas kernels, attn_backward(): pl.pallas_call(attn_backward_kernel, grid=(images,), in_specs=[tile, tile...  21 us
    pallas_call x1, Pallas kernels, attn_forward(): pl.pallas_call(attn_forward_kernel, grid=(images,), in_specs=[pl.BlockSpe...  14.7 us
    all_to_all x3, starting transfers between devices, to_all(): return lax.all_to_all(values, axis, 0, 0)  12.4 us
    all_to_all x3, waiting for transfers between devices, to_all(): return lax.all_to_all(values, axis, 0, 0)  11.2 us
    ppermute x6, waiting for transfers between devices, swap_heads(): return lax.ppermute(values, 'head', [(0, 1), (1, 0)])  6.2 us
  transfers between devices with their start and end apart: 9, of which 6 were waited for; matrix products, arithmetic and copies ran while one was open for 5% of the time, Pallas kernels for 31%

profile of v3, /device:TPU:0, one launch (start us, length us, event | category | flops | bytes accessed | tf_op | source)
XLA Modules:
  0.0 156.7 jit_solution(6163053776606118959)
XLA Ops:
  0.6 1.1 convert_bitcast_fusion
  2.1 18.9 %all_to_all.25 = bf16[4,3,48,384]{3,2,1,0:T(8,128)(2,1)S(1)} all-to-all(bf16[4,3,48,384]{3,2,1,0:T(8,128)(2,1)S(1)} %broadcast_in_dim.45), channel_id=1, replica_groups=mesh['outer'=4,'inner'=4,'head'=2] {'outer'}, dimensions={0} | all-to-all | bytes 884736 | tf_op jit(solution)/shard_map/all_to_all | solution.py:514
  21.0 12.1 %all_to_all.26 = bf16[4,4,48,384]{3,2,1,0:T(8,128)(2,1)S(1)} all-to-all(bf16[4,4,48,384]{3,2,1,0:T(8,128)(2,1)S(1)} %broadcast_in_dim.47), channel_id=1, replica_groups=mesh['outer'=4,'inner'=4,'head'=2] {'inner'}, dimensions={0} | all-to-all | bytes 1179648 | tf_op jit(solution)/shard_map/all_to_all | solution.py:514
  33.1 1.2 broadcast_in_dim.48
  34.3 3.7 %all-to-all-start.2 = ((bf16[4,4,2,48,384]{4,3,2,1,0:T(8,128)(2,1)}), bf16[4,4,2,48,384]{4,3,2,1,0:T(8,128)(2,1)S(1)}, u32[]{:S(2)}, u32[]{:S(2)}) async-start(bf16[4,4,2,48,384]{4,3,2,1,0:T(8,128)(2,1)} %broadcast_in_dim.48), calls=%async_computation.2 | async-start | bytes 2359296 | tf_op jit(solution)/shard_map/all_to_all | solution.py:514
  40.2 0.8 copy-done.7
  41.1 14.7 %attn_forward.1 = (bf16[6,3,512,256]{3,2,1,0:T(8,128)(2,1)}, bf16[1536,1152]{1,0:T(8,128)(2,1)}, bf16[1536,384]{1,0:T(8,128)(2,1)}, f32[1536,384]{1,0:T(8,128)},...) custom-call(s32[6]{0:T(128)} %dynamic_slice.9.counts_ref, bf16[1536,384]{1,0:T(8,128)(2,1)} %x_ref.3, ...), custom_call_target="tpu_custom_call" | custom-call | flops 4227858432 | bytes 16777216 | tf_op jit(solution)/shard_map/attn_forward/pallas_call | solution.py:125
  56.1 2.5 %collective-permute-done.2.other_ref = bf16[16,2,48,384]{3,2,1,0:T(8,128)(2,1)S(1)} collective-permute-done((bf16[16,2,48,384]{3,2,1,0:T(8,128)(2,1)S(1)}, bf16[16,2,48,384]{3,2,1,0:T(8,128)(2,1)S(1)}, u32[]{:S(2)}, u32[]{:S(2)}) %collective-permute-start.2) | collective-permute-done | bytes 1179680 | tf_op jit(solution)/shard_map/ppermute | solution.py:510
  58.7 1.0 copy-done.6
  59.7 21.2 %mlp.1 = (f32[1536,384]{1,0:T(8,128)}, f32[1536,384]{1,0:T(8,128)}, f32[16,2,48,384]{3,2,1,0:T(8,128)}, bf16[16,2,48,384]{3,2,1,0:T(8,128)(2,1)}, f32[2,384]{1,0:T(2,128)}) custom-call(f32[1536,384]{1,0:T(8,128)} %get-tuple-element.43.middle_ref, bf16[1536,384]{1,0:T(8,128)(2,1)} %cot_ref.1, f32[4,384]{1,0:T(4,128)} %norm_ref.5, ...), custom_call_target="tpu_custom_call" | custom-call | flops 10871635968 | bytes 20971520 | tf_op jit(solution)/shard_map/mlp/pallas_call | solution.py:225
  81.3 2.7 %collective-permute-done.3 = bf16[16,2,48,384]{3,2,1,0:T(8,128)(2,1)S(1)} collective-permute-done((bf16[16,2,48,384]{3,2,1,0:T(8,128)(2,1)}, bf16[16,2,48,384]{3,2,1,0:T(8,128)(2,1)S(1)}, u32[]{:S(2)}, u32[]{:S(2)}) %collective-permute-start.3) | collective-permute-done | bytes 1179680 | tf_op jit(solution)/shard_map/ppermute | solution.py:510
  84.0 3.0 %add_convert_fusion = bf16[16,2,48,384]{3,2,1,0:T(8,128)(2,1)} fusion(f32[16,2,48,384]{3,2,1,0:T(8,128)} %get-tuple-element.46, bf16[16,2,48,384]{3,2,1,0:T(8,128)(2,1)S(1)} %collective-permute-done.3), kind=kLoop, calls=%fused_computation.1 | loop fusion | flops 1769472 | bytes 4718592 | tf_op jit(solution)/shard_map/convert_element_type | solution.py:588
  87.0 5.1 %all-to-all-start.3 = ((bf16[16,2,48,384]{3,2,1,0:T(8,128)(2,1)}), bf16[16,2,48,384]{3,2,1,0:T(8,128)(2,1)S(1)}, u32[]{:S(2)}, u32[]{:S(2)}) async-start(bf16[16,2,48,384]{3,2,1,0:T(8,128)(2,1)} %add_convert_fusion), calls=%async_computation.3 | async-start | bytes 2359296 | tf_op jit(solution)/shard_map/all_to_all | solution.py:514
  92.1 21.0 %attn_backward.1 = (f32[1536,384]{1,0:T(8,128)}, f32[16,48,384]{2,1,0:T(8,128)}, bf16[16,48,384]{2,1,0:T(8,128)(2,1)}, f32[2,384]{1,0:T(2,128)}) custom-call(bf16[1536,384]{1,0:T(8,128)(2,1)} %x_ref.3, f32[1536,384]{1,0:T(8,128)} %get-tuple-element.49.grad_ref, bf16[6,3,512,256]{3,2,1,0:T(8,128)(2,1)} %get-tuple-element.50.prob_ref, ...), custom_call_target="tpu_custom_call" | custom-call | flops 8455716864 | bytes 20971520 | tf_op jit(solution)/shard_map/attn_backward/pallas_call | solution.py:326
  113.1 0.7 pad_maximum_fusion.1
  114.4 0.7 collective-permute-done.5
  115.9 1.4 add_convert_fusion.1
  117.3 1.0 pad_maximum_fusion
  118.4 4.3 %all-to-all-done.3 = bf16[16,2,48,384]{3,2,1,0:T(8,128)(2,1)S(1)} async-done(((bf16[16,2,48,384]{3,2,1,0:T(8,128)(2,1)}), bf16[16,2,48,384]{3,2,1,0:T(8,128)(2,1)S(1)}, u32[]{:S(2)}, u32[]{:S(2)}) %all-to-all-start.3) | async-done | bytes 1179680 | tf_op jit(solution)/shard_map/all_to_all | solution.py:514
  122.7 3.6 %all-to-all-start.4 = ((bf16[16,64,384]{2,1,0:T(8,128)(2,1)}), bf16[16,64,384]{2,1,0:T(8,128)(2,1)S(1)}, u32[]{:S(2)}, u32[]{:S(2)}) async-start(bf16[16,64,384]{2,1,0:T(8,128)(2,1)} %pad_maximum_fusion), calls=%async_computation.4 | async-start | bytes 1572864 | tf_op jit(solution)/shard_map/all_to_all | solution.py:514
  126.3 0.8 convert_reduce_fusion.refs_0_
  127.1 13.6 %shampoo.2 = (f32[3,8,48,48]{3,2,1,0:T(8,128)}, f32[3,8,48,48]{3,2,1,0:T(8,128)}, f32[3,8,48,48]{3,2,1,0:T(8,128)}, f32[3,8,48,48]{3,2,1,0:T(8,128)}) custom-call(f32[2,48,384]{2,1,0:T(8,128)} %convert_reduce_fusion.refs_0_, f32[3,8,48,48]{3,2,1,0:T(8,128)} %bitcast.20, f32[3,8,48,48]{3,2,1,0:T(8,128)} %bitcast.24, f32[3,8,48,48]{3,2,1,0:T(8,128)} %bitcast.26), custom_call_target="tpu_custom_call" | custom-call | flops 6442450944 | bytes 4194304 | tf_op jit(solution)/shard_map/shampoo/pallas_call | solution.py:487
  140.8 6.8 %all-to-all-done.4 = bf16[16,64,384]{2,1,0:T(8,128)(2,1)S(1)} async-done(((bf16[16,64,384]{2,1,0:T(8,128)(2,1)}), bf16[16,64,384]{2,1,0:T(8,128)(2,1)S(1)}, u32[]{:S(2)}, u32[]{:S(2)}) %all-to-all-start.4) | async-done | bytes 786464 | tf_op jit(solution)/shard_map/all_to_all | solution.py:514
  148.9 7.8 %shampoo.3 = (f32[3,8,48,48]{3,2,1,0:T(8,128)}, f32[3,8,48,48]{3,2,1,0:T(8,128)}, f32[3,8,48,48]{3,2,1,0:T(8,128)}, f32[3,8,48,48]{3,2,1,0:T(8,128)}) custom-call(f32[1,48,384]{2,1,0:T(8,128)} %slice_bitcast_fusion.1.refs_0_, f32[3,8,48,48]{3,2,1,0:T(8,128)} %bitcast.21, ...), custom_call_target="tpu_custom_call", output_to_operand_aliasing={{0}: (4, {}), {1}: (5, {}), {2}: (6, {}), {3}: (7, {})} | custom-call | flops 3221225472 | bytes 4194304 | tf_op jit(solution)/shard_map/shampoo/pallas_call | solution.py:487
  (46 shorter events, 6.3 us)
Async XLA Ops:
  33.1 1.2 copy-start.1
  33.1 7.1 %collective-permute-start.1 = (bf16[16,48,384]{2,1,0:T(8,128)(2,1)S(1)}, bf16[16,48,384]{2,1,0:T(8,128)(2,1)S(1)}, u32[]{:S(2)}, u32[]{:S(2)}) collective-permute-start(bf16[16,48,384]{2,1,0:T(8,128)(2,1)S(1)} %bitcast.22), channel_id=1, source_target_pairs={{0,1},{1,0},{2,3},{3,2},{4,5},{5,4},{6,7},{7,6},{8,9},{9,8},{10,11... | collective-permute-start | bytes 1769480 | tf_op jit(solution)/shard_map/ppermute | solution.py:510
  34.3 3.7 %copy-start.3 = (s32[12,3]{0,1:T(4,128)S(1)}, s32[12,3]{0,1:T(4,128)}, u32[]{:S(2)}) copy-start(s32[12,3]{0,1:T(4,128)} %param.12) | copy-start | bytes 436
  34.3 4.2 %copy-start.8 = (s32[12]{0:T(128)S(1)}, s32[12]{0:T(128)}, u32[]{:S(2)}) copy-start(s32[12]{0:T(128)} %param.11) | copy-start | bytes 148
  34.3 21.4 %all-to-all-start.2 = ((bf16[4,4,2,48,384]{4,3,2,1,0:T(8,128)(2,1)}), bf16[4,4,2,48,384]{4,3,2,1,0:T(8,128)(2,1)S(1)}, u32[]{:S(2)}, u32[]{:S(2)}) async-start(bf16[4,4,2,48,384]{4,3,2,1,0:T(8,128)(2,1)} %broadcast_in_dim.48), calls=%async_computation.2 | async-start | bytes 2359296 | tf_op jit(solution)/shard_map/all_to_all | solution.py:514
  38.1 1.3 collective-permute-start
  40.2 0.8 copy-start.7
  55.7 2.9 %copy-start = (bf16[4,4,2,48,384]{4,3,2,1,0:T(8,128)(2,1)}, bf16[4,4,2,48,384]{4,3,2,1,0:T(8,128)(2,1)S(1)}, u32[]{:S(2)}) copy-start(bf16[4,4,2,48,384]{4,3,2,1,0:T(8,128)(2,1)S(1)} %all-to-all-done.2) | copy-start | bytes 3538948
  55.7 2.9 %collective-permute-start.2 = (bf16[16,2,48,384]{3,2,1,0:T(8,128)(2,1)S(1)}, bf16[16,2,48,384]{3,2,1,0:T(8,128)(2,1)S(1)}, u32[]{:S(2)}, u32[]{:S(2)}) collective-permute-start(bf16[16,2,48,384]{3,2,1,0:T(8,128)(2,1)S(1)} %bitcast.18), channel_id=1, source_target_pairs={{0,1},{1,0},{2,3},{3,2},{4,5},{5,4},{6,7},{7,6},{8,9},{9,8},{10,11... | collective-permute-start | bytes 3538952 | tf_op jit(solution)/shard_map/ppermute | solution.py:510
  58.7 1.0 copy-start.6
  80.9 3.1 %collective-permute-start.3 = (bf16[16,2,48,384]{3,2,1,0:T(8,128)(2,1)}, bf16[16,2,48,384]{3,2,1,0:T(8,128)(2,1)S(1)}, u32[]{:S(2)}, u32[]{:S(2)}) collective-permute-start(bf16[16,2,48,384]{3,2,1,0:T(8,128)(2,1)} %get-tuple-element.47), channel_id=1, source_target_pairs={{0,1},{1,0},{2,3},{3,2},{4,5},{5,4},{6,7},{7,6},{8,9},{9,8},{10,11... | collective-permute-start | bytes 3538952 | tf_op jit(solution)/shard_map/ppermute | solution.py:510
  87.0 35.7 %all-to-all-start.3 = ((bf16[16,2,48,384]{3,2,1,0:T(8,128)(2,1)}), bf16[16,2,48,384]{3,2,1,0:T(8,128)(2,1)S(1)}, u32[]{:S(2)}, u32[]{:S(2)}) async-start(bf16[16,2,48,384]{3,2,1,0:T(8,128)(2,1)} %add_convert_fusion), calls=%async_computation.3 | async-start | bytes 2359296 | tf_op jit(solution)/shard_map/all_to_all | solution.py:514
  92.1 21.1 %copy-start.2 = (f32[2,384]{1,0:T(2,128)S(1)}, f32[2,384]{1,0:T(2,128)}, u32[]{:S(2)}) copy-start(f32[2,384]{1,0:T(2,128)} %get-tuple-element.60) | copy-start | bytes 9220
  113.1 2.9 %collective-permute-start.4 = (bf16[16,48,384]{2,1,0:T(8,128)(2,1)}, bf16[16,48,384]{2,1,0:T(8,128)(2,1)S(1)}, u32[]{:S(2)}, u32[]{:S(2)}) collective-permute-start(bf16[16,48,384]{2,1,0:T(8,128)(2,1)} %get-tuple-element.58), channel_id=1, source_target_pairs={{0,1},{1,0},{2,3},{3,2},{4,5},{5,4},{6,7},{7,6},{8,9},{9,8},{10,11... | collective-permute-start | bytes 1769480 | tf_op jit(solution)/shard_map/ppermute | solution.py:510
  113.8 1.3 collective-permute-start.5
  122.7 24.9 %all-to-all-start.4 = ((bf16[16,64,384]{2,1,0:T(8,128)(2,1)}), bf16[16,64,384]{2,1,0:T(8,128)(2,1)S(1)}, u32[]{:S(2)}, u32[]{:S(2)}) async-start(bf16[16,64,384]{2,1,0:T(8,128)(2,1)} %pad_maximum_fusion), calls=%async_computation.4 | async-start | bytes 1572864 | tf_op jit(solution)/shard_map/all_to_all | solution.py:514
  127.1 21.2 %copy-start.4 = (f32[4,384]{1,0:T(4,128)S(1)}, f32[4,384]{1,0:T(4,128)}, u32[]{:S(2)}) copy-start(f32[4,384]{1,0:T(4,128)} %norm_ref.5) | copy-start | bytes 18436
  127.1 21.2 %copy-start.5 = (f32[4,384]{1,0:T(4,128)S(1)}, f32[4,384]{1,0:T(4,128)}, u32[]{:S(2)}) copy-start(f32[4,384]{1,0:T(4,128)} %param.14) | copy-start | bytes 18436

commit v4 on v3

--- a/solution.py
+++ b/solution.py
@@ -18,13 +18,16 @@
 SLABS = 16
 INNER = 4
 TILE = 512
+IMAGES = TILE // S
+NORM_ROWS = 8
 HIDDEN = 768
 PACK = 2
 ROOT_HALF = 0.7071067811865476
 DENSITY_FACTOR = 0.3989422804014327
 BF = jnp.bfloat16
 F32 = jnp.float32
-VMEM_LIMIT = 56 << 20
+VMEM_LIMIT = 40 << 20
+SMALL_VMEM = 8 << 20
 
 
 def nn(left, right):
@@ -70,8 +73,19 @@
     return jnp.concatenate([values * first, values * second], axis=0)
 
 
+def mask_lanes(half_ref, own_ref, other_ref, image, pair):
+    image = half_ref[0] * (own_ref.shape[0] // 2) + image
+    heads = own_ref.shape[1]
+    on = [
+        own_ref[image, head] if head < heads else other_ref[image, head - heads]
+        for head in (2 * pair, 2 * pair + 1)
+    ]
+    lane = lax.broadcasted_iota(jnp.int32, (1, PAIR), 1)
+    return jnp.where(lane < HEAD_DIM, on[0], on[1]).astype(F32)
+
+
 def attn_forward_kernel(
-    counts_ref, x_ref, mask_ref, norm_ref, own_ref, other_ref,
+    half_ref, counts_ref, own_mask_ref, other_mask_ref, x_ref, norm_ref, own_ref, other_ref,
     prob_ref, qkv_ref, out_ref, middle_ref, wqkv_ref, wo_ref,
 ):
     step = pl.program_id(0)
@@ -99,45 +113,54 @@
     rows = (normed * norm_ref[0:1, :] + norm_ref[1:2, :]).astype(BF)
     qkv_ref[...] = nn(rows, wqkv_ref[...]).astype(BF)
     first, second = lane_halves()
-    count = counts_ref[step]
     column = lax.broadcasted_iota(jnp.int32, (1, S), 1)
-    valid = column < count
-    for pair in range(PAIRS):
-        lanes = slice(PAIR * pair, PAIR * (pair + 1))
-        queries = qkv_ref[:, lanes]
-        keys = qkv_ref[:, D + PAIR * pair : D + PAIR * (pair + 1)]
-        values = qkv_ref[:, 2 * D + PAIR * pair : 2 * D + PAIR * (pair + 1)]
-        scores = nt(stacked(queries, first, second), keys)
-        scores = jnp.where(valid, scores, -1e30)
+    tasks = [(image, pair) for image in range(IMAGES) for pair in range(PAIRS)]
+
+    def places(task):
+        image, pair = task
+        here = slice(S * image, S * image + S)
+        return here, *(slice(D * t + PAIR * pair, D * t + PAIR * (pair + 1)) for t in range(3))
+
+    def get_scores(task):
+        here, query_lanes, key_lanes, _ = places(task)
+        return nt(stacked(qkv_ref[here, query_lanes], first, second), qkv_ref[here, key_lanes])
+
+    def get_prob(task, scores):
+        image = half_ref[0] * (counts_ref.shape[0] // 2) + IMAGES * step + task[0]
+        scores = jnp.where(column < counts_ref[image], scores, -1e30)
         top = jnp.max(scores, axis=-1, keepdims=True)
         exp_scores = jnp.exp(scores - top)
         total = jnp.sum(exp_scores, axis=-1, keepdims=True)
         prob = (exp_scores * (1.0 / total)).astype(BF)
-        prob_ref[0, pair] = prob
+        prob_ref[task] = prob
+        return prob
+
+    all_scores = [get_scores(task) for task in tasks]
+    probs = [get_prob(task, scores) for task, scores in zip(tasks, all_scores)]
+    for task, prob in zip(tasks, probs):
+        here, lanes, _, value_lanes = places(task)
+        values = qkv_ref[here, value_lanes]
         head_out = nn(prob[:S], values * first) + nn(prob[S:], values * second)
-        out_ref[:, lanes] = (head_out * mask_ref[0, :, lanes]).astype(BF)
+        mask = mask_lanes(half_ref, own_mask_ref, other_mask_ref, IMAGES * step + task[0], task[1])
+        out_ref[here, lanes] = (head_out * mask).astype(BF)
     middle_ref[...] = x + nn(out_ref[...], wo_ref[...])
 
 
-def attn_forward(counts, tokens, mask_lanes, norm_params, own, other):
+def attn_forward(half, counts, own_mask, other_mask, tokens, norm_params, own, other):
     rows = tokens.shape[0]
     images = rows // S
+    tile = pl.BlockSpec((TILE, D), lambda i: (i, 0))
+    slab = pl.BlockSpec((SLABS, 48, D), lambda i: (0, 0, 0))
+    smem = pl.BlockSpec(memory_space=pltpu.SMEM)
     return pl.pallas_call(
         attn_forward_kernel,
-        grid=(images,),
-        in_specs=[
-            pl.BlockSpec(memory_space=pltpu.SMEM),
-            pl.BlockSpec((S, D), lambda i: (i, 0)),
-            pl.BlockSpec((1, 1, D), lambda i: (i, 0, 0)),
-            pl.BlockSpec((4, D), lambda i: (0, 0)),
-            pl.BlockSpec((SLABS, 48, D), lambda i: (0, 0, 0)),
-            pl.BlockSpec((SLABS, 48, D), lambda i: (0, 0, 0)),
-        ],
+        grid=(rows // TILE,),
+        in_specs=[smem] * 4 + [tile, pl.BlockSpec((4, D), lambda i: (0, 0)), slab, slab],
         out_specs=[
-            pl.BlockSpec((1, PAIRS, 2 * S, S), lambda i: (i, 0, 0, 0)),
-            pl.BlockSpec((S, 3 * D), lambda i: (i, 0)),
-            pl.BlockSpec((S, D), lambda i: (i, 0)),
-            pl.BlockSpec((S, D), lambda i: (i, 0)),
+            pl.BlockSpec((IMAGES, PAIRS, 2 * S, S), lambda i: (i, 0, 0, 0)),
+            pl.BlockSpec((TILE, 3 * D), lambda i: (i, 0)),
+            tile,
+            tile,
             pl.BlockSpec((D, 3 * D), lambda i: (0, 0)),
             pl.BlockSpec((D, D), lambda i: (0, 0)),
         ],
@@ -154,7 +177,7 @@
             flops=rows * D * (8 * D + 16 * S), bytes_accessed=16 << 20, transcendentals=rows * 6 * S
         ),
         name="attn_forward",
-    )(counts, tokens, mask_lanes, norm_params, own, other)
+    )(half, counts, own_mask, other_mask, tokens, norm_params, own, other)
 
 
 def mlp_kernel(
@@ -230,7 +253,7 @@
         out_shape=[
             jax.ShapeDtypeStruct((rows, D), F32),
             jax.ShapeDtypeStruct((rows, D), F32),
-            jax.ShapeDtypeStruct(slabs, F32),
+            jax.ShapeDtypeStruct(slabs, BF),
             jax.ShapeDtypeStruct(slabs, BF),
             jax.ShapeDtypeStruct((2, D), F32),
         ],
@@ -249,8 +272,10 @@
 
 
 def attn_backward_kernel(
-    x_ref, grad_ref, prob_ref, qkv_ref, out_ref, mask_ref, norm_ref, wqkv_ref, wo_ref,
-    in_grad_ref, own_grad_ref, sent_grad_ref, norm_grad_ref, dqkv_ref, wqkv_grad_ref, wo_grad_ref,
+    half_ref, own_mask_ref, other_mask_ref, x_ref, grad_ref, prob_ref, qkv_ref, out_ref,
+    norm_ref, later_norm_ref, wqkv_ref, wo_ref,
+    in_grad_ref, own_grad_ref, sent_grad_ref, norm_grad_ref,
+    dqkv_ref, wqkv_grad_ref, wo_grad_ref,
 ):
     step = pl.program_id(0)
 
@@ -258,7 +283,8 @@
     def _():
         wqkv_grad_ref[...] = jnp.zeros_like(wqkv_grad_ref)
         wo_grad_ref[...] = jnp.zeros_like(wo_grad_ref)
-        norm_grad_ref[...] = jnp.zeros_like(norm_grad_ref)
+        norm_grad_ref[0:2, :] = jnp.zeros((2, D), F32)
+        norm_grad_ref[2:4, :] = later_norm_ref[...]
 
     x = x_ref[...].astype(F32)
     normed, inverse_std = normalize(x)
@@ -267,37 +293,49 @@
     low_grad = grad.astype(BF)
     head_out = out_ref[...]
     wo_grad_ref[...] += tn(head_out, low_grad)
-    out_grad = (nt(low_grad, wo_ref[...]).astype(BF) * mask_ref[0].astype(BF))
+    whole_grad = nt(low_grad, wo_ref[...]).astype(BF)
     first, second = lane_halves()
-    for pair in range(PAIRS):
-        lanes = slice(PAIR * pair, PAIR * (pair + 1))
-        key_lanes = slice(D + PAIR * pair, D + PAIR * (pair + 1))
-        value_lanes = slice(2 * D + PAIR * pair, 2 * D + PAIR * (pair + 1))
-        queries = qkv_ref[:, lanes]
-        keys = qkv_ref[:, key_lanes]
-        values = qkv_ref[:, value_lanes]
-        prob = prob_ref[0, pair]
-        pair_grad = stacked(out_grad[:, lanes], first, second)
-        dots = out_grad[:, lanes].astype(F32) * head_out[:, lanes].astype(F32)
-        row_dot = jnp.concatenate(
-            [
-                jnp.sum(dots * first.astype(F32), axis=-1, keepdims=True),
-                jnp.sum(dots * second.astype(F32), axis=-1, keepdims=True),
-            ],
-            axis=0,
-        )
-        prob_grad = nt(pair_grad, values)
-        score_grad = (prob.astype(F32) * (prob_grad - row_dot)).astype(BF)
-        dqkv_ref[:, lanes] = (
-            nn(score_grad[:S], keys * first) + nn(score_grad[S:], keys * second)
-        ).astype(BF)
-        dqkv_ref[:, key_lanes] = tn(score_grad, stacked(queries, first, second)).astype(BF)
-        dqkv_ref[:, value_lanes] = tn(prob, pair_grad).astype(BF)
+    first_wide, second_wide = first.astype(F32), second.astype(F32)
+    tasks = [(image, pair) for image in range(IMAGES) for pair in range(PAIRS)]
+
+    def places(task):
+        image, pair = task
+        here = slice(S * image, S * image + S)
+        return here, *(slice(D * t + PAIR * pair, D * t + PAIR * (pair + 1)) for t in range(3))
+
+    def get_pair_grad(task):
+        here, lanes, _, _ = places(task)
+        mask = mask_lanes(half_ref, own_mask_ref, other_mask_ref, IMAGES * step + task[0], task[1])
+        grad = whole_grad[here, lanes] * mask.astype(BF)
+        dots = grad.astype(F32) * head_out[here, lanes].astype(F32)
+        first_dot = jnp.sum(dots * first_wide, axis=-1, keepdims=True)
+        second_dot = jnp.sum(dots * second_wide, axis=-1, keepdims=True)
+        return stacked(grad, first, second), jnp.concatenate([first_dot, second_dot], axis=0)
+
+    pair_grads = [get_pair_grad(task) for task in tasks]
+    prob_grads = [
+        nt(pair_grad[0], qkv_ref[places(task)[0], places(task)[3]])
+        for task, pair_grad in zip(tasks, pair_grads)
+    ]
+    score_grads = [
+        (prob_ref[task].astype(F32) * (prob_grad - pair_grad[1])).astype(BF)
+        for task, prob_grad, pair_grad in zip(tasks, prob_grads, pair_grads)
+    ]
+    for task, score_grad, (pair_grad, _) in zip(tasks, score_grads, pair_grads):
+        here, query_lanes, key_lanes, value_lanes = places(task)
+        keys = qkv_ref[here, key_lanes]
+        queries = stacked(qkv_ref[here, query_lanes], first, second)
+        query_grad = nn(score_grad[:S], keys * first) + nn(score_grad[S:], keys * second)
+        key_grad = nn(jnp.transpose(queries), score_grad)
+        value_grad = nn(jnp.transpose(pair_grad), prob_ref[task])
+        dqkv_ref[here, query_lanes] = query_grad.astype(BF)
+        dqkv_ref[here, key_lanes] = jnp.transpose(key_grad).astype(BF)
+        dqkv_ref[here, value_lanes] = jnp.transpose(value_grad).astype(BF)
     dqkv = dqkv_ref[...]
     wqkv_grad_ref[...] += tn(rows, dqkv)
     back = nt(dqkv, wqkv_ref[...])
     grad_in, norm_part = norm_backward(back, normed, inverse_std, norm_ref[0:1, :])
-    norm_grad_ref[...] += norm_part
+    norm_grad_ref[0:2, :] += norm_part
     in_grad_ref[...] = grad + grad_in
 
     @pl.when(step == pl.num_programs(0) - 1)
@@ -310,47 +348,51 @@
                     piece = wqkv_grad_ref[48 * row : 48 * row + 48, D * part : D * part + D]
                     piece = piece[:, HALF * side : HALF * side + HALF]
                     pieces.append(piece * 0.125 if part == 0 else piece)
-                joined = jnp.concatenate(pieces, axis=1)
-                slab_grads[slab_at(slab)] = joined.astype(slab_grads.dtype)
+                slab_grads[slab_at(slab)] = jnp.concatenate(pieces, axis=1).astype(BF)
             for row in range(HALF // 48):
                 start = HALF * side + 48 * row
-                joined = wo_grad_ref[start : start + 48, :]
-                slab_grads[slab_at(12 + row)] = joined.astype(slab_grads.dtype)
-
-
-def attn_backward(tokens, grad, prob, qkv, out, mask_lanes, norm_params, wqkv, wo):
+                slab_grads[slab_at(12 + row)] = wo_grad_ref[start : start + 48, :].astype(BF)
+        sent_grad_ref[SLABS, :NORM_ROWS] = jnp.concatenate(split(norm_grad_ref[...]), axis=0)
+        sent_grad_ref[SLABS, NORM_ROWS:] = jnp.zeros((48 - NORM_ROWS, D), BF)
+
+
+def attn_backward(
+    half, own_mask, other_mask, tokens, grad, prob, qkv, out, norm_params, later_norms, wqkv, wo
+):
     rows = tokens.shape[0]
-    images = rows // S
-    tile = pl.BlockSpec((S, D), lambda i: (i, 0))
-    slab = pl.BlockSpec((SLABS, 48, D), lambda i: (0, 0, 0))
+    tile = pl.BlockSpec((TILE, D), lambda i: (i, 0))
+    smem = pl.BlockSpec(memory_space=pltpu.SMEM)
     return pl.pallas_call(
         attn_backward_kernel,
-        grid=(images,),
+        grid=(rows // TILE,),
         in_specs=[
+            smem,
+            smem,
+            smem,
             tile,
             tile,
-            pl.BlockSpec((1, PAIRS, 2 * S, S), lambda i: (i, 0, 0, 0)),
-            pl.BlockSpec((S, 3 * D), lambda i: (i, 0)),
+            pl.BlockSpec((IMAGES, PAIRS, 2 * S, S), lambda i: (i, 0, 0, 0)),
+            pl.BlockSpec((TILE, 3 * D), lambda i: (i, 0)),
             tile,
-            pl.BlockSpec((1, 1, D), lambda i: (i, 0, 0)),
             pl.BlockSpec((4, D), lambda i: (0, 0)),
+            pl.BlockSpec((2, D), lambda i: (0, 0)),
             pl.BlockSpec((D, 3 * D), lambda i: (0, 0)),
             pl.BlockSpec((D, D), lambda i: (0, 0)),
         ],
         out_specs=[
             tile,
-            slab,
-            slab,
-            pl.BlockSpec((2, D), lambda i: (0, 0)),
+            pl.BlockSpec((SLABS, 48, D), lambda i: (0, 0, 0)),
+            pl.BlockSpec((SLABS + 1, 48, D), lambda i: (0, 0, 0)),
+            pl.BlockSpec((4, D), lambda i: (0, 0)),
         ],
         out_shape=[
             jax.ShapeDtypeStruct((rows, D), F32),
-            jax.ShapeDtypeStruct((SLABS, 48, D), F32),
             jax.ShapeDtypeStruct((SLABS, 48, D), BF),
-            jax.ShapeDtypeStruct((2, D), F32),
+            jax.ShapeDtypeStruct((SLABS + 1, 48, D), BF),
+            jax.ShapeDtypeStruct((4, D), F32),
         ],
         scratch_shapes=[
-            pltpu.VMEM((S, 3 * D), BF),
+            pltpu.VMEM((TILE, 3 * D), BF),
             pltpu.VMEM((D, 3 * D), F32),
             pltpu.VMEM((D, D), F32),
         ],
@@ -359,7 +401,68 @@
             flops=rows * D * (16 * D + 32 * S), bytes_accessed=20 << 20, transcendentals=0
         ),
         name="attn_backward",
-    )(tokens, grad, prob, qkv, out, mask_lanes, norm_params, wqkv, wo)
+    )(half, own_mask, other_mask, tokens, grad, prob, qkv, out, norm_params, later_norms, wqkv, wo)
+
+
+def pack_kernel(weight_ref, early_ref, late_ref):
+    groups, count, _, _ = weight_ref.shape
+    for group in range(groups):
+        blocks = [weight_ref[group, block] for block in range(count)]
+        slab = jnp.concatenate(blocks, axis=1).astype(BF)
+        for copy in range(early_ref.shape[0]):
+            if group == 0:
+                early_ref[copy] = slab
+            else:
+                late_ref[copy, group - 1] = slab
+
+
+def pack(weights, number):
+    groups, count, edge, _ = weights.shape
+    return pl.pallas_call(
+        pack_kernel,
+        out_shape=[
+            jax.ShapeDtypeStruct((number, edge, count * edge), BF),
+            jax.ShapeDtypeStruct((number, groups - 1, edge, count * edge), BF),
+        ],
+        compiler_params=pltpu.CompilerParams(vmem_limit_bytes=SMALL_VMEM),
+        name="pack",
+    )(weights)
+
+
+def add_kernel(one_ref, two_ref, out_ref):
+    out_ref[...] = (one_ref[...].astype(F32) + two_ref[...].astype(F32)).astype(BF)
+
+
+def add_slabs(one, two):
+    block = pl.BlockSpec((4,) + one.shape[1:], lambda i: (i, 0, 0, 0))
+    return pl.pallas_call(
+        add_kernel,
+        grid=(one.shape[0] // 4,),
+        in_specs=[block, block],
+        out_specs=block,
+        out_shape=jax.ShapeDtypeStruct(one.shape, BF),
+        compiler_params=pltpu.CompilerParams(vmem_limit_bytes=SMALL_VMEM),
+        name="add_slabs",
+    )(one, two)
+
+
+def combine_kernel(own_ref, received_ref, norm_ref, out_ref):
+    slabs = own_ref.shape[0]
+    total = own_ref[...].astype(F32) + received_ref[:slabs].astype(F32)
+    out_ref[:, :48] = total.astype(BF)
+    norms = received_ref[slabs, :NORM_ROWS].astype(F32)
+    norms = norm_ref[...] + (norms[:4] + norms[4:])
+    rows = jnp.concatenate(split(norms), axis=0)
+    out_ref[:, 48:] = jnp.broadcast_to(rows[None], (slabs, NORM_ROWS, D))
+
+
+def combine(own, received, norms):
+    return pl.pallas_call(
+        combine_kernel,
+        out_shape=jax.ShapeDtypeStruct((SLABS, 48 + NORM_ROWS, D), BF),
+        compiler_params=pltpu.CompilerParams(vmem_limit_bytes=SMALL_VMEM),
+        name="combine",
+    )(own, received, norms)
 
 
 def split(values):
@@ -390,9 +493,26 @@
     return both[0] + (both[2] + high[0]), both[1] + (both[3] + high[1])
 
 
-def shampoo_kernel(scale, grad_ref, weight_ref, left_ref, right_ref, *refs):
+def update_norms(scale, total, param_ref, state_ref, grad_ref, new_state_ref, new_ref):
+    grads = total * scale
+    state = 0.5 * state_ref[...] + 0.5 * grads * grads
+    grad_ref[...] = grads
+    new_state_ref[...] = state
+    new_ref[...] = param_ref[...] - 0.2 * grads / jnp.sqrt(state)
+
+
+def shampoo_kernel(scale, with_norms, received_ref, weight_ref, left_ref, right_ref, *refs):
+    if with_norms:
+        norm_ins, norm_outs, refs = refs[:2], refs[-5:-2], refs[:-5] + refs[-2:]
     out_grad_ref, left_new_ref, right_new_ref, new_weight_ref, root_ref, power_ref = refs[-6:]
     count, edge = weight_ref.shape[1], weight_ref.shape[2]
+    received = received_ref[0].astype(F32)
+    for number in range(1, received_ref.shape[0]):
+        received = received + received_ref[number].astype(F32)
+    received = received.reshape(received.shape[-2:])
+    if with_norms:
+        total = received[edge : edge + 4] + received[edge + 4 : edge + NORM_ROWS]
+        update_norms(scale, total, *norm_ins, *norm_outs)
     pack = min(PACK, count)
     packs = count // pack
     width = pack * edge
@@ -417,7 +537,7 @@
 
     grads, parts = [], []
     for number in range(packs):
-        grad = grad_ref[0, :, width * number : width * number + width] * scale
+        grad = received[:edge, width * number : width * number + width] * scale
         blocks = [cut(grad, index) for index in range(pack)]
         for index in range(pack):
             out_grad_ref[0, pack * number + index] = blocks[index]
@@ -477,33 +597,38 @@
             new_weight_ref[0, block] = weight_ref[0, block] - 0.25 * cut(steps[number], index)
 
 
-def shampoo(grads, weights, stat_left, stat_right, scale, first, earlier=()):
-    groups, edge, _ = grads.shape
-    _, count, _, _ = weights.shape
+def shampoo(received, weights, stat_left, stat_right, scale, first, earlier=(), norms=()):
+    sources, groups, rows, lanes = received.shape
+    _, count, edge, _ = weights.shape
     packs = count // min(PACK, count)
     width = min(PACK, count) * edge
     block = pl.BlockSpec((1, count, edge, edge), lambda i: (i + first, 0, 0, 0))
     shape = jax.ShapeDtypeStruct(weights.shape, F32)
+    norm = pl.BlockSpec((4, D), lambda i: (0, 0))
+    norm_outs = 3 if norms else 0
+    ins = 4 + len(norms)
     return pl.pallas_call(
-        lambda *refs: shampoo_kernel(scale, *refs),
+        lambda *refs: shampoo_kernel(scale, bool(norms), *refs),
         grid=(groups,),
         in_specs=[
-            pl.BlockSpec((1, edge, count * edge), lambda i: (i, 0, 0)), block, block, block,
-            *[pl.BlockSpec(memory_space=pl.ANY) for _ in earlier],
-        ],
-        out_specs=[block] * 4,
-        out_shape=[shape] * 4,
+            pl.BlockSpec((sources, 1, rows, lanes), lambda i: (0, i, 0, 0)),
+            *[block] * 3,
+            *[norm] * len(norms),
+            *[pl.BlockSpec(memory_space=pl.ANY)] * len(earlier),
+        ],
+        out_specs=[block] * 4 + [norm] * norm_outs,
+        out_shape=[shape] * 4 + [jax.ShapeDtypeStruct((4, D), F32)] * norm_outs,
         scratch_shapes=[
             pltpu.VMEM((2 * packs, edge, width), F32),
             pltpu.VMEM((2 * packs, edge, width), F32),
         ],
-        input_output_aliases={4 + i: i for i in range(len(earlier))},
-        compiler_params=pltpu.CompilerParams(vmem_limit_bytes=VMEM_LIMIT),
+        input_output_aliases={ins + i: i for i in range(len(earlier))},
+        compiler_params=pltpu.CompilerParams(vmem_limit_bytes=SMALL_VMEM),
         cost_estimate=pl.CostEstimate(
             flops=groups * (3 << 30), bytes_accessed=4 << 20, transcendentals=0
         ),
         name="shampoo",
-    )(grads, weights, stat_left, stat_right, *earlier)
+    )(received, weights, stat_left, stat_right, *norms, *earlier)
 
 
 def swap_heads(values):
@@ -518,14 +643,19 @@
     return jnp.broadcast_to(values[None], (number,) + values.shape)
 
 
-def gather_slabs(local):
+def flat(slabs):
+    return slabs.reshape((SLABS,) + slabs.shape[2:])
+
+
+def gather_slabs(weights, other_mask):
     inner, outer = lax.axis_size("inner"), lax.axis_size("outer")
-    column = to_all(copies(local, outer), "outer")
-    early = to_all(copies(column[:, 0], inner), "inner")
-    early = early.reshape((SLABS,) + early.shape[2:])
-    column, early = lax.optimization_barrier((column, early))
-    late = to_all(copies(column[:, 1:], inner), "inner")
-    return early, late.reshape((SLABS,) + late.shape[2:])
+    early, late = pack(weights, outer)
+    early = to_all(early, "outer")
+    early, late = lax.optimization_barrier((early, late))
+    early = to_all(copies(early, inner), "inner")
+    late = copies(to_all(late, "outer"), inner)
+    early, late, other_mask = lax.optimization_barrier((early, late, other_mask))
+    return flat(early), flat(to_all(late, "inner")), other_mask
 
 
 def gather_blocks(local):
@@ -542,12 +672,6 @@
     blocks = blocks.transpose(2, 1, 0, 4, 3, 5).reshape(groups, SLABS * (D // edge), edge, edge)
     owned = lax.psum_scatter(blocks, ("outer", "inner"), scatter_dimension=1, tiled=True)
     return owned.transpose(0, 2, 1, 3).reshape(groups, edge, count * edge)
-
-
-def with_norms(slabs, norms):
-    high, low = split(norms)
-    rows = jnp.concatenate([high, low, jnp.zeros_like(high), jnp.zeros_like(high)], axis=0)
-    return jnp.concatenate([slabs, copies(rows, SLABS)], axis=1)
 
 
 def per_device(
@@ -564,64 +688,47 @@
     weights, stat_left, stat_right = weights[0], stat_left[0], stat_right[0]
     _, count, edge, _ = weights.shape
     whole_slabs = count * edge == D
-    images = tokens.shape[0] // S
-    half = lax.axis_index("head")
-    counts = lax.dynamic_slice_in_dim(token_counts, half * images, images)
-    own_mask = lax.dynamic_slice_in_dim(head_mask, half * images, images)
-    sent_mask = lax.dynamic_slice_in_dim(head_mask, (1 - half) * images, images)
-    mask = jnp.concatenate([own_mask, swap_heads(sent_mask)], axis=1)
-    mask_lanes = jnp.repeat(mask.astype(F32), HEAD_DIM, axis=1)[:, None, :]
-
-    local = weights.astype(BF)
+    half = lax.axis_index("head").reshape(1)
+    other_mask = swap_heads(head_mask)
     if whole_slabs:
-        local = local.transpose(0, 2, 1, 3).reshape(-1, edge, D)
-        early, late = gather_slabs(local)
+        early, late, other_mask = gather_slabs(weights, other_mask)
     else:
+        local = weights.astype(BF)
         early, late = gather_blocks(local[:1]), gather_blocks(local[1:])
+    masks = (head_mask, other_mask)
     prob, qkv, out, middle, wqkv, wo = attn_forward(
-        counts, tokens, mask_lanes, norm_params, early, swap_heads(early)
+        half, token_counts, *masks, tokens, norm_params, early, swap_heads(early)
     )
     late, middle = lax.optimization_barrier((late, middle))
     block_out, middle_grad, own_late, sent_late, norm_two = mlp(
         middle, cotangent, norm_params, late, swap_heads(late)
     )
-    late_slabs = (own_late + swap_heads(sent_late).astype(F32)).astype(BF)
+    late_slabs = add_slabs(own_late, swap_heads(sent_late))
     late_slabs, middle_grad = lax.optimization_barrier((late_slabs, middle_grad))
-    input_grad, own_early, sent_early, norm_one = attn_backward(
-        tokens, middle_grad, prob, qkv, out, mask_lanes, norm_params, wqkv, wo
+    input_grad, own_early, sent_early, norm_sums = attn_backward(
+        half, *masks, tokens, middle_grad, prob, qkv, out, norm_params, norm_two, wqkv, wo
     )
-    early_slabs = (own_early + swap_heads(sent_early).astype(F32)).astype(BF)
-    norms = jnp.concatenate([norm_one, norm_two], axis=0)
-    if whole_slabs:
-        late_received = to_all(late_slabs, ("inner", "outer"))
-        sent = with_norms(early_slabs, norms + swap_heads(norms))
-        late_received, sent = lax.optimization_barrier((late_received, sent))
-        late_owned = jnp.sum(late_received.astype(F32), axis=0)
-        received = jnp.sum(to_all(sent, ("inner", "outer")).astype(F32), axis=0)
-        early_owned, norm_total = received[None, :48], received[48:52] + received[52:56]
-    else:
-        late_owned = scatter_blocks(late_slabs, count, edge).astype(F32)
-        early_owned = scatter_blocks(early_slabs[:, None], count, edge).astype(F32)
-        norm_total = lax.psum(norms, ("outer", "inner", "head"))
+    early_slabs = combine(own_early, swap_heads(sent_early), norm_sums)
     devices = lax.axis_size("outer") * lax.axis_size("inner") * lax.axis_size("head")
     scale = 1.0 / math.sqrt(tokens.shape[0] * devices)
     state = (weights, stat_left, stat_right, scale)
-    results = shampoo(late_owned, *state, 1)
-    grads, left_new, right_new, new_weights = shampoo(early_owned, *state, 0, results)
-    norm_grads = norm_total * scale
-    state_new = 0.5 * norm_state + 0.5 * norm_grads * norm_grads
-    norm_new = norm_params - 0.2 * norm_grads / jnp.sqrt(state_new)
-    return (
-        block_out,
-        input_grad,
-        grads[None],
-        left_new[None],
-        right_new[None],
-        new_weights[None],
-        norm_grads,
-        state_new,
-        norm_new,
-    )
+    norms = (norm_params, norm_state)
+    if whole_slabs:
+        late_received = to_all(late_slabs, ("inner", "outer"))
+        late_received, early_slabs = lax.optimization_barrier((late_received, early_slabs))
+        results = shampoo(late_received, *state, 1)
+        early_received = to_all(early_slabs, ("inner", "outer"))[:, None]
+        results = shampoo(early_received, *state, 0, results, norms)
+    else:
+        late_received = scatter_blocks(late_slabs, count, edge)[None]
+        early_received = scatter_blocks(early_slabs[:, None, :48], count, edge)[None]
+        norm_total = lax.psum(norm_sums, ("outer", "inner", "head"))
+        results = shampoo(late_received, *state, 1)
+        results = list(shampoo(early_received, *state, 0, results))
+        norm_grads = norm_total * scale
+        state_new = 0.5 * norm_state + 0.5 * norm_grads * norm_grads
+        results += [norm_grads, state_new, norm_params - 0.2 * norm_grads / jnp.sqrt(state_new)]
+    return (block_out, input_grad, *[result[None] for result in results[:4]], *results[4:])
 
 
 def solution(mesh):

time: 157 us -> 157 us (level)
  local copies, waits for them, and re-layouts: 5.7 us -> 22.2 us
  Pallas kernels: 78.2 us -> 64.8 us
  other arithmetic: 9.48 us -> 0 us
  waiting for transfers between devices: 17.4 us -> 26.1 us
  blocking collectives: 30.9 us -> 24.2 us
  starting transfers between devices: 14.2 us -> 17.9 us
    unnamed x18 -> x53, local copies, waits for them, and re-layouts: 1.86 us -> 20.2 us
    pallas_call x4 -> x7, Pallas kernels: 57 us -> 47 us  [the longest x2 19.3 us: shampoo(): pl.pallas_call(lambda *refs: shampoo_kernel(scale, bool(norms), *refs), g...]
    all_to_all x3 -> x4, waiting for transfers between devices: 11.2 us -> 17.9 us  [to_all(): return lax.all_to_all(values, axis, 0, 0)]
    all_to_all x2, blocking collectives: 30.9 us -> 24.2 us  [to_all(): return lax.all_to_all(values, axis, 0, 0)]
    convert_element_type x4 -> x0, other arithmetic: 5.05 us -> none  [the longest x1 2.96 us: per_device(): late_slabs = (own_late + swap_heads(sent_late).astype(F32)).astype(BF)]
    all_to_all x3 -> x4, starting transfers between devices: 12.4 us -> 17 us  [to_all(): return lax.all_to_all(values, axis, 0, 0)]
    pallas_call x1, Pallas kernels: 21.2 us -> 17.8 us  [mlp(): pl.pallas_call(mlp_kernel, grid=(rows // TILE,), in_specs=[tile, tile, pl...]
    ppermute x6 -> x5, waiting for transfers between devices: 6.2 us -> 8.19 us  [swap_heads(): return lax.ppermute(values, 'head', [(0, 1), (1, 0)])]
  transfers between devices with their start and end apart: 9 -> 9, of which waited for: 6 -> 7; matrix products, arithmetic and copies ran while one was open for 5% -> 0% of each run, Pallas kernels for 31% -> 25%
where the time goes in v4:
time: 157 us; the launch traced here: 156 us
  Pallas kernels  64.8 us (41%)
  waiting for transfers between devices  26.1 us (17%)
  blocking collectives  24.2 us (15%)
  local copies, waits for them, and re-layouts  22.2 us (14%)
  starting transfers between devices  17.9 us (11%)
    all_to_all x2, blocking collectives, to_all(): return lax.all_to_all(values, axis, 0, 0)  24.2 us
    unnamed x53, local copies, waits for them, and re-layouts  20.2 us
    pallas_call x2, Pallas kernels, shampoo(): pl.pallas_call(lambda *refs: shampoo_kernel(scale, bool(norms), *refs), g...  19.3 us
    all_to_all x4, waiting for transfers between devices, to_all(): return lax.all_to_all(values, axis, 0, 0)  17.9 us
    pallas_call x1, Pallas kernels, mlp(): pl.pallas_call(mlp_kernel, grid=(rows // TILE,), in_specs=[tile, tile, pl...  17.8 us
    all_to_all x4, starting transfers between devices, to_all(): return lax.all_to_all(values, axis, 0, 0)  17 us
    pallas_call x1, Pallas kernels, attn_backward(): pl.pallas_call(attn_backward_kernel, grid=(rows // TILE,), in_specs=[smem...  14.6 us
    pallas_call x1, Pallas kernels, attn_forward(): pl.pallas_call(attn_forward_kernel, grid=(rows // TILE,), in_specs=[smem]...  10.2 us
  transfers between devices with their start and end apart: 9, of which 7 were waited for; matrix products, arithmetic and copies ran while one was open for 0% of the time, Pallas kernels for 25%

profile of v4, /device:TPU:0, one launch (start us, length us, event | category | flops | bytes accessed | tf_op | source)
XLA Modules:
  0.0 156.0 jit_solution(3647939239218943566)
XLA Ops:
  1.9 12.8 %all_to_all.30 = bf16[4,48,384]{2,1,0:T(8,128)(2,1)S(1)} all-to-all(bf16[4,48,384]{2,1,0:T(8,128)(2,1)S(1)} %get-tuple-element.48), channel_id=1, replica_groups=mesh['outer'=4,'inner'=4,'head'=2] {'outer'}, dimensions={0} | all-to-all | bytes 294912 | tf_op jit(solution)/shard_map/all_to_all | solution.py:639
  14.6 11.4 %all_to_all.31 = bf16[4,2,48,384]{3,2,1,0:T(8,128)(2,1)S(1)} all-to-all(bf16[4,2,48,384]{3,2,1,0:T(8,128)(2,1)S(1)} %get-tuple-element.51), channel_id=1, replica_groups=mesh['outer'=4,'inner'=4,'head'=2] {'outer'}, dimensions={0} | all-to-all | bytes 589824 | tf_op jit(solution)/shard_map/all_to_all | solution.py:639
  26.9 3.7 %all-to-all-start.1 = ((bf16[4,4,48,384]{3,2,1,0:T(8,128)(2,1)}), bf16[4,4,48,384]{3,2,1,0:T(8,128)(2,1)S(1)}, u32[]{:S(2)}, u32[]{:S(2)}) async-start(bf16[4,4,48,384]{3,2,1,0:T(8,128)(2,1)} %broadcast_in_dim.27), calls=%async_computation.1 | async-start | bytes 1179648 | tf_op jit(solution)/shard_map/all_to_all | solution.py:639
  31.9 5.7 %all-to-all-done.1 = bf16[4,4,48,384]{3,2,1,0:T(8,128)(2,1)S(1)} async-done(((bf16[4,4,48,384]{3,2,1,0:T(8,128)(2,1)}), bf16[4,4,48,384]{3,2,1,0:T(8,128)(2,1)S(1)}, u32[]{:S(2)}, u32[]{:S(2)}) %all-to-all-start.1) | async-done | bytes 589856 | tf_op jit(solution)/shard_map/all_to_all | solution.py:639
  38.8 3.5 %all-to-all-start.3 = ((bf16[4,4,2,48,384]{4,3,2,1,0:T(8,128)(2,1)}), bf16[4,4,2,48,384]{4,3,2,1,0:T(8,128)(2,1)S(1)}, u32[]{:S(2)}, u32[]{:S(2)}) async-start(bf16[4,4,2,48,384]{4,3,2,1,0:T(8,128)(2,1)} %broadcast_in_dim.28), calls=%async_computation.3 | async-start | bytes 2359296 | tf_op jit(solution)/shard_map/all_to_all | solution.py:639
  44.9 10.2 %attn_forward.1 = (bf16[6,3,512,256]{3,2,1,0:T(8,128)(2,1)}, bf16[1536,1152]{1,0:T(8,128)(2,1)S(1)}, bf16[1536,384]{1,0:T(8,128)(2,1)S(1)}, f32[1536,384]{1,0:T(...) custom-call(s32[1]{0:T(128)} %bitcast.2.half_ref, s32[12]{0:T(128)S(1)} %copy-done.12, ...), custom_call_target="tpu_custom_call" | custom-call | flops 4227858432 | bytes 16777216 | tf_op jit(solution)/shard_map/attn_forward/pallas_call | solution.py:155
  55.1 1.8 %copy-done.13 = bf16[1536,1152]{1,0:T(8,128)(2,1)} copy-done((bf16[1536,1152]{1,0:T(8,128)(2,1)}, bf16[1536,1152]{1,0:T(8,128)(2,1)S(1)}, u32[]{:S(2)}) %copy-start.13) | copy-done | bytes 3538968
  56.9 1.4 copy-done.15
  61.5 2.5 %collective-permute-done.2.other_ref = bf16[16,2,48,384]{3,2,1,0:T(8,128)(2,1)S(1)} collective-permute-done((bf16[16,2,48,384]{3,2,1,0:T(8,128)(2,1)S(1)}, bf16[16,2,48,384]{3,2,1,0:T(8,128)(2,1)S(1)}, u32[]{:S(2)}, u32[]{:S(2)}) %collective-permute-start.2) | collective-permute-done | bytes 1179680 | tf_op jit(solution)/shard_map/ppermute | solution.py:635
  64.6 1.7 %copy-done.16 = f32[1536,384]{1,0:T(8,128)S(1)} copy-done((f32[1536,384]{1,0:T(8,128)S(1)}, f32[1536,384]{1,0:T(8,128)}, u32[]{:S(2)}) %copy-start.16) | copy-done | bytes 2359320
  66.3 17.8 %mlp.1 = (f32[1536,384]{1,0:T(8,128)}, f32[1536,384]{1,0:T(8,128)S(1)}, bf16[16,2,48,384]{3,2,1,0:T(8,128)(2,1)S(1)}, bf16[16,2,48,384]{3,2,1,0:T(8,128)(2,1)S(1)}, f32[2,384]{1,0:T(2,128)S(1)}) custom-call(f32[1536,384]{1,0:T(8,128)S(1)} %copy-done.16, bf16[1536,384]{1,0:T(8,128)(2,1)S(1)} %copy-done.2, f32[4,384]{1,0:T(4,128)S(1)} %copy-done.9, ...), custom_call_target="tpu_custom_call" | custom-call | flops 10871635968 | bytes 20971520 | tf_op jit(solution)/shard_map/mlp/pallas_call | solution.py:248
  84.5 2.5 %collective-permute-done.3.two_ref = bf16[16,2,48,384]{3,2,1,0:T(8,128)(2,1)S(1)} collective-permute-done((bf16[16,2,48,384]{3,2,1,0:T(8,128)(2,1)S(1)}, bf16[16,2,48,384]{3,2,1,0:T(8,128)(2,1)S(1)}, u32[]{:S(2)}, u32[]{:S(2)}) %collective-permute-start.3) | collective-permute-done | bytes 1179680 | tf_op jit(solution)/shard_map/ppermute | solution.py:635
  87.0 1.7 %add_slabs.1 = bf16[16,2,48,384]{3,2,1,0:T(8,128)(2,1)} custom-call(bf16[16,2,48,384]{3,2,1,0:T(8,128)(2,1)S(1)} %get-tuple-element.59.one_ref, bf16[16,2,48,384]{3,2,1,0:T(8,128)(2,1)S(1)} %collective-permute-done.3.two_ref), custom_call_target="tpu_custom_call" | custom-call | tf_op jit(solution)/shard_map/add_slabs/pallas_call | solution.py:438
  88.7 6.2 %all-to-all-start.4 = ((bf16[16,2,48,384]{3,2,1,0:T(8,128)(2,1)}), bf16[16,2,48,384]{3,2,1,0:T(8,128)(2,1)S(1)}, u32[]{:S(2)}, u32[]{:S(2)}) async-start(bf16[16,2,48,384]{3,2,1,0:T(8,128)(2,1)} %add_slabs.1), calls=%async_computation.4 | async-start | bytes 2359296 | tf_op jit(solution)/shard_map/all_to_all | solution.py:639
  94.9 2.0 %copy-done.14 = bf16[1536,1152]{1,0:T(8,128)(2,1)S(1)} copy-done((bf16[1536,1152]{1,0:T(8,128)(2,1)S(1)}, bf16[1536,1152]{1,0:T(8,128)(2,1)}, u32[]{:S(2)}) %copy-start.14) | copy-done | bytes 3538968
  96.9 1.7 %copy-done.18 = f32[1536,384]{1,0:T(8,128)S(1)} copy-done((f32[1536,384]{1,0:T(8,128)S(1)}, f32[1536,384]{1,0:T(8,128)}, u32[]{:S(2)}) %copy-start.18) | copy-done | bytes 2359320
  98.6 1.3 copy-done.20
  101.0 14.6 %attn_backward.1 = (f32[1536,384]{1,0:T(8,128)}, bf16[16,48,384]{2,1,0:T(8,128)(2,1)S(1)}, bf16[17,48,384]{2,1,0:T(8,128)(2,1)S(1)}, f32[4,384]{1,0:T(4,128)S(1)}) custom-call(s32[1]{0:T(128)} %bitcast.2.half_ref, s32[12,3]{1,0:T(8,128)S(1)} %copy.22.own_mask_ref, s32[12,3]{1,0:T(8,128)S(1)} %collective-permute-done.other_mask_ref, ...), custom_call_target="tpu_custom_call" | custom-call | flops 8455716864 | bytes 20971520 | tf_op jit(solution)/shard_map/attn_backward/pallas_call | solution.py:365
  115.7 2.1 %collective-permute-done.4.received_ref = bf16[17,48,384]{2,1,0:T(8,128)(2,1)S(1)} collective-permute-done((bf16[17,48,384]{2,1,0:T(8,128)(2,1)S(1)}, bf16[17,48,384]{2,1,0:T(8,128)(2,1)S(1)}, u32[]{:S(2)}, u32[]{:S(2)}) %collective-permute-start.4) | collective-permute-done | bytes 626720 | tf_op jit(solution)/shard_map/ppermute | solution.py:635
  118.8 6.8 %all-to-all-done.4.refs_0_ = bf16[16,2,48,384]{3,2,1,0:T(8,128)(2,1)S(1)} async-done(((bf16[16,2,48,384]{3,2,1,0:T(8,128)(2,1)}), bf16[16,2,48,384]{3,2,1,0:T(8,128)(2,1)S(1)}, u32[]{:S(2)}, u32[]{:S(2)}) %all-to-all-start.4) | async-done | bytes 1179680 | tf_op jit(solution)/shard_map/all_to_all | solution.py:639
  125.6 3.6 %all-to-all-start.5 = ((bf16[16,56,384]{2,1,0:T(8,128)(2,1)}), bf16[16,56,384]{2,1,0:T(8,128)(2,1)S(1)}, u32[]{:S(2)}, u32[]{:S(2)}) async-start(bf16[16,56,384]{2,1,0:T(8,128)(2,1)} %combine.1), calls=%async_computation.5 | async-start | bytes 1376256 | tf_op jit(solution)/shard_map/all_to_all | solution.py:639
  130.3 12.7 %shampoo.2 = (f32[3,8,48,48]{3,2,1,0:T(8,128)}, f32[3,8,48,48]{3,2,1,0:T(8,128)}, f32[3,8,48,48]{3,2,1,0:T(8,128)}, f32[3,8,48,48]{3,2,1,0:T(8,128)}) custom-call(bf16[16,2,48,384]{3,2,1,0:T(8,128)(2,1)S(1)} %all-to-all-done.4.refs_0_, f32[3,8,48,48]{3,2,1,0:T(8,128)S(1)} %bitcast.15, f32[3,8,48,48]{3,2,1,0:T(8,128)S(1)} %bitcast.19, ...), custom_call_target="tpu_custom_call" | custom-call | flops 6442450944 | bytes 4194304 | tf_op jit(solution)/shard_map/shampoo/pallas_call | solution.py:610
  142.9 5.4 %all-to-all-done.5 = bf16[16,56,384]{2,1,0:T(8,128)(2,1)S(1)} async-done(((bf16[16,56,384]{2,1,0:T(8,128)(2,1)}), bf16[16,56,384]{2,1,0:T(8,128)(2,1)S(1)}, u32[]{:S(2)}, u32[]{:S(2)}) %all-to-all-start.5) | async-done | bytes 688160 | tf_op jit(solution)/shard_map/all_to_all | solution.py:639
  149.4 6.6 %shampoo.3 = (f32[3,8,48,48]{3,2,1,0:T(8,128)}, f32[3,8,48,48]{3,2,1,0:T(8,128)}, f32[3,8,48,48]{3,2,1,0:T(8,128)}, f32[3,8,48,48]{3,2,1,0:T(8,128)}, f32[4,384]...) custom-call(bf16[16,1,56,384]{3,2,1,0:T(8,128)(2,1)S(1)} %bitcast.13, ...), custom_call_target="tpu_custom_call", output_to_operand_aliasing={{0}: (6, {}), {1}: (7, {}), {2}: (8, {}), {3}: (9, {})} | custom-call | flops 3221225472 | bytes 4194304 | tf_op jit(solution)/shard_map/shampoo/pallas_call | solution.py:610
  (59 shorter events, 15.6 us)
Async XLA Ops:
  14.6 16.0 %copy-start.25 = (s32[12,3]{0,1:T(4,128)S(1)}, s32[12,3]{0,1:T(4,128)}, u32[]{:S(2)}) copy-start(s32[12,3]{0,1:T(4,128)} %param.12) | copy-start | bytes 436
  26.9 10.7 %all-to-all-start.1 = ((bf16[4,4,48,384]{3,2,1,0:T(8,128)(2,1)}), bf16[4,4,48,384]{3,2,1,0:T(8,128)(2,1)S(1)}, u32[]{:S(2)}, u32[]{:S(2)}) async-start(bf16[4,4,48,384]{3,2,1,0:T(8,128)(2,1)} %broadcast_in_dim.27), calls=%async_computation.1 | async-start | bytes 1179648 | tf_op jit(solution)/shard_map/all_to_all | solution.py:639
  30.8 1.2 collective-permute-start
  38.8 3.5 %collective-permute-start.1 = (bf16[16,48,384]{2,1,0:T(8,128)(2,1)S(1)}, bf16[16,48,384]{2,1,0:T(8,128)(2,1)S(1)}, u32[]{:S(2)}, u32[]{:S(2)}) collective-permute-start(bf16[16,48,384]{2,1,0:T(8,128)(2,1)S(1)} %bitcast.17), channel_id=1, source_target_pairs={{0,1},{1,0},{2,3},{3,2},{4,5},{5,4},{6,7},{7,6},{8,9},{9,8},{10,11... | collective-permute-start | bytes 1769480 | tf_op jit(solution)/shard_map/ppermute | solution.py:635
  38.8 22.2 %all-to-all-start.3 = ((bf16[4,4,2,48,384]{4,3,2,1,0:T(8,128)(2,1)}), bf16[4,4,2,48,384]{4,3,2,1,0:T(8,128)(2,1)S(1)}, u32[]{:S(2)}, u32[]{:S(2)}) async-start(bf16[4,4,2,48,384]{4,3,2,1,0:T(8,128)(2,1)} %broadcast_in_dim.28), calls=%async_computation.3 | async-start | bytes 2359296 | tf_op jit(solution)/shard_map/all_to_all | solution.py:639
  42.3 1.3 copy-start.3
  44.9 19.0 %copy-start.2 = (bf16[1536,384]{1,0:T(8,128)(2,1)S(1)}, bf16[1536,384]{1,0:T(8,128)(2,1)}, u32[]{:S(2)}) copy-start(bf16[1536,384]{1,0:T(8,128)(2,1)} %cot_ref.1) | copy-start | bytes 3538948
  55.1 1.8 %copy-start.13 = (bf16[1536,1152]{1,0:T(8,128)(2,1)}, bf16[1536,1152]{1,0:T(8,128)(2,1)S(1)}, u32[]{:S(2)}) copy-start(bf16[1536,1152]{1,0:T(8,128)(2,1)S(1)} %get-tuple-element.64.qkv_ref) | copy-start | bytes 10616836
  56.9 1.4 copy-start.15
  61.0 3.0 %collective-permute-start.2 = (bf16[16,2,48,384]{3,2,1,0:T(8,128)(2,1)S(1)}, bf16[16,2,48,384]{3,2,1,0:T(8,128)(2,1)S(1)}, u32[]{:S(2)}, u32[]{:S(2)}) collective-permute-start(bf16[16,2,48,384]{3,2,1,0:T(8,128)(2,1)S(1)} %bitcast.11), channel_id=1, source_target_pairs={{0,1},{1,0},{2,3},{3,2},{4,5},{5,4},{6,7},{7,6},{8,9},{9,8},{10,11... | collective-permute-start | bytes 3538952 | tf_op jit(solution)/shard_map/ppermute | solution.py:635
  64.6 1.7 %copy-start.16 = (f32[1536,384]{1,0:T(8,128)S(1)}, f32[1536,384]{1,0:T(8,128)}, u32[]{:S(2)}) copy-start(f32[1536,384]{1,0:T(8,128)} %copy-done.15) | copy-start | bytes 7077892
  84.1 4.6 %copy-start.17 = (f32[1536,384]{1,0:T(8,128)}, f32[1536,384]{1,0:T(8,128)S(1)}, u32[]{:S(2)}) copy-start(f32[1536,384]{1,0:T(8,128)S(1)} %get-tuple-element.62.grad_ref) | copy-start | bytes 7077892
  84.1 2.8 %collective-permute-start.3 = (bf16[16,2,48,384]{3,2,1,0:T(8,128)(2,1)S(1)}, bf16[16,2,48,384]{3,2,1,0:T(8,128)(2,1)S(1)}, u32[]{:S(2)}, u32[]{:S(2)}) collective-permute-start(bf16[16,2,48,384]{3,2,1,0:T(8,128)(2,1)S(1)} %get-tuple-element.60), channel_id=1, source_target_pairs={{0,1},{1,0},{2,3},{3,2},{4,5},{5,4},{6,7},{7,6},{8,9},{9,8},{10,11... | collective-permute-start | bytes 3538952 | tf_op jit(solution)/shard_map/ppermute | solution.py:635
  88.7 6.2 %copy-start.4 = (bf16[1536,384]{1,0:T(8,128)(2,1)S(1)}, bf16[1536,384]{1,0:T(8,128)(2,1)}, u32[]{:S(2)}) copy-start(bf16[1536,384]{1,0:T(8,128)(2,1)} %x_ref.3) | copy-start | bytes 3538948
  88.7 6.2 %copy-start.10 = (f32[4,384]{1,0:T(4,128)S(1)}, f32[4,384]{1,0:T(4,128)}, u32[]{:S(2)}) copy-start(f32[4,384]{1,0:T(4,128)} %refs_4_.1) | copy-start | bytes 18436
  88.7 6.2 %copy-start.24 = (bf16[384,384]{1,0:T(8,128)(2,1)S(1)}, bf16[384,384]{1,0:T(8,128)(2,1)}, u32[]{:S(2)}) copy-start(bf16[384,384]{1,0:T(8,128)(2,1)} %copy-done.23) | copy-start | bytes 884740
  88.7 36.9 %all-to-all-start.4 = ((bf16[16,2,48,384]{3,2,1,0:T(8,128)(2,1)}), bf16[16,2,48,384]{3,2,1,0:T(8,128)(2,1)S(1)}, u32[]{:S(2)}, u32[]{:S(2)}) async-start(bf16[16,2,48,384]{3,2,1,0:T(8,128)(2,1)} %add_slabs.1), calls=%async_computation.4 | async-start | bytes 2359296 | tf_op jit(solution)/shard_map/all_to_all | solution.py:639
  94.9 2.0 %copy-start.14 = (bf16[1536,1152]{1,0:T(8,128)(2,1)S(1)}, bf16[1536,1152]{1,0:T(8,128)(2,1)}, u32[]{:S(2)}) copy-start(bf16[1536,1152]{1,0:T(8,128)(2,1)} %copy-done.13) | copy-start | bytes 10616836
  96.9 1.7 %copy-start.18 = (f32[1536,384]{1,0:T(8,128)S(1)}, f32[1536,384]{1,0:T(8,128)}, u32[]{:S(2)}) copy-start(f32[1536,384]{1,0:T(8,128)} %copy-done.17) | copy-start | bytes 7077892
  115.7 2.1 %collective-permute-start.4 = (bf16[17,48,384]{2,1,0:T(8,128)(2,1)S(1)}, bf16[17,48,384]{2,1,0:T(8,128)(2,1)S(1)}, u32[]{:S(2)}, u32[]{:S(2)}) collective-permute-start(bf16[17,48,384]{2,1,0:T(8,128)(2,1)S(1)} %get-tuple-element.72), channel_id=1, source_target_pairs={{0,1},{1,0},{2,3},{3,2},{4,5},{5,4},{6,7},{7,6},{8,9},{9,8},{10,11... | collective-permute-start | bytes 1880072 | tf_op jit(solution)/shard_map/ppermute | solution.py:635
  117.7 11.4 %copy-start.1 = (f32[1,3,8,48,48]{4,3,2,1,0:T(8,128)S(1)}, f32[1,3,8,48,48]{4,3,2,1,0:T(8,128)}, u32[]{:S(2)}) copy-start(f32[1,3,8,48,48]{4,3,2,1,0:T(8,128)} %param.15) | copy-start | bytes 663556
  117.7 11.5 %copy-start.5 = (f32[1,3,8,48,48]{4,3,2,1,0:T(8,128)S(1)}, f32[1,3,8,48,48]{4,3,2,1,0:T(8,128)}, u32[]{:S(2)}) copy-start(f32[1,3,8,48,48]{4,3,2,1,0:T(8,128)} %param.16) | copy-start | bytes 663556
  125.6 22.7 %all-to-all-start.5 = ((bf16[16,56,384]{2,1,0:T(8,128)(2,1)}), bf16[16,56,384]{2,1,0:T(8,128)(2,1)S(1)}, u32[]{:S(2)}, u32[]{:S(2)}) async-start(bf16[16,56,384]{2,1,0:T(8,128)(2,1)} %combine.1), calls=%async_computation.5 | async-start | bytes 1376256 | tf_op jit(solution)/shard_map/all_to_all | solution.py:639
  130.3 18.0 %copy-start.11 = (f32[4,384]{1,0:T(4,128)S(1)}, f32[4,384]{1,0:T(4,128)}, u32[]{:S(2)}) copy-start(f32[4,384]{1,0:T(4,128)} %refs_5_.1) | copy-start | bytes 18436
  (11 other events, 10.3 us)

commit v5 on v4

--- a/solution.py
+++ b/solution.py
@@ -30,6 +30,10 @@
 SMALL_VMEM = 8 << 20
 
 
+def in_hbm(values):
+    return pltpu.with_memory_space_constraint(values, pltpu.HBM)
+
+
 def nn(left, right):
     return jnp.dot(left, right, preferred_element_type=F32)
 
@@ -165,19 +169,19 @@
             pl.BlockSpec((D, D), lambda i: (0, 0)),
         ],
         out_shape=[
-            jax.ShapeDtypeStruct((images, PAIRS, 2 * S, S), BF),
-            jax.ShapeDtypeStruct((rows, 3 * D), BF),
-            jax.ShapeDtypeStruct((rows, D), BF),
-            jax.ShapeDtypeStruct((rows, D), F32),
-            jax.ShapeDtypeStruct((D, 3 * D), BF),
-            jax.ShapeDtypeStruct((D, D), BF),
+            pltpu.HBM((images, PAIRS, 2 * S, S), BF),
+            pltpu.HBM((rows, 3 * D), BF),
+            pltpu.HBM((rows, D), BF),
+            pltpu.HBM((rows, D), F32),
+            pltpu.HBM((D, 3 * D), BF),
+            pltpu.HBM((D, D), BF),
         ],
         compiler_params=pltpu.CompilerParams(vmem_limit_bytes=VMEM_LIMIT),
         cost_estimate=pl.CostEstimate(
             flops=rows * D * (8 * D + 16 * S), bytes_accessed=16 << 20, transcendentals=rows * 6 * S
         ),
         name="attn_forward",
-    )(half, counts, own_mask, other_mask, tokens, norm_params, own, other)
+    )(half, counts, own_mask, other_mask, in_hbm(tokens), in_hbm(norm_params), own, other)
 
 
 def mlp_kernel(
@@ -252,7 +256,7 @@
         out_specs=[tile, tile, slab, slab, pl.BlockSpec((2, D), lambda i: (0, 0))],
         out_shape=[
             jax.ShapeDtypeStruct((rows, D), F32),
-            jax.ShapeDtypeStruct((rows, D), F32),
+            pltpu.HBM((rows, D), F32),
             jax.ShapeDtypeStruct(slabs, BF),
             jax.ShapeDtypeStruct(slabs, BF),
             jax.ShapeDtypeStruct((2, D), F32),
@@ -268,7 +272,7 @@
             flops=12 * rows * D * MLP, bytes_accessed=20 << 20, transcendentals=2 * rows * MLP
         ),
         name="mlp",
-    )(middle, cotangent, norm_params, own, other)
+    )(in_hbm(middle), in_hbm(cotangent), in_hbm(norm_params), own, other)
 
 
 def attn_backward_kernel(
@@ -401,7 +405,10 @@
             flops=rows * D * (16 * D + 32 * S), bytes_accessed=20 << 20, transcendentals=0
         ),
         name="attn_backward",
-    )(half, own_mask, other_mask, tokens, grad, prob, qkv, out, norm_params, later_norms, wqkv, wo)
+    )(
+        half, own_mask, other_mask,
+        *map(in_hbm, (tokens, grad, prob, qkv, out, norm_params, later_norms, wqkv, wo)),
+    )
 
 
 def pack_kernel(weight_ref, early_ref, late_ref):
@@ -628,7 +635,7 @@
             flops=groups * (3 << 30), bytes_accessed=4 << 20, transcendentals=0
         ),
         name="shampoo",
-    )(received, weights, stat_left, stat_right, *norms, *earlier)
+    )(received, in_hbm(weights), in_hbm(stat_left), in_hbm(stat_right), *map(in_hbm, norms), *earlier)
 
 
 def swap_heads(values):

time: 157 us -> 151 us (0.962)
  local copies, waits for them, and re-layouts: 22.2 us -> 3.15 us
  waiting for transfers between devices: 26.1 us -> 35.8 us
  Pallas kernels: 64.8 us -> 70.9 us
  starting transfers between devices: 17.9 us -> 15.9 us
    unnamed x53 -> x9, local copies, waits for them, and re-layouts: 20.2 us -> 1.16 us
    all_to_all x4, waiting for transfers between devices: 17.9 us -> 27 us  [to_all(): return lax.all_to_all(values, axis, 0, 0)]
    pallas_call x2, Pallas kernels: 19.3 us -> 21.5 us  [shampoo(): pl.pallas_call(lambda *refs: shampoo_kernel(scale, bool(norms), *refs), g...]
  transfers between devices with their start and end apart: 9 -> 9, of which waited for: 7 -> 8; matrix products, arithmetic and copies ran while one was open for 0% -> 0% of each run, Pallas kernels for 25% -> 28%
where the time goes in v5:
time: 151 us
  Pallas kernels  70.9 us (47%)
  waiting for transfers between devices  35.8 us (24%)
  blocking collectives  24.2 us (16%)
  starting transfers between devices  15.9 us (11%)
  local copies, waits for them, and re-layouts  3.15 us (2%)
    all_to_all x4, waiting for transfers between devices, to_all(): return lax.all_to_all(values, axis, 0, 0)  27 us
    all_to_all x2, blocking collectives, to_all(): return lax.all_to_all(values, axis, 0, 0)  24.2 us
    pallas_call x2, Pallas kernels, shampoo(): pl.pallas_call(lambda *refs: shampoo_kernel(scale, bool(norms), *refs), g...  21.5 us
    pallas_call x1, Pallas kernels, mlp(): pl.pallas_call(mlp_kernel, grid=(rows // TILE,), in_specs=[tile, tile, pl...  19.1 us
    pallas_call x1, Pallas kernels, attn_backward(): pl.pallas_call(attn_backward_kernel, grid=(rows // TILE,), in_specs=[smem...  16.1 us
    all_to_all x4, starting transfers between devices, to_all(): return lax.all_to_all(values, axis, 0, 0)  15.7 us
    pallas_call x1, Pallas kernels, attn_forward(): pl.pallas_call(attn_forward_kernel, grid=(rows // TILE,), in_specs=[smem]...  11.2 us
    ppermute x5, waiting for transfers between devices, swap_heads(): return lax.ppermute(values, 'head', [(0, 1), (1, 0)])  8.76 us
  transfers between devices with their start and end apart: 9, of which 8 were waited for; matrix products, arithmetic and copies ran while one was open for 0% of the time, Pallas kernels for 28%

profile of v5, /device:TPU:0, one launch (start us, length us, event | category | flops | bytes accessed | tf_op | source)
XLA Modules:
  0.0 150.7 jit_solution(5123833250460620209)
XLA Ops:
  0.7 1.1 copy-done
  1.9 12.8 %all_to_all.30 = bf16[4,48,384]{2,1,0:T(8,128)(2,1)S(1)} all-to-all(bf16[4,48,384]{2,1,0:T(8,128)(2,1)S(1)} %get-tuple-element.48), channel_id=1, replica_groups=mesh['outer'=4,'inner'=4,'head'=2] {'outer'}, dimensions={0} | all-to-all | bytes 294912 | tf_op jit(solution)/shard_map/all_to_all | solution.py:646
  14.6 11.4 %all_to_all.31 = bf16[4,2,48,384]{3,2,1,0:T(8,128)(2,1)S(1)} all-to-all(bf16[4,2,48,384]{3,2,1,0:T(8,128)(2,1)S(1)} %get-tuple-element.51), channel_id=1, replica_groups=mesh['outer'=4,'inner'=4,'head'=2] {'outer'}, dimensions={0} | all-to-all | bytes 589824 | tf_op jit(solution)/shard_map/all_to_all | solution.py:646
  26.1 0.9 broadcast_in_dim.27
  26.9 3.7 %all-to-all-start.1 = ((bf16[4,4,48,384]{3,2,1,0:T(8,128)(2,1)}), bf16[4,4,48,384]{3,2,1,0:T(8,128)(2,1)S(1)}, u32[]{:S(2)}, u32[]{:S(2)}) async-start(bf16[4,4,48,384]{3,2,1,0:T(8,128)(2,1)} %broadcast_in_dim.27), calls=%async_computation.1 | async-start | bytes 1179648 | tf_op jit(solution)/shard_map/all_to_all | solution.py:646
  30.8 1.2 collective-permute-done.other_mask_ref
  31.9 5.7 %all-to-all-done.1 = bf16[4,4,48,384]{3,2,1,0:T(8,128)(2,1)S(1)} async-done(((bf16[4,4,48,384]{3,2,1,0:T(8,128)(2,1)}), bf16[4,4,48,384]{3,2,1,0:T(8,128)(2,1)S(1)}, u32[]{:S(2)}, u32[]{:S(2)}) %all-to-all-start.1) | async-done | bytes 589856 | tf_op jit(solution)/shard_map/all_to_all | solution.py:646
  37.6 1.1 broadcast_in_dim.28
  38.8 3.7 %all-to-all-start.3 = ((bf16[4,4,2,48,384]{4,3,2,1,0:T(8,128)(2,1)}), bf16[4,4,2,48,384]{4,3,2,1,0:T(8,128)(2,1)S(1)}, u32[]{:S(2)}, u32[]{:S(2)}) async-start(bf16[4,4,2,48,384]{4,3,2,1,0:T(8,128)(2,1)} %broadcast_in_dim.28), calls=%async_computation.3 | async-start | bytes 2359296 | tf_op jit(solution)/shard_map/all_to_all | solution.py:646
  42.5 11.2 %attn_forward.1 = (bf16[6,3,512,256]{3,2,1,0:T(8,128)(2,1)}, bf16[1536,1152]{1,0:T(8,128)(2,1)}, bf16[1536,384]{1,0:T(8,128)(2,1)}, f32[1536,384]{1,0:T(8,128)},...) custom-call(s32[1]{0:T(128)} %bitcast.2.half_ref, s32[12]{0:T(128)S(1)} %copy-done.1, ...), custom_call_target="tpu_custom_call" | custom-call | flops 4227858432 | bytes 16777216 | tf_op jit(solution)/shard_map/attn_forward/pallas_call | solution.py:159
  53.7 4.6 %all-to-all-done.3 = bf16[4,4,2,48,384]{4,3,2,1,0:T(8,128)(2,1)S(1)} async-done(((bf16[4,4,2,48,384]{4,3,2,1,0:T(8,128)(2,1)}), bf16[4,4,2,48,384]{4,3,2,1,0:T(8,128)(2,1)S(1)}, u32[]{:S(2)}, u32[]{:S(2)}) %all-to-all-start.3) | async-done | bytes 1179680 | tf_op jit(solution)/shard_map/all_to_all | solution.py:646
  58.3 2.8 %collective-permute-done.2.other_ref = bf16[16,2,48,384]{3,2,1,0:T(8,128)(2,1)S(1)} collective-permute-done((bf16[16,2,48,384]{3,2,1,0:T(8,128)(2,1)S(1)}, bf16[16,2,48,384]{3,2,1,0:T(8,128)(2,1)S(1)}, u32[]{:S(2)}, u32[]{:S(2)}) %collective-permute-start.2) | collective-permute-done | bytes 1179680 | tf_op jit(solution)/shard_map/ppermute | solution.py:642
  61.1 19.1 %mlp.1 = (f32[1536,384]{1,0:T(8,128)}, f32[1536,384]{1,0:T(8,128)}, bf16[16,2,48,384]{3,2,1,0:T(8,128)(2,1)S(1)}, bf16[16,2,48,384]{3,2,1,0:T(8,128)(2,1)S(1)}, f32[2,384]{1,0:T(2,128)S(1)}) custom-call(f32[1536,384]{1,0:T(8,128)} %get-tuple-element.56.middle_ref, bf16[1536,384]{1,0:T(8,128)(2,1)} %cot_ref.1, f32[4,384]{1,0:T(4,128)} %refs_4_.1, ...), custom_call_target="tpu_custom_call" | custom-call | flops 10871635968 | bytes 20971520 | tf_op jit(solution)/shard_map/mlp/pallas_call | solution.py:252
  80.4 2.7 %collective-permute-done.3.two_ref = bf16[16,2,48,384]{3,2,1,0:T(8,128)(2,1)S(1)} collective-permute-done((bf16[16,2,48,384]{3,2,1,0:T(8,128)(2,1)S(1)}, bf16[16,2,48,384]{3,2,1,0:T(8,128)(2,1)S(1)}, u32[]{:S(2)}, u32[]{:S(2)}) %collective-permute-start.3) | collective-permute-done | bytes 1179680 | tf_op jit(solution)/shard_map/ppermute | solution.py:642
  83.1 1.7 %add_slabs.1 = bf16[16,2,48,384]{3,2,1,0:T(8,128)(2,1)} custom-call(bf16[16,2,48,384]{3,2,1,0:T(8,128)(2,1)S(1)} %get-tuple-element.59.one_ref, bf16[16,2,48,384]{3,2,1,0:T(8,128)(2,1)S(1)} %collective-permute-done.3.two_ref), custom_call_target="tpu_custom_call" | custom-call | tf_op jit(solution)/shard_map/add_slabs/pallas_call | solution.py:445
  84.8 4.8 %all-to-all-start.4 = ((bf16[16,2,48,384]{3,2,1,0:T(8,128)(2,1)}), bf16[16,2,48,384]{3,2,1,0:T(8,128)(2,1)S(1)}, u32[]{:S(2)}, u32[]{:S(2)}) async-start(bf16[16,2,48,384]{3,2,1,0:T(8,128)(2,1)} %add_slabs.1), calls=%async_computation.4 | async-start | bytes 2359296 | tf_op jit(solution)/shard_map/all_to_all | solution.py:646
  89.6 16.1 %attn_backward.1 = (f32[1536,384]{1,0:T(8,128)}, bf16[16,48,384]{2,1,0:T(8,128)(2,1)S(1)}, bf16[17,48,384]{2,1,0:T(8,128)(2,1)S(1)}, f32[4,384]{1,0:T(4,128)S(1)}) custom-call(s32[1]{0:T(128)} %bitcast.2.half_ref, s32[12,3]{1,0:T(8,128)S(1)} %copy.22.own_mask_ref, s32[12,3]{1,0:T(8,128)S(1)} %collective-permute-done.other_mask_ref, bf16[1536,384]{1,0:T(8,128)(2,1)} %x_ref.3, ...), custom_call_target="tpu_custom_call" | custom-call | flops 8455716864 | bytes 20971520 | tf_op jit(solution)/shard_map/attn_backward/pallas_call | solution.py:369
  105.7 2.0 %collective-permute-done.4.received_ref = bf16[17,48,384]{2,1,0:T(8,128)(2,1)S(1)} collective-permute-done((bf16[17,48,384]{2,1,0:T(8,128)(2,1)S(1)}, bf16[17,48,384]{2,1,0:T(8,128)(2,1)S(1)}, u32[]{:S(2)}, u32[]{:S(2)}) %collective-permute-start.4) | collective-permute-done | bytes 626720 | tf_op jit(solution)/shard_map/ppermute | solution.py:642
  107.8 1.0 combine.1
  108.8 11.4 %all-to-all-done.4.refs_0_ = bf16[16,2,48,384]{3,2,1,0:T(8,128)(2,1)S(1)} async-done(((bf16[16,2,48,384]{3,2,1,0:T(8,128)(2,1)}), bf16[16,2,48,384]{3,2,1,0:T(8,128)(2,1)S(1)}, u32[]{:S(2)}, u32[]{:S(2)}) %all-to-all-start.4) | async-done | bytes 1179680 | tf_op jit(solution)/shard_map/all_to_all | solution.py:646
  120.2 3.6 %all-to-all-start.5 = ((bf16[16,56,384]{2,1,0:T(8,128)(2,1)}), bf16[16,56,384]{2,1,0:T(8,128)(2,1)S(1)}, u32[]{:S(2)}, u32[]{:S(2)}) async-start(bf16[16,56,384]{2,1,0:T(8,128)(2,1)} %combine.1), calls=%async_computation.5 | async-start | bytes 1376256 | tf_op jit(solution)/shard_map/all_to_all | solution.py:646
  123.8 13.7 %shampoo.2 = (f32[3,8,48,48]{3,2,1,0:T(8,128)}, f32[3,8,48,48]{3,2,1,0:T(8,128)}, f32[3,8,48,48]{3,2,1,0:T(8,128)}, f32[3,8,48,48]{3,2,1,0:T(8,128)}) custom-call(bf16[16,2,48,384]{3,2,1,0:T(8,128)(2,1)S(1)} %all-to-all-done.4.refs_0_, f32[3,8,48,48]{3,2,1,0:T(8,128)} %bitcast.14, f32[3,8,48,48]{3,2,1,0:T(8,128)} %bitcast.19, f32[3,8,48,48]{3,2,1,0:T(8,128)} %bitcast.21), custom_call_target="tpu_custom_call" | custom-call | flops 6442450944 | bytes 4194304 | tf_op jit(solution)/shard_map/shampoo/pallas_call | solution.py:617
  137.5 5.4 %all-to-all-done.5 = bf16[16,56,384]{2,1,0:T(8,128)(2,1)S(1)} async-done(((bf16[16,56,384]{2,1,0:T(8,128)(2,1)}), bf16[16,56,384]{2,1,0:T(8,128)(2,1)S(1)}, u32[]{:S(2)}, u32[]{:S(2)}) %all-to-all-start.5) | async-done | bytes 688160 | tf_op jit(solution)/shard_map/all_to_all | solution.py:646
  142.8 7.8 %shampoo.3 = (f32[3,8,48,48]{3,2,1,0:T(8,128)}, f32[3,8,48,48]{3,2,1,0:T(8,128)}, f32[3,8,48,48]{3,2,1,0:T(8,128)}, f32[3,8,48,48]{3,2,1,0:T(8,128)}, f32[4,384]...) custom-call(bf16[16,1,56,384]{3,2,1,0:T(8,128)(2,1)S(1)} %bitcast.13, ...), custom_call_target="tpu_custom_call", output_to_operand_aliasing={{0}: (6, {}), {1}: (7, {}), {2}: (8, {}), {3}: (9, {})} | custom-call | flops 3221225472 | bytes 4194304 | tf_op jit(solution)/shard_map/shampoo/pallas_call | solution.py:617
  (15 shorter events, 0.4 us)
Async XLA Ops:
  0.6 1.1 copy-start
  14.6 16.0 %copy-start.3 = (s32[12,3]{0,1:T(4,128)S(1)}, s32[12,3]{0,1:T(4,128)}, u32[]{:S(2)}) copy-start(s32[12,3]{0,1:T(4,128)} %param.12) | copy-start | bytes 436
  26.9 10.7 %all-to-all-start.1 = ((bf16[4,4,48,384]{3,2,1,0:T(8,128)(2,1)}), bf16[4,4,48,384]{3,2,1,0:T(8,128)(2,1)S(1)}, u32[]{:S(2)}, u32[]{:S(2)}) async-start(bf16[4,4,48,384]{3,2,1,0:T(8,128)(2,1)} %broadcast_in_dim.27), calls=%async_computation.1 | async-start | bytes 1179648 | tf_op jit(solution)/shard_map/all_to_all | solution.py:646
  30.8 1.2 collective-permute-start
  38.8 3.7 %copy-start.1 = (s32[12]{0:T(128)S(1)}, s32[12]{0:T(128)}, u32[]{:S(2)}) copy-start(s32[12]{0:T(128)} %counts_ref.1) | copy-start | bytes 148
  38.8 3.7 %collective-permute-start.1 = (bf16[16,48,384]{2,1,0:T(8,128)(2,1)S(1)}, bf16[16,48,384]{2,1,0:T(8,128)(2,1)S(1)}, u32[]{:S(2)}, u32[]{:S(2)}) collective-permute-start(bf16[16,48,384]{2,1,0:T(8,128)(2,1)S(1)} %bitcast.17), channel_id=1, source_target_pairs={{0,1},{1,0},{2,3},{3,2},{4,5},{5,4},{6,7},{7,6},{8,9},{9,8},{10,11... | collective-permute-start | bytes 1769480 | tf_op jit(solution)/shard_map/ppermute | solution.py:642
  38.8 19.5 %all-to-all-start.3 = ((bf16[4,4,2,48,384]{4,3,2,1,0:T(8,128)(2,1)}), bf16[4,4,2,48,384]{4,3,2,1,0:T(8,128)(2,1)S(1)}, u32[]{:S(2)}, u32[]{:S(2)}) async-start(bf16[4,4,2,48,384]{4,3,2,1,0:T(8,128)(2,1)} %broadcast_in_dim.28), calls=%async_computation.3 | async-start | bytes 2359296 | tf_op jit(solution)/shard_map/all_to_all | solution.py:646
  58.3 2.8 %collective-permute-start.2 = (bf16[16,2,48,384]{3,2,1,0:T(8,128)(2,1)S(1)}, bf16[16,2,48,384]{3,2,1,0:T(8,128)(2,1)S(1)}, u32[]{:S(2)}, u32[]{:S(2)}) collective-permute-start(bf16[16,2,48,384]{3,2,1,0:T(8,128)(2,1)S(1)} %bitcast.11), channel_id=1, source_target_pairs={{0,1},{1,0},{2,3},{3,2},{4,5},{5,4},{6,7},{7,6},{8,9},{9,8},{10,11... | collective-permute-start | bytes 3538952 | tf_op jit(solution)/shard_map/ppermute | solution.py:642
  80.2 4.5 %copy-start.2 = (f32[2,384]{1,0:T(2,128)}, f32[2,384]{1,0:T(2,128)S(1)}, u32[]{:S(2)}) copy-start(f32[2,384]{1,0:T(2,128)S(1)} %get-tuple-element.66.later_norm_ref) | copy-start | bytes 9220
  80.2 2.8 %collective-permute-start.3 = (bf16[16,2,48,384]{3,2,1,0:T(8,128)(2,1)S(1)}, bf16[16,2,48,384]{3,2,1,0:T(8,128)(2,1)S(1)}, u32[]{:S(2)}, u32[]{:S(2)}) collective-permute-start(bf16[16,2,48,384]{3,2,1,0:T(8,128)(2,1)S(1)} %get-tuple-element.60), channel_id=1, source_target_pairs={{0,1},{1,0},{2,3},{3,2},{4,5},{5,4},{6,7},{7,6},{8,9},{9,8},{10,11... | collective-permute-start | bytes 3538952 | tf_op jit(solution)/shard_map/ppermute | solution.py:642
  84.8 35.4 %all-to-all-start.4 = ((bf16[16,2,48,384]{3,2,1,0:T(8,128)(2,1)}), bf16[16,2,48,384]{3,2,1,0:T(8,128)(2,1)S(1)}, u32[]{:S(2)}, u32[]{:S(2)}) async-start(bf16[16,2,48,384]{3,2,1,0:T(8,128)(2,1)} %add_slabs.1), calls=%async_computation.4 | async-start | bytes 2359296 | tf_op jit(solution)/shard_map/all_to_all | solution.py:646
  105.7 2.1 %collective-permute-start.4 = (bf16[17,48,384]{2,1,0:T(8,128)(2,1)S(1)}, bf16[17,48,384]{2,1,0:T(8,128)(2,1)S(1)}, u32[]{:S(2)}, u32[]{:S(2)}) collective-permute-start(bf16[17,48,384]{2,1,0:T(8,128)(2,1)S(1)} %get-tuple-element.72), channel_id=1, source_target_pairs={{0,1},{1,0},{2,3},{3,2},{4,5},{5,4},{6,7},{7,6},{8,9},{9,8},{10,11... | collective-permute-start | bytes 1880072 | tf_op jit(solution)/shard_map/ppermute | solution.py:642
  120.2 22.7 %all-to-all-start.5 = ((bf16[16,56,384]{2,1,0:T(8,128)(2,1)}), bf16[16,56,384]{2,1,0:T(8,128)(2,1)S(1)}, u32[]{:S(2)}, u32[]{:S(2)}) async-start(bf16[16,56,384]{2,1,0:T(8,128)(2,1)} %combine.1), calls=%async_computation.5 | async-start | bytes 1376256 | tf_op jit(solution)/shard_map/all_to_all | solution.py:646

commit v6 on v5

--- a/solution.py
+++ b/solution.py
@@ -17,10 +17,10 @@
 HALF = D // 2
 SLABS = 16
 INNER = 4
+OUTER = SLABS // INNER
 TILE = 512
 IMAGES = TILE // S
 NORM_ROWS = 8
-HIDDEN = 768
 PACK = 2
 ROOT_HALF = 0.7071067811865476
 DENSITY_FACTOR = 0.3989422804014327
@@ -28,6 +28,7 @@
 F32 = jnp.float32
 VMEM_LIMIT = 40 << 20
 SMALL_VMEM = 8 << 20
+SHAMPOO_VMEM = 24 << 20
 
 
 def in_hbm(values):
@@ -64,7 +65,7 @@
 
 
 def slab_at(owner):
-    return (owner % INNER) * (SLABS // INNER) + owner // INNER
+    return (owner % INNER) * OUTER + owner // INNER
 
 
 def lane_halves():
@@ -77,8 +78,8 @@
     return jnp.concatenate([values * first, values * second], axis=0)
 
 
-def mask_lanes(half_ref, own_ref, other_ref, image, pair):
-    image = half_ref[0] * (own_ref.shape[0] // 2) + image
+def mask_lanes(place_ref, own_ref, other_ref, image, pair):
+    image = place_ref[0] * (own_ref.shape[0] // 2) + image
     heads = own_ref.shape[1]
     on = [
         own_ref[image, head] if head < heads else other_ref[image, head - heads]
@@ -89,28 +90,36 @@
 
 
 def attn_forward_kernel(
-    half_ref, counts_ref, own_mask_ref, other_mask_ref, x_ref, norm_ref, own_ref, other_ref,
-    prob_ref, qkv_ref, out_ref, middle_ref, wqkv_ref, wo_ref,
+    place_ref, counts_ref, own_mask_ref, other_mask_ref, x_ref, norm_ref, *refs
 ):
+    slab_refs, refs = refs[: 2 * INNER], refs[2 * INNER :]
+    prob_ref, qkv_ref, out_ref, middle_ref, wqkv_ref, wo_ref, held_ref = refs
     step = pl.program_id(0)
 
     @pl.when(step == 0)
     def _():
-        slabs = (own_ref, other_ref)
+        for number, ref in enumerate(slab_refs):
+            side, apart = divmod(number, INNER)
+            held_ref[side, place_ref[1] ^ apart] = ref[...]
+
+        def slab_of(side, owner):
+            return held_ref[side, owner % INNER, owner // INNER]
+
         for row in range(D // 48):
             for part in range(3):
                 pieces = []
-                for ref in slabs:
+                for number in range(2):
                     slab, side = divmod(3 * row + part, 2)
-                    pieces.append(ref[slab_at(slab)][:, side * HALF : (side + 1) * HALF])
+                    piece = slab_of(number, slab)[:, side * HALF : (side + 1) * HALF]
+                    pieces.append(piece)
                 joined = jnp.concatenate(pieces, axis=1)
                 if part == 0:
                     joined = joined * 0.125
                 wqkv_ref[48 * row : 48 * row + 48, D * part : D * part + D] = joined
-        for side, ref in enumerate(slabs):
+        for side in range(2):
             for row in range(HALF // 48):
                 start = side * HALF + 48 * row
-                wo_ref[start : start + 48, :] = ref[slab_at(12 + row)]
+                wo_ref[start : start + 48, :] = slab_of(side, 12 + row)
 
     x = x_ref[...].astype(F32)
     normed, _ = normalize(x)
@@ -130,7 +139,7 @@
         return nt(stacked(qkv_ref[here, query_lanes], first, second), qkv_ref[here, key_lanes])
 
     def get_prob(task, scores):
-        image = half_ref[0] * (counts_ref.shape[0] // 2) + IMAGES * step + task[0]
+        image = place_ref[0] * (counts_ref.shape[0] // 2) + IMAGES * step + task[0]
         scores = jnp.where(column < counts_ref[image], scores, -1e30)
         top = jnp.max(scores, axis=-1, keepdims=True)
         exp_scores = jnp.exp(scores - top)
@@ -145,21 +154,21 @@
         here, lanes, _, value_lanes = places(task)
         values = qkv_ref[here, value_lanes]
         head_out = nn(prob[:S], values * first) + nn(prob[S:], values * second)
-        mask = mask_lanes(half_ref, own_mask_ref, other_mask_ref, IMAGES * step + task[0], task[1])
+        mask = mask_lanes(place_ref, own_mask_ref, other_mask_ref, IMAGES * step + task[0], task[1])
         out_ref[here, lanes] = (head_out * mask).astype(BF)
     middle_ref[...] = x + nn(out_ref[...], wo_ref[...])
 
 
-def attn_forward(half, counts, own_mask, other_mask, tokens, norm_params, own, other):
+def attn_forward(place, counts, own_mask, other_mask, tokens, norm_params, slabs):
     rows = tokens.shape[0]
     images = rows // S
     tile = pl.BlockSpec((TILE, D), lambda i: (i, 0))
-    slab = pl.BlockSpec((SLABS, 48, D), lambda i: (0, 0, 0))
+    slab = pl.BlockSpec((OUTER, 48, D), lambda i: (0, 0, 0))
     smem = pl.BlockSpec(memory_space=pltpu.SMEM)
     return pl.pallas_call(
         attn_forward_kernel,
         grid=(rows // TILE,),
-        in_specs=[smem] * 4 + [tile, pl.BlockSpec((4, D), lambda i: (0, 0)), slab, slab],
+        in_specs=[smem] * 4 + [tile, pl.BlockSpec((4, D), lambda i: (0, 0))] + [slab] * 2 * INNER,
         out_specs=[
             pl.BlockSpec((IMAGES, PAIRS, 2 * S, S), lambda i: (i, 0, 0, 0)),
             pl.BlockSpec((TILE, 3 * D), lambda i: (i, 0)),
@@ -176,38 +185,40 @@
             pltpu.HBM((D, 3 * D), BF),
             pltpu.HBM((D, D), BF),
         ],
+        scratch_shapes=[pltpu.VMEM((2, INNER, OUTER, 48, D), BF)],
         compiler_params=pltpu.CompilerParams(vmem_limit_bytes=VMEM_LIMIT),
         cost_estimate=pl.CostEstimate(
             flops=rows * D * (8 * D + 16 * S), bytes_accessed=16 << 20, transcendentals=rows * 6 * S
         ),
         name="attn_forward",
-    )(half, counts, own_mask, other_mask, in_hbm(tokens), in_hbm(norm_params), own, other)
-
-
-def mlp_kernel(
-    middle_ref, cot_ref, norm_ref, own_ref, other_ref,
-    out_ref, grad_ref, own_grad_ref, sent_grad_ref, norm_grad_ref,
-    up_ref, down_ref, up_grad_ref, down_grad_ref,
-):
+    )(place, counts, own_mask, other_mask, in_hbm(tokens), in_hbm(norm_params), *slabs)
+
+
+def mlp_kernel(place_ref, middle_ref, cot_ref, norm_ref, *refs):
+    slab_refs, refs = refs[: 2 * INNER], refs[2 * INNER :]
+    out_ref, grad_ref, norm_grad_ref, *refs = refs
+    sent_refs, (up_ref, down_ref, up_grad_ref, down_grad_ref) = refs[:INNER], refs[INNER:]
     step = pl.program_id(0)
-    sides = ((own_ref, own_grad_ref), (other_ref, sent_grad_ref))
-    places = [
-        (side, part, MLP // 2 * side + D * part, row)
-        for side in range(2)
-        for part in range(2)
-        for row in range(8)
-    ]
+    half = MLP // 2
+
+    def places(apart, outer):
+        inner = place_ref[1] ^ apart
+        row = pl.multiple_of(48 * (2 * outer + inner // 2), 16)
+        lane = pl.multiple_of(D * (inner % 2), 128)
+        down_row = pl.multiple_of(48 * (INNER * outer + inner), 16)
+        return row, lane, down_row
 
     @pl.when(step == 0)
     def _():
         up_grad_ref[...] = jnp.zeros_like(up_grad_ref)
         down_grad_ref[...] = jnp.zeros_like(down_grad_ref)
         norm_grad_ref[...] = jnp.zeros_like(norm_grad_ref)
-        for side, part, start, row in places:
-            up = sides[side][0][slab_at(2 * row + part), 0]
-            up_ref[48 * row : 48 * row + 48, start : start + D] = up
-            down = sides[side][0][slab_at(8 * part + row), 1]
-            down_ref[start + 48 * row : start + 48 * row + 48, :] = down
+        for number, ref in enumerate(slab_refs):
+            side, apart = divmod(number, INNER)
+            for outer in range(OUTER):
+                row, lane, down_row = places(apart, outer)
+                up_ref[side, pl.ds(row, 48), pl.ds(lane, D)] = ref[outer, 0]
+                down_ref[side, pl.ds(down_row, 48), :] = ref[outer, 1]
 
     middle = middle_ref[...]
     normed, inverse_std = normalize(middle)
@@ -215,9 +226,8 @@
     cot = cot_ref[...]
     total = middle
     back = None
-    for start in range(0, MLP, HIDDEN):
-        hidden = slice(start, start + HIDDEN)
-        up, down = up_ref[:, hidden], down_ref[hidden, :]
+    for side in range(2):
+        up, down = up_ref[side], down_ref[side]
         pre = nn(rows, up)
         act_grad = nt(cot, down)
         cumulative = 0.5 * (1.0 + lax.erf(pre * ROOT_HALF))
@@ -227,8 +237,8 @@
         total = total + nn(act, down)
         term = nt(pre_grad, up)
         back = term if back is None else back + term
-        down_grad_ref[hidden, :] += tn(act, cot)
-        up_grad_ref[:, hidden] += tn(rows, pre_grad)
+        down_grad_ref[side] += tn(act, cot)
+        up_grad_ref[side] += tn(rows, pre_grad)
     out_ref[...] = total
     grad_in, norm_part = norm_backward(back, normed, inverse_std, norm_ref[2:3, :])
     norm_grad_ref[...] += norm_part
@@ -236,47 +246,53 @@
 
     @pl.when(step == pl.num_programs(0) - 1)
     def _():
-        for side, part, start, row in places:
-            ref = sides[side][1]
-            up = up_grad_ref[48 * row : 48 * row + 48, start : start + D]
-            ref[slab_at(2 * row + part), 0] = up.astype(ref.dtype)
-            down = down_grad_ref[start + 48 * row : start + 48 * row + 48, :]
-            ref[slab_at(8 * part + row), 1] = down.astype(ref.dtype)
-
-
-def mlp(middle, cotangent, norm_params, own, other):
+        for apart, ref in enumerate(sent_refs):
+            for outer in range(OUTER):
+                row, lane, down_row = places(apart, outer)
+                for side in range(2):
+                    up = up_grad_ref[side, pl.ds(row, 48), pl.ds(lane, D)]
+                    ref[side, outer, 0] = up.astype(BF)
+                    ref[side, outer, 1] = down_grad_ref[side, pl.ds(down_row, 48), :].astype(BF)
+
+
+def mlp(place, middle, cotangent, norm_params, slabs):
     rows = middle.shape[0]
-    slabs = (SLABS, 2, 48, D)
-    slab = pl.BlockSpec(slabs, lambda i: (0, 0, 0, 0))
+    slab = pl.BlockSpec((OUTER, 2, 48, D), lambda i: (0, 0, 0, 0))
+    sent = pl.BlockSpec((2, OUTER, 2, 48, D), lambda i: (0, 0, 0, 0, 0))
     tile = pl.BlockSpec((TILE, D), lambda i: (i, 0))
     return pl.pallas_call(
         mlp_kernel,
         grid=(rows // TILE,),
-        in_specs=[tile, tile, pl.BlockSpec((4, D), lambda i: (0, 0)), slab, slab],
-        out_specs=[tile, tile, slab, slab, pl.BlockSpec((2, D), lambda i: (0, 0))],
+        in_specs=[
+            pl.BlockSpec(memory_space=pltpu.SMEM),
+            tile,
+            tile,
+            pl.BlockSpec((4, D), lambda i: (0, 0)),
+            *[slab] * 2 * INNER,
+        ],
+        out_specs=[tile, tile, pl.BlockSpec((2, D), lambda i: (0, 0)), *[sent] * INNER],
         out_shape=[
             jax.ShapeDtypeStruct((rows, D), F32),
             pltpu.HBM((rows, D), F32),
-            jax.ShapeDtypeStruct(slabs, BF),
-            jax.ShapeDtypeStruct(slabs, BF),
             jax.ShapeDtypeStruct((2, D), F32),
+            *[jax.ShapeDtypeStruct((2, OUTER, 2, 48, D), BF)] * INNER,
         ],
         scratch_shapes=[
-            pltpu.VMEM((D, MLP), BF),
-            pltpu.VMEM((MLP, D), BF),
-            pltpu.VMEM((D, MLP), F32),
-            pltpu.VMEM((MLP, D), F32),
+            pltpu.VMEM((2, D, MLP // 2), BF),
+            pltpu.VMEM((2, MLP // 2, D), BF),
+            pltpu.VMEM((2, D, MLP // 2), F32),
+            pltpu.VMEM((2, MLP // 2, D), F32),
         ],
         compiler_params=pltpu.CompilerParams(vmem_limit_bytes=VMEM_LIMIT),
         cost_estimate=pl.CostEstimate(
             flops=12 * rows * D * MLP, bytes_accessed=20 << 20, transcendentals=2 * rows * MLP
         ),
         name="mlp",
-    )(in_hbm(middle), in_hbm(cotangent), in_hbm(norm_params), own, other)
+    )(place, in_hbm(middle), in_hbm(cotangent), in_hbm(norm_params), *slabs)
 
 
 def attn_backward_kernel(
-    half_ref, own_mask_ref, other_mask_ref, x_ref, grad_ref, prob_ref, qkv_ref, out_ref,
+    place_ref, own_mask_ref, other_mask_ref, x_ref, grad_ref, prob_ref, qkv_ref, out_ref,
     norm_ref, later_norm_ref, wqkv_ref, wo_ref,
     in_grad_ref, own_grad_ref, sent_grad_ref, norm_grad_ref,
     dqkv_ref, wqkv_grad_ref, wo_grad_ref,
@@ -309,7 +325,7 @@
 
     def get_pair_grad(task):
         here, lanes, _, _ = places(task)
-        mask = mask_lanes(half_ref, own_mask_ref, other_mask_ref, IMAGES * step + task[0], task[1])
+        mask = mask_lanes(place_ref, own_mask_ref, other_mask_ref, IMAGES * step + task[0], task[1])
         grad = whole_grad[here, lanes] * mask.astype(BF)
         dots = grad.astype(F32) * head_out[here, lanes].astype(F32)
         first_dot = jnp.sum(dots * first_wide, axis=-1, keepdims=True)
@@ -361,7 +377,7 @@
 
 
 def attn_backward(
-    half, own_mask, other_mask, tokens, grad, prob, qkv, out, norm_params, later_norms, wqkv, wo
+    place, own_mask, other_mask, tokens, grad, prob, qkv, out, norm_params, later_norms, wqkv, wo
 ):
     rows = tokens.shape[0]
     tile = pl.BlockSpec((TILE, D), lambda i: (i, 0))
@@ -406,7 +422,7 @@
         ),
         name="attn_backward",
     )(
-        half, own_mask, other_mask,
+        place, own_mask, other_mask,
         *map(in_hbm, (tokens, grad, prob, qkv, out, norm_params, later_norms, wqkv, wo)),
     )
 
@@ -436,40 +452,70 @@
     )(weights)
 
 
-def add_kernel(one_ref, two_ref, out_ref):
-    out_ref[...] = (one_ref[...].astype(F32) + two_ref[...].astype(F32)).astype(BF)
-
-
-def add_slabs(one, two):
-    block = pl.BlockSpec((4,) + one.shape[1:], lambda i: (i, 0, 0, 0))
+def sum_kernel(*refs):
+    *in_refs, kept_ref, sent_ref = refs
+    for side, out_ref in enumerate((kept_ref, sent_ref)):
+        total = in_refs[0][side].astype(F32)
+        for ref in in_refs[1:]:
+            total = total + ref[side].astype(F32)
+        out_ref[...] = total.astype(out_ref.dtype)
+
+
+def sum_late(pieces):
+    shape = pieces[0].shape[1:]
     return pl.pallas_call(
-        add_kernel,
-        grid=(one.shape[0] // 4,),
-        in_specs=[block, block],
-        out_specs=block,
-        out_shape=jax.ShapeDtypeStruct(one.shape, BF),
+        sum_kernel,
+        out_shape=[jax.ShapeDtypeStruct(shape, F32), jax.ShapeDtypeStruct(shape, BF)],
         compiler_params=pltpu.CompilerParams(vmem_limit_bytes=SMALL_VMEM),
-        name="add_slabs",
-    )(one, two)
-
-
-def combine_kernel(own_ref, received_ref, norm_ref, out_ref):
-    slabs = own_ref.shape[0]
-    total = own_ref[...].astype(F32) + received_ref[:slabs].astype(F32)
-    out_ref[:, :48] = total.astype(BF)
-    norms = received_ref[slabs, :NORM_ROWS].astype(F32)
+        name="sum_late",
+    )(*pieces)
+
+
+def combine_kernel(place_ref, own_ref, received_ref, norm_ref, *out_refs):
+    norms = received_ref[SLABS, :NORM_ROWS].astype(F32)
     norms = norm_ref[...] + (norms[:4] + norms[4:])
     rows = jnp.concatenate(split(norms), axis=0)
-    out_ref[:, 48:] = jnp.broadcast_to(rows[None], (slabs, NORM_ROWS, D))
-
-
-def combine(own, received, norms):
+    for apart, out_ref in enumerate(out_refs):
+        start = OUTER * (place_ref[1] ^ apart)
+        for outer in range(OUTER):
+            total = own_ref[start + outer].astype(F32) + received_ref[start + outer].astype(F32)
+            out_ref[48 * outer : 48 * outer + 48, :] = total.astype(BF)
+        out_ref[48 * OUTER :, :] = rows
+
+
+def combine(place, own, received, norms):
+    vmem = pl.BlockSpec(memory_space=pltpu.VMEM)
+    shape = jax.ShapeDtypeStruct((48 * OUTER + NORM_ROWS, D), BF)
     return pl.pallas_call(
         combine_kernel,
-        out_shape=jax.ShapeDtypeStruct((SLABS, 48 + NORM_ROWS, D), BF),
+        in_specs=[pl.BlockSpec(memory_space=pltpu.SMEM), vmem, vmem, vmem],
+        out_shape=[shape] * INNER,
         compiler_params=pltpu.CompilerParams(vmem_limit_bytes=SMALL_VMEM),
         name="combine",
-    )(own, received, norms)
+    )(place, own, received, norms)
+
+
+def join_kernel(*refs):
+    *early_refs, kept_ref, received_ref, out_ref = refs
+    total = early_refs[0][...].astype(F32)
+    for ref in early_refs[1:]:
+        total = total + ref[...].astype(F32)
+    norms = total[48 * OUTER : 48 * OUTER + 4] + total[48 * OUTER + 4 :]
+    late = kept_ref[...] + received_ref[...].astype(F32)
+    for outer in range(OUTER):
+        out_ref[outer, :48] = total[48 * outer : 48 * outer + 48].astype(BF)
+        for group in range(late.shape[1]):
+            out_ref[outer, 48 * group + 48 : 48 * group + 96] = late[outer, group].astype(BF)
+        out_ref[outer, 144:] = jnp.concatenate(split(norms), axis=0)
+
+
+def join(early, kept, received):
+    return pl.pallas_call(
+        join_kernel,
+        out_shape=jax.ShapeDtypeStruct((OUTER, 144 + NORM_ROWS, D), BF),
+        compiler_params=pltpu.CompilerParams(vmem_limit_bytes=SMALL_VMEM),
+        name="join",
+    )(*early, kept, received)
 
 
 def split(values):
@@ -510,19 +556,19 @@
 
 def shampoo_kernel(scale, with_norms, received_ref, weight_ref, left_ref, right_ref, *refs):
     if with_norms:
-        norm_ins, norm_outs, refs = refs[:2], refs[-5:-2], refs[:-5] + refs[-2:]
-    out_grad_ref, left_new_ref, right_new_ref, new_weight_ref, root_ref, power_ref = refs[-6:]
-    count, edge = weight_ref.shape[1], weight_ref.shape[2]
+        norm_ins, norm_outs, refs = refs[:2], refs[6:9], refs[2:6] + refs[9:]
+    out_grad_ref, left_new_ref, right_new_ref, new_weight_ref, root_ref, power_ref = refs
+    groups, count, edge = weight_ref.shape[:3]
     received = received_ref[0].astype(F32)
     for number in range(1, received_ref.shape[0]):
         received = received + received_ref[number].astype(F32)
-    received = received.reshape(received.shape[-2:])
     if with_norms:
-        total = received[edge : edge + 4] + received[edge + 4 : edge + NORM_ROWS]
-        update_norms(scale, total, *norm_ins, *norm_outs)
+        norms = received[groups * edge :]
+        update_norms(scale, norms[:4] + norms[4:], *norm_ins, *norm_outs)
     pack = min(PACK, count)
-    packs = count // pack
     width = pack * edge
+    places = [(g, pack * n) for g in range(groups) for n in range(count // pack)]
+    packs = len(places)
 
     def block_of(shape, dim):
         return lax.broadcasted_iota(jnp.int32, shape, dim) // edge
@@ -539,15 +585,16 @@
     def cut(packed, index):
         return packed[:, edge * index : edge * index + edge]
 
-    def beside(ref, number):
-        return jnp.concatenate([ref[0, pack * number + i] for i in range(pack)], axis=1)
+    def beside(ref, place):
+        return jnp.concatenate([ref[place[0], place[1] + i] for i in range(pack)], axis=1)
 
     grads, parts = [], []
-    for number in range(packs):
-        grad = received[:edge, width * number : width * number + width] * scale
+    for group, start in places:
+        rows = received[edge * group : edge * group + edge]
+        grad = rows[:, edge * start : edge * start + width] * scale
         blocks = [cut(grad, index) for index in range(pack)]
         for index in range(pack):
-            out_grad_ref[0, pack * number + index] = blocks[index]
+            out_grad_ref[group, start + index] = blocks[index]
         grad_t = jnp.concatenate([jnp.transpose(block) for block in blocks], axis=1)
         one, two = split(grad), split(grad_t)
         one_diagonal, two_diagonal = spread(one), spread(two)
@@ -556,9 +603,10 @@
         parts.append((right_ref, right_new_ref, two, one_diagonal))
     grams = [product(left, right) for _, _, left, right in parts]
     for slot, (old_ref, new_ref, _, _) in enumerate(parts):
-        new = 0.5 * beside(old_ref, slot // 2) + 0.5 * grams[slot]
+        group, start = places[slot // 2]
+        new = 0.5 * beside(old_ref, places[slot // 2]) + 0.5 * grams[slot]
         for index in range(pack):
-            new_ref[0, pack * (slot // 2) + index] = cut(new, index)
+            new_ref[group, start + index] = cut(new, index)
         columns = jnp.sum(new * new, axis=0, keepdims=True)
         squares = jnp.zeros((1, width), F32)
         for index in range(pack):
@@ -598,44 +646,29 @@
     steps = [product(split(root_ref[2 * n]), grads[n]) for n in range(packs)]
     rights = [spread(split(root_ref[2 * n + 1])) for n in range(packs)]
     steps = [product(split(steps[n]), rights[n]) for n in range(packs)]
-    for number in range(packs):
+    for number, (group, start) in enumerate(places):
         for index in range(pack):
-            block = pack * number + index
-            new_weight_ref[0, block] = weight_ref[0, block] - 0.25 * cut(steps[number], index)
-
-
-def shampoo(received, weights, stat_left, stat_right, scale, first, earlier=(), norms=()):
-    sources, groups, rows, lanes = received.shape
-    _, count, edge, _ = weights.shape
-    packs = count // min(PACK, count)
+            step = 0.25 * cut(steps[number], index)
+            new_weight_ref[group, start + index] = weight_ref[group, start + index] - step
+
+
+def shampoo(received, weights, stat_left, stat_right, scale, norms=()):
+    groups, count, edge, _ = weights.shape
+    slots = 2 * groups * count // min(PACK, count)
     width = min(PACK, count) * edge
-    block = pl.BlockSpec((1, count, edge, edge), lambda i: (i + first, 0, 0, 0))
     shape = jax.ShapeDtypeStruct(weights.shape, F32)
-    norm = pl.BlockSpec((4, D), lambda i: (0, 0))
-    norm_outs = 3 if norms else 0
-    ins = 4 + len(norms)
+    norm_shapes = [jax.ShapeDtypeStruct((4, D), F32)] * (3 if norms else 0)
     return pl.pallas_call(
         lambda *refs: shampoo_kernel(scale, bool(norms), *refs),
-        grid=(groups,),
-        in_specs=[
-            pl.BlockSpec((sources, 1, rows, lanes), lambda i: (0, i, 0, 0)),
-            *[block] * 3,
-            *[norm] * len(norms),
-            *[pl.BlockSpec(memory_space=pl.ANY)] * len(earlier),
-        ],
-        out_specs=[block] * 4 + [norm] * norm_outs,
-        out_shape=[shape] * 4 + [jax.ShapeDtypeStruct((4, D), F32)] * norm_outs,
+        out_shape=[shape] * 4 + norm_shapes,
         scratch_shapes=[
-            pltpu.VMEM((2 * packs, edge, width), F32),
-            pltpu.VMEM((2 * packs, edge, width), F32),
-        ],
-        input_output_aliases={ins + i: i for i in range(len(earlier))},
-        compiler_params=pltpu.CompilerParams(vmem_limit_bytes=SMALL_VMEM),
-        cost_estimate=pl.CostEstimate(
-            flops=groups * (3 << 30), bytes_accessed=4 << 20, transcendentals=0
-        ),
+            pltpu.VMEM((slots, edge, width), F32),
+            pltpu.VMEM((slots, edge, width), F32),
+        ],
+        compiler_params=pltpu.CompilerParams(vmem_limit_bytes=SHAMPOO_VMEM),
+        cost_estimate=pl.CostEstimate(flops=9 << 30, bytes_accessed=4 << 20, transcendentals=0),
         name="shampoo",
-    )(received, in_hbm(weights), in_hbm(stat_left), in_hbm(stat_right), *map(in_hbm, norms), *earlier)
+    )(received, weights, stat_left, stat_right, *norms)
 
 
 def swap_heads(values):
@@ -646,23 +679,22 @@
     return lax.all_to_all(values, axis, 0, 0)
 
 
-def copies(values, number):
-    return jnp.broadcast_to(values[None], (number,) + values.shape)
-
-
-def flat(slabs):
-    return slabs.reshape((SLABS,) + slabs.shape[2:])
+def across(values, apart):
+    pairs = [(i, i ^ apart) for i in range(INNER)]
+    return lax.ppermute(values, "inner", pairs)
+
+
+def from_all(values):
+    return [values] + [across(values, apart) for apart in range(1, INNER)]
 
 
 def gather_slabs(weights, other_mask):
-    inner, outer = lax.axis_size("inner"), lax.axis_size("outer")
-    early, late = pack(weights, outer)
+    early, late = pack(weights, OUTER)
     early = to_all(early, "outer")
     early, late = lax.optimization_barrier((early, late))
-    early = to_all(copies(early, inner), "inner")
-    late = copies(to_all(late, "outer"), inner)
-    early, late, other_mask = lax.optimization_barrier((early, late, other_mask))
-    return flat(early), flat(to_all(late, "inner")), other_mask
+    late = to_all(late, "outer")
+    early, late, other_mask = lax.optimization_barrier((from_all(early), late, other_mask))
+    return early, from_all(late), other_mask
 
 
 def gather_blocks(local):
@@ -695,44 +727,48 @@
     weights, stat_left, stat_right = weights[0], stat_left[0], stat_right[0]
     _, count, edge, _ = weights.shape
     whole_slabs = count * edge == D
-    half = lax.axis_index("head").reshape(1)
     other_mask = swap_heads(head_mask)
     if whole_slabs:
+        place = jnp.stack([lax.axis_index("head"), lax.axis_index("inner")])
         early, late, other_mask = gather_slabs(weights, other_mask)
     else:
+        place = jnp.stack([lax.axis_index("head"), 0])
         local = weights.astype(BF)
-        early, late = gather_blocks(local[:1]), gather_blocks(local[1:])
+        early = jnp.split(gather_blocks(local[:1]), INNER)
+        late = jnp.split(gather_blocks(local[1:]), INNER)
+    early, late = list(early), list(late)
     masks = (head_mask, other_mask)
+    early += [swap_heads(piece) for piece in early]
     prob, qkv, out, middle, wqkv, wo = attn_forward(
-        half, token_counts, *masks, tokens, norm_params, early, swap_heads(early)
+        place, token_counts, *masks, tokens, norm_params, early
     )
     late, middle = lax.optimization_barrier((late, middle))
-    block_out, middle_grad, own_late, sent_late, norm_two = mlp(
-        middle, cotangent, norm_params, late, swap_heads(late)
+    late = [*late, *[swap_heads(piece) for piece in late]]
+    block_out, middle_grad, norm_two, *late_grads = mlp(place, middle, cotangent, norm_params, late)
+    if whole_slabs:
+        late_grads[1:] = [across(late_grads[apart], apart) for apart in range(1, INNER)]
+    input_grad, own_early, sent_early, norm_sums = attn_backward(
+        place, *masks, tokens, middle_grad, prob, qkv, out, norm_params, norm_two, wqkv, wo
     )
-    late_slabs = add_slabs(own_late, swap_heads(sent_late))
-    late_slabs, middle_grad = lax.optimization_barrier((late_slabs, middle_grad))
-    input_grad, own_early, sent_early, norm_sums = attn_backward(
-        half, *masks, tokens, middle_grad, prob, qkv, out, norm_params, norm_two, wqkv, wo
-    )
-    early_slabs = combine(own_early, swap_heads(sent_early), norm_sums)
+    late_grads, sent_early = lax.optimization_barrier((late_grads, sent_early))
+    early_received = swap_heads(sent_early)
     devices = lax.axis_size("outer") * lax.axis_size("inner") * lax.axis_size("head")
     scale = 1.0 / math.sqrt(tokens.shape[0] * devices)
     state = (weights, stat_left, stat_right, scale)
-    norms = (norm_params, norm_state)
     if whole_slabs:
-        late_received = to_all(late_slabs, ("inner", "outer"))
-        late_received, early_slabs = lax.optimization_barrier((late_received, early_slabs))
-        results = shampoo(late_received, *state, 1)
-        early_received = to_all(early_slabs, ("inner", "outer"))[:, None]
-        results = shampoo(early_received, *state, 0, results, norms)
+        kept, sent_late = sum_late(late_grads)
+        early_grads = list(combine(place, own_early, early_received, norm_sums))
+        early_grads[1:] = [across(early_grads[apart], apart) for apart in range(1, INNER)]
+        received = to_all(join(early_grads, kept, swap_heads(sent_late)), "outer")
+        results = shampoo(received, *state, (norm_params, norm_state))
     else:
-        late_received = scatter_blocks(late_slabs, count, edge)[None]
-        early_received = scatter_blocks(early_slabs[:, None, :48], count, edge)[None]
-        norm_total = lax.psum(norm_sums, ("outer", "inner", "head"))
-        results = shampoo(late_received, *state, 1)
-        results = list(shampoo(early_received, *state, 0, results))
-        norm_grads = norm_total * scale
+        early_slabs = own_early.astype(F32) + early_received[:SLABS].astype(F32)
+        late_slabs = jnp.concatenate([grad[0].astype(F32) for grad in late_grads])
+        late_slabs += jnp.concatenate([swap_heads(grad[1]).astype(F32) for grad in late_grads])
+        slabs = jnp.concatenate([early_slabs[:, None], late_slabs], axis=1).astype(BF)
+        owned = scatter_blocks(slabs, count, edge)
+        results = list(shampoo(owned.reshape(1, -1, count * edge), *state))
+        norm_grads = lax.psum(norm_sums, ("outer", "inner", "head")) * scale
         state_new = 0.5 * norm_state + 0.5 * norm_grads * norm_grads
         results += [norm_grads, state_new, norm_params - 0.2 * norm_grads / jnp.sqrt(state_new)]
     return (block_out, input_grad, *[result[None] for result in results[:4]], *results[4:])

time: 151 us -> 138 us (0.914)
  waiting for transfers between devices: 35.8 us -> 23.7 us
  Pallas kernels: 70.9 us -> 61 us
  blocking collectives: 24.2 us -> 29.7 us
  starting transfers between devices: 15.9 us -> 20.2 us
    all_to_all x4 -> x1, waiting for transfers between devices: 27 us -> 0.12 us  [to_all(): return lax.all_to_all(values, axis, 0, 0)]
    ppermute x0 -> x12, waiting for transfers between devices: none -> 19.5 us  [across(): return lax.ppermute(values, 'inner', pairs)]
    ppermute x0 -> x12, starting transfers between devices: none -> 14.1 us  [across(): return lax.ppermute(values, 'inner', pairs)]
    all_to_all x4 -> x1, starting transfers between devices: 15.7 us -> 3.45 us  [to_all(): return lax.all_to_all(values, axis, 0, 0)]
    pallas_call x5, Pallas kernels: 43.4 us -> 32.7 us  [the longest x1 19.2 us: mlp(): pl.pallas_call(mlp_kernel, grid=(rows // TILE,), in_specs=[pl.BlockSpec(m...]
    all_to_all x2, blocking collectives: 24.2 us -> 29.7 us  [to_all(): return lax.all_to_all(values, axis, 0, 0)]
    ppermute x5 -> x11, waiting for transfers between devices: 8.76 us -> 4.13 us  [swap_heads(): return lax.ppermute(values, 'head', [(0, 1), (1, 0)])]
    ppermute x5 -> x11, starting transfers between devices: 0.17 us -> 2.62 us  [swap_heads(): return lax.ppermute(values, 'head', [(0, 1), (1, 0)])]
  transfers between devices with their start and end apart: 9 -> 24, of which waited for: 8 -> 15; matrix products, arithmetic and copies ran while one was open for 0% -> 1% of each run, Pallas kernels for 28% -> 21%
where the time goes in v6:
time: 138 us
  Pallas kernels  61 us (44%)
  blocking collectives  29.7 us (22%)
  waiting for transfers between devices  23.7 us (17%)
  starting transfers between devices  20.2 us (15%)
  local copies, waits for them, and re-layouts  2.52 us (2%)
    all_to_all x2, blocking collectives, to_all(): return lax.all_to_all(values, axis, 0, 0)  29.7 us
    ppermute x12, waiting for transfers between devices, across(): return lax.ppermute(values, 'inner', pairs)  19.5 us
    pallas_call x1, Pallas kernels, mlp(): pl.pallas_call(mlp_kernel, grid=(rows // TILE,), in_specs=[pl.BlockSpec(m...  19.2 us
    pallas_call x1, Pallas kernels, attn_backward(): pl.pallas_call(attn_backward_kernel, grid=(rows // TILE,), in_specs=[smem...  16.3 us
    ppermute x12, starting transfers between devices, across(): return lax.ppermute(values, 'inner', pairs)  14.1 us
    pallas_call x1, Pallas kernels, shampoo(): pl.pallas_call(lambda *refs: shampoo_kernel(scale, bool(norms), *refs), o...  12.3 us
    pallas_call x1, Pallas kernels, attn_forward(): pl.pallas_call(attn_forward_kernel, grid=(rows // TILE,), in_specs=[smem]...  11.2 us
    ppermute x11, waiting for transfers between devices, swap_heads(): return lax.ppermute(values, 'head', [(0, 1), (1, 0)])  4.13 us
  transfers between devices with their start and end apart: 24, of which 15 were waited for; matrix products, arithmetic and copies ran while one was open for 1% of the time, Pallas kernels for 21%

profile of v6, /device:TPU:0, one launch (start us, length us, event | category | flops | bytes accessed | tf_op | source)
XLA Modules:
  0.0 138.0 jit_solution(16321868946299782984)
XLA Ops:
  0.7 1.1 copy-done
  1.7 0.9 pack.1
  2.6 12.8 %all_to_all.15.refs_0_ = bf16[4,48,384]{2,1,0:T(8,128)(2,1)S(1)} all-to-all(bf16[4,48,384]{2,1,0:T(8,128)(2,1)S(1)} %get-tuple-element.59), channel_id=1, replica_groups=mesh['outer'=4,'inner'=4,'head'=2] {'outer'}, dimensions={0} | all-to-all | bytes 294912 | tf_op jit(solution)/shard_map/all_to_all | solution.py:679
  15.3 3.5 %all-to-all-start.1 = ((bf16[4,2,48,384]{3,2,1,0:T(8,128)(2,1)}), bf16[4,2,48,384]{3,2,1,0:T(8,128)(2,1)S(1)}, u32[]{:S(2)}, u32[]{:S(2)}) async-start(bf16[4,2,48,384]{3,2,1,0:T(8,128)(2,1)} %get-tuple-element.62), calls=%async_computation.1 | async-start | bytes 589824 | tf_op jit(solution)/shard_map/all_to_all | solution.py:679
  18.8 2.5 %collective-permute-start.2 = (bf16[4,48,384]{2,1,0:T(8,128)(2,1)S(1)}, bf16[4,48,384]{2,1,0:T(8,128)(2,1)S(1)}, u32[]{:S(2)}, u32[]{:S(2)}) collective-permute-start(bf16[4,48,384]{2,1,0:T(8,128)(2,1)S(1)} %all_to_all.15.refs_0_), channel_id=1, source_target_pairs={{0,6},{2,4},{4,2},{6,0},{1,7},{3,5},{5,3},{7,1},{8,14},{10,12},{12... | collective-permute-start | bytes 442376 | tf_op jit(solution)/shard_map/ppermute | solution.py:684
  22.4 0.8 copy.18.own_mask_ref
  23.1 1.2 collective-permute-done.3.other_mask_ref
  24.3 2.3 %collective-permute-done.2.refs_3_ = bf16[4,48,384]{2,1,0:T(8,128)(2,1)S(1)} collective-permute-done((bf16[4,48,384]{2,1,0:T(8,128)(2,1)S(1)}, bf16[4,48,384]{2,1,0:T(8,128)(2,1)S(1)}, u32[]{:S(2)}, u32[]{:S(2)}) %collective-permute-start.2) | collective-permute-done | bytes 147488 | tf_op jit(solution)/shard_map/ppermute | solution.py:684
  28.5 2.4 %collective-permute-start.6 = (bf16[4,2,48,384]{3,2,1,0:T(8,128)(2,1)S(1)}, bf16[4,2,48,384]{3,2,1,0:T(8,128)(2,1)S(1)}, u32[]{:S(2)}, u32[]{:S(2)}) collective-permute-start(bf16[4,2,48,384]{3,2,1,0:T(8,128)(2,1)S(1)} %all-to-all-done.1.refs_0_), channel_id=1, source_target_pairs={{0,6},{2,4},{4,2},{6,0},{1,7},{3,5},{5,3},{7,1},{8,14},{10,12},{12... | collective-permute-start | bytes 884744 | tf_op jit(solution)/shard_map/ppermute | solution.py:684
  32.6 11.2 %attn_forward.1 = (bf16[6,3,512,256]{3,2,1,0:T(8,128)(2,1)}, bf16[1536,1152]{1,0:T(8,128)(2,1)}, bf16[1536,384]{1,0:T(8,128)(2,1)}, f32[1536,384]{1,0:T(8,128)},...) custom-call(s32[2]{0:T(128)S(1)} %pad_add_fusion.place_ref, s32[12]{0:T(128)S(1)} %copy-done.6, ...), custom_call_target="tpu_custom_call" | custom-call | flops 4227858432 | bytes 16777216 | tf_op jit(solution)/shard_map/attn_forward/pallas_call | solution.py:168
  43.9 0.7 collective-permute-done.5.refs_2_
  47.6 19.2 %mlp.1 = (f32[1536,384]{1,0:T(8,128)}, f32[1536,384]{1,0:T(8,128)}, f32[2,384]{1,0:T(2,128)S(1)}, bf16[2,4,2,48,384]{4,3,2,1,0:T(8,128)(2,1)S(1)}, bf16[2,4,2,48...) custom-call(s32[2]{0:T(128)S(1)} %pad_add_fusion.place_ref, ...), custom_call_target="tpu_custom_call" | custom-call | flops 10871635968 | bytes 20971520 | tf_op jit(solution)/shard_map/mlp/pallas_call | solution.py:263
  66.8 1.5 %collective-permute-start.15 = (bf16[2,4,2,48,384]{4,3,2,1,0:T(8,128)(2,1)S(1)}, bf16[2,4,2,48,384]{4,3,2,1,0:T(8,128)(2,1)S(1)}, u32[]{:S(2)}, u32[]{:S(2)}) collective-permute-start(bf16[2,4,2,48,384]{4,3,2,1,0:T(8,128)(2,1)S(1)} %get-tuple-element.86), channel_id=1, source_target_pairs={{0,2},{2,0},{4,6},{6,4},{1,3},{3,1},{5,7},{7,5},{8,10},{10,8},{12,... | collective-permute-start | bytes 1769480 | tf_op jit(solution)/shard_map/ppermute | solution.py:684
  68.3 0.9 collective-permute-start.16
  69.2 1.1 collective-permute-start.17
  70.3 16.3 %attn_backward.1 = (f32[1536,384]{1,0:T(8,128)}, bf16[16,48,384]{2,1,0:T(8,128)(2,1)S(1)}, bf16[17,48,384]{2,1,0:T(8,128)(2,1)S(1)}, f32[4,384]{1,0:T(4,128)S(1)}) custom-call(s32[2]{0:T(128)S(1)} %pad_add_fusion.place_ref, s32[12,3]{1,0:T(8,128)S(1)} %copy.18.own_mask_ref, s32[12,3]{1,0:T(8,128)S(1)} %collective-permute-done.3.other_mask_ref, ...), custom_call_target="tpu_custom_call" | custom-call | flops 8455716864 | bytes 20971520 | tf_op jit(solution)/shard_map/attn_backward/pallas_call | solution.py:385
  86.5 9.5 %collective-permute-done.16.refs_2_ = bf16[2,4,2,48,384]{4,3,2,1,0:T(8,128)(2,1)S(1)} collective-permute-done((bf16[2,4,2,48,384]{4,3,2,1,0:T(8,128)(2,1)S(1)}, bf16[2,4,2,48,384]{4,3,2,1,0:T(8,128)(2,1)S(1)}, u32[]{:S(2)}, u32[]{:S(2)}) %collective-permute-start.16) | collective-permute-done | bytes 589856 | tf_op jit(solution)/shard_map/ppermute | solution.py:684
  96.9 1.1 collective-permute-done.18.received_ref
  99.5 1.3 collective-permute-start.20
  100.8 1.5 %collective-permute-start.21 = (bf16[200,384]{1,0:T(8,128)(2,1)S(1)}, bf16[200,384]{1,0:T(8,128)(2,1)S(1)}, u32[]{:S(2)}, u32[]{:S(2)}) collective-permute-start(bf16[200,384]{1,0:T(8,128)(2,1)S(1)} %get-tuple-element.95), channel_id=1, source_target_pairs={{0,6},{2,4},{4,2},{6,0},{1,7},{3,5},{5,3},{7,1},{8,14},{10,12},{12... | collective-permute-start | bytes 460808 | tf_op jit(solution)/shard_map/ppermute | solution.py:684
  102.3 3.3 %collective-permute-done.19.refs_1_ = bf16[200,384]{1,0:T(8,128)(2,1)S(1)} collective-permute-done((bf16[200,384]{1,0:T(8,128)(2,1)S(1)}, bf16[200,384]{1,0:T(8,128)(2,1)S(1)}, u32[]{:S(2)}, u32[]{:S(2)}) %collective-permute-start.19) | collective-permute-done | bytes 153632 | tf_op jit(solution)/shard_map/ppermute | solution.py:684
  106.0 2.5 %collective-permute-done.21.refs_3_ = bf16[200,384]{1,0:T(8,128)(2,1)S(1)} collective-permute-done((bf16[200,384]{1,0:T(8,128)(2,1)S(1)}, bf16[200,384]{1,0:T(8,128)(2,1)S(1)}, u32[]{:S(2)}, u32[]{:S(2)}) %collective-permute-start.21) | collective-permute-done | bytes 153632 | tf_op jit(solution)/shard_map/ppermute | solution.py:684
  108.7 16.9 %all_to_all.16.refs_0_ = bf16[4,152,384]{2,1,0:T(8,128)(2,1)S(1)} all-to-all(bf16[4,152,384]{2,1,0:T(8,128)(2,1)S(1)} %join.1), channel_id=1, replica_groups=mesh['outer'=4,'inner'=4,'head'=2] {'outer'}, dimensions={0} | all-to-all | bytes 933888 | tf_op jit(solution)/shard_map/all_to_all | solution.py:679
  125.6 12.3 %shampoo.1 = (f32[3,8,48,48]{3,2,1,0:T(8,128)}, f32[3,8,48,48]{3,2,1,0:T(8,128)}, f32[3,8,48,48]{3,2,1,0:T(8,128)}, f32[3,8,48,48]{3,2,1,0:T(8,128)}, f32[4,384]...) custom-call(bf16[4,152,384]{2,1,0:T(8,128)(2,1)S(1)} %all_to_all.16.refs_0_, f32[3,8,48,48]{3,2,1,0:T(8,128)S(1)} %bitcast.10, ...), custom_call_target="tpu_custom_call" | custom-call | flops 9663676416 | bytes 4194304 | tf_op jit(solution)/shard_map/shampoo/pallas_call | solution.py:661
  (52 shorter events, 10.4 us)
Async XLA Ops:
  15.3 12.0 %all-to-all-start.1 = ((bf16[4,2,48,384]{3,2,1,0:T(8,128)(2,1)}), bf16[4,2,48,384]{3,2,1,0:T(8,128)(2,1)S(1)}, u32[]{:S(2)}, u32[]{:S(2)}) async-start(bf16[4,2,48,384]{3,2,1,0:T(8,128)(2,1)} %get-tuple-element.62), calls=%async_computation.1 | async-start | bytes 589824 | tf_op jit(solution)/shard_map/all_to_all | solution.py:679
  18.8 7.8 %collective-permute-start.2 = (bf16[4,48,384]{2,1,0:T(8,128)(2,1)S(1)}, bf16[4,48,384]{2,1,0:T(8,128)(2,1)S(1)}, u32[]{:S(2)}, u32[]{:S(2)}) collective-permute-start(bf16[4,48,384]{2,1,0:T(8,128)(2,1)S(1)} %all_to_all.15.refs_0_), channel_id=1, source_target_pairs={{0,6},{2,4},{4,2},{6,0},{1,7},{3,5},{5,3},{7,1},{8,14},{10,12},{12... | collective-permute-start | bytes 442376 | tf_op jit(solution)/shard_map/ppermute | solution.py:684
  21.3 6.0 %collective-permute-start.1 = (bf16[4,48,384]{2,1,0:T(8,128)(2,1)S(1)}, bf16[4,48,384]{2,1,0:T(8,128)(2,1)S(1)}, u32[]{:S(2)}, u32[]{:S(2)}) collective-permute-start(bf16[4,48,384]{2,1,0:T(8,128)(2,1)S(1)} %all_to_all.15.refs_0_), channel_id=1, source_target_pairs={{0,4},{2,6},{4,0},{6,2},{1,5},{3,7},{5,1},{7,3},{8,12},{10,14},{12... | collective-permute-start | bytes 442376 | tf_op jit(solution)/shard_map/ppermute | solution.py:684
  21.8 5.4 %collective-permute-start = (bf16[4,48,384]{2,1,0:T(8,128)(2,1)S(1)}, bf16[4,48,384]{2,1,0:T(8,128)(2,1)S(1)}, u32[]{:S(2)}, u32[]{:S(2)}) collective-permute-start(bf16[4,48,384]{2,1,0:T(8,128)(2,1)S(1)} %all_to_all.15.refs_0_), channel_id=1, source_target_pairs={{0,2},{2,0},{4,6},{6,4},{1,3},{3,1},{5,7},{7,5},{8,10},{10,8},{12,... | collective-permute-start | bytes 442376 | tf_op jit(solution)/shard_map/ppermute | solution.py:684
  23.1 1.2 collective-permute-start.3
  27.4 3.5 %collective-permute-start.7 = (bf16[4,48,384]{2,1,0:T(8,128)(2,1)S(1)}, bf16[4,48,384]{2,1,0:T(8,128)(2,1)S(1)}, u32[]{:S(2)}, u32[]{:S(2)}) collective-permute-start(bf16[4,48,384]{2,1,0:T(8,128)(2,1)S(1)} %all_to_all.15.refs_0_), channel_id=1, source_target_pairs={{0,1},{1,0},{2,3},{3,2},{4,5},{5,4},{6,7},{7,6},{8,9},{9,8},{10,11... | collective-permute-start | bytes 442376 | tf_op jit(solution)/shard_map/ppermute | solution.py:675
  27.4 4.1 %collective-permute-start.8 = (bf16[4,48,384]{2,1,0:T(8,128)(2,1)S(1)}, bf16[4,48,384]{2,1,0:T(8,128)(2,1)S(1)}, u32[]{:S(2)}, u32[]{:S(2)}) collective-permute-start(bf16[4,48,384]{2,1,0:T(8,128)(2,1)S(1)} %collective-permute-done.refs_1_), channel_id=1, source_target_pairs={{0,1},{1,0},{2,3},{3,2},{4,5},{5,4},{6,7},{7,6},{8,9},{9,8},{10,11... | collective-permute-start | bytes 442376 | tf_op jit(solution)/shard_map/ppermute | solution.py:675
  27.9 4.1 %collective-permute-start.9 = (bf16[4,48,384]{2,1,0:T(8,128)(2,1)S(1)}, bf16[4,48,384]{2,1,0:T(8,128)(2,1)S(1)}, u32[]{:S(2)}, u32[]{:S(2)}) collective-permute-start(bf16[4,48,384]{2,1,0:T(8,128)(2,1)S(1)} %collective-permute-done.1.refs_2_), channel_id=1, source_target_pairs={{0,1},{1,0},{2,3},{3,2},{4,5},{5,4},{6,7},{7,6},{8,9},{9,8},{10,11... | collective-permute-start | bytes 442376 | tf_op jit(solution)/shard_map/ppermute | solution.py:675
  27.9 4.1 %collective-permute-start.10 = (bf16[4,48,384]{2,1,0:T(8,128)(2,1)S(1)}, bf16[4,48,384]{2,1,0:T(8,128)(2,1)S(1)}, u32[]{:S(2)}, u32[]{:S(2)}) collective-permute-start(bf16[4,48,384]{2,1,0:T(8,128)(2,1)S(1)} %collective-permute-done.2.refs_3_), channel_id=1, source_target_pairs={{0,1},{1,0},{2,3},{3,2},{4,5},{5,4},{6,7},{7,6},{8,9},{9,8},{10,11... | collective-permute-start | bytes 442376 | tf_op jit(solution)/shard_map/ppermute | solution.py:675
  28.5 15.4 %collective-permute-start.6 = (bf16[4,2,48,384]{3,2,1,0:T(8,128)(2,1)S(1)}, bf16[4,2,48,384]{3,2,1,0:T(8,128)(2,1)S(1)}, u32[]{:S(2)}, u32[]{:S(2)}) collective-permute-start(bf16[4,2,48,384]{3,2,1,0:T(8,128)(2,1)S(1)} %all-to-all-done.1.refs_0_), channel_id=1, source_target_pairs={{0,6},{2,4},{4,2},{6,0},{1,7},{3,5},{5,3},{7,1},{8,14},{10,12},{12... | collective-permute-start | bytes 884744 | tf_op jit(solution)/shard_map/ppermute | solution.py:684
  30.9 13.7 %collective-permute-start.5 = (bf16[4,2,48,384]{3,2,1,0:T(8,128)(2,1)S(1)}, bf16[4,2,48,384]{3,2,1,0:T(8,128)(2,1)S(1)}, u32[]{:S(2)}, u32[]{:S(2)}) collective-permute-start(bf16[4,2,48,384]{3,2,1,0:T(8,128)(2,1)S(1)} %all-to-all-done.1.refs_0_), channel_id=1, source_target_pairs={{0,4},{2,6},{4,0},{6,2},{1,5},{3,7},{5,1},{7,3},{8,12},{10,14},{12... | collective-permute-start | bytes 884744 | tf_op jit(solution)/shard_map/ppermute | solution.py:684
  31.4 13.3 %collective-permute-start.4 = (bf16[4,2,48,384]{3,2,1,0:T(8,128)(2,1)S(1)}, bf16[4,2,48,384]{3,2,1,0:T(8,128)(2,1)S(1)}, u32[]{:S(2)}, u32[]{:S(2)}) collective-permute-start(bf16[4,2,48,384]{3,2,1,0:T(8,128)(2,1)S(1)} %all-to-all-done.1.refs_0_), channel_id=1, source_target_pairs={{0,2},{2,0},{4,6},{6,4},{1,3},{3,1},{5,7},{7,5},{8,10},{10,8},{12,... | collective-permute-start | bytes 884744 | tf_op jit(solution)/shard_map/ppermute | solution.py:684
  44.7 1.6 %collective-permute-start.11 = (bf16[4,2,48,384]{3,2,1,0:T(8,128)(2,1)S(1)}, bf16[4,2,48,384]{3,2,1,0:T(8,128)(2,1)S(1)}, u32[]{:S(2)}, u32[]{:S(2)}) collective-permute-start(bf16[4,2,48,384]{3,2,1,0:T(8,128)(2,1)S(1)} %all-to-all-done.1.refs_0_), channel_id=1, source_target_pairs={{0,1},{1,0},{2,3},{3,2},{4,5},{5,4},{6,7},{7,6},{8,9},{9,8},{10,11... | collective-permute-start | bytes 884744 | tf_op jit(solution)/shard_map/ppermute | solution.py:675
  44.7 2.0 %collective-permute-start.12 = (bf16[4,2,48,384]{3,2,1,0:T(8,128)(2,1)S(1)}, bf16[4,2,48,384]{3,2,1,0:T(8,128)(2,1)S(1)}, u32[]{:S(2)}, u32[]{:S(2)}) collective-permute-start(bf16[4,2,48,384]{3,2,1,0:T(8,128)(2,1)S(1)} %collective-permute-done.4.refs_1_), channel_id=1, source_target_pairs={{0,1},{1,0},{2,3},{3,2},{4,5},{5,4},{6,7},{7,6},{8,9},{9,8},{10,11... | collective-permute-start | bytes 884744 | tf_op jit(solution)/shard_map/ppermute | solution.py:675
  45.2 1.9 %collective-permute-start.13 = (bf16[4,2,48,384]{3,2,1,0:T(8,128)(2,1)S(1)}, bf16[4,2,48,384]{3,2,1,0:T(8,128)(2,1)S(1)}, u32[]{:S(2)}, u32[]{:S(2)}) collective-permute-start(bf16[4,2,48,384]{3,2,1,0:T(8,128)(2,1)S(1)} %collective-permute-done.5.refs_2_), channel_id=1, source_target_pairs={{0,1},{1,0},{2,3},{3,2},{4,5},{5,4},{6,7},{7,6},{8,9},{9,8},{10,11... | collective-permute-start | bytes 884744 | tf_op jit(solution)/shard_map/ppermute | solution.py:675
  45.2 2.3 %collective-permute-start.14 = (bf16[4,2,48,384]{3,2,1,0:T(8,128)(2,1)S(1)}, bf16[4,2,48,384]{3,2,1,0:T(8,128)(2,1)S(1)}, u32[]{:S(2)}, u32[]{:S(2)}) collective-permute-start(bf16[4,2,48,384]{3,2,1,0:T(8,128)(2,1)S(1)} %collective-permute-done.6.refs_3_), channel_id=1, source_target_pairs={{0,1},{1,0},{2,3},{3,2},{4,5},{5,4},{6,7},{7,6},{8,9},{9,8},{10,11... | collective-permute-start | bytes 884744 | tf_op jit(solution)/shard_map/ppermute | solution.py:675
  66.8 19.8 %collective-permute-start.15 = (bf16[2,4,2,48,384]{4,3,2,1,0:T(8,128)(2,1)S(1)}, bf16[2,4,2,48,384]{4,3,2,1,0:T(8,128)(2,1)S(1)}, u32[]{:S(2)}, u32[]{:S(2)}) collective-permute-start(bf16[2,4,2,48,384]{4,3,2,1,0:T(8,128)(2,1)S(1)} %get-tuple-element.86), channel_id=1, source_target_pairs={{0,2},{2,0},{4,6},{6,4},{1,3},{3,1},{5,7},{7,5},{8,10},{10,8},{12,... | collective-permute-start | bytes 1769480 | tf_op jit(solution)/shard_map/ppermute | solution.py:684
  68.3 27.7 %collective-permute-start.16 = (bf16[2,4,2,48,384]{4,3,2,1,0:T(8,128)(2,1)S(1)}, bf16[2,4,2,48,384]{4,3,2,1,0:T(8,128)(2,1)S(1)}, u32[]{:S(2)}, u32[]{:S(2)}) collective-permute-start(bf16[2,4,2,48,384]{4,3,2,1,0:T(8,128)(2,1)S(1)} %get-tuple-element.87), channel_id=1, source_target_pairs={{0,4},{2,6},{4,0},{6,2},{1,5},{3,7},{5,1},{7,3},{8,12},{10,14},{12... | collective-permute-start | bytes 1769480 | tf_op jit(solution)/shard_map/ppermute | solution.py:684
  69.2 26.8 %collective-permute-start.17 = (bf16[2,4,2,48,384]{4,3,2,1,0:T(8,128)(2,1)S(1)}, bf16[2,4,2,48,384]{4,3,2,1,0:T(8,128)(2,1)S(1)}, u32[]{:S(2)}, u32[]{:S(2)}) collective-permute-start(bf16[2,4,2,48,384]{4,3,2,1,0:T(8,128)(2,1)S(1)} %get-tuple-element.88), channel_id=1, source_target_pairs={{0,6},{2,4},{4,2},{6,0},{1,7},{3,5},{5,3},{7,1},{8,14},{10,12},{12... | collective-permute-start | bytes 1769480 | tf_op jit(solution)/shard_map/ppermute | solution.py:684
  96.0 2.1 %collective-permute-start.18 = (bf16[17,48,384]{2,1,0:T(8,128)(2,1)S(1)}, bf16[17,48,384]{2,1,0:T(8,128)(2,1)S(1)}, u32[]{:S(2)}, u32[]{:S(2)}) collective-permute-start(bf16[17,48,384]{2,1,0:T(8,128)(2,1)S(1)} %get-tuple-element.90), channel_id=1, source_target_pairs={{0,1},{1,0},{2,3},{3,2},{4,5},{5,4},{6,7},{7,6},{8,9},{9,8},{10,11... | collective-permute-start | bytes 1880072 | tf_op jit(solution)/shard_map/ppermute | solution.py:675
  96.4 6.0 %collective-permute-start.22 = (bf16[4,2,48,384]{3,2,1,0:T(8,128)(2,1)S(1)}, bf16[4,2,48,384]{3,2,1,0:T(8,128)(2,1)S(1)}, u32[]{:S(2)}, u32[]{:S(2)}) collective-permute-start(bf16[4,2,48,384]{3,2,1,0:T(8,128)(2,1)S(1)} %get-tuple-element.101), channel_id=1, source_target_pairs={{0,1},{1,0},{2,3},{3,2},{4,5},{5,4},{6,7},{7,6},{8,9},{9,8},{10,11... | collective-permute-start | bytes 884744 | tf_op jit(solution)/shard_map/ppermute | solution.py:675
  98.8 6.9 %collective-permute-start.19 = (bf16[200,384]{1,0:T(8,128)(2,1)S(1)}, bf16[200,384]{1,0:T(8,128)(2,1)S(1)}, u32[]{:S(2)}, u32[]{:S(2)}) collective-permute-start(bf16[200,384]{1,0:T(8,128)(2,1)S(1)} %get-tuple-element.93), channel_id=1, source_target_pairs={{0,2},{2,0},{4,6},{6,4},{1,3},{3,1},{5,7},{7,5},{8,10},{10,8},{12,... | collective-permute-start | bytes 460808 | tf_op jit(solution)/shard_map/ppermute | solution.py:684
  99.5 6.5 %collective-permute-start.20 = (bf16[200,384]{1,0:T(8,128)(2,1)S(1)}, bf16[200,384]{1,0:T(8,128)(2,1)S(1)}, u32[]{:S(2)}, u32[]{:S(2)}) collective-permute-start(bf16[200,384]{1,0:T(8,128)(2,1)S(1)} %get-tuple-element.94), channel_id=1, source_target_pairs={{0,4},{2,6},{4,0},{6,2},{1,5},{3,7},{5,1},{7,3},{8,12},{10,14},{12... | collective-permute-start | bytes 460808 | tf_op jit(solution)/shard_map/ppermute | solution.py:684
  100.8 7.7 %collective-permute-start.21 = (bf16[200,384]{1,0:T(8,128)(2,1)S(1)}, bf16[200,384]{1,0:T(8,128)(2,1)S(1)}, u32[]{:S(2)}, u32[]{:S(2)}) collective-permute-start(bf16[200,384]{1,0:T(8,128)(2,1)S(1)} %get-tuple-element.95), channel_id=1, source_target_pairs={{0,6},{2,4},{4,2},{6,0},{1,7},{3,5},{5,3},{7,1},{8,14},{10,12},{12... | collective-permute-start | bytes 460808 | tf_op jit(solution)/shard_map/ppermute | solution.py:684
  (8 other events, 151.7 us)

commit v7 on v6

--- a/solution.py
+++ b/solution.py
@@ -197,7 +197,7 @@
 def mlp_kernel(place_ref, middle_ref, cot_ref, norm_ref, *refs):
     slab_refs, refs = refs[: 2 * INNER], refs[2 * INNER :]
     out_ref, grad_ref, norm_grad_ref, *refs = refs
-    sent_refs, (up_ref, down_ref, up_grad_ref, down_grad_ref) = refs[:INNER], refs[INNER:]
+    own_ref, sent_ref, up_ref, down_ref, up_grad_ref, down_grad_ref = refs
     step = pl.program_id(0)
     half = MLP // 2
 
@@ -246,19 +246,21 @@
 
     @pl.when(step == pl.num_programs(0) - 1)
     def _():
-        for apart, ref in enumerate(sent_refs):
+        for apart in range(INNER):
             for outer in range(OUTER):
                 row, lane, down_row = places(apart, outer)
-                for side in range(2):
+                for side, ref in enumerate((own_ref, sent_ref)):
                     up = up_grad_ref[side, pl.ds(row, 48), pl.ds(lane, D)]
-                    ref[side, outer, 0] = up.astype(BF)
-                    ref[side, outer, 1] = down_grad_ref[side, pl.ds(down_row, 48), :].astype(BF)
+                    down = down_grad_ref[side, pl.ds(down_row, 48), :]
+                    ref[apart, outer, 0] = up.astype(BF)
+                    ref[apart, outer, 1] = down.astype(BF)
 
 
 def mlp(place, middle, cotangent, norm_params, slabs):
     rows = middle.shape[0]
     slab = pl.BlockSpec((OUTER, 2, 48, D), lambda i: (0, 0, 0, 0))
-    sent = pl.BlockSpec((2, OUTER, 2, 48, D), lambda i: (0, 0, 0, 0, 0))
+    grads = (INNER, OUTER, 2, 48, D)
+    grad = pl.BlockSpec(grads, lambda i: (0, 0, 0, 0, 0))
     tile = pl.BlockSpec((TILE, D), lambda i: (i, 0))
     return pl.pallas_call(
         mlp_kernel,
@@ -270,12 +272,12 @@
             pl.BlockSpec((4, D), lambda i: (0, 0)),
             *[slab] * 2 * INNER,
         ],
-        out_specs=[tile, tile, pl.BlockSpec((2, D), lambda i: (0, 0)), *[sent] * INNER],
+        out_specs=[tile, tile, pl.BlockSpec((2, D), lambda i: (0, 0)), grad, grad],
         out_shape=[
             jax.ShapeDtypeStruct((rows, D), F32),
             pltpu.HBM((rows, D), F32),
             jax.ShapeDtypeStruct((2, D), F32),
-            *[jax.ShapeDtypeStruct((2, OUTER, 2, 48, D), BF)] * INNER,
+            *[jax.ShapeDtypeStruct(grads, BF)] * 2,
         ],
         scratch_shapes=[
             pltpu.VMEM((2, D, MLP // 2), BF),
@@ -452,20 +454,33 @@
     )(weights)
 
 
+def add_kernel(own_ref, received_ref, *out_refs):
+    for apart, out_ref in enumerate(out_refs):
+        total = own_ref[apart].astype(F32) + received_ref[apart].astype(F32)
+        out_ref[...] = total.astype(BF)
+
+
+def add_late(own, received):
+    return pl.pallas_call(
+        add_kernel,
+        out_shape=[jax.ShapeDtypeStruct(own.shape[1:], BF)] * own.shape[0],
+        compiler_params=pltpu.CompilerParams(vmem_limit_bytes=SMALL_VMEM),
+        name="add_late",
+    )(own, received)
+
+
 def sum_kernel(*refs):
-    *in_refs, kept_ref, sent_ref = refs
-    for side, out_ref in enumerate((kept_ref, sent_ref)):
-        total = in_refs[0][side].astype(F32)
-        for ref in in_refs[1:]:
-            total = total + ref[side].astype(F32)
-        out_ref[...] = total.astype(out_ref.dtype)
+    *in_refs, out_ref = refs
+    total = in_refs[0][...].astype(F32)
+    for ref in in_refs[1:]:
+        total = total + ref[...].astype(F32)
+    out_ref[...] = total.astype(BF)
 
 
 def sum_late(pieces):
-    shape = pieces[0].shape[1:]
     return pl.pallas_call(
         sum_kernel,
-        out_shape=[jax.ShapeDtypeStruct(shape, F32), jax.ShapeDtypeStruct(shape, BF)],
+        out_shape=jax.ShapeDtypeStruct(pieces[0].shape, BF),
         compiler_params=pltpu.CompilerParams(vmem_limit_bytes=SMALL_VMEM),
         name="sum_late",
     )(*pieces)
@@ -496,26 +511,23 @@
 
 
 def join_kernel(*refs):
-    *early_refs, kept_ref, received_ref, out_ref = refs
+    *early_refs, out_ref = refs
     total = early_refs[0][...].astype(F32)
     for ref in early_refs[1:]:
         total = total + ref[...].astype(F32)
     norms = total[48 * OUTER : 48 * OUTER + 4] + total[48 * OUTER + 4 :]
-    late = kept_ref[...] + received_ref[...].astype(F32)
     for outer in range(OUTER):
         out_ref[outer, :48] = total[48 * outer : 48 * outer + 48].astype(BF)
-        for group in range(late.shape[1]):
-            out_ref[outer, 48 * group + 48 : 48 * group + 96] = late[outer, group].astype(BF)
-        out_ref[outer, 144:] = jnp.concatenate(split(norms), axis=0)
-
-
-def join(early, kept, received):
+        out_ref[outer, 48:] = jnp.concatenate(split(norms), axis=0)
+
+
+def join(early):
     return pl.pallas_call(
         join_kernel,
-        out_shape=jax.ShapeDtypeStruct((OUTER, 144 + NORM_ROWS, D), BF),
+        out_shape=jax.ShapeDtypeStruct((OUTER, 48 + NORM_ROWS, D), BF),
         compiler_params=pltpu.CompilerParams(vmem_limit_bytes=SMALL_VMEM),
         name="join",
-    )(*early, kept, received)
+    )(*early)
 
 
 def split(values):
@@ -554,16 +566,22 @@
     new_ref[...] = param_ref[...] - 0.2 * grads / jnp.sqrt(state)
 
 
-def shampoo_kernel(scale, with_norms, received_ref, weight_ref, left_ref, right_ref, *refs):
+def shampoo_kernel(scale, with_norms, early_ref, late_ref, weight_ref, left_ref, right_ref, *refs):
     if with_norms:
         norm_ins, norm_outs, refs = refs[:2], refs[6:9], refs[2:6] + refs[9:]
     out_grad_ref, left_new_ref, right_new_ref, new_weight_ref, root_ref, power_ref = refs
     groups, count, edge = weight_ref.shape[:3]
-    received = received_ref[0].astype(F32)
-    for number in range(1, received_ref.shape[0]):
-        received = received + received_ref[number].astype(F32)
+
+    def total_of(ref):
+        total = ref[0].astype(F32)
+        for number in range(1, ref.shape[0]):
+            total = total + ref[number].astype(F32)
+        return total
+
+    early, late = total_of(early_ref), total_of(late_ref)
+    received = [early[:edge], *[late[group] for group in range(groups - 1)]]
     if with_norms:
-        norms = received[groups * edge :]
+        norms = early[edge:]
         update_norms(scale, norms[:4] + norms[4:], *norm_ins, *norm_outs)
     pack = min(PACK, count)
     width = pack * edge
@@ -590,8 +608,7 @@
 
     grads, parts = [], []
     for group, start in places:
-        rows = received[edge * group : edge * group + edge]
-        grad = rows[:, edge * start : edge * start + width] * scale
+        grad = received[group][:, edge * start : edge * start + width] * scale
         blocks = [cut(grad, index) for index in range(pack)]
         for index in range(pack):
             out_grad_ref[group, start + index] = blocks[index]
@@ -652,7 +669,7 @@
             new_weight_ref[group, start + index] = weight_ref[group, start + index] - step
 
 
-def shampoo(received, weights, stat_left, stat_right, scale, norms=()):
+def shampoo(early, late, weights, stat_left, stat_right, scale, norms=()):
     groups, count, edge, _ = weights.shape
     slots = 2 * groups * count // min(PACK, count)
     width = min(PACK, count) * edge
@@ -668,7 +685,7 @@
         compiler_params=pltpu.CompilerParams(vmem_limit_bytes=SHAMPOO_VMEM),
         cost_estimate=pl.CostEstimate(flops=9 << 30, bytes_accessed=4 << 20, transcendentals=0),
         name="shampoo",
-    )(received, weights, stat_left, stat_right, *norms)
+    )(early, late, weights, stat_left, stat_right, *norms)
 
 
 def swap_heads(values):
@@ -693,7 +710,8 @@
     early = to_all(early, "outer")
     early, late = lax.optimization_barrier((early, late))
     late = to_all(late, "outer")
-    early, late, other_mask = lax.optimization_barrier((from_all(early), late, other_mask))
+    early = from_all(early)
+    early[-1], late, other_mask = lax.optimization_barrier((early[-1], late, other_mask))
     return early, from_all(late), other_mask
 
 
@@ -742,32 +760,38 @@
     prob, qkv, out, middle, wqkv, wo = attn_forward(
         place, token_counts, *masks, tokens, norm_params, early
     )
-    late, middle = lax.optimization_barrier((late, middle))
-    late = [*late, *[swap_heads(piece) for piece in late]]
-    block_out, middle_grad, norm_two, *late_grads = mlp(place, middle, cotangent, norm_params, late)
+    late[1:], middle = lax.optimization_barrier((late[1:], middle))
+    late += [swap_heads(piece) for piece in late]
+    block_out, middle_grad, norm_two, own_late, sent_late = mlp(
+        place, middle, cotangent, norm_params, late
+    )
+    late_received = swap_heads(sent_late)
     if whole_slabs:
+        late_grads = list(add_late(own_late, late_received))
+        late_grads, middle_grad = lax.optimization_barrier((late_grads, middle_grad))
         late_grads[1:] = [across(late_grads[apart], apart) for apart in range(1, INNER)]
     input_grad, own_early, sent_early, norm_sums = attn_backward(
         place, *masks, tokens, middle_grad, prob, qkv, out, norm_params, norm_two, wqkv, wo
     )
-    late_grads, sent_early = lax.optimization_barrier((late_grads, sent_early))
+    if whole_slabs:
+        late_grads, sent_early = lax.optimization_barrier((late_grads, sent_early))
     early_received = swap_heads(sent_early)
     devices = lax.axis_size("outer") * lax.axis_size("inner") * lax.axis_size("head")
     scale = 1.0 / math.sqrt(tokens.shape[0] * devices)
     state = (weights, stat_left, stat_right, scale)
     if whole_slabs:
-        kept, sent_late = sum_late(late_grads)
+        late_grads = to_all(sum_late(late_grads), "outer")
         early_grads = list(combine(place, own_early, early_received, norm_sums))
         early_grads[1:] = [across(early_grads[apart], apart) for apart in range(1, INNER)]
-        received = to_all(join(early_grads, kept, swap_heads(sent_late)), "outer")
-        results = shampoo(received, *state, (norm_params, norm_state))
+        joined, late_grads = lax.optimization_barrier((join(early_grads), late_grads))
+        results = shampoo(to_all(joined, "outer"), late_grads, *state, (norm_params, norm_state))
     else:
         early_slabs = own_early.astype(F32) + early_received[:SLABS].astype(F32)
-        late_slabs = jnp.concatenate([grad[0].astype(F32) for grad in late_grads])
-        late_slabs += jnp.concatenate([swap_heads(grad[1]).astype(F32) for grad in late_grads])
+        late_slabs = own_late.astype(F32) + late_received.astype(F32)
+        late_slabs = late_slabs.reshape(SLABS, 2, edge, D)
         slabs = jnp.concatenate([early_slabs[:, None], late_slabs], axis=1).astype(BF)
         owned = scatter_blocks(slabs, count, edge)
-        results = list(shampoo(owned.reshape(1, -1, count * edge), *state))
+        results = list(shampoo(owned[:1], owned[None, 1:], *state))
         norm_grads = lax.psum(norm_sums, ("outer", "inner", "head")) * scale
         state_new = 0.5 * norm_state + 0.5 * norm_grads * norm_grads
         results += [norm_grads, state_new, norm_params - 0.2 * norm_grads / jnp.sqrt(state_new)]

time: 138 us -> 130 us (0.942)
  waiting for transfers between devices: 23.7 us -> 16.4 us
  blocking collectives: 29.7 us -> 24.1 us
  starting transfers between devices: 20.2 us -> 24.2 us
    ppermute x12, waiting for transfers between devices: 19.5 us -> 11.7 us  [across(): return lax.ppermute(values, 'inner', pairs)]
    all_to_all x2, blocking collectives: 29.7 us -> 24.1 us  [to_all(): return lax.all_to_all(values, axis, 0, 0)]
    all_to_all x1 -> x2, starting transfers between devices: 3.45 us -> 8.31 us  [to_all(): return lax.all_to_all(values, axis, 0, 0)]
  transfers between devices with their start and end apart: 24 -> 25, of which waited for: 15 -> 10; matrix products, arithmetic and copies ran while one was open for 1% -> 1% of each run, Pallas kernels for 21% -> 22%
where the time goes in v7:
time: 130 us
  Pallas kernels  61.9 us (48%)
  starting transfers between devices  24.2 us (19%)
  blocking collectives  24.1 us (19%)
  waiting for transfers between devices  16.4 us (13%)
  local copies, waits for them, and re-layouts  2.51 us (2%)
    all_to_all x2, blocking collectives, to_all(): return lax.all_to_all(values, axis, 0, 0)  24.1 us
    pallas_call x1, Pallas kernels, mlp(): pl.pallas_call(mlp_kernel, grid=(rows // TILE,), in_specs=[pl.BlockSpec(m...  19.2 us
    pallas_call x1, Pallas kernels, attn_backward(): pl.pallas_call(attn_backward_kernel, grid=(rows // TILE,), in_specs=[smem...  16.3 us
    ppermute x12, starting transfers between devices, across(): return lax.ppermute(values, 'inner', pairs)  14.1 us
    pallas_call x1, Pallas kernels, shampoo(): pl.pallas_call(lambda *refs: shampoo_kernel(scale, bool(norms), *refs), o...  12.4 us
    ppermute x12, waiting for transfers between devices, across(): return lax.ppermute(values, 'inner', pairs)  11.7 us
    pallas_call x1, Pallas kernels, attn_forward(): pl.pallas_call(attn_forward_kernel, grid=(rows // TILE,), in_specs=[smem]...  11.3 us
    all_to_all x2, starting transfers between devices, to_all(): return lax.all_to_all(values, axis, 0, 0)  8.31 us
  transfers between devices with their start and end apart: 25, of which 10 were waited for; matrix products, arithmetic and copies ran while one was open for 1% of the time, Pallas kernels for 22%

profile of v7, /device:TPU:0, one launch (start us, length us, event | category | flops | bytes accessed | tf_op | source)
XLA Modules:
  0.0 130.0 jit_solution(9639011557163910227)
XLA Ops:
  0.7 1.1 copy-done
  2.6 12.8 %all_to_all.20.refs_0_ = bf16[4,48,384]{2,1,0:T(8,128)(2,1)S(1)} all-to-all(bf16[4,48,384]{2,1,0:T(8,128)(2,1)S(1)} %get-tuple-element.62), channel_id=1, replica_groups=mesh['outer'=4,'inner'=4,'head'=2] {'outer'}, dimensions={0} | all-to-all | bytes 294912 | tf_op jit(solution)/shard_map/all_to_all | solution.py:696
  15.3 3.5 %all-to-all-start.1 = ((bf16[4,2,48,384]{3,2,1,0:T(8,128)(2,1)}), bf16[4,2,48,384]{3,2,1,0:T(8,128)(2,1)S(1)}, u32[]{:S(2)}, u32[]{:S(2)}) async-start(bf16[4,2,48,384]{3,2,1,0:T(8,128)(2,1)} %get-tuple-element.65), calls=%async_computation.1 | async-start | bytes 589824 | tf_op jit(solution)/shard_map/all_to_all | solution.py:696
  18.8 1.6 %collective-permute-start.6 = (bf16[4,48,384]{2,1,0:T(8,128)(2,1)S(1)}, bf16[4,48,384]{2,1,0:T(8,128)(2,1)S(1)}, u32[]{:S(2)}, u32[]{:S(2)}) collective-permute-start(bf16[4,48,384]{2,1,0:T(8,128)(2,1)S(1)} %all_to_all.20.refs_0_), channel_id=1, source_target_pairs={{0,4},{2,6},{4,0},{6,2},{1,5},{3,7},{5,1},{7,3},{8,12},{10,14},{12... | collective-permute-start | bytes 442376 | tf_op jit(solution)/shard_map/ppermute | solution.py:701
  20.4 1.5 %collective-permute-start.5 = (bf16[4,48,384]{2,1,0:T(8,128)(2,1)S(1)}, bf16[4,48,384]{2,1,0:T(8,128)(2,1)S(1)}, u32[]{:S(2)}, u32[]{:S(2)}) collective-permute-start(bf16[4,48,384]{2,1,0:T(8,128)(2,1)S(1)} %all_to_all.20.refs_0_), channel_id=1, source_target_pairs={{0,2},{2,0},{4,6},{6,4},{1,3},{3,1},{5,7},{7,5},{8,10},{10,8},{12,... | collective-permute-start | bytes 442376 | tf_op jit(solution)/shard_map/ppermute | solution.py:701
  23.6 1.6 %collective-permute-done.6.refs_2_ = bf16[4,48,384]{2,1,0:T(8,128)(2,1)S(1)} collective-permute-done((bf16[4,48,384]{2,1,0:T(8,128)(2,1)S(1)}, bf16[4,48,384]{2,1,0:T(8,128)(2,1)S(1)}, u32[]{:S(2)}, u32[]{:S(2)}) %collective-permute-start.6) | collective-permute-done | bytes 147488 | tf_op jit(solution)/shard_map/ppermute | solution.py:701
  26.0 2.1 %collective-permute-done.refs_3_ = bf16[4,48,384]{2,1,0:T(8,128)(2,1)S(1)} collective-permute-done((bf16[4,48,384]{2,1,0:T(8,128)(2,1)S(1)}, bf16[4,48,384]{2,1,0:T(8,128)(2,1)S(1)}, u32[]{:S(2)}, u32[]{:S(2)}) %collective-permute-start) | collective-permute-done | bytes 147488 | tf_op jit(solution)/shard_map/ppermute | solution.py:701
  28.6 1.9 %collective-permute-start.4 = (bf16[4,2,48,384]{3,2,1,0:T(8,128)(2,1)S(1)}, bf16[4,2,48,384]{3,2,1,0:T(8,128)(2,1)S(1)}, u32[]{:S(2)}, u32[]{:S(2)}) collective-permute-start(bf16[4,2,48,384]{3,2,1,0:T(8,128)(2,1)S(1)} %all-to-all-done.1.refs_0_), channel_id=1, source_target_pairs={{0,6},{2,4},{4,2},{6,0},{1,7},{3,5},{5,3},{7,1},{8,14},{10,12},{12... | collective-permute-start | bytes 884744 | tf_op jit(solution)/shard_map/ppermute | solution.py:701
  31.1 1.1 collective-permute-start.2
  32.8 11.3 %attn_forward.1 = (bf16[6,3,512,256]{3,2,1,0:T(8,128)(2,1)}, bf16[1536,1152]{1,0:T(8,128)(2,1)}, bf16[1536,384]{1,0:T(8,128)(2,1)}, f32[1536,384]{1,0:T(8,128)},...) custom-call(s32[2]{0:T(128)S(1)} %pad_add_fusion.place_ref, s32[12]{0:T(128)S(1)} %copy-done.6, ...), custom_call_target="tpu_custom_call" | custom-call | flops 4227858432 | bytes 16777216 | tf_op jit(solution)/shard_map/attn_forward/pallas_call | solution.py:168
  45.4 1.1 collective-permute-done.12.refs_5_
  47.3 19.2 %mlp.1 = (f32[1536,384]{1,0:T(8,128)}, f32[1536,384]{1,0:T(8,128)}, f32[2,384]{1,0:T(2,128)S(1)}, bf16[4,4,2,48,384]{4,3,2,1,0:T(8,128)(2,1)S(1)}, bf16[4,4,2,48,384]{4,3,2,1,0:T(8,128)(2,1)S(1)}) custom-call(s32[2]{0:T(128)S(1)} %pad_add_fusion.place_ref, f32[1536,384]{1,0:T(8,128)} %get-tuple-element.70.middle_ref, bf16[1536,384]{1,0:T(8,128)(2,1)} %cot_ref.1, ...), custom_call_target="tpu_custom_call" | custom-call | flops 10871635968 | bytes 20971520 | tf_op jit(solution)/shard_map/mlp/pallas_call | solution.py:265
  66.6 2.7 %collective-permute-done.15.received_ref = bf16[4,4,2,48,384]{4,3,2,1,0:T(8,128)(2,1)S(1)} collective-permute-done((bf16[4,4,2,48,384]{4,3,2,1,0:T(8,128)(2,1)S(1)}, bf16[4,4,2,48,384]{4,3,2,1,0:T(8,128)(2,1)S(1)}, u32[]{:S(2)}, u32[]{:S(2)}) %collective-permute-start.15) | collective-permute-done | bytes 1179680 | tf_op jit(solution)/shard_map/ppermute | solution.py:692
  69.6 1.1 collective-permute-start.16
  70.7 1.3 collective-permute-start.17
  72.0 1.2 collective-permute-start.18
  73.2 16.3 %attn_backward.1 = (f32[1536,384]{1,0:T(8,128)}, bf16[16,48,384]{2,1,0:T(8,128)(2,1)S(1)}, bf16[17,48,384]{2,1,0:T(8,128)(2,1)S(1)}, f32[4,384]{1,0:T(4,128)S(1)}) custom-call(s32[2]{0:T(128)S(1)} %pad_add_fusion.place_ref, s32[12,3]{1,0:T(8,128)S(1)} %copy.18.own_mask_ref, s32[12,3]{1,0:T(8,128)S(1)} %collective-permute-done.1.other_mask_ref, ...), custom_call_target="tpu_custom_call" | custom-call | flops 8455716864 | bytes 20971520 | tf_op jit(solution)/shard_map/attn_backward/pallas_call | solution.py:387
  90.5 4.9 %all-to-all-start.2 = ((bf16[4,2,48,384]{3,2,1,0:T(8,128)(2,1)}), bf16[4,2,48,384]{3,2,1,0:T(8,128)(2,1)S(1)}, u32[]{:S(2)}, u32[]{:S(2)}) async-start(bf16[4,2,48,384]{3,2,1,0:T(8,128)(2,1)} %sum_late.1), calls=%async_computation.2 | async-start | bytes 589824 | tf_op jit(solution)/shard_map/all_to_all | solution.py:696
  97.1 1.4 %collective-permute-start.21 = (bf16[200,384]{1,0:T(8,128)(2,1)S(1)}, bf16[200,384]{1,0:T(8,128)(2,1)S(1)}, u32[]{:S(2)}, u32[]{:S(2)}) collective-permute-start(bf16[200,384]{1,0:T(8,128)(2,1)S(1)} %get-tuple-element.100), channel_id=1, source_target_pairs={{0,4},{2,6},{4,0},{6,2},{1,5},{3,7},{5,1},{7,3},{8,12},{10,14},{12... | collective-permute-start | bytes 460808 | tf_op jit(solution)/shard_map/ppermute | solution.py:701
  98.4 1.2 collective-permute-start.22
  99.6 3.3 %collective-permute-done.20.refs_1_ = bf16[200,384]{1,0:T(8,128)(2,1)S(1)} collective-permute-done((bf16[200,384]{1,0:T(8,128)(2,1)S(1)}, bf16[200,384]{1,0:T(8,128)(2,1)S(1)}, u32[]{:S(2)}, u32[]{:S(2)}) %collective-permute-start.20) | collective-permute-done | bytes 153632 | tf_op jit(solution)/shard_map/ppermute | solution.py:701
  103.0 3.2 %collective-permute-done.21.refs_2_ = bf16[200,384]{1,0:T(8,128)(2,1)S(1)} collective-permute-done((bf16[200,384]{1,0:T(8,128)(2,1)S(1)}, bf16[200,384]{1,0:T(8,128)(2,1)S(1)}, u32[]{:S(2)}, u32[]{:S(2)}) %collective-permute-start.21) | collective-permute-done | bytes 153632 | tf_op jit(solution)/shard_map/ppermute | solution.py:701
  106.3 11.3 %all_to_all.21.refs_0_ = bf16[4,56,384]{2,1,0:T(8,128)(2,1)S(1)} all-to-all(bf16[4,56,384]{2,1,0:T(8,128)(2,1)S(1)} %join.1), channel_id=1, replica_groups=mesh['outer'=4,'inner'=4,'head'=2] {'outer'}, dimensions={0} | all-to-all | bytes 344064 | tf_op jit(solution)/shard_map/all_to_all | solution.py:696
  117.7 12.4 %shampoo.1 = (f32[3,8,48,48]{3,2,1,0:T(8,128)}, f32[3,8,48,48]{3,2,1,0:T(8,128)}, f32[3,8,48,48]{3,2,1,0:T(8,128)}, f32[3,8,48,48]{3,2,1,0:T(8,128)}, f32[4,384]...) custom-call(bf16[4,56,384]{2,1,0:T(8,128)(2,1)S(1)} %all_to_all.21.refs_0_, ...), custom_call_target="tpu_custom_call" | custom-call | flops 9663676416 | bytes 4194304 | tf_op jit(solution)/shard_map/shampoo/pallas_call | solution.py:678
  (55 shorter events, 10.5 us)
Async XLA Ops:
  15.3 12.7 %all-to-all-start.1 = ((bf16[4,2,48,384]{3,2,1,0:T(8,128)(2,1)}), bf16[4,2,48,384]{3,2,1,0:T(8,128)(2,1)S(1)}, u32[]{:S(2)}, u32[]{:S(2)}) async-start(bf16[4,2,48,384]{3,2,1,0:T(8,128)(2,1)} %get-tuple-element.65), calls=%async_computation.1 | async-start | bytes 589824 | tf_op jit(solution)/shard_map/all_to_all | solution.py:696
  18.8 6.4 %collective-permute-start.6 = (bf16[4,48,384]{2,1,0:T(8,128)(2,1)S(1)}, bf16[4,48,384]{2,1,0:T(8,128)(2,1)S(1)}, u32[]{:S(2)}, u32[]{:S(2)}) collective-permute-start(bf16[4,48,384]{2,1,0:T(8,128)(2,1)S(1)} %all_to_all.20.refs_0_), channel_id=1, source_target_pairs={{0,4},{2,6},{4,0},{6,2},{1,5},{3,7},{5,1},{7,3},{8,12},{10,14},{12... | collective-permute-start | bytes 442376 | tf_op jit(solution)/shard_map/ppermute | solution.py:701
  20.4 5.6 %collective-permute-start.5 = (bf16[4,48,384]{2,1,0:T(8,128)(2,1)S(1)}, bf16[4,48,384]{2,1,0:T(8,128)(2,1)S(1)}, u32[]{:S(2)}, u32[]{:S(2)}) collective-permute-start(bf16[4,48,384]{2,1,0:T(8,128)(2,1)S(1)} %all_to_all.20.refs_0_), channel_id=1, source_target_pairs={{0,2},{2,0},{4,6},{6,4},{1,3},{3,1},{5,7},{7,5},{8,10},{10,8},{12,... | collective-permute-start | bytes 442376 | tf_op jit(solution)/shard_map/ppermute | solution.py:701
  21.9 6.2 %collective-permute-start = (bf16[4,48,384]{2,1,0:T(8,128)(2,1)S(1)}, bf16[4,48,384]{2,1,0:T(8,128)(2,1)S(1)}, u32[]{:S(2)}, u32[]{:S(2)}) collective-permute-start(bf16[4,48,384]{2,1,0:T(8,128)(2,1)S(1)} %all_to_all.20.refs_0_), channel_id=1, source_target_pairs={{0,6},{2,4},{4,2},{6,0},{1,7},{3,5},{5,3},{7,1},{8,14},{10,12},{12... | collective-permute-start | bytes 442376 | tf_op jit(solution)/shard_map/ppermute | solution.py:701
  23.1 2.9 %collective-permute-start.1 = (s32[12,3]{1,0:T(8,128)S(1)}, s32[12,3]{1,0:T(8,128)S(1)}, u32[]{:S(2)}, u32[]{:S(2)}) collective-permute-start(s32[12,3]{1,0:T(8,128)S(1)} %copy.18.own_mask_ref), channel_id=1, source_target_pairs={{0,1},{1,0},{2,3},{3,2},{4,5},{5,4},{6,7},{7,6},{8,9},{9,8},{10,11... | collective-permute-start | bytes 440 | tf_op jit(solution)/shard_map/ppermute | solution.py:692
  23.1 5.5 %collective-permute-start.7 = (bf16[4,48,384]{2,1,0:T(8,128)(2,1)S(1)}, bf16[4,48,384]{2,1,0:T(8,128)(2,1)S(1)}, u32[]{:S(2)}, u32[]{:S(2)}) collective-permute-start(bf16[4,48,384]{2,1,0:T(8,128)(2,1)S(1)} %all_to_all.20.refs_0_), channel_id=1, source_target_pairs={{0,1},{1,0},{2,3},{3,2},{4,5},{5,4},{6,7},{7,6},{8,9},{9,8},{10,11... | collective-permute-start | bytes 442376 | tf_op jit(solution)/shard_map/ppermute | solution.py:692
  25.2 5.3 %collective-permute-start.9 = (bf16[4,48,384]{2,1,0:T(8,128)(2,1)S(1)}, bf16[4,48,384]{2,1,0:T(8,128)(2,1)S(1)}, u32[]{:S(2)}, u32[]{:S(2)}) collective-permute-start(bf16[4,48,384]{2,1,0:T(8,128)(2,1)S(1)} %collective-permute-done.6.refs_2_), channel_id=1, source_target_pairs={{0,1},{1,0},{2,3},{3,2},{4,5},{5,4},{6,7},{7,6},{8,9},{9,8},{10,11... | collective-permute-start | bytes 442376 | tf_op jit(solution)/shard_map/ppermute | solution.py:692
  26.0 5.1 %collective-permute-start.8 = (bf16[4,48,384]{2,1,0:T(8,128)(2,1)S(1)}, bf16[4,48,384]{2,1,0:T(8,128)(2,1)S(1)}, u32[]{:S(2)}, u32[]{:S(2)}) collective-permute-start(bf16[4,48,384]{2,1,0:T(8,128)(2,1)S(1)} %collective-permute-done.5.refs_1_), channel_id=1, source_target_pairs={{0,1},{1,0},{2,3},{3,2},{4,5},{5,4},{6,7},{7,6},{8,9},{9,8},{10,11... | collective-permute-start | bytes 442376 | tf_op jit(solution)/shard_map/ppermute | solution.py:692
  28.1 4.1 %collective-permute-start.10 = (bf16[4,48,384]{2,1,0:T(8,128)(2,1)S(1)}, bf16[4,48,384]{2,1,0:T(8,128)(2,1)S(1)}, u32[]{:S(2)}, u32[]{:S(2)}) collective-permute-start(bf16[4,48,384]{2,1,0:T(8,128)(2,1)S(1)} %collective-permute-done.refs_3_), channel_id=1, source_target_pairs={{0,1},{1,0},{2,3},{3,2},{4,5},{5,4},{6,7},{7,6},{8,9},{9,8},{10,11... | collective-permute-start | bytes 442376 | tf_op jit(solution)/shard_map/ppermute | solution.py:692
  28.1 17.3 %collective-permute-start.11 = (bf16[4,2,48,384]{3,2,1,0:T(8,128)(2,1)S(1)}, bf16[4,2,48,384]{3,2,1,0:T(8,128)(2,1)S(1)}, u32[]{:S(2)}, u32[]{:S(2)}) collective-permute-start(bf16[4,2,48,384]{3,2,1,0:T(8,128)(2,1)S(1)} %all-to-all-done.1.refs_0_), channel_id=1, source_target_pairs={{0,1},{1,0},{2,3},{3,2},{4,5},{5,4},{6,7},{7,6},{8,9},{9,8},{10,11... | collective-permute-start | bytes 884744 | tf_op jit(solution)/shard_map/ppermute | solution.py:692
  28.6 15.4 %collective-permute-start.4 = (bf16[4,2,48,384]{3,2,1,0:T(8,128)(2,1)S(1)}, bf16[4,2,48,384]{3,2,1,0:T(8,128)(2,1)S(1)}, u32[]{:S(2)}, u32[]{:S(2)}) collective-permute-start(bf16[4,2,48,384]{3,2,1,0:T(8,128)(2,1)S(1)} %all-to-all-done.1.refs_0_), channel_id=1, source_target_pairs={{0,6},{2,4},{4,2},{6,0},{1,7},{3,5},{5,3},{7,1},{8,14},{10,12},{12... | collective-permute-start | bytes 884744 | tf_op jit(solution)/shard_map/ppermute | solution.py:701
  30.6 14.3 %collective-permute-start.3 = (bf16[4,2,48,384]{3,2,1,0:T(8,128)(2,1)S(1)}, bf16[4,2,48,384]{3,2,1,0:T(8,128)(2,1)S(1)}, u32[]{:S(2)}, u32[]{:S(2)}) collective-permute-start(bf16[4,2,48,384]{3,2,1,0:T(8,128)(2,1)S(1)} %all-to-all-done.1.refs_0_), channel_id=1, source_target_pairs={{0,4},{2,6},{4,0},{6,2},{1,5},{3,7},{5,1},{7,3},{8,12},{10,14},{12... | collective-permute-start | bytes 884744 | tf_op jit(solution)/shard_map/ppermute | solution.py:701
  31.1 13.8 %collective-permute-start.2 = (bf16[4,2,48,384]{3,2,1,0:T(8,128)(2,1)S(1)}, bf16[4,2,48,384]{3,2,1,0:T(8,128)(2,1)S(1)}, u32[]{:S(2)}, u32[]{:S(2)}) collective-permute-start(bf16[4,2,48,384]{3,2,1,0:T(8,128)(2,1)S(1)} %all-to-all-done.1.refs_0_), channel_id=1, source_target_pairs={{0,2},{2,0},{4,6},{6,4},{1,3},{3,1},{5,7},{7,5},{8,10},{10,8},{12,... | collective-permute-start | bytes 884744 | tf_op jit(solution)/shard_map/ppermute | solution.py:701
  44.9 2.0 %collective-permute-start.13 = (bf16[4,2,48,384]{3,2,1,0:T(8,128)(2,1)S(1)}, bf16[4,2,48,384]{3,2,1,0:T(8,128)(2,1)S(1)}, u32[]{:S(2)}, u32[]{:S(2)}) collective-permute-start(bf16[4,2,48,384]{3,2,1,0:T(8,128)(2,1)S(1)} %collective-permute-done.3.refs_2_), channel_id=1, source_target_pairs={{0,1},{1,0},{2,3},{3,2},{4,5},{5,4},{6,7},{7,6},{8,9},{9,8},{10,11... | collective-permute-start | bytes 884744 | tf_op jit(solution)/shard_map/ppermute | solution.py:692
  45.4 1.9 %collective-permute-start.14 = (bf16[4,2,48,384]{3,2,1,0:T(8,128)(2,1)S(1)}, bf16[4,2,48,384]{3,2,1,0:T(8,128)(2,1)S(1)}, u32[]{:S(2)}, u32[]{:S(2)}) collective-permute-start(bf16[4,2,48,384]{3,2,1,0:T(8,128)(2,1)S(1)} %collective-permute-done.4.refs_3_), channel_id=1, source_target_pairs={{0,1},{1,0},{2,3},{3,2},{4,5},{5,4},{6,7},{7,6},{8,9},{9,8},{10,11... | collective-permute-start | bytes 884744 | tf_op jit(solution)/shard_map/ppermute | solution.py:692
  66.5 2.8 %collective-permute-start.15 = (bf16[4,4,2,48,384]{4,3,2,1,0:T(8,128)(2,1)S(1)}, bf16[4,4,2,48,384]{4,3,2,1,0:T(8,128)(2,1)S(1)}, u32[]{:S(2)}, u32[]{:S(2)}) collective-permute-start(bf16[4,4,2,48,384]{4,3,2,1,0:T(8,128)(2,1)S(1)} %get-tuple-element.76), channel_id=1, source_target_pairs={{0,1},{1,0},{2,3},{3,2},{4,5},{5,4},{6,7},{7,6},{8,9},{9,8},{10,11... | collective-permute-start | bytes 3538952 | tf_op jit(solution)/shard_map/ppermute | solution.py:692
  69.6 19.9 %collective-permute-start.16 = (bf16[4,2,48,384]{3,2,1,0:T(8,128)(2,1)S(1)}, bf16[4,2,48,384]{3,2,1,0:T(8,128)(2,1)S(1)}, u32[]{:S(2)}, u32[]{:S(2)}) collective-permute-start(bf16[4,2,48,384]{3,2,1,0:T(8,128)(2,1)S(1)} %get-tuple-element.92), channel_id=1, source_target_pairs={{0,2},{2,0},{4,6},{6,4},{1,3},{3,1},{5,7},{7,5},{8,10},{10,8},{12,... | collective-permute-start | bytes 884744 | tf_op jit(solution)/shard_map/ppermute | solution.py:701
  70.7 18.8 %collective-permute-start.17 = (bf16[4,2,48,384]{3,2,1,0:T(8,128)(2,1)S(1)}, bf16[4,2,48,384]{3,2,1,0:T(8,128)(2,1)S(1)}, u32[]{:S(2)}, u32[]{:S(2)}) collective-permute-start(bf16[4,2,48,384]{3,2,1,0:T(8,128)(2,1)S(1)} %get-tuple-element.93), channel_id=1, source_target_pairs={{0,4},{2,6},{4,0},{6,2},{1,5},{3,7},{5,1},{7,3},{8,12},{10,14},{12... | collective-permute-start | bytes 884744 | tf_op jit(solution)/shard_map/ppermute | solution.py:701
  72.0 17.5 %collective-permute-start.18 = (bf16[4,2,48,384]{3,2,1,0:T(8,128)(2,1)S(1)}, bf16[4,2,48,384]{3,2,1,0:T(8,128)(2,1)S(1)}, u32[]{:S(2)}, u32[]{:S(2)}) collective-permute-start(bf16[4,2,48,384]{3,2,1,0:T(8,128)(2,1)S(1)} %get-tuple-element.94), channel_id=1, source_target_pairs={{0,6},{2,4},{4,2},{6,0},{1,7},{3,5},{5,3},{7,1},{8,14},{10,12},{12... | collective-permute-start | bytes 884744 | tf_op jit(solution)/shard_map/ppermute | solution.py:701
  89.5 5.8 %collective-permute-start.19 = (bf16[17,48,384]{2,1,0:T(8,128)(2,1)S(1)}, bf16[17,48,384]{2,1,0:T(8,128)(2,1)S(1)}, u32[]{:S(2)}, u32[]{:S(2)}) collective-permute-start(bf16[17,48,384]{2,1,0:T(8,128)(2,1)S(1)} %get-tuple-element.96), channel_id=1, source_target_pairs={{0,1},{1,0},{2,3},{3,2},{4,5},{5,4},{6,7},{7,6},{8,9},{9,8},{10,11... | collective-permute-start | bytes 1880072 | tf_op jit(solution)/shard_map/ppermute | solution.py:692
  90.5 15.8 %all-to-all-start.2 = ((bf16[4,2,48,384]{3,2,1,0:T(8,128)(2,1)}), bf16[4,2,48,384]{3,2,1,0:T(8,128)(2,1)S(1)}, u32[]{:S(2)}, u32[]{:S(2)}) async-start(bf16[4,2,48,384]{3,2,1,0:T(8,128)(2,1)} %sum_late.1), calls=%async_computation.2 | async-start | bytes 589824 | tf_op jit(solution)/shard_map/all_to_all | solution.py:696
  96.1 6.9 %collective-permute-start.20 = (bf16[200,384]{1,0:T(8,128)(2,1)S(1)}, bf16[200,384]{1,0:T(8,128)(2,1)S(1)}, u32[]{:S(2)}, u32[]{:S(2)}) collective-permute-start(bf16[200,384]{1,0:T(8,128)(2,1)S(1)} %get-tuple-element.99), channel_id=1, source_target_pairs={{0,2},{2,0},{4,6},{6,4},{1,3},{3,1},{5,7},{7,5},{8,10},{10,8},{12,... | collective-permute-start | bytes 460808 | tf_op jit(solution)/shard_map/ppermute | solution.py:701
  97.1 9.1 %collective-permute-start.21 = (bf16[200,384]{1,0:T(8,128)(2,1)S(1)}, bf16[200,384]{1,0:T(8,128)(2,1)S(1)}, u32[]{:S(2)}, u32[]{:S(2)}) collective-permute-start(bf16[200,384]{1,0:T(8,128)(2,1)S(1)} %get-tuple-element.100), channel_id=1, source_target_pairs={{0,4},{2,6},{4,0},{6,2},{1,5},{3,7},{5,1},{7,3},{8,12},{10,14},{12... | collective-permute-start | bytes 460808 | tf_op jit(solution)/shard_map/ppermute | solution.py:701
  98.4 7.7 %collective-permute-start.22 = (bf16[200,384]{1,0:T(8,128)(2,1)S(1)}, bf16[200,384]{1,0:T(8,128)(2,1)S(1)}, u32[]{:S(2)}, u32[]{:S(2)}) collective-permute-start(bf16[200,384]{1,0:T(8,128)(2,1)S(1)} %get-tuple-element.101), channel_id=1, source_target_pairs={{0,6},{2,4},{4,2},{6,0},{1,7},{3,5},{5,3},{7,1},{8,14},{10,12},{12... | collective-permute-start | bytes 460808 | tf_op jit(solution)/shard_map/ppermute | solution.py:701
  (9 other events, 144.9 us)

commit v8 on v7

--- a/solution.py
+++ b/solution.py
@@ -90,7 +90,7 @@
 
 
 def attn_forward_kernel(
-    place_ref, counts_ref, own_mask_ref, other_mask_ref, x_ref, norm_ref, *refs
+    place_ref, own_mask_ref, other_mask_ref, x_ref, norm_ref, *refs
 ):
     slab_refs, refs = refs[: 2 * INNER], refs[2 * INNER :]
     prob_ref, qkv_ref, out_ref, middle_ref, wqkv_ref, wo_ref, held_ref = refs
@@ -139,8 +139,8 @@
         return nt(stacked(qkv_ref[here, query_lanes], first, second), qkv_ref[here, key_lanes])
 
     def get_prob(task, scores):
-        image = place_ref[0] * (counts_ref.shape[0] // 2) + IMAGES * step + task[0]
-        scores = jnp.where(column < counts_ref[image], scores, -1e30)
+        image = place_ref[0] * (own_mask_ref.shape[0] // 2) + IMAGES * step + task[0]
+        scores = jnp.where(column < place_ref[2 + image], scores, -1e30)
         top = jnp.max(scores, axis=-1, keepdims=True)
         exp_scores = jnp.exp(scores - top)
         total = jnp.sum(exp_scores, axis=-1, keepdims=True)
@@ -159,7 +159,7 @@
     middle_ref[...] = x + nn(out_ref[...], wo_ref[...])
 
 
-def attn_forward(place, counts, own_mask, other_mask, tokens, norm_params, slabs):
+def attn_forward(place, own_mask, other_mask, tokens, norm_params, slabs):
     rows = tokens.shape[0]
     images = rows // S
     tile = pl.BlockSpec((TILE, D), lambda i: (i, 0))
@@ -168,7 +168,7 @@
     return pl.pallas_call(
         attn_forward_kernel,
         grid=(rows // TILE,),
-        in_specs=[smem] * 4 + [tile, pl.BlockSpec((4, D), lambda i: (0, 0))] + [slab] * 2 * INNER,
+        in_specs=[smem] * 3 + [tile, pl.BlockSpec((4, D), lambda i: (0, 0))] + [slab] * 2 * INNER,
         out_specs=[
             pl.BlockSpec((IMAGES, PAIRS, 2 * S, S), lambda i: (i, 0, 0, 0)),
             pl.BlockSpec((TILE, 3 * D), lambda i: (i, 0)),
@@ -191,7 +191,7 @@
             flops=rows * D * (8 * D + 16 * S), bytes_accessed=16 << 20, transcendentals=rows * 6 * S
         ),
         name="attn_forward",
-    )(place, counts, own_mask, other_mask, in_hbm(tokens), in_hbm(norm_params), *slabs)
+    )(place, own_mask, other_mask, in_hbm(tokens), in_hbm(norm_params), *slabs)
 
 
 def mlp_kernel(place_ref, middle_ref, cot_ref, norm_ref, *refs):
@@ -451,7 +451,7 @@
         ],
         compiler_params=pltpu.CompilerParams(vmem_limit_bytes=SMALL_VMEM),
         name="pack",
-    )(weights)
+    )(in_hbm(weights))
 
 
 def add_kernel(own_ref, received_ref, *out_refs):
@@ -566,22 +566,17 @@
     new_ref[...] = param_ref[...] - 0.2 * grads / jnp.sqrt(state)
 
 
-def shampoo_kernel(scale, with_norms, early_ref, late_ref, weight_ref, left_ref, right_ref, *refs):
+def shampoo_kernel(scale, with_norms, received_ref, weight_ref, left_ref, right_ref, *refs):
     if with_norms:
-        norm_ins, norm_outs, refs = refs[:2], refs[6:9], refs[2:6] + refs[9:]
-    out_grad_ref, left_new_ref, right_new_ref, new_weight_ref, root_ref, power_ref = refs
+        norm_ins, norm_outs, refs = refs[:2], refs[-5:-2], refs[:-5] + refs[-2:]
+    out_grad_ref, left_new_ref, right_new_ref, new_weight_ref, root_ref, power_ref = refs[-6:]
     groups, count, edge = weight_ref.shape[:3]
 
-    def total_of(ref):
-        total = ref[0].astype(F32)
-        for number in range(1, ref.shape[0]):
-            total = total + ref[number].astype(F32)
-        return total
-
-    early, late = total_of(early_ref), total_of(late_ref)
-    received = [early[:edge], *[late[group] for group in range(groups - 1)]]
+    received = received_ref[0].astype(F32)
+    for number in range(1, received_ref.shape[0]):
+        received = received + received_ref[number].astype(F32)
     if with_norms:
-        norms = early[edge:]
+        norms = received[0, edge:]
         update_norms(scale, norms[:4] + norms[4:], *norm_ins, *norm_outs)
     pack = min(PACK, count)
     width = pack * edge
@@ -608,7 +603,7 @@
 
     grads, parts = [], []
     for group, start in places:
-        grad = received[group][:, edge * start : edge * start + width] * scale
+        grad = received[group, :edge, edge * start : edge * start + width] * scale
         blocks = [cut(grad, index) for index in range(pack)]
         for index in range(pack):
             out_grad_ref[group, start + index] = blocks[index]
@@ -669,23 +664,41 @@
             new_weight_ref[group, start + index] = weight_ref[group, start + index] - step
 
 
-def shampoo(early, late, weights, stat_left, stat_right, scale, norms=()):
-    groups, count, edge, _ = weights.shape
+def shampoo(received, weights, stat_left, stat_right, scale, first, earlier=(), norms=()):
+    groups = received.shape[1]
+    _, count, edge, _ = weights.shape
     slots = 2 * groups * count // min(PACK, count)
     width = min(PACK, count) * edge
+    block = pl.BlockSpec(
+        (pl.Element(groups), pl.Element(count), pl.Element(edge), pl.Element(edge)),
+        lambda i: (first, 0, 0, 0),
+    )
     shape = jax.ShapeDtypeStruct(weights.shape, F32)
-    norm_shapes = [jax.ShapeDtypeStruct((4, D), F32)] * (3 if norms else 0)
+    norm = pl.BlockSpec((4, D), lambda i: (0, 0))
+    norm_outs = 3 if norms else 0
+    ins = 4 + len(norms)
     return pl.pallas_call(
         lambda *refs: shampoo_kernel(scale, bool(norms), *refs),
-        out_shape=[shape] * 4 + norm_shapes,
+        grid=(1,),
+        in_specs=[
+            pl.BlockSpec(received.shape, lambda i: (0, 0, 0, 0)),
+            *[block] * 3,
+            *[norm] * len(norms),
+            *[pl.BlockSpec(memory_space=pl.ANY)] * len(earlier),
+        ],
+        out_specs=[block] * 4 + [norm] * norm_outs,
+        out_shape=[shape] * 4 + [jax.ShapeDtypeStruct((4, D), F32)] * norm_outs,
         scratch_shapes=[
             pltpu.VMEM((slots, edge, width), F32),
             pltpu.VMEM((slots, edge, width), F32),
         ],
+        input_output_aliases={ins + i: i for i in range(len(earlier))},
         compiler_params=pltpu.CompilerParams(vmem_limit_bytes=SHAMPOO_VMEM),
-        cost_estimate=pl.CostEstimate(flops=9 << 30, bytes_accessed=4 << 20, transcendentals=0),
+        cost_estimate=pl.CostEstimate(
+            flops=groups * (3 << 30), bytes_accessed=4 << 20, transcendentals=0
+        ),
         name="shampoo",
-    )(early, late, weights, stat_left, stat_right, *norms)
+    )(received, in_hbm(weights), in_hbm(stat_left), in_hbm(stat_right), *map(in_hbm, norms), *earlier)
 
 
 def swap_heads(values):
@@ -746,11 +759,11 @@
     _, count, edge, _ = weights.shape
     whole_slabs = count * edge == D
     other_mask = swap_heads(head_mask)
+    inner = lax.axis_index("inner") if whole_slabs else 0
+    place = jnp.concatenate([jnp.stack([lax.axis_index("head"), inner]), token_counts])
     if whole_slabs:
-        place = jnp.stack([lax.axis_index("head"), lax.axis_index("inner")])
         early, late, other_mask = gather_slabs(weights, other_mask)
     else:
-        place = jnp.stack([lax.axis_index("head"), 0])
         local = weights.astype(BF)
         early = jnp.split(gather_blocks(local[:1]), INNER)
         late = jnp.split(gather_blocks(local[1:]), INNER)
@@ -758,7 +771,7 @@
     masks = (head_mask, other_mask)
     early += [swap_heads(piece) for piece in early]
     prob, qkv, out, middle, wqkv, wo = attn_forward(
-        place, token_counts, *masks, tokens, norm_params, early
+        place, *masks, tokens, norm_params, early
     )
     late[1:], middle = lax.optimization_barrier((late[1:], middle))
     late += [swap_heads(piece) for piece in late]
@@ -784,14 +797,16 @@
         early_grads = list(combine(place, own_early, early_received, norm_sums))
         early_grads[1:] = [across(early_grads[apart], apart) for apart in range(1, INNER)]
         joined, late_grads = lax.optimization_barrier((join(early_grads), late_grads))
-        results = shampoo(to_all(joined, "outer"), late_grads, *state, (norm_params, norm_state))
+        joined = to_all(joined, "outer")[:, None]
+        results = shampoo(late_grads, *state, 1)
+        results = shampoo(joined, *state, 0, results, (norm_params, norm_state))
     else:
         early_slabs = own_early.astype(F32) + early_received[:SLABS].astype(F32)
         late_slabs = own_late.astype(F32) + late_received.astype(F32)
         late_slabs = late_slabs.reshape(SLABS, 2, edge, D)
         slabs = jnp.concatenate([early_slabs[:, None], late_slabs], axis=1).astype(BF)
         owned = scatter_blocks(slabs, count, edge)
-        results = list(shampoo(owned[:1], owned[None, 1:], *state))
+        results = list(shampoo(owned[None], *state, 0))
         norm_grads = lax.psum(norm_sums, ("outer", "inner", "head")) * scale
         state_new = 0.5 * norm_state + 0.5 * norm_grads * norm_grads
         results += [norm_grads, state_new, norm_params - 0.2 * norm_grads / jnp.sqrt(state_new)]

time: 130 us -> 131 us (level)
  blocking collectives: 24.1 us -> 12.8 us
  Pallas kernels: 61.9 us -> 69.2 us
  starting transfers between devices: 24.2 us -> 29 us
  local copies, waits for them, and re-layouts: 2.51 us -> 0.77 us
    all_to_all x2 -> x1, blocking collectives: 24.1 us -> 12.8 us  [to_all(): return lax.all_to_all(values, axis, 0, 0)]
    pallas_call x1 -> x2, Pallas kernels: 12.4 us -> 17.9 us  [shampoo(): pl.pallas_call(lambda *refs: shampoo_kernel(scale, bool(norms), *refs), g...]
    all_to_all x2 -> x3, starting transfers between devices: 8.31 us -> 13.1 us  [to_all(): return lax.all_to_all(values, axis, 0, 0)]
    unnamed x17 -> x3, local copies, waits for them, and re-layouts: 2.51 us -> 0.77 us
  transfers between devices with their start and end apart: 25 -> 26, of which waited for: 10 -> 10; matrix products, arithmetic and copies ran while one was open for 1% -> 1% of each run, Pallas kernels for 22% -> 31%
where the time goes in v8:
time: 131 us; the launch traced here: 130 us
  Pallas kernels  69.2 us (53%)
  starting transfers between devices  29 us (22%)
  waiting for transfers between devices  17 us (13%)
  blocking collectives  12.8 us (10%)
    pallas_call x1, Pallas kernels, mlp(): pl.pallas_call(mlp_kernel, grid=(rows // TILE,), in_specs=[pl.BlockSpec(m...  19.2 us
    pallas_call x2, Pallas kernels, shampoo(): pl.pallas_call(lambda *refs: shampoo_kernel(scale, bool(norms), *refs), g...  17.9 us
    pallas_call x1, Pallas kernels, attn_backward(): pl.pallas_call(attn_backward_kernel, grid=(rows // TILE,), in_specs=[smem...  16.3 us
    ppermute x12, starting transfers between devices, across(): return lax.ppermute(values, 'inner', pairs)  14.1 us
    all_to_all x3, starting transfers between devices, to_all(): return lax.all_to_all(values, axis, 0, 0)  13.1 us
    all_to_all x1, blocking collectives, to_all(): return lax.all_to_all(values, axis, 0, 0)  12.8 us
    ppermute x12, waiting for transfers between devices, across(): return lax.ppermute(values, 'inner', pairs)  12.4 us
    pallas_call x1, Pallas kernels, attn_forward(): pl.pallas_call(attn_forward_kernel, grid=(rows // TILE,), in_specs=[smem]...  11.3 us
  transfers between devices with their start and end apart: 26, of which 10 were waited for; matrix products, arithmetic and copies ran while one was open for 1% of the time, Pallas kernels for 31%

profile of v8, /device:TPU:0, one launch (start us, length us, event | category | flops | bytes accessed | tf_op | source)
XLA Modules:
  0.0 130.3 jit_solution(14976395204835842957)
XLA Ops:
  0.6 1.9 %pack.1 = (bf16[4,48,384]{2,1,0:T(8,128)(2,1)S(1)}, bf16[4,2,48,384]{3,2,1,0:T(8,128)(2,1)}) custom-call(f32[3,8,48,48]{3,2,1,0:T(8,128)} %bitcast.11), custom_call_target="tpu_custom_call" | custom-call | tf_op jit(solution)/shard_map/pack/pallas_call | solution.py:446
  2.6 12.8 %all_to_all.20.refs_0_ = bf16[4,48,384]{2,1,0:T(8,128)(2,1)S(1)} all-to-all(bf16[4,48,384]{2,1,0:T(8,128)(2,1)S(1)} %get-tuple-element.66), channel_id=1, replica_groups=mesh['outer'=4,'inner'=4,'head'=2] {'outer'}, dimensions={0} | all-to-all | bytes 294912 | tf_op jit(solution)/shard_map/all_to_all | solution.py:709
  15.3 3.5 %all-to-all-start.1 = ((bf16[4,2,48,384]{3,2,1,0:T(8,128)(2,1)}), bf16[4,2,48,384]{3,2,1,0:T(8,128)(2,1)S(1)}, u32[]{:S(2)}, u32[]{:S(2)}) async-start(bf16[4,2,48,384]{3,2,1,0:T(8,128)(2,1)} %get-tuple-element.69), calls=%async_computation.1 | async-start | bytes 589824 | tf_op jit(solution)/shard_map/all_to_all | solution.py:709
  18.8 1.6 %collective-permute-start.6 = (bf16[4,48,384]{2,1,0:T(8,128)(2,1)S(1)}, bf16[4,48,384]{2,1,0:T(8,128)(2,1)S(1)}, u32[]{:S(2)}, u32[]{:S(2)}) collective-permute-start(bf16[4,48,384]{2,1,0:T(8,128)(2,1)S(1)} %all_to_all.20.refs_0_), channel_id=1, source_target_pairs={{0,4},{2,6},{4,0},{6,2},{1,5},{3,7},{5,1},{7,3},{8,12},{10,14},{12... | collective-permute-start | bytes 442376 | tf_op jit(solution)/shard_map/ppermute | solution.py:714
  20.4 1.5 %collective-permute-start.5 = (bf16[4,48,384]{2,1,0:T(8,128)(2,1)S(1)}, bf16[4,48,384]{2,1,0:T(8,128)(2,1)S(1)}, u32[]{:S(2)}, u32[]{:S(2)}) collective-permute-start(bf16[4,48,384]{2,1,0:T(8,128)(2,1)S(1)} %all_to_all.20.refs_0_), channel_id=1, source_target_pairs={{0,2},{2,0},{4,6},{6,4},{1,3},{3,1},{5,7},{7,5},{8,10},{10,8},{12,... | collective-permute-start | bytes 442376 | tf_op jit(solution)/shard_map/ppermute | solution.py:714
  23.6 1.6 %collective-permute-done.6.refs_2_ = bf16[4,48,384]{2,1,0:T(8,128)(2,1)S(1)} collective-permute-done((bf16[4,48,384]{2,1,0:T(8,128)(2,1)S(1)}, bf16[4,48,384]{2,1,0:T(8,128)(2,1)S(1)}, u32[]{:S(2)}, u32[]{:S(2)}) %collective-permute-start.6) | collective-permute-done | bytes 147488 | tf_op jit(solution)/shard_map/ppermute | solution.py:714
  26.0 2.1 %collective-permute-done.refs_3_ = bf16[4,48,384]{2,1,0:T(8,128)(2,1)S(1)} collective-permute-done((bf16[4,48,384]{2,1,0:T(8,128)(2,1)S(1)}, bf16[4,48,384]{2,1,0:T(8,128)(2,1)S(1)}, u32[]{:S(2)}, u32[]{:S(2)}) %collective-permute-start) | collective-permute-done | bytes 147488 | tf_op jit(solution)/shard_map/ppermute | solution.py:714
  29.3 1.9 %collective-permute-start.4 = (bf16[4,2,48,384]{3,2,1,0:T(8,128)(2,1)S(1)}, bf16[4,2,48,384]{3,2,1,0:T(8,128)(2,1)S(1)}, u32[]{:S(2)}, u32[]{:S(2)}) collective-permute-start(bf16[4,2,48,384]{3,2,1,0:T(8,128)(2,1)S(1)} %all-to-all-done.1.refs_0_), channel_id=1, source_target_pairs={{0,6},{2,4},{4,2},{6,0},{1,7},{3,5},{5,3},{7,1},{8,14},{10,12},{12... | collective-permute-start | bytes 884744 | tf_op jit(solution)/shard_map/ppermute | solution.py:714
  32.8 11.3 %attn_forward.1 = (bf16[6,3,512,256]{3,2,1,0:T(8,128)(2,1)}, bf16[1536,1152]{1,0:T(8,128)(2,1)}, bf16[1536,384]{1,0:T(8,128)(2,1)}, f32[1536,384]{1,0:T(8,128)},...) custom-call(s32[14]{0:T(128)S(1)} %pad_add_fusion.place_ref, s32[12,3]{1,0:T(8,128)S(1)} %copy.22.own_mask_ref, ...), custom_call_target="tpu_custom_call" | custom-call | flops 4227858432 | bytes 16777216 | tf_op jit(solution)/shard_map/attn_forward/pallas_call | solution.py:168
  44.1 1.4 %collective-permute-done.3.refs_2_ = bf16[4,2,48,384]{3,2,1,0:T(8,128)(2,1)S(1)} collective-permute-done((bf16[4,2,48,384]{3,2,1,0:T(8,128)(2,1)S(1)}, bf16[4,2,48,384]{3,2,1,0:T(8,128)(2,1)S(1)}, u32[]{:S(2)}, u32[]{:S(2)}) %collective-permute-start.3) | collective-permute-done | bytes 294944 | tf_op jit(solution)/shard_map/ppermute | solution.py:714
  47.9 19.2 %mlp.1 = (f32[1536,384]{1,0:T(8,128)}, f32[1536,384]{1,0:T(8,128)}, f32[2,384]{1,0:T(2,128)S(1)}, bf16[4,4,2,48,384]{4,3,2,1,0:T(8,128)(2,1)S(1)}, bf16[4,4,2,48,384]{4,3,2,1,0:T(8,128)(2,1)S(1)}) custom-call(s32[14]{0:T(128)S(1)} %pad_add_fusion.place_ref, f32[1536,384]{1,0:T(8,128)} %get-tuple-element.74.middle_ref, bf16[1536,384]{1,0:T(8,128)(2,1)} %cot_ref.1, ...), custom_call_target="tpu_custom_call" | custom-call | flops 10871635968 | bytes 20971520 | tf_op jit(solution)/shard_map/mlp/pallas_call | solution.py:265
  67.3 2.7 %collective-permute-done.15.received_ref = bf16[4,4,2,48,384]{4,3,2,1,0:T(8,128)(2,1)S(1)} collective-permute-done((bf16[4,4,2,48,384]{4,3,2,1,0:T(8,128)(2,1)S(1)}, bf16[4,4,2,48,384]{4,3,2,1,0:T(8,128)(2,1)S(1)}, u32[]{:S(2)}, u32[]{:S(2)}) %collective-permute-start.15) | collective-permute-done | bytes 1179680 | tf_op jit(solution)/shard_map/ppermute | solution.py:705
  70.3 1.1 collective-permute-start.16
  71.4 1.3 collective-permute-start.17
  72.7 1.2 collective-permute-start.18
  73.8 16.3 %attn_backward.1 = (f32[1536,384]{1,0:T(8,128)}, bf16[16,48,384]{2,1,0:T(8,128)(2,1)S(1)}, bf16[17,48,384]{2,1,0:T(8,128)(2,1)S(1)}, f32[4,384]{1,0:T(4,128)S(1)}) custom-call(s32[14]{0:T(128)S(1)} %pad_add_fusion.place_ref, s32[12,3]{1,0:T(8,128)S(1)} %copy.22.own_mask_ref, s32[12,3]{1,0:T(8,128)S(1)} %collective-permute-done.1.other_mask_ref, ...), custom_call_target="tpu_custom_call" | custom-call | flops 8455716864 | bytes 20971520 | tf_op jit(solution)/shard_map/attn_backward/pallas_call | solution.py:387
  91.1 4.8 %all-to-all-start.2 = ((bf16[4,2,48,384]{3,2,1,0:T(8,128)(2,1)}), bf16[4,2,48,384]{3,2,1,0:T(8,128)(2,1)S(1)}, u32[]{:S(2)}, u32[]{:S(2)}) async-start(bf16[4,2,48,384]{3,2,1,0:T(8,128)(2,1)} %sum_late.1), calls=%async_computation.2 | async-start | bytes 589824 | tf_op jit(solution)/shard_map/all_to_all | solution.py:709
  97.7 1.4 %collective-permute-start.21 = (bf16[200,384]{1,0:T(8,128)(2,1)S(1)}, bf16[200,384]{1,0:T(8,128)(2,1)S(1)}, u32[]{:S(2)}, u32[]{:S(2)}) collective-permute-start(bf16[200,384]{1,0:T(8,128)(2,1)S(1)} %get-tuple-element.104), channel_id=1, source_target_pairs={{0,4},{2,6},{4,0},{6,2},{1,5},{3,7},{5,1},{7,3},{8,12},{10,14},{12... | collective-permute-start | bytes 460808 | tf_op jit(solution)/shard_map/ppermute | solution.py:714
  99.1 1.1 collective-permute-start.22
  100.2 3.3 %collective-permute-done.20.refs_1_ = bf16[200,384]{1,0:T(8,128)(2,1)S(1)} collective-permute-done((bf16[200,384]{1,0:T(8,128)(2,1)S(1)}, bf16[200,384]{1,0:T(8,128)(2,1)S(1)}, u32[]{:S(2)}, u32[]{:S(2)}) %collective-permute-start.20) | collective-permute-done | bytes 153632 | tf_op jit(solution)/shard_map/ppermute | solution.py:714
  103.5 3.2 %collective-permute-done.21.refs_2_ = bf16[200,384]{1,0:T(8,128)(2,1)S(1)} collective-permute-done((bf16[200,384]{1,0:T(8,128)(2,1)S(1)}, bf16[200,384]{1,0:T(8,128)(2,1)S(1)}, u32[]{:S(2)}, u32[]{:S(2)}) %collective-permute-start.21) | collective-permute-done | bytes 153632 | tf_op jit(solution)/shard_map/ppermute | solution.py:714
  107.5 4.8 %all-to-all-start.3 = ((bf16[4,56,384]{2,1,0:T(8,128)(2,1)}), bf16[4,56,384]{2,1,0:T(8,128)(2,1)S(1)}, u32[]{:S(2)}, u32[]{:S(2)}) async-start(bf16[4,56,384]{2,1,0:T(8,128)(2,1)} %join.1), calls=%async_computation.3 | async-start | bytes 344064 | tf_op jit(solution)/shard_map/all_to_all | solution.py:709
  112.3 10.2 %shampoo.2 = (f32[3,8,48,48]{3,2,1,0:T(8,128)}, f32[3,8,48,48]{3,2,1,0:T(8,128)}, f32[3,8,48,48]{3,2,1,0:T(8,128)}, f32[3,8,48,48]{3,2,1,0:T(8,128)}) custom-call(bf16[4,2,48,384]{3,2,1,0:T(8,128)(2,1)S(1)} %all-to-all-done.2.refs_0_, f32[3,8,48,48]{3,2,1,0:T(8,128)} %bitcast.12, f32[3,8,48,48]{3,2,1,0:T(8,128)} %bitcast.14, f32[3,8,48,48]{3,2,1,0:T(8,128)} %bitcast.16), custom_call_target="tpu_custom_call" | custom-call | flops 6442450944 | bytes 4194304 | tf_op jit(solution)/shard_map/shampoo/pallas_call | solution.py:680
  122.5 7.8 %shampoo.3 = (f32[3,8,48,48]{3,2,1,0:T(8,128)}, f32[3,8,48,48]{3,2,1,0:T(8,128)}, f32[3,8,48,48]{3,2,1,0:T(8,128)}, f32[3,8,48,48]{3,2,1,0:T(8,128)}, f32[4,384]...) custom-call(bf16[4,1,56,384]{3,2,1,0:T(8,128)(2,1)S(1)} %bitcast.10,, ...), custom_call_target="tpu_custom_call", output_to_operand_aliasing={{0}: (6, {}), {1}: (7, {}), {2}: (8, {}), {3}: (9, {})} | custom-call | flops 3221225472 | bytes 4194304 | tf_op jit(solution)/shard_map/shampoo/pallas_call | solution.py:680
  (43 shorter events, 11.7 us)
Async XLA Ops:
  15.3 12.7 %all-to-all-start.1 = ((bf16[4,2,48,384]{3,2,1,0:T(8,128)(2,1)}), bf16[4,2,48,384]{3,2,1,0:T(8,128)(2,1)S(1)}, u32[]{:S(2)}, u32[]{:S(2)}) async-start(bf16[4,2,48,384]{3,2,1,0:T(8,128)(2,1)} %get-tuple-element.69), calls=%async_computation.1 | async-start | bytes 589824 | tf_op jit(solution)/shard_map/all_to_all | solution.py:709
  18.8 6.4 %collective-permute-start.6 = (bf16[4,48,384]{2,1,0:T(8,128)(2,1)S(1)}, bf16[4,48,384]{2,1,0:T(8,128)(2,1)S(1)}, u32[]{:S(2)}, u32[]{:S(2)}) collective-permute-start(bf16[4,48,384]{2,1,0:T(8,128)(2,1)S(1)} %all_to_all.20.refs_0_), channel_id=1, source_target_pairs={{0,4},{2,6},{4,0},{6,2},{1,5},{3,7},{5,1},{7,3},{8,12},{10,14},{12... | collective-permute-start | bytes 442376 | tf_op jit(solution)/shard_map/ppermute | solution.py:714
  20.4 5.6 %collective-permute-start.5 = (bf16[4,48,384]{2,1,0:T(8,128)(2,1)S(1)}, bf16[4,48,384]{2,1,0:T(8,128)(2,1)S(1)}, u32[]{:S(2)}, u32[]{:S(2)}) collective-permute-start(bf16[4,48,384]{2,1,0:T(8,128)(2,1)S(1)} %all_to_all.20.refs_0_), channel_id=1, source_target_pairs={{0,2},{2,0},{4,6},{6,4},{1,3},{3,1},{5,7},{7,5},{8,10},{10,8},{12,... | collective-permute-start | bytes 442376 | tf_op jit(solution)/shard_map/ppermute | solution.py:714
  21.9 6.2 %collective-permute-start = (bf16[4,48,384]{2,1,0:T(8,128)(2,1)S(1)}, bf16[4,48,384]{2,1,0:T(8,128)(2,1)S(1)}, u32[]{:S(2)}, u32[]{:S(2)}) collective-permute-start(bf16[4,48,384]{2,1,0:T(8,128)(2,1)S(1)} %all_to_all.20.refs_0_), channel_id=1, source_target_pairs={{0,6},{2,4},{4,2},{6,0},{1,7},{3,5},{5,3},{7,1},{8,14},{10,12},{12... | collective-permute-start | bytes 442376 | tf_op jit(solution)/shard_map/ppermute | solution.py:714
  23.1 2.9 %collective-permute-start.1 = (s32[12,3]{1,0:T(8,128)S(1)}, s32[12,3]{1,0:T(8,128)S(1)}, u32[]{:S(2)}, u32[]{:S(2)}) collective-permute-start(s32[12,3]{1,0:T(8,128)S(1)} %copy.22.own_mask_ref), channel_id=1, source_target_pairs={{0,1},{1,0},{2,3},{3,2},{4,5},{5,4},{6,7},{7,6},{8,9},{9,8},{10,11... | collective-permute-start | bytes 440 | tf_op jit(solution)/shard_map/ppermute | solution.py:705
  23.1 6.2 %collective-permute-start.7 = (bf16[4,48,384]{2,1,0:T(8,128)(2,1)S(1)}, bf16[4,48,384]{2,1,0:T(8,128)(2,1)S(1)}, u32[]{:S(2)}, u32[]{:S(2)}) collective-permute-start(bf16[4,48,384]{2,1,0:T(8,128)(2,1)S(1)} %all_to_all.20.refs_0_), channel_id=1, source_target_pairs={{0,1},{1,0},{2,3},{3,2},{4,5},{5,4},{6,7},{7,6},{8,9},{9,8},{10,11... | collective-permute-start | bytes 442376 | tf_op jit(solution)/shard_map/ppermute | solution.py:705
  25.2 6.0 %collective-permute-start.9 = (bf16[4,48,384]{2,1,0:T(8,128)(2,1)S(1)}, bf16[4,48,384]{2,1,0:T(8,128)(2,1)S(1)}, u32[]{:S(2)}, u32[]{:S(2)}) collective-permute-start(bf16[4,48,384]{2,1,0:T(8,128)(2,1)S(1)} %collective-permute-done.6.refs_2_), channel_id=1, source_target_pairs={{0,1},{1,0},{2,3},{3,2},{4,5},{5,4},{6,7},{7,6},{8,9},{9,8},{10,11... | collective-permute-start | bytes 442376 | tf_op jit(solution)/shard_map/ppermute | solution.py:705
  26.0 5.7 %collective-permute-start.8 = (bf16[4,48,384]{2,1,0:T(8,128)(2,1)S(1)}, bf16[4,48,384]{2,1,0:T(8,128)(2,1)S(1)}, u32[]{:S(2)}, u32[]{:S(2)}) collective-permute-start(bf16[4,48,384]{2,1,0:T(8,128)(2,1)S(1)} %collective-permute-done.5.refs_1_), channel_id=1, source_target_pairs={{0,1},{1,0},{2,3},{3,2},{4,5},{5,4},{6,7},{7,6},{8,9},{9,8},{10,11... | collective-permute-start | bytes 442376 | tf_op jit(solution)/shard_map/ppermute | solution.py:705
  28.1 4.7 %collective-permute-start.10 = (bf16[4,48,384]{2,1,0:T(8,128)(2,1)S(1)}, bf16[4,48,384]{2,1,0:T(8,128)(2,1)S(1)}, u32[]{:S(2)}, u32[]{:S(2)}) collective-permute-start(bf16[4,48,384]{2,1,0:T(8,128)(2,1)S(1)} %collective-permute-done.refs_3_), channel_id=1, source_target_pairs={{0,1},{1,0},{2,3},{3,2},{4,5},{5,4},{6,7},{7,6},{8,9},{9,8},{10,11... | collective-permute-start | bytes 442376 | tf_op jit(solution)/shard_map/ppermute | solution.py:705
  28.8 17.2 %collective-permute-start.11 = (bf16[4,2,48,384]{3,2,1,0:T(8,128)(2,1)S(1)}, bf16[4,2,48,384]{3,2,1,0:T(8,128)(2,1)S(1)}, u32[]{:S(2)}, u32[]{:S(2)}) collective-permute-start(bf16[4,2,48,384]{3,2,1,0:T(8,128)(2,1)S(1)} %all-to-all-done.1.refs_0_), channel_id=1, source_target_pairs={{0,1},{1,0},{2,3},{3,2},{4,5},{5,4},{6,7},{7,6},{8,9},{9,8},{10,11... | collective-permute-start | bytes 884744 | tf_op jit(solution)/shard_map/ppermute | solution.py:705
  29.3 14.8 %collective-permute-start.4 = (bf16[4,2,48,384]{3,2,1,0:T(8,128)(2,1)S(1)}, bf16[4,2,48,384]{3,2,1,0:T(8,128)(2,1)S(1)}, u32[]{:S(2)}, u32[]{:S(2)}) collective-permute-start(bf16[4,2,48,384]{3,2,1,0:T(8,128)(2,1)S(1)} %all-to-all-done.1.refs_0_), channel_id=1, source_target_pairs={{0,6},{2,4},{4,2},{6,0},{1,7},{3,5},{5,3},{7,1},{8,14},{10,12},{12... | collective-permute-start | bytes 884744 | tf_op jit(solution)/shard_map/ppermute | solution.py:714
  31.2 14.3 %collective-permute-start.3 = (bf16[4,2,48,384]{3,2,1,0:T(8,128)(2,1)S(1)}, bf16[4,2,48,384]{3,2,1,0:T(8,128)(2,1)S(1)}, u32[]{:S(2)}, u32[]{:S(2)}) collective-permute-start(bf16[4,2,48,384]{3,2,1,0:T(8,128)(2,1)S(1)} %all-to-all-done.1.refs_0_), channel_id=1, source_target_pairs={{0,4},{2,6},{4,0},{6,2},{1,5},{3,7},{5,1},{7,3},{8,12},{10,14},{12... | collective-permute-start | bytes 884744 | tf_op jit(solution)/shard_map/ppermute | solution.py:714
  31.7 13.8 %collective-permute-start.2 = (bf16[4,2,48,384]{3,2,1,0:T(8,128)(2,1)S(1)}, bf16[4,2,48,384]{3,2,1,0:T(8,128)(2,1)S(1)}, u32[]{:S(2)}, u32[]{:S(2)}) collective-permute-start(bf16[4,2,48,384]{3,2,1,0:T(8,128)(2,1)S(1)} %all-to-all-done.1.refs_0_), channel_id=1, source_target_pairs={{0,2},{2,0},{4,6},{6,4},{1,3},{3,1},{5,7},{7,5},{8,10},{10,8},{12,... | collective-permute-start | bytes 884744 | tf_op jit(solution)/shard_map/ppermute | solution.py:714
  45.5 2.0 %collective-permute-start.13 = (bf16[4,2,48,384]{3,2,1,0:T(8,128)(2,1)S(1)}, bf16[4,2,48,384]{3,2,1,0:T(8,128)(2,1)S(1)}, u32[]{:S(2)}, u32[]{:S(2)}) collective-permute-start(bf16[4,2,48,384]{3,2,1,0:T(8,128)(2,1)S(1)} %collective-permute-done.3.refs_2_), channel_id=1, source_target_pairs={{0,1},{1,0},{2,3},{3,2},{4,5},{5,4},{6,7},{7,6},{8,9},{9,8},{10,11... | collective-permute-start | bytes 884744 | tf_op jit(solution)/shard_map/ppermute | solution.py:705
  67.2 2.8 %collective-permute-start.15 = (bf16[4,4,2,48,384]{4,3,2,1,0:T(8,128)(2,1)S(1)}, bf16[4,4,2,48,384]{4,3,2,1,0:T(8,128)(2,1)S(1)}, u32[]{:S(2)}, u32[]{:S(2)}) collective-permute-start(bf16[4,4,2,48,384]{4,3,2,1,0:T(8,128)(2,1)S(1)} %get-tuple-element.80), channel_id=1, source_target_pairs={{0,1},{1,0},{2,3},{3,2},{4,5},{5,4},{6,7},{7,6},{8,9},{9,8},{10,11... | collective-permute-start | bytes 3538952 | tf_op jit(solution)/shard_map/ppermute | solution.py:705
  70.3 19.8 %collective-permute-start.16 = (bf16[4,2,48,384]{3,2,1,0:T(8,128)(2,1)S(1)}, bf16[4,2,48,384]{3,2,1,0:T(8,128)(2,1)S(1)}, u32[]{:S(2)}, u32[]{:S(2)}) collective-permute-start(bf16[4,2,48,384]{3,2,1,0:T(8,128)(2,1)S(1)} %get-tuple-element.96), channel_id=1, source_target_pairs={{0,2},{2,0},{4,6},{6,4},{1,3},{3,1},{5,7},{7,5},{8,10},{10,8},{12,... | collective-permute-start | bytes 884744 | tf_op jit(solution)/shard_map/ppermute | solution.py:714
  71.4 18.7 %collective-permute-start.17 = (bf16[4,2,48,384]{3,2,1,0:T(8,128)(2,1)S(1)}, bf16[4,2,48,384]{3,2,1,0:T(8,128)(2,1)S(1)}, u32[]{:S(2)}, u32[]{:S(2)}) collective-permute-start(bf16[4,2,48,384]{3,2,1,0:T(8,128)(2,1)S(1)} %get-tuple-element.97), channel_id=1, source_target_pairs={{0,4},{2,6},{4,0},{6,2},{1,5},{3,7},{5,1},{7,3},{8,12},{10,14},{12... | collective-permute-start | bytes 884744 | tf_op jit(solution)/shard_map/ppermute | solution.py:714
  72.7 17.4 %collective-permute-start.18 = (bf16[4,2,48,384]{3,2,1,0:T(8,128)(2,1)S(1)}, bf16[4,2,48,384]{3,2,1,0:T(8,128)(2,1)S(1)}, u32[]{:S(2)}, u32[]{:S(2)}) collective-permute-start(bf16[4,2,48,384]{3,2,1,0:T(8,128)(2,1)S(1)} %get-tuple-element.98), channel_id=1, source_target_pairs={{0,6},{2,4},{4,2},{6,0},{1,7},{3,5},{5,3},{7,1},{8,14},{10,12},{12... | collective-permute-start | bytes 884744 | tf_op jit(solution)/shard_map/ppermute | solution.py:714
  90.1 5.8 %collective-permute-start.19 = (bf16[17,48,384]{2,1,0:T(8,128)(2,1)S(1)}, bf16[17,48,384]{2,1,0:T(8,128)(2,1)S(1)}, u32[]{:S(2)}, u32[]{:S(2)}) collective-permute-start(bf16[17,48,384]{2,1,0:T(8,128)(2,1)S(1)} %get-tuple-element.100), channel_id=1, source_target_pairs={{0,1},{1,0},{2,3},{3,2},{4,5},{5,4},{6,7},{7,6},{8,9},{9,8},{10,11... | collective-permute-start | bytes 1880072 | tf_op jit(solution)/shard_map/ppermute | solution.py:705
  91.1 16.4 %all-to-all-start.2 = ((bf16[4,2,48,384]{3,2,1,0:T(8,128)(2,1)}), bf16[4,2,48,384]{3,2,1,0:T(8,128)(2,1)S(1)}, u32[]{:S(2)}, u32[]{:S(2)}) async-start(bf16[4,2,48,384]{3,2,1,0:T(8,128)(2,1)} %sum_late.1), calls=%async_computation.2 | async-start | bytes 589824 | tf_op jit(solution)/shard_map/all_to_all | solution.py:709
  96.7 6.9 %collective-permute-start.20 = (bf16[200,384]{1,0:T(8,128)(2,1)S(1)}, bf16[200,384]{1,0:T(8,128)(2,1)S(1)}, u32[]{:S(2)}, u32[]{:S(2)}) collective-permute-start(bf16[200,384]{1,0:T(8,128)(2,1)S(1)} %get-tuple-element.103), channel_id=1, source_target_pairs={{0,2},{2,0},{4,6},{6,4},{1,3},{3,1},{5,7},{7,5},{8,10},{10,8},{12,... | collective-permute-start | bytes 460808 | tf_op jit(solution)/shard_map/ppermute | solution.py:714
  97.7 9.1 %collective-permute-start.21 = (bf16[200,384]{1,0:T(8,128)(2,1)S(1)}, bf16[200,384]{1,0:T(8,128)(2,1)S(1)}, u32[]{:S(2)}, u32[]{:S(2)}) collective-permute-start(bf16[200,384]{1,0:T(8,128)(2,1)S(1)} %get-tuple-element.104), channel_id=1, source_target_pairs={{0,4},{2,6},{4,0},{6,2},{1,5},{3,7},{5,1},{7,3},{8,12},{10,14},{12... | collective-permute-start | bytes 460808 | tf_op jit(solution)/shard_map/ppermute | solution.py:714
  99.1 7.7 %collective-permute-start.22 = (bf16[200,384]{1,0:T(8,128)(2,1)S(1)}, bf16[200,384]{1,0:T(8,128)(2,1)S(1)}, u32[]{:S(2)}, u32[]{:S(2)}) collective-permute-start(bf16[200,384]{1,0:T(8,128)(2,1)S(1)} %get-tuple-element.105), channel_id=1, source_target_pairs={{0,6},{2,4},{4,2},{6,0},{1,7},{3,5},{5,3},{7,1},{8,14},{10,12},{12... | collective-permute-start | bytes 460808 | tf_op jit(solution)/shard_map/ppermute | solution.py:714
  107.5 15.0 %all-to-all-start.3 = ((bf16[4,56,384]{2,1,0:T(8,128)(2,1)}), bf16[4,56,384]{2,1,0:T(8,128)(2,1)S(1)}, u32[]{:S(2)}, u32[]{:S(2)}) async-start(bf16[4,56,384]{2,1,0:T(8,128)(2,1)} %join.1), calls=%async_computation.3 | async-start | bytes 344064 | tf_op jit(solution)/shard_map/all_to_all | solution.py:709
  (3 other events, 10.2 us)

commit v9 on v8

--- a/solution.py
+++ b/solution.py
@@ -296,23 +296,19 @@
 def attn_backward_kernel(
     place_ref, own_mask_ref, other_mask_ref, x_ref, grad_ref, prob_ref, qkv_ref, out_ref,
     norm_ref, later_norm_ref, wqkv_ref, wo_ref,
-    in_grad_ref, own_grad_ref, sent_grad_ref, norm_grad_ref,
-    dqkv_ref, wqkv_grad_ref, wo_grad_ref,
+    dqkv_ref, own_grad_ref, sent_grad_ref, norm_grad_ref,
+    cross_ref, column_ref, wo_grad_ref,
 ):
     step = pl.program_id(0)
 
     @pl.when(step == 0)
     def _():
-        wqkv_grad_ref[...] = jnp.zeros_like(wqkv_grad_ref)
+        cross_ref[...] = jnp.zeros_like(cross_ref)
+        column_ref[...] = jnp.zeros_like(column_ref)
         wo_grad_ref[...] = jnp.zeros_like(wo_grad_ref)
-        norm_grad_ref[0:2, :] = jnp.zeros((2, D), F32)
-        norm_grad_ref[2:4, :] = later_norm_ref[...]
-
-    x = x_ref[...].astype(F32)
-    normed, inverse_std = normalize(x)
-    rows = (normed * norm_ref[0:1, :] + norm_ref[1:2, :]).astype(BF)
-    grad = grad_ref[...]
-    low_grad = grad.astype(BF)
+
+    normed, _ = normalize(x_ref[...].astype(F32))
+    low_grad = grad_ref[...].astype(BF)
     head_out = out_ref[...]
     wo_grad_ref[...] += tn(head_out, low_grad)
     whole_grad = nt(low_grad, wo_ref[...]).astype(BF)
@@ -354,20 +350,29 @@
         dqkv_ref[here, key_lanes] = jnp.transpose(key_grad).astype(BF)
         dqkv_ref[here, value_lanes] = jnp.transpose(value_grad).astype(BF)
     dqkv = dqkv_ref[...]
-    wqkv_grad_ref[...] += tn(rows, dqkv)
-    back = nt(dqkv, wqkv_ref[...])
-    grad_in, norm_part = norm_backward(back, normed, inverse_std, norm_ref[0:1, :])
-    norm_grad_ref[0:2, :] += norm_part
-    in_grad_ref[...] = grad + grad_in
+    cross_ref[...] += tn(normed.astype(BF), dqkv)
+    column_ref[...] += jnp.sum(dqkv.astype(F32), axis=0, keepdims=True)
 
     @pl.when(step == pl.num_programs(0) - 1)
     def _():
+        wqkv = wqkv_ref[...]
+        products = wqkv.astype(F32) * cross_ref[...]
+        gain_grad = jnp.sum(products, axis=1, keepdims=True)
+        gain_grad = jnp.transpose(jnp.broadcast_to(gain_grad, (D, 128)))
+        columns = column_ref[...]
+        shift_grad = nt(jnp.concatenate(split(jnp.broadcast_to(columns, (8, 3 * D)))), wqkv)
+        norm_grad_ref[0:1, :] = gain_grad[0:1]
+        norm_grad_ref[1:2, :] = shift_grad[0:1] + shift_grad[8:9]
+        norm_grad_ref[2:4, :] = later_norm_ref[...]
+        gain = jnp.transpose(jnp.broadcast_to(norm_ref[0:1, :], (128, D)))[:, :1]
+        shift = jnp.transpose(jnp.broadcast_to(norm_ref[1:2, :], (128, D)))[:, :1]
+        cross_ref[...] = cross_ref[...] * gain + shift * columns
         for side, slab_grads in enumerate((own_grad_ref, sent_grad_ref)):
             for slab in range(12):
                 pieces = []
                 for unit in (2 * slab, 2 * slab + 1):
                     row, part = divmod(unit, 3)
-                    piece = wqkv_grad_ref[48 * row : 48 * row + 48, D * part : D * part + D]
+                    piece = cross_ref[48 * row : 48 * row + 48, D * part : D * part + D]
                     piece = piece[:, HALF * side : HALF * side + HALF]
                     pieces.append(piece * 0.125 if part == 0 else piece)
                 slab_grads[slab_at(slab)] = jnp.concatenate(pieces, axis=1).astype(BF)
@@ -402,31 +407,62 @@
             pl.BlockSpec((D, D), lambda i: (0, 0)),
         ],
         out_specs=[
-            tile,
+            pl.BlockSpec((TILE, 3 * D), lambda i: (i, 0)),
             pl.BlockSpec((SLABS, 48, D), lambda i: (0, 0, 0)),
             pl.BlockSpec((SLABS + 1, 48, D), lambda i: (0, 0, 0)),
             pl.BlockSpec((4, D), lambda i: (0, 0)),
         ],
         out_shape=[
-            jax.ShapeDtypeStruct((rows, D), F32),
+            pltpu.HBM((rows, 3 * D), BF),
             jax.ShapeDtypeStruct((SLABS, 48, D), BF),
             jax.ShapeDtypeStruct((SLABS + 1, 48, D), BF),
             jax.ShapeDtypeStruct((4, D), F32),
         ],
         scratch_shapes=[
-            pltpu.VMEM((TILE, 3 * D), BF),
             pltpu.VMEM((D, 3 * D), F32),
+            pltpu.VMEM((1, 3 * D), F32),
             pltpu.VMEM((D, D), F32),
         ],
         compiler_params=pltpu.CompilerParams(vmem_limit_bytes=VMEM_LIMIT),
         cost_estimate=pl.CostEstimate(
-            flops=rows * D * (16 * D + 32 * S), bytes_accessed=20 << 20, transcendentals=0
+            flops=rows * D * (10 * D + 32 * S), bytes_accessed=20 << 20, transcendentals=0
         ),
         name="attn_backward",
     )(
         place, own_mask, other_mask,
         *map(in_hbm, (tokens, grad, prob, qkv, out, norm_params, later_norms, wqkv, wo)),
     )
+
+
+def input_grad_kernel(x_ref, grad_ref, dqkv_ref, norm_ref, wqkv_ref, out_ref):
+    normed, inverse_std = normalize(x_ref[...].astype(F32))
+    back = nt(dqkv_ref[...], wqkv_ref[...]) * norm_ref[0:1, :]
+    mean_first = jnp.mean(back, axis=-1, keepdims=True)
+    mean_second = jnp.mean(back * normed, axis=-1, keepdims=True)
+    out_ref[...] = grad_ref[...] + inverse_std * (back - mean_first - normed * mean_second)
+
+
+def input_gradient(tokens, grad, dqkv, norm_params, wqkv):
+    rows = tokens.shape[0]
+    tile = pl.BlockSpec((TILE, D), lambda i: (i, 0))
+    return pl.pallas_call(
+        input_grad_kernel,
+        grid=(rows // TILE,),
+        in_specs=[
+            tile,
+            tile,
+            pl.BlockSpec((TILE, 3 * D), lambda i: (i, 0)),
+            pl.BlockSpec((4, D), lambda i: (0, 0)),
+            pl.BlockSpec((D, 3 * D), lambda i: (0, 0)),
+        ],
+        out_specs=tile,
+        out_shape=jax.ShapeDtypeStruct((rows, D), F32),
+        compiler_params=pltpu.CompilerParams(vmem_limit_bytes=VMEM_LIMIT),
+        cost_estimate=pl.CostEstimate(
+            flops=rows * D * 6 * D, bytes_accessed=10 << 20, transcendentals=0
+        ),
+        name="input_gradient",
+    )(*map(in_hbm, (tokens, grad, dqkv, norm_params, wqkv)))
 
 
 def pack_kernel(weight_ref, early_ref, late_ref):
@@ -698,7 +734,7 @@
             flops=groups * (3 << 30), bytes_accessed=4 << 20, transcendentals=0
         ),
         name="shampoo",
-    )(received, in_hbm(weights), in_hbm(stat_left), in_hbm(stat_right), *map(in_hbm, norms), *earlier)
+    )(received, weights, stat_left, stat_right, *norms, *earlier)
 
 
 def swap_heads(values):
@@ -718,14 +754,14 @@
     return [values] + [across(values, apart) for apart in range(1, INNER)]
 
 
-def gather_slabs(weights, other_mask):
+def gather_slabs(weights, small):
     early, late = pack(weights, OUTER)
     early = to_all(early, "outer")
     early, late = lax.optimization_barrier((early, late))
     late = to_all(late, "outer")
     early = from_all(early)
-    early[-1], late, other_mask = lax.optimization_barrier((early[-1], late, other_mask))
-    return early, from_all(late), other_mask
+    early[-1], late, small = lax.optimization_barrier((early[-1], late, small))
+    return early, from_all(late), small
 
 
 def gather_blocks(local):
@@ -762,7 +798,7 @@
     inner = lax.axis_index("inner") if whole_slabs else 0
     place = jnp.concatenate([jnp.stack([lax.axis_index("head"), inner]), token_counts])
     if whole_slabs:
-        early, late, other_mask = gather_slabs(weights, other_mask)
+        early, late, (other_mask, place) = gather_slabs(weights, (other_mask, place))
     else:
         local = weights.astype(BF)
         early = jnp.split(gather_blocks(local[:1]), INNER)
@@ -783,7 +819,7 @@
         late_grads = list(add_late(own_late, late_received))
         late_grads, middle_grad = lax.optimization_barrier((late_grads, middle_grad))
         late_grads[1:] = [across(late_grads[apart], apart) for apart in range(1, INNER)]
-    input_grad, own_early, sent_early, norm_sums = attn_backward(
+    dqkv, own_early, sent_early, norm_sums = attn_backward(
         place, *masks, tokens, middle_grad, prob, qkv, out, norm_params, norm_two, wqkv, wo
     )
     if whole_slabs:
@@ -795,12 +831,16 @@
     if whole_slabs:
         late_grads = to_all(sum_late(late_grads), "outer")
         early_grads = list(combine(place, own_early, early_received, norm_sums))
+        early_grads, dqkv = lax.optimization_barrier((early_grads, dqkv))
         early_grads[1:] = [across(early_grads[apart], apart) for apart in range(1, INNER)]
+        input_grad = input_gradient(tokens, middle_grad, dqkv, norm_params, wqkv)
+        early_grads, input_grad = lax.optimization_barrier((early_grads, input_grad))
         joined, late_grads = lax.optimization_barrier((join(early_grads), late_grads))
         joined = to_all(joined, "outer")[:, None]
         results = shampoo(late_grads, *state, 1)
         results = shampoo(joined, *state, 0, results, (norm_params, norm_state))
     else:
+        input_grad = input_gradient(tokens, middle_grad, dqkv, norm_params, wqkv)
         early_slabs = own_early.astype(F32) + early_received[:SLABS].astype(F32)
         late_slabs = own_late.astype(F32) + late_received.astype(F32)
         late_slabs = late_slabs.reshape(SLABS, 2, edge, D)

time: 131 us -> 127 us (0.969)
  waiting for transfers between devices: 17 us -> 9.68 us
  Pallas kernels: 69.2 us -> 72 us
    ppermute x12, waiting for transfers between devices: 12.4 us -> 5.06 us  [across(): return lax.ppermute(values, 'inner', pairs)]
    pallas_call x0 -> x1, Pallas kernels: none -> 7.03 us  [input_gradient(): pl.pallas_call(input_grad_kernel, grid=(rows // TILE,), in_specs=[tile, t...]
    pallas_call x2, Pallas kernels: 17.9 us -> 15.5 us  [shampoo(): pl.pallas_call(lambda *refs: shampoo_kernel(scale, bool(norms), *refs), g...]
    pallas_call x1, Pallas kernels: 16.3 us -> 14.5 us  [attn_backward(): pl.pallas_call(attn_backward_kernel, grid=(rows // TILE,), in_specs=[smem...]
  transfers between devices with their start and end apart: 26 -> 26, of which waited for: 10 -> 8; matrix products, arithmetic and copies ran while one was open for 1% -> 1% of each run, Pallas kernels for 31% -> 35%
where the time goes in v9:
time: 127 us; the launch traced here: 126 us
  Pallas kernels  72 us (57%)
  starting transfers between devices  29.3 us (23%)
  blocking collectives  12.8 us (10%)
  waiting for transfers between devices  9.68 us (8%)
    pallas_call x1, Pallas kernels, mlp(): pl.pallas_call(mlp_kernel, grid=(rows // TILE,), in_specs=[pl.BlockSpec(m...  19.2 us
    pallas_call x2, Pallas kernels, shampoo(): pl.pallas_call(lambda *refs: shampoo_kernel(scale, bool(norms), *refs), g...  15.5 us
    pallas_call x1, Pallas kernels, attn_backward(): pl.pallas_call(attn_backward_kernel, grid=(rows // TILE,), in_specs=[smem...  14.5 us
    ppermute x12, starting transfers between devices, across(): return lax.ppermute(values, 'inner', pairs)  14.1 us
    all_to_all x3, starting transfers between devices, to_all(): return lax.all_to_all(values, axis, 0, 0)  13.4 us
    all_to_all x1, blocking collectives, to_all(): return lax.all_to_all(values, axis, 0, 0)  12.8 us
    pallas_call x1, Pallas kernels, attn_forward(): pl.pallas_call(attn_forward_kernel, grid=(rows // TILE,), in_specs=[smem]...  11.3 us
    pallas_call x1, Pallas kernels, input_gradient(): pl.pallas_call(input_grad_kernel, grid=(rows // TILE,), in_specs=[tile, t...  7.03 us
  transfers between devices with their start and end apart: 26, of which 8 were waited for; matrix products, arithmetic and copies ran while one was open for 1% of the time, Pallas kernels for 35%

profile of v9, /device:TPU:0, one launch (start us, length us, event | category | flops | bytes accessed | tf_op | source)
XLA Modules:
  0.0 126.1 jit_solution(16092586165123514821)
XLA Ops:
  0.6 1.9 %pack.1 = (bf16[4,48,384]{2,1,0:T(8,128)(2,1)S(1)}, bf16[4,2,48,384]{3,2,1,0:T(8,128)(2,1)}) custom-call(f32[3,8,48,48]{3,2,1,0:T(8,128)} %bitcast.10), custom_call_target="tpu_custom_call" | custom-call | tf_op jit(solution)/shard_map/pack/pallas_call | solution.py:482
  2.6 12.8 %all_to_all.20.refs_0_ = bf16[4,48,384]{2,1,0:T(8,128)(2,1)S(1)} all-to-all(bf16[4,48,384]{2,1,0:T(8,128)(2,1)S(1)} %get-tuple-element.77), channel_id=1, replica_groups=mesh['outer'=4,'inner'=4,'head'=2] {'outer'}, dimensions={0} | all-to-all | bytes 294912 | tf_op jit(solution)/shard_map/all_to_all | solution.py:745
  15.3 3.5 %all-to-all-start.1 = ((bf16[4,2,48,384]{3,2,1,0:T(8,128)(2,1)}), bf16[4,2,48,384]{3,2,1,0:T(8,128)(2,1)S(1)}, u32[]{:S(2)}, u32[]{:S(2)}) async-start(bf16[4,2,48,384]{3,2,1,0:T(8,128)(2,1)} %get-tuple-element.80), calls=%async_computation.1 | async-start | bytes 589824 | tf_op jit(solution)/shard_map/all_to_all | solution.py:745
  18.8 1.6 %collective-permute-start.6 = (bf16[4,48,384]{2,1,0:T(8,128)(2,1)S(1)}, bf16[4,48,384]{2,1,0:T(8,128)(2,1)S(1)}, u32[]{:S(2)}, u32[]{:S(2)}) collective-permute-start(bf16[4,48,384]{2,1,0:T(8,128)(2,1)S(1)} %all_to_all.20.refs_0_), channel_id=1, source_target_pairs={{0,4},{2,6},{4,0},{6,2},{1,5},{3,7},{5,1},{7,3},{8,12},{10,14},{12... | collective-permute-start | bytes 442376 | tf_op jit(solution)/shard_map/ppermute | solution.py:750
  20.4 1.5 %collective-permute-start.5 = (bf16[4,48,384]{2,1,0:T(8,128)(2,1)S(1)}, bf16[4,48,384]{2,1,0:T(8,128)(2,1)S(1)}, u32[]{:S(2)}, u32[]{:S(2)}) collective-permute-start(bf16[4,48,384]{2,1,0:T(8,128)(2,1)S(1)} %all_to_all.20.refs_0_), channel_id=1, source_target_pairs={{0,2},{2,0},{4,6},{6,4},{1,3},{3,1},{5,7},{7,5},{8,10},{10,8},{12,... | collective-permute-start | bytes 442376 | tf_op jit(solution)/shard_map/ppermute | solution.py:750
  26.0 2.1 %collective-permute-done.refs_3_ = bf16[4,48,384]{2,1,0:T(8,128)(2,1)S(1)} collective-permute-done((bf16[4,48,384]{2,1,0:T(8,128)(2,1)S(1)}, bf16[4,48,384]{2,1,0:T(8,128)(2,1)S(1)}, u32[]{:S(2)}, u32[]{:S(2)}) %collective-permute-start) | collective-permute-done | bytes 147488 | tf_op jit(solution)/shard_map/ppermute | solution.py:750
  28.6 1.9 %collective-permute-start.4 = (bf16[4,2,48,384]{3,2,1,0:T(8,128)(2,1)S(1)}, bf16[4,2,48,384]{3,2,1,0:T(8,128)(2,1)S(1)}, u32[]{:S(2)}, u32[]{:S(2)}) collective-permute-start(bf16[4,2,48,384]{3,2,1,0:T(8,128)(2,1)S(1)} %all-to-all-done.1.refs_0_), channel_id=1, source_target_pairs={{0,6},{2,4},{4,2},{6,0},{1,7},{3,5},{5,3},{7,1},{8,14},{10,12},{12... | collective-permute-start | bytes 884744 | tf_op jit(solution)/shard_map/ppermute | solution.py:750
  31.0 1.1 collective-permute-start.2
  32.1 11.3 %attn_forward.1 = (bf16[6,3,512,256]{3,2,1,0:T(8,128)(2,1)}, bf16[1536,1152]{1,0:T(8,128)(2,1)}, bf16[1536,384]{1,0:T(8,128)(2,1)}, f32[1536,384]{1,0:T(8,128)},...) custom-call(s32[14]{0:T(128)S(1)} %pad_add_fusion.place_ref, s32[12,3]{1,0:T(8,128)S(1)} %copy.22.own_mask_ref, ...), custom_call_target="tpu_custom_call" | custom-call | flops 4227858432 | bytes 16777216 | tf_op jit(solution)/shard_map/attn_forward/pallas_call | solution.py:168
  43.3 1.4 %collective-permute-done.3.refs_2_ = bf16[4,2,48,384]{3,2,1,0:T(8,128)(2,1)S(1)} collective-permute-done((bf16[4,2,48,384]{3,2,1,0:T(8,128)(2,1)S(1)}, bf16[4,2,48,384]{3,2,1,0:T(8,128)(2,1)S(1)}, u32[]{:S(2)}, u32[]{:S(2)}) %collective-permute-start.3) | collective-permute-done | bytes 294944 | tf_op jit(solution)/shard_map/ppermute | solution.py:750
  45.2 1.1 collective-permute-done.12.refs_5_
  47.1 19.2 %mlp.1 = (f32[1536,384]{1,0:T(8,128)}, f32[1536,384]{1,0:T(8,128)}, f32[2,384]{1,0:T(2,128)S(1)}, bf16[4,4,2,48,384]{4,3,2,1,0:T(8,128)(2,1)S(1)}, bf16[4,4,2,48,384]{4,3,2,1,0:T(8,128)(2,1)S(1)}) custom-call(s32[14]{0:T(128)S(1)} %pad_add_fusion.place_ref, f32[1536,384]{1,0:T(8,128)} %get-tuple-element.86.middle_ref, bf16[1536,384]{1,0:T(8,128)(2,1)} %cot_ref.1, ...), custom_call_target="tpu_custom_call" | custom-call | flops 10871635968 | bytes 20971520 | tf_op jit(solution)/shard_map/mlp/pallas_call | solution.py:265
  66.5 2.7 %collective-permute-done.15.received_ref = bf16[4,4,2,48,384]{4,3,2,1,0:T(8,128)(2,1)S(1)} collective-permute-done((bf16[4,4,2,48,384]{4,3,2,1,0:T(8,128)(2,1)S(1)}, bf16[4,4,2,48,384]{4,3,2,1,0:T(8,128)(2,1)S(1)}, u32[]{:S(2)}, u32[]{:S(2)}) %collective-permute-start.15) | collective-permute-done | bytes 1179680 | tf_op jit(solution)/shard_map/ppermute | solution.py:741
  69.5 1.1 collective-permute-start.16
  70.6 1.3 %collective-permute-start.17 = (bf16[4,2,48,384]{3,2,1,0:T(8,128)(2,1)S(1)}, bf16[4,2,48,384]{3,2,1,0:T(8,128)(2,1)S(1)}, u32[]{:S(2)}, u32[]{:S(2)}) collective-permute-start(bf16[4,2,48,384]{3,2,1,0:T(8,128)(2,1)S(1)} %get-tuple-element.108), channel_id=1, source_target_pairs={{0,4},{2,6},{4,0},{6,2},{1,5},{3,7},{5,1},{7,3},{8,12},{10,14},{12... | collective-permute-start | bytes 884744 | tf_op jit(solution)/shard_map/ppermute | solution.py:750
  71.9 1.2 collective-permute-start.18
  73.1 14.5 %attn_backward.1 = (bf16[1536,1152]{1,0:T(8,128)(2,1)}, bf16[16,48,384]{2,1,0:T(8,128)(2,1)S(1)}, bf16[17,48,384]{2,1,0:T(8,128)(2,1)S(1)}, f32[4,384]{1,0:T(4,128)S(1)}) custom-call(s32[14]{0:T(128)S(1)} %pad_add_fusion.place_ref, s32[12,3]{1,0:T(8,128)S(1)} %copy.22.own_mask_ref, s32[12,3]{1,0:T(8,128)S(1)} %collective-permute-done.1.other_mask_ref, ...), custom_call_target="tpu_custom_call" | custom-call | flops 7096762368 | bytes 20971520 | tf_op jit(solution)/shard_map/attn_backward/pallas_call | solution.py:392
  88.5 4.9 %all-to-all-start.2 = ((bf16[4,2,48,384]{3,2,1,0:T(8,128)(2,1)}), bf16[4,2,48,384]{3,2,1,0:T(8,128)(2,1)S(1)}, u32[]{:S(2)}, u32[]{:S(2)}) async-start(bf16[4,2,48,384]{3,2,1,0:T(8,128)(2,1)} %sum_late.1), calls=%async_computation.2 | async-start | bytes 589824 | tf_op jit(solution)/shard_map/all_to_all | solution.py:745
  95.1 1.4 %collective-permute-start.21 = (bf16[200,384]{1,0:T(8,128)(2,1)S(1)}, bf16[200,384]{1,0:T(8,128)(2,1)S(1)}, u32[]{:S(2)}, u32[]{:S(2)}) collective-permute-start(bf16[200,384]{1,0:T(8,128)(2,1)S(1)} %get-tuple-element.120), channel_id=1, source_target_pairs={{0,4},{2,6},{4,0},{6,2},{1,5},{3,7},{5,1},{7,3},{8,12},{10,14},{12... | collective-permute-start | bytes 460808 | tf_op jit(solution)/shard_map/ppermute | solution.py:750
  96.5 1.2 collective-permute-start.22
  97.7 7.0 %input_gradient.1 = f32[1536,384]{1,0:T(8,128)} custom-call(bf16[1536,384]{1,0:T(8,128)(2,1)} %x_ref.5, f32[1536,384]{1,0:T(8,128)} %get-tuple-element.98.grad_ref, bf16[1536,1152]{1,0:T(8,128)(2,1)} %get-tuple-element.122.dqkv_ref, f32[4,384]{1,0:T(4,128)} %refs_4_.1, bf16[384,1152]{1,0:T(8,128)(2,1)} %get-tuple-element.103.wqkv_ref), custom_call_target="tpu_custom_call" | custom-call | flops 1358954496 | bytes 10485760 | tf_op jit(solution)/shard_map/input_gradient/pallas_call | solution.py:448
  105.4 5.1 %all-to-all-start.3 = ((bf16[4,56,384]{2,1,0:T(8,128)(2,1)}), bf16[4,56,384]{2,1,0:T(8,128)(2,1)S(1)}, u32[]{:S(2)}, u32[]{:S(2)}) async-start(bf16[4,56,384]{2,1,0:T(8,128)(2,1)} %join.1), calls=%async_computation.3 | async-start | bytes 344064 | tf_op jit(solution)/shard_map/all_to_all | solution.py:745
  110.6 9.0 %shampoo.2 = (f32[3,8,48,48]{3,2,1,0:T(8,128)}, f32[3,8,48,48]{3,2,1,0:T(8,128)}, f32[3,8,48,48]{3,2,1,0:T(8,128)}, f32[3,8,48,48]{3,2,1,0:T(8,128)}) custom-call(bf16[4,2,48,384]{3,2,1,0:T(8,128)(2,1)S(1)} %all-to-all-done.2.refs_0_, f32[3,8,48,48]{3,2,1,0:T(8,128)S(1)} %bitcast.11, f32[3,8,48,48]{3,2,1,0:T(8,128)S(1)} %bitcast.14, ...), custom_call_target="tpu_custom_call" | custom-call | flops 6442450944 | bytes 4194304 | tf_op jit(solution)/shard_map/shampoo/pallas_call | solution.py:716
  119.6 6.6 %shampoo.3 = (f32[3,8,48,48]{3,2,1,0:T(8,128)}, f32[3,8,48,48]{3,2,1,0:T(8,128)}, f32[3,8,48,48]{3,2,1,0:T(8,128)}, f32[3,8,48,48]{3,2,1,0:T(8,128)}, f32[4,384]...) custom-call(bf16[4,1,56,384]{3,2,1,0:T(8,128)(2,1)S(1)} %bitcast.13,, ...), custom_call_target="tpu_custom_call", output_to_operand_aliasing={{0}: (6, {}), {1}: (7, {}), {2}: (8, {}), {3}: (9, {})} | custom-call | flops 3221225472 | bytes 4194304 | tf_op jit(solution)/shard_map/shampoo/pallas_call | solution.py:716
  (54 shorter events, 10.4 us)
Async XLA Ops:
  15.3 12.7 %all-to-all-start.1 = ((bf16[4,2,48,384]{3,2,1,0:T(8,128)(2,1)}), bf16[4,2,48,384]{3,2,1,0:T(8,128)(2,1)S(1)}, u32[]{:S(2)}, u32[]{:S(2)}) async-start(bf16[4,2,48,384]{3,2,1,0:T(8,128)(2,1)} %get-tuple-element.80), calls=%async_computation.1 | async-start | bytes 589824 | tf_op jit(solution)/shard_map/all_to_all | solution.py:745
  18.8 6.4 %collective-permute-start.6 = (bf16[4,48,384]{2,1,0:T(8,128)(2,1)S(1)}, bf16[4,48,384]{2,1,0:T(8,128)(2,1)S(1)}, u32[]{:S(2)}, u32[]{:S(2)}) collective-permute-start(bf16[4,48,384]{2,1,0:T(8,128)(2,1)S(1)} %all_to_all.20.refs_0_), channel_id=1, source_target_pairs={{0,4},{2,6},{4,0},{6,2},{1,5},{3,7},{5,1},{7,3},{8,12},{10,14},{12... | collective-permute-start | bytes 442376 | tf_op jit(solution)/shard_map/ppermute | solution.py:750
  20.4 5.6 %collective-permute-start.5 = (bf16[4,48,384]{2,1,0:T(8,128)(2,1)S(1)}, bf16[4,48,384]{2,1,0:T(8,128)(2,1)S(1)}, u32[]{:S(2)}, u32[]{:S(2)}) collective-permute-start(bf16[4,48,384]{2,1,0:T(8,128)(2,1)S(1)} %all_to_all.20.refs_0_), channel_id=1, source_target_pairs={{0,2},{2,0},{4,6},{6,4},{1,3},{3,1},{5,7},{7,5},{8,10},{10,8},{12,... | collective-permute-start | bytes 442376 | tf_op jit(solution)/shard_map/ppermute | solution.py:750
  21.9 6.2 %collective-permute-start = (bf16[4,48,384]{2,1,0:T(8,128)(2,1)S(1)}, bf16[4,48,384]{2,1,0:T(8,128)(2,1)S(1)}, u32[]{:S(2)}, u32[]{:S(2)}) collective-permute-start(bf16[4,48,384]{2,1,0:T(8,128)(2,1)S(1)} %all_to_all.20.refs_0_), channel_id=1, source_target_pairs={{0,6},{2,4},{4,2},{6,0},{1,7},{3,5},{5,3},{7,1},{8,14},{10,12},{12... | collective-permute-start | bytes 442376 | tf_op jit(solution)/shard_map/ppermute | solution.py:750
  23.1 2.9 %collective-permute-start.1 = (s32[12,3]{1,0:T(8,128)S(1)}, s32[12,3]{1,0:T(8,128)S(1)}, u32[]{:S(2)}, u32[]{:S(2)}) collective-permute-start(s32[12,3]{1,0:T(8,128)S(1)} %copy.22.own_mask_ref), channel_id=1, source_target_pairs={{0,1},{1,0},{2,3},{3,2},{4,5},{5,4},{6,7},{7,6},{8,9},{9,8},{10,11... | collective-permute-start | bytes 440 | tf_op jit(solution)/shard_map/ppermute | solution.py:741
  23.9 4.7 %collective-permute-start.7 = (bf16[4,48,384]{2,1,0:T(8,128)(2,1)S(1)}, bf16[4,48,384]{2,1,0:T(8,128)(2,1)S(1)}, u32[]{:S(2)}, u32[]{:S(2)}) collective-permute-start(bf16[4,48,384]{2,1,0:T(8,128)(2,1)S(1)} %all_to_all.20.refs_0_), channel_id=1, source_target_pairs={{0,1},{1,0},{2,3},{3,2},{4,5},{5,4},{6,7},{7,6},{8,9},{9,8},{10,11... | collective-permute-start | bytes 442376 | tf_op jit(solution)/shard_map/ppermute | solution.py:741
  25.2 5.3 %collective-permute-start.9 = (bf16[4,48,384]{2,1,0:T(8,128)(2,1)S(1)}, bf16[4,48,384]{2,1,0:T(8,128)(2,1)S(1)}, u32[]{:S(2)}, u32[]{:S(2)}) collective-permute-start(bf16[4,48,384]{2,1,0:T(8,128)(2,1)S(1)} %collective-permute-done.6.refs_2_), channel_id=1, source_target_pairs={{0,1},{1,0},{2,3},{3,2},{4,5},{5,4},{6,7},{7,6},{8,9},{9,8},{10,11... | collective-permute-start | bytes 442376 | tf_op jit(solution)/shard_map/ppermute | solution.py:741
  26.0 5.0 %collective-permute-start.8 = (bf16[4,48,384]{2,1,0:T(8,128)(2,1)S(1)}, bf16[4,48,384]{2,1,0:T(8,128)(2,1)S(1)}, u32[]{:S(2)}, u32[]{:S(2)}) collective-permute-start(bf16[4,48,384]{2,1,0:T(8,128)(2,1)S(1)} %collective-permute-done.5.refs_1_), channel_id=1, source_target_pairs={{0,1},{1,0},{2,3},{3,2},{4,5},{5,4},{6,7},{7,6},{8,9},{9,8},{10,11... | collective-permute-start | bytes 442376 | tf_op jit(solution)/shard_map/ppermute | solution.py:741
  28.1 4.0 %collective-permute-start.10 = (bf16[4,48,384]{2,1,0:T(8,128)(2,1)S(1)}, bf16[4,48,384]{2,1,0:T(8,128)(2,1)S(1)}, u32[]{:S(2)}, u32[]{:S(2)}) collective-permute-start(bf16[4,48,384]{2,1,0:T(8,128)(2,1)S(1)} %collective-permute-done.refs_3_), channel_id=1, source_target_pairs={{0,1},{1,0},{2,3},{3,2},{4,5},{5,4},{6,7},{7,6},{8,9},{9,8},{10,11... | collective-permute-start | bytes 442376 | tf_op jit(solution)/shard_map/ppermute | solution.py:741
  28.1 17.2 %collective-permute-start.11 = (bf16[4,2,48,384]{3,2,1,0:T(8,128)(2,1)S(1)}, bf16[4,2,48,384]{3,2,1,0:T(8,128)(2,1)S(1)}, u32[]{:S(2)}, u32[]{:S(2)}) collective-permute-start(bf16[4,2,48,384]{3,2,1,0:T(8,128)(2,1)S(1)} %all-to-all-done.1.refs_0_), channel_id=1, source_target_pairs={{0,1},{1,0},{2,3},{3,2},{4,5},{5,4},{6,7},{7,6},{8,9},{9,8},{10,11... | collective-permute-start | bytes 884744 | tf_op jit(solution)/shard_map/ppermute | solution.py:741
  28.6 14.8 %collective-permute-start.4 = (bf16[4,2,48,384]{3,2,1,0:T(8,128)(2,1)S(1)}, bf16[4,2,48,384]{3,2,1,0:T(8,128)(2,1)S(1)}, u32[]{:S(2)}, u32[]{:S(2)}) collective-permute-start(bf16[4,2,48,384]{3,2,1,0:T(8,128)(2,1)S(1)} %all-to-all-done.1.refs_0_), channel_id=1, source_target_pairs={{0,6},{2,4},{4,2},{6,0},{1,7},{3,5},{5,3},{7,1},{8,14},{10,12},{12... | collective-permute-start | bytes 884744 | tf_op jit(solution)/shard_map/ppermute | solution.py:750
  30.5 14.2 %collective-permute-start.3 = (bf16[4,2,48,384]{3,2,1,0:T(8,128)(2,1)S(1)}, bf16[4,2,48,384]{3,2,1,0:T(8,128)(2,1)S(1)}, u32[]{:S(2)}, u32[]{:S(2)}) collective-permute-start(bf16[4,2,48,384]{3,2,1,0:T(8,128)(2,1)S(1)} %all-to-all-done.1.refs_0_), channel_id=1, source_target_pairs={{0,4},{2,6},{4,0},{6,2},{1,5},{3,7},{5,1},{7,3},{8,12},{10,14},{12... | collective-permute-start | bytes 884744 | tf_op jit(solution)/shard_map/ppermute | solution.py:750
  31.0 13.7 %collective-permute-start.2 = (bf16[4,2,48,384]{3,2,1,0:T(8,128)(2,1)S(1)}, bf16[4,2,48,384]{3,2,1,0:T(8,128)(2,1)S(1)}, u32[]{:S(2)}, u32[]{:S(2)}) collective-permute-start(bf16[4,2,48,384]{3,2,1,0:T(8,128)(2,1)S(1)} %all-to-all-done.1.refs_0_), channel_id=1, source_target_pairs={{0,2},{2,0},{4,6},{6,4},{1,3},{3,1},{5,7},{7,5},{8,10},{10,8},{12,... | collective-permute-start | bytes 884744 | tf_op jit(solution)/shard_map/ppermute | solution.py:750
  44.7 2.0 %collective-permute-start.13 = (bf16[4,2,48,384]{3,2,1,0:T(8,128)(2,1)S(1)}, bf16[4,2,48,384]{3,2,1,0:T(8,128)(2,1)S(1)}, u32[]{:S(2)}, u32[]{:S(2)}) collective-permute-start(bf16[4,2,48,384]{3,2,1,0:T(8,128)(2,1)S(1)} %collective-permute-done.3.refs_2_), channel_id=1, source_target_pairs={{0,1},{1,0},{2,3},{3,2},{4,5},{5,4},{6,7},{7,6},{8,9},{9,8},{10,11... | collective-permute-start | bytes 884744 | tf_op jit(solution)/shard_map/ppermute | solution.py:741
  66.4 2.8 %collective-permute-start.15 = (bf16[4,4,2,48,384]{4,3,2,1,0:T(8,128)(2,1)S(1)}, bf16[4,4,2,48,384]{4,3,2,1,0:T(8,128)(2,1)S(1)}, u32[]{:S(2)}, u32[]{:S(2)}) collective-permute-start(bf16[4,4,2,48,384]{4,3,2,1,0:T(8,128)(2,1)S(1)} %get-tuple-element.92), channel_id=1, source_target_pairs={{0,1},{1,0},{2,3},{3,2},{4,5},{5,4},{6,7},{7,6},{8,9},{9,8},{10,11... | collective-permute-start | bytes 3538952 | tf_op jit(solution)/shard_map/ppermute | solution.py:741
  69.5 18.0 %collective-permute-start.16 = (bf16[4,2,48,384]{3,2,1,0:T(8,128)(2,1)S(1)}, bf16[4,2,48,384]{3,2,1,0:T(8,128)(2,1)S(1)}, u32[]{:S(2)}, u32[]{:S(2)}) collective-permute-start(bf16[4,2,48,384]{3,2,1,0:T(8,128)(2,1)S(1)} %get-tuple-element.107), channel_id=1, source_target_pairs={{0,2},{2,0},{4,6},{6,4},{1,3},{3,1},{5,7},{7,5},{8,10},{10,8},{12,... | collective-permute-start | bytes 884744 | tf_op jit(solution)/shard_map/ppermute | solution.py:750
  70.6 16.9 %collective-permute-start.17 = (bf16[4,2,48,384]{3,2,1,0:T(8,128)(2,1)S(1)}, bf16[4,2,48,384]{3,2,1,0:T(8,128)(2,1)S(1)}, u32[]{:S(2)}, u32[]{:S(2)}) collective-permute-start(bf16[4,2,48,384]{3,2,1,0:T(8,128)(2,1)S(1)} %get-tuple-element.108), channel_id=1, source_target_pairs={{0,4},{2,6},{4,0},{6,2},{1,5},{3,7},{5,1},{7,3},{8,12},{10,14},{12... | collective-permute-start | bytes 884744 | tf_op jit(solution)/shard_map/ppermute | solution.py:750
  71.9 15.6 %collective-permute-start.18 = (bf16[4,2,48,384]{3,2,1,0:T(8,128)(2,1)S(1)}, bf16[4,2,48,384]{3,2,1,0:T(8,128)(2,1)S(1)}, u32[]{:S(2)}, u32[]{:S(2)}) collective-permute-start(bf16[4,2,48,384]{3,2,1,0:T(8,128)(2,1)S(1)} %get-tuple-element.109), channel_id=1, source_target_pairs={{0,6},{2,4},{4,2},{6,0},{1,7},{3,5},{5,3},{7,1},{8,14},{10,12},{12... | collective-permute-start | bytes 884744 | tf_op jit(solution)/shard_map/ppermute | solution.py:750
  87.5 5.8 %collective-permute-start.19 = (bf16[17,48,384]{2,1,0:T(8,128)(2,1)S(1)}, bf16[17,48,384]{2,1,0:T(8,128)(2,1)S(1)}, u32[]{:S(2)}, u32[]{:S(2)}) collective-permute-start(bf16[17,48,384]{2,1,0:T(8,128)(2,1)S(1)} %get-tuple-element.111), channel_id=1, source_target_pairs={{0,1},{1,0},{2,3},{3,2},{4,5},{5,4},{6,7},{7,6},{8,9},{9,8},{10,11... | collective-permute-start | bytes 1880072 | tf_op jit(solution)/shard_map/ppermute | solution.py:741
  88.5 16.9 %all-to-all-start.2 = ((bf16[4,2,48,384]{3,2,1,0:T(8,128)(2,1)}), bf16[4,2,48,384]{3,2,1,0:T(8,128)(2,1)S(1)}, u32[]{:S(2)}, u32[]{:S(2)}) async-start(bf16[4,2,48,384]{3,2,1,0:T(8,128)(2,1)} %sum_late.1), calls=%async_computation.2 | async-start | bytes 589824 | tf_op jit(solution)/shard_map/all_to_all | solution.py:745
  94.1 10.6 %collective-permute-start.20 = (bf16[200,384]{1,0:T(8,128)(2,1)S(1)}, bf16[200,384]{1,0:T(8,128)(2,1)S(1)}, u32[]{:S(2)}, u32[]{:S(2)}) collective-permute-start(bf16[200,384]{1,0:T(8,128)(2,1)S(1)} %get-tuple-element.119), channel_id=1, source_target_pairs={{0,2},{2,0},{4,6},{6,4},{1,3},{3,1},{5,7},{7,5},{8,10},{10,8},{12,... | collective-permute-start | bytes 460808 | tf_op jit(solution)/shard_map/ppermute | solution.py:750
  95.1 9.6 %collective-permute-start.21 = (bf16[200,384]{1,0:T(8,128)(2,1)S(1)}, bf16[200,384]{1,0:T(8,128)(2,1)S(1)}, u32[]{:S(2)}, u32[]{:S(2)}) collective-permute-start(bf16[200,384]{1,0:T(8,128)(2,1)S(1)} %get-tuple-element.120), channel_id=1, source_target_pairs={{0,4},{2,6},{4,0},{6,2},{1,5},{3,7},{5,1},{7,3},{8,12},{10,14},{12... | collective-permute-start | bytes 460808 | tf_op jit(solution)/shard_map/ppermute | solution.py:750
  96.5 8.2 %collective-permute-start.22 = (bf16[200,384]{1,0:T(8,128)(2,1)S(1)}, bf16[200,384]{1,0:T(8,128)(2,1)S(1)}, u32[]{:S(2)}, u32[]{:S(2)}) collective-permute-start(bf16[200,384]{1,0:T(8,128)(2,1)S(1)} %get-tuple-element.121), channel_id=1, source_target_pairs={{0,6},{2,4},{4,2},{6,0},{1,7},{3,5},{5,3},{7,1},{8,14},{10,12},{12... | collective-permute-start | bytes 460808 | tf_op jit(solution)/shard_map/ppermute | solution.py:750
  105.4 14.1 %all-to-all-start.3 = ((bf16[4,56,384]{2,1,0:T(8,128)(2,1)}), bf16[4,56,384]{2,1,0:T(8,128)(2,1)S(1)}, u32[]{:S(2)}, u32[]{:S(2)}) async-start(bf16[4,56,384]{2,1,0:T(8,128)(2,1)} %join.1), calls=%async_computation.3 | async-start | bytes 344064 | tf_op jit(solution)/shard_map/all_to_all | solution.py:745
  (8 other events, 77.6 us)

commit v10 on v9

--- a/solution.py
+++ b/solution.py
@@ -19,6 +19,7 @@
 INNER = 4
 OUTER = SLABS // INNER
 TILE = 512
+INPUT_TILE = 768
 IMAGES = TILE // S
 NORM_ROWS = 8
 PACK = 2
@@ -197,7 +198,8 @@
 def mlp_kernel(place_ref, middle_ref, cot_ref, norm_ref, *refs):
     slab_refs, refs = refs[: 2 * INNER], refs[2 * INNER :]
     out_ref, grad_ref, norm_grad_ref, *refs = refs
-    own_ref, sent_ref, up_ref, down_ref, up_grad_ref, down_grad_ref = refs
+    own_refs, sent_refs, refs = refs[:2], refs[2:4], refs[4:]
+    up_ref, down_ref, up_grad_ref, down_grad_ref = refs
     step = pl.program_id(0)
     half = MLP // 2
 
@@ -249,17 +251,18 @@
         for apart in range(INNER):
             for outer in range(OUTER):
                 row, lane, down_row = places(apart, outer)
-                for side, ref in enumerate((own_ref, sent_ref)):
+                for side, halves in enumerate((own_refs, sent_refs)):
+                    ref = halves[apart // 2]
                     up = up_grad_ref[side, pl.ds(row, 48), pl.ds(lane, D)]
                     down = down_grad_ref[side, pl.ds(down_row, 48), :]
-                    ref[apart, outer, 0] = up.astype(BF)
-                    ref[apart, outer, 1] = down.astype(BF)
+                    ref[apart % 2, outer, 0] = up.astype(BF)
+                    ref[apart % 2, outer, 1] = down.astype(BF)
 
 
 def mlp(place, middle, cotangent, norm_params, slabs):
     rows = middle.shape[0]
     slab = pl.BlockSpec((OUTER, 2, 48, D), lambda i: (0, 0, 0, 0))
-    grads = (INNER, OUTER, 2, 48, D)
+    grads = (INNER // 2, OUTER, 2, 48, D)
     grad = pl.BlockSpec(grads, lambda i: (0, 0, 0, 0, 0))
     tile = pl.BlockSpec((TILE, D), lambda i: (i, 0))
     return pl.pallas_call(
@@ -272,12 +275,12 @@
             pl.BlockSpec((4, D), lambda i: (0, 0)),
             *[slab] * 2 * INNER,
         ],
-        out_specs=[tile, tile, pl.BlockSpec((2, D), lambda i: (0, 0)), grad, grad],
+        out_specs=[tile, tile, pl.BlockSpec((2, D), lambda i: (0, 0)), *[grad] * 4],
         out_shape=[
             jax.ShapeDtypeStruct((rows, D), F32),
             pltpu.HBM((rows, D), F32),
             jax.ShapeDtypeStruct((2, D), F32),
-            *[jax.ShapeDtypeStruct(grads, BF)] * 2,
+            *[jax.ShapeDtypeStruct(grads, BF)] * 4,
         ],
         scratch_shapes=[
             pltpu.VMEM((2, D, MLP // 2), BF),
@@ -444,14 +447,14 @@
 
 def input_gradient(tokens, grad, dqkv, norm_params, wqkv):
     rows = tokens.shape[0]
-    tile = pl.BlockSpec((TILE, D), lambda i: (i, 0))
+    tile = pl.BlockSpec((INPUT_TILE, D), lambda i: (i, 0))
     return pl.pallas_call(
         input_grad_kernel,
-        grid=(rows // TILE,),
+        grid=(rows // INPUT_TILE,),
         in_specs=[
             tile,
             tile,
-            pl.BlockSpec((TILE, 3 * D), lambda i: (i, 0)),
+            pl.BlockSpec((INPUT_TILE, 3 * D), lambda i: (i, 0)),
             pl.BlockSpec((4, D), lambda i: (0, 0)),
             pl.BlockSpec((D, 3 * D), lambda i: (0, 0)),
         ],
@@ -465,26 +468,29 @@
     )(*map(in_hbm, (tokens, grad, dqkv, norm_params, wqkv)))
 
 
-def pack_kernel(weight_ref, early_ref, late_ref):
+def pack_kernel(weight_ref, out_ref):
     groups, count, _, _ = weight_ref.shape
     for group in range(groups):
         blocks = [weight_ref[group, block] for block in range(count)]
         slab = jnp.concatenate(blocks, axis=1).astype(BF)
-        for copy in range(early_ref.shape[0]):
-            if group == 0:
-                early_ref[copy] = slab
-            else:
-                late_ref[copy, group - 1] = slab
-
-
-def pack(weights, number):
-    groups, count, edge, _ = weights.shape
+        for copy in range(OUTER):
+            out_ref[copy, group] = slab
+
+
+def pack(weights, first, groups):
+    _, count, edge, _ = weights.shape
+    shape = (OUTER, groups, edge, count * edge)
     return pl.pallas_call(
         pack_kernel,
-        out_shape=[
-            jax.ShapeDtypeStruct((number, edge, count * edge), BF),
-            jax.ShapeDtypeStruct((number, groups - 1, edge, count * edge), BF),
-        ],
+        grid=(1,),
+        in_specs=[
+            pl.BlockSpec(
+                (pl.Element(groups), pl.Element(count), pl.Element(edge), pl.Element(edge)),
+                lambda i: (first, 0, 0, 0),
+            )
+        ],
+        out_specs=pl.BlockSpec(shape, lambda i: (0, 0, 0, 0)),
+        out_shape=jax.ShapeDtypeStruct(shape, BF),
         compiler_params=pltpu.CompilerParams(vmem_limit_bytes=SMALL_VMEM),
         name="pack",
     )(in_hbm(weights))
@@ -755,12 +761,11 @@
 
 
 def gather_slabs(weights, small):
-    early, late = pack(weights, OUTER)
-    early = to_all(early, "outer")
-    early, late = lax.optimization_barrier((early, late))
+    early = to_all(pack(weights, 0, 1), "outer")[:, 0]
+    early, late = lax.optimization_barrier((early, pack(weights, 1, 2)))
     late = to_all(late, "outer")
     early = from_all(early)
-    early[-1], late, small = lax.optimization_barrier((early[-1], late, small))
+    early[1], late, small = lax.optimization_barrier((early[1], late, small))
     return early, from_all(late), small
 
 
@@ -811,14 +816,14 @@
     )
     late[1:], middle = lax.optimization_barrier((late[1:], middle))
     late += [swap_heads(piece) for piece in late]
-    block_out, middle_grad, norm_two, own_late, sent_late = mlp(
-        place, middle, cotangent, norm_params, late
-    )
-    late_received = swap_heads(sent_late)
+    block_out, middle_grad, norm_two, *late_sums = mlp(place, middle, cotangent, norm_params, late)
+    own_late, late_received = late_sums[:2], [swap_heads(sent) for sent in late_sums[2:]]
     if whole_slabs:
-        late_grads = list(add_late(own_late, late_received))
-        late_grads, middle_grad = lax.optimization_barrier((late_grads, middle_grad))
-        late_grads[1:] = [across(late_grads[apart], apart) for apart in range(1, INNER)]
+        far = add_late(own_late[1], late_received[1])
+        near = add_late(own_late[0], late_received[0])
+        far = [across(far[number], 2 + number) for number in range(2)]
+        near, middle_grad = lax.optimization_barrier((list(near), middle_grad))
+        late_grads = [near[0], across(near[1], 1), *far]
     dqkv, own_early, sent_early, norm_sums = attn_backward(
         place, *masks, tokens, middle_grad, prob, qkv, out, norm_params, norm_two, wqkv, wo
     )
@@ -842,7 +847,7 @@
     else:
         input_grad = input_gradient(tokens, middle_grad, dqkv, norm_params, wqkv)
         early_slabs = own_early.astype(F32) + early_received[:SLABS].astype(F32)
-        late_slabs = own_late.astype(F32) + late_received.astype(F32)
+        late_slabs = jnp.concatenate(own_late).astype(F32) + jnp.concatenate(late_received)
         late_slabs = late_slabs.reshape(SLABS, 2, edge, D)
         slabs = jnp.concatenate([early_slabs[:, None], late_slabs], axis=1).astype(BF)
         owned = scatter_blocks(slabs, count, edge)

time: 127 us -> 125 us (0.984)
  blocking collectives: 12.8 us -> 0 us
  starting transfers between devices: 29.3 us -> 36.1 us
  waiting for transfers between devices: 9.68 us -> 14 us
    all_to_all x1 -> x0, blocking collectives: 12.8 us -> none  [to_all(): return lax.all_to_all(values, axis, 0, 0)]
    all_to_all x3 -> x4, starting transfers between devices: 13.4 us -> 19.7 us  [to_all(): return lax.all_to_all(values, axis, 0, 0)]
    all_to_all x3 -> x4, waiting for transfers between devices: 0.01 us -> 4.49 us  [to_all(): return lax.all_to_all(values, axis, 0, 0)]
    ppermute x11 -> x12, waiting for transfers between devices: 4.61 us -> 3.41 us  [swap_heads(): return lax.ppermute(values, 'head', [(0, 1), (1, 0)])]
    pallas_call x2 -> x3, Pallas kernels: 8.95 us -> 10.1 us  [the longest x1 6.62 us: input_gradient(): pl.pallas_call(input_grad_kernel, grid=(rows // INPUT_TILE,), in_specs=[t...]
  transfers between devices with their start and end apart: 26 -> 28, of which waited for: 8 -> 10; matrix products, arithmetic and copies ran while one was open for 1% -> 0% of each run, Pallas kernels for 35% -> 37%
where the time goes in v10:
time: 125 us; the launch traced here: 124 us
  Pallas kernels  73.2 us (59%)
  starting transfers between devices  36.1 us (29%)
  waiting for transfers between devices  14 us (11%)
    all_to_all x4, starting transfers between devices, to_all(): return lax.all_to_all(values, axis, 0, 0)  19.7 us
    pallas_call x1, Pallas kernels, mlp(): pl.pallas_call(mlp_kernel, grid=(rows // TILE,), in_specs=[pl.BlockSpec(m...  19.2 us
    pallas_call x2, Pallas kernels, shampoo(): pl.pallas_call(lambda *refs: shampoo_kernel(scale, bool(norms), *refs), g...  15.5 us
    pallas_call x1, Pallas kernels, attn_backward(): pl.pallas_call(attn_backward_kernel, grid=(rows // TILE,), in_specs=[smem...  14.5 us
    ppermute x12, starting transfers between devices, across(): return lax.ppermute(values, 'inner', pairs)  14.2 us
    pallas_call x1, Pallas kernels, attn_forward(): pl.pallas_call(attn_forward_kernel, grid=(rows // TILE,), in_specs=[smem]...  11.3 us
    pallas_call x1, Pallas kernels, input_gradient(): pl.pallas_call(input_grad_kernel, grid=(rows // INPUT_TILE,), in_specs=[t...  6.62 us
    ppermute x12, waiting for transfers between devices, across(): return lax.ppermute(values, 'inner', pairs)  6.14 us
  transfers between devices with their start and end apart: 28, of which 10 were waited for; matrix products, arithmetic and copies ran while one was open for 0% of the time, Pallas kernels for 37%

profile of v10, /device:TPU:0, one launch (start us, length us, event | category | flops | bytes accessed | tf_op | source)
XLA Modules:
  0.0 124.4 jit_solution(17603310034583219494)
XLA Ops:
  0.7 1.7 %pack.2 = bf16[4,1,48,384]{3,2,1,0:T(8,128)(2,1)} custom-call(f32[3,8,48,48]{3,2,1,0:T(8,128)} %bitcast.11), custom_call_target="tpu_custom_call" | custom-call | tf_op jit(solution)/shard_map/pack/pallas_call | solution.py:483
  2.4 6.3 %all-to-all-start = ((bf16[4,1,48,384]{3,2,1,0:T(8,128)(2,1)}), bf16[4,1,48,384]{3,2,1,0:T(8,128)(2,1)S(1)}, u32[]{:S(2)}, u32[]{:S(2)}) async-start(bf16[4,1,48,384]{3,2,1,0:T(8,128)(2,1)} %pack.2), calls=%async_computation | async-start | bytes 294912 | tf_op jit(solution)/shard_map/all_to_all | solution.py:751
  8.7 1.8 %pack.3 = bf16[4,2,48,384]{3,2,1,0:T(8,128)(2,1)} custom-call(f32[3,8,48,48]{3,2,1,0:T(8,128)} %bitcast.12), custom_call_target="tpu_custom_call" | custom-call | tf_op jit(solution)/shard_map/pack/pallas_call | solution.py:483
  10.5 4.4 %all-to-all-done = bf16[4,1,48,384]{3,2,1,0:T(8,128)(2,1)S(1)} async-done(((bf16[4,1,48,384]{3,2,1,0:T(8,128)(2,1)}), bf16[4,1,48,384]{3,2,1,0:T(8,128)(2,1)S(1)}, u32[]{:S(2)}, u32[]{:S(2)}) %all-to-all-start) | async-done | bytes 147488 | tf_op jit(solution)/shard_map/all_to_all | solution.py:751
  14.9 3.5 %all-to-all-start.1 = ((bf16[4,2,48,384]{3,2,1,0:T(8,128)(2,1)}), bf16[4,2,48,384]{3,2,1,0:T(8,128)(2,1)S(1)}, u32[]{:S(2)}, u32[]{:S(2)}) async-start(bf16[4,2,48,384]{3,2,1,0:T(8,128)(2,1)} %pack.3), calls=%async_computation.1 | async-start | bytes 589824 | tf_op jit(solution)/shard_map/all_to_all | solution.py:751
  18.4 2.5 %collective-permute-start.6 = (bf16[4,48,384]{2,1,0:T(8,128)(2,1)S(1)}, bf16[4,48,384]{2,1,0:T(8,128)(2,1)S(1)}, u32[]{:S(2)}, u32[]{:S(2)}) collective-permute-start(bf16[4,48,384]{2,1,0:T(8,128)(2,1)S(1)} %bitcast.16), channel_id=1, source_target_pairs={{0,6},{2,4},{4,2},{6,0},{1,7},{3,5},{5,3},{7,1},{8,14},{10,12},{12... | collective-permute-start | bytes 442376 | tf_op jit(solution)/shard_map/ppermute | solution.py:756
  22.6 3.4 %collective-permute-done.6.refs_3_ = bf16[4,48,384]{2,1,0:T(8,128)(2,1)S(1)} collective-permute-done((bf16[4,48,384]{2,1,0:T(8,128)(2,1)S(1)}, bf16[4,48,384]{2,1,0:T(8,128)(2,1)S(1)}, u32[]{:S(2)}, u32[]{:S(2)}) %collective-permute-start.6) | collective-permute-done | bytes 147488 | tf_op jit(solution)/shard_map/ppermute | solution.py:756
  27.5 2.4 %collective-permute-start.4 = (bf16[4,2,48,384]{3,2,1,0:T(8,128)(2,1)S(1)}, bf16[4,2,48,384]{3,2,1,0:T(8,128)(2,1)S(1)}, u32[]{:S(2)}, u32[]{:S(2)}) collective-permute-start(bf16[4,2,48,384]{3,2,1,0:T(8,128)(2,1)S(1)} %all-to-all-done.1.refs_0_), channel_id=1, source_target_pairs={{0,6},{2,4},{4,2},{6,0},{1,7},{3,5},{5,3},{7,1},{8,14},{10,12},{12... | collective-permute-start | bytes 884744 | tf_op jit(solution)/shard_map/ppermute | solution.py:756
  31.0 11.3 %attn_forward.1 = (bf16[6,3,512,256]{3,2,1,0:T(8,128)(2,1)}, bf16[1536,1152]{1,0:T(8,128)(2,1)}, bf16[1536,384]{1,0:T(8,128)(2,1)}, f32[1536,384]{1,0:T(8,128)},...) custom-call(s32[14]{0:T(128)S(1)} %pad_add_fusion.place_ref, s32[12,3]{1,0:T(8,128)S(1)} %copy.26.own_mask_ref, ...), custom_call_target="tpu_custom_call" | custom-call | flops 4227858432 | bytes 16777216 | tf_op jit(solution)/shard_map/attn_forward/pallas_call | solution.py:169
  42.3 1.8 %collective-permute-done.3.refs_2_ = bf16[4,2,48,384]{3,2,1,0:T(8,128)(2,1)S(1)} collective-permute-done((bf16[4,2,48,384]{3,2,1,0:T(8,128)(2,1)S(1)}, bf16[4,2,48,384]{3,2,1,0:T(8,128)(2,1)S(1)}, u32[]{:S(2)}, u32[]{:S(2)}) %collective-permute-start.3) | collective-permute-done | bytes 294944 | tf_op jit(solution)/shard_map/ppermute | solution.py:756
  44.6 1.1 collective-permute-done.12.refs_5_
  46.5 19.2 %mlp.1 = (f32[1536,384]{1,0:T(8,128)}, f32[1536,384]{1,0:T(8,128)}, f32[2,384]{1,0:T(2,128)S(1)}, bf16[2,4,2,48,384]{4,3,2,1,0:T(8,128)(2,1)S(1)}, bf16[2,4,2,48...) custom-call(s32[14]{0:T(128)S(1)} %pad_add_fusion.place_ref, ...), custom_call_target="tpu_custom_call" | custom-call | flops 10871635968 | bytes 20971520 | tf_op jit(solution)/shard_map/mlp/pallas_call | solution.py:268
  66.2 1.5 %collective-permute-done.15.received_ref = bf16[2,4,2,48,384]{4,3,2,1,0:T(8,128)(2,1)S(1)} collective-permute-done((bf16[2,4,2,48,384]{4,3,2,1,0:T(8,128)(2,1)S(1)}, bf16[2,4,2,48,384]{4,3,2,1,0:T(8,128)(2,1)S(1)}, u32[]{:S(2)}, u32[]{:S(2)}) %collective-permute-start.15) | collective-permute-done | bytes 589856 | tf_op jit(solution)/shard_map/ppermute | solution.py:747
  67.9 1.3 %collective-permute-start.16 = (bf16[4,2,48,384]{3,2,1,0:T(8,128)(2,1)S(1)}, bf16[4,2,48,384]{3,2,1,0:T(8,128)(2,1)S(1)}, u32[]{:S(2)}, u32[]{:S(2)}) collective-permute-start(bf16[4,2,48,384]{3,2,1,0:T(8,128)(2,1)S(1)} %get-tuple-element.101), channel_id=1, source_target_pairs={{0,2},{2,0},{4,6},{6,4},{1,3},{3,1},{5,7},{7,5},{8,10},{10,8},{12,... | collective-permute-start | bytes 884744 | tf_op jit(solution)/shard_map/ppermute | solution.py:756
  69.3 1.2 collective-permute-start.18
  70.5 1.2 collective-permute-start.19
  71.7 14.5 %attn_backward.1 = (bf16[1536,1152]{1,0:T(8,128)(2,1)}, bf16[16,48,384]{2,1,0:T(8,128)(2,1)S(1)}, bf16[17,48,384]{2,1,0:T(8,128)(2,1)S(1)}, f32[4,384]{1,0:T(4,128)S(1)}) custom-call(s32[14]{0:T(128)S(1)} %pad_add_fusion.place_ref, s32[12,3]{1,0:T(8,128)S(1)} %copy.26.own_mask_ref, s32[12,3]{1,0:T(8,128)S(1)} %collective-permute-done.1.other_mask_ref, ...), custom_call_target="tpu_custom_call" | custom-call | flops 7096762368 | bytes 20971520 | tf_op jit(solution)/shard_map/attn_backward/pallas_call | solution.py:395
  87.1 4.9 %all-to-all-start.2 = ((bf16[4,2,48,384]{3,2,1,0:T(8,128)(2,1)}), bf16[4,2,48,384]{3,2,1,0:T(8,128)(2,1)S(1)}, u32[]{:S(2)}, u32[]{:S(2)}) async-start(bf16[4,2,48,384]{3,2,1,0:T(8,128)(2,1)} %sum_late.1), calls=%async_computation.2 | async-start | bytes 589824 | tf_op jit(solution)/shard_map/all_to_all | solution.py:751
  92.8 1.2 collective-permute-start.21
  94.8 1.6 %collective-permute-start.23 = (bf16[200,384]{1,0:T(8,128)(2,1)S(1)}, bf16[200,384]{1,0:T(8,128)(2,1)S(1)}, u32[]{:S(2)}, u32[]{:S(2)}) collective-permute-start(bf16[200,384]{1,0:T(8,128)(2,1)S(1)} %get-tuple-element.117), channel_id=1, source_target_pairs={{0,6},{2,4},{4,2},{6,0},{1,7},{3,5},{5,3},{7,1},{8,14},{10,12},{12... | collective-permute-start | bytes 460808 | tf_op jit(solution)/shard_map/ppermute | solution.py:756
  96.3 6.6 %input_gradient.1 = f32[1536,384]{1,0:T(8,128)} custom-call(bf16[1536,384]{1,0:T(8,128)(2,1)} %x_ref.5, f32[1536,384]{1,0:T(8,128)} %get-tuple-element.92.grad_ref, bf16[1536,1152]{1,0:T(8,128)(2,1)} %get-tuple-element.118.dqkv_ref, f32[4,384]{1,0:T(4,128)} %refs_4_.1, bf16[384,1152]{1,0:T(8,128)(2,1)} %get-tuple-element.97.wqkv_ref), custom_call_target="tpu_custom_call" | custom-call | flops 1358954496 | bytes 10485760 | tf_op jit(solution)/shard_map/input_gradient/pallas_call | solution.py:451
  103.8 5.0 %all-to-all-start.3 = ((bf16[4,56,384]{2,1,0:T(8,128)(2,1)}), bf16[4,56,384]{2,1,0:T(8,128)(2,1)S(1)}, u32[]{:S(2)}, u32[]{:S(2)}) async-start(bf16[4,56,384]{2,1,0:T(8,128)(2,1)} %join.1), calls=%async_computation.3 | async-start | bytes 344064 | tf_op jit(solution)/shard_map/all_to_all | solution.py:751
  108.9 9.0 %shampoo.2 = (f32[3,8,48,48]{3,2,1,0:T(8,128)}, f32[3,8,48,48]{3,2,1,0:T(8,128)}, f32[3,8,48,48]{3,2,1,0:T(8,128)}, f32[3,8,48,48]{3,2,1,0:T(8,128)}) custom-call(bf16[4,2,48,384]{3,2,1,0:T(8,128)(2,1)S(1)} %all-to-all-done.2.refs_0_, f32[3,8,48,48]{3,2,1,0:T(8,128)S(1)} %bitcast.13, f32[3,8,48,48]{3,2,1,0:T(8,128)S(1)} %bitcast.21, ...), custom_call_target="tpu_custom_call" | custom-call | flops 6442450944 | bytes 4194304 | tf_op jit(solution)/shard_map/shampoo/pallas_call | solution.py:722
  117.8 6.6 %shampoo.3 = (f32[3,8,48,48]{3,2,1,0:T(8,128)}, f32[3,8,48,48]{3,2,1,0:T(8,128)}, f32[3,8,48,48]{3,2,1,0:T(8,128)}, f32[3,8,48,48]{3,2,1,0:T(8,128)}, f32[4,384]...) custom-call(bf16[4,1,56,384]{3,2,1,0:T(8,128)(2,1)S(1)} %bitcast.15,, ...), custom_call_target="tpu_custom_call", output_to_operand_aliasing={{0}: (6, {}), {1}: (7, {}), {2}: (8, {}), {3}: (9, {})} | custom-call | flops 3221225472 | bytes 4194304 | tf_op jit(solution)/shard_map/shampoo/pallas_call | solution.py:722
  (63 shorter events, 9.9 us)
Async XLA Ops:
  2.4 12.6 %all-to-all-start = ((bf16[4,1,48,384]{3,2,1,0:T(8,128)(2,1)}), bf16[4,1,48,384]{3,2,1,0:T(8,128)(2,1)S(1)}, u32[]{:S(2)}, u32[]{:S(2)}) async-start(bf16[4,1,48,384]{3,2,1,0:T(8,128)(2,1)} %pack.2), calls=%async_computation | async-start | bytes 294912 | tf_op jit(solution)/shard_map/all_to_all | solution.py:751
  14.9 12.0 %all-to-all-start.1 = ((bf16[4,2,48,384]{3,2,1,0:T(8,128)(2,1)}), bf16[4,2,48,384]{3,2,1,0:T(8,128)(2,1)S(1)}, u32[]{:S(2)}, u32[]{:S(2)}) async-start(bf16[4,2,48,384]{3,2,1,0:T(8,128)(2,1)} %pack.3), calls=%async_computation.1 | async-start | bytes 589824 | tf_op jit(solution)/shard_map/all_to_all | solution.py:751
  18.4 7.6 %collective-permute-start.6 = (bf16[4,48,384]{2,1,0:T(8,128)(2,1)S(1)}, bf16[4,48,384]{2,1,0:T(8,128)(2,1)S(1)}, u32[]{:S(2)}, u32[]{:S(2)}) collective-permute-start(bf16[4,48,384]{2,1,0:T(8,128)(2,1)S(1)} %bitcast.16), channel_id=1, source_target_pairs={{0,6},{2,4},{4,2},{6,0},{1,7},{3,5},{5,3},{7,1},{8,14},{10,12},{12... | collective-permute-start | bytes 442376 | tf_op jit(solution)/shard_map/ppermute | solution.py:756
  20.9 6.0 %collective-permute-start.5 = (bf16[4,48,384]{2,1,0:T(8,128)(2,1)S(1)}, bf16[4,48,384]{2,1,0:T(8,128)(2,1)S(1)}, u32[]{:S(2)}, u32[]{:S(2)}) collective-permute-start(bf16[4,48,384]{2,1,0:T(8,128)(2,1)S(1)} %bitcast.17), channel_id=1, source_target_pairs={{0,4},{2,6},{4,0},{6,2},{1,5},{3,7},{5,1},{7,3},{8,12},{10,14},{12... | collective-permute-start | bytes 442376 | tf_op jit(solution)/shard_map/ppermute | solution.py:756
  21.4 5.5 %collective-permute-start = (bf16[4,48,384]{2,1,0:T(8,128)(2,1)S(1)}, bf16[4,48,384]{2,1,0:T(8,128)(2,1)S(1)}, u32[]{:S(2)}, u32[]{:S(2)}) collective-permute-start(bf16[4,48,384]{2,1,0:T(8,128)(2,1)S(1)} %bitcast.18), channel_id=1, source_target_pairs={{0,2},{2,0},{4,6},{6,4},{1,3},{3,1},{5,7},{7,5},{8,10},{10,8},{12,... | collective-permute-start | bytes 442376 | tf_op jit(solution)/shard_map/ppermute | solution.py:756
  22.0 4.8 %collective-permute-start.1 = (s32[12,3]{1,0:T(8,128)S(1)}, s32[12,3]{1,0:T(8,128)S(1)}, u32[]{:S(2)}, u32[]{:S(2)}) collective-permute-start(s32[12,3]{1,0:T(8,128)S(1)} %copy.26.own_mask_ref), channel_id=1, source_target_pairs={{0,1},{1,0},{2,3},{3,2},{4,5},{5,4},{6,7},{7,6},{8,9},{9,8},{10,11... | collective-permute-start | bytes 440 | tf_op jit(solution)/shard_map/ppermute | solution.py:747
  22.1 5.4 %collective-permute-start.7 = (bf16[4,48,384]{2,1,0:T(8,128)(2,1)S(1)}, bf16[4,48,384]{2,1,0:T(8,128)(2,1)S(1)}, u32[]{:S(2)}, u32[]{:S(2)}) collective-permute-start(bf16[4,48,384]{2,1,0:T(8,128)(2,1)S(1)} %bitcast.19), channel_id=1, source_target_pairs={{0,1},{1,0},{2,3},{3,2},{4,5},{5,4},{6,7},{7,6},{8,9},{9,8},{10,11... | collective-permute-start | bytes 442376 | tf_op jit(solution)/shard_map/ppermute | solution.py:747
  26.0 3.9 %collective-permute-start.10 = (bf16[4,48,384]{2,1,0:T(8,128)(2,1)S(1)}, bf16[4,48,384]{2,1,0:T(8,128)(2,1)S(1)}, u32[]{:S(2)}, u32[]{:S(2)}) collective-permute-start(bf16[4,48,384]{2,1,0:T(8,128)(2,1)S(1)} %collective-permute-done.6.refs_3_), channel_id=1, source_target_pairs={{0,1},{1,0},{2,3},{3,2},{4,5},{5,4},{6,7},{7,6},{8,9},{9,8},{10,11... | collective-permute-start | bytes 442376 | tf_op jit(solution)/shard_map/ppermute | solution.py:747
  26.8 3.6 %collective-permute-start.9 = (bf16[4,48,384]{2,1,0:T(8,128)(2,1)S(1)}, bf16[4,48,384]{2,1,0:T(8,128)(2,1)S(1)}, u32[]{:S(2)}, u32[]{:S(2)}) collective-permute-start(bf16[4,48,384]{2,1,0:T(8,128)(2,1)S(1)} %collective-permute-done.5.refs_2_), channel_id=1, source_target_pairs={{0,1},{1,0},{2,3},{3,2},{4,5},{5,4},{6,7},{7,6},{8,9},{9,8},{10,11... | collective-permute-start | bytes 442376 | tf_op jit(solution)/shard_map/ppermute | solution.py:747
  26.9 4.1 %collective-permute-start.8 = (bf16[4,48,384]{2,1,0:T(8,128)(2,1)S(1)}, bf16[4,48,384]{2,1,0:T(8,128)(2,1)S(1)}, u32[]{:S(2)}, u32[]{:S(2)}) collective-permute-start(bf16[4,48,384]{2,1,0:T(8,128)(2,1)S(1)} %collective-permute-done.refs_1_), channel_id=1, source_target_pairs={{0,1},{1,0},{2,3},{3,2},{4,5},{5,4},{6,7},{7,6},{8,9},{9,8},{10,11... | collective-permute-start | bytes 442376 | tf_op jit(solution)/shard_map/ppermute | solution.py:747
  27.4 17.2 %collective-permute-start.11 = (bf16[4,2,48,384]{3,2,1,0:T(8,128)(2,1)S(1)}, bf16[4,2,48,384]{3,2,1,0:T(8,128)(2,1)S(1)}, u32[]{:S(2)}, u32[]{:S(2)}) collective-permute-start(bf16[4,2,48,384]{3,2,1,0:T(8,128)(2,1)S(1)} %all-to-all-done.1.refs_0_), channel_id=1, source_target_pairs={{0,1},{1,0},{2,3},{3,2},{4,5},{5,4},{6,7},{7,6},{8,9},{9,8},{10,11... | collective-permute-start | bytes 884744 | tf_op jit(solution)/shard_map/ppermute | solution.py:747
  27.5 14.8 %collective-permute-start.4 = (bf16[4,2,48,384]{3,2,1,0:T(8,128)(2,1)S(1)}, bf16[4,2,48,384]{3,2,1,0:T(8,128)(2,1)S(1)}, u32[]{:S(2)}, u32[]{:S(2)}) collective-permute-start(bf16[4,2,48,384]{3,2,1,0:T(8,128)(2,1)S(1)} %all-to-all-done.1.refs_0_), channel_id=1, source_target_pairs={{0,6},{2,4},{4,2},{6,0},{1,7},{3,5},{5,3},{7,1},{8,14},{10,12},{12... | collective-permute-start | bytes 884744 | tf_op jit(solution)/shard_map/ppermute | solution.py:756
  29.9 14.2 %collective-permute-start.3 = (bf16[4,2,48,384]{3,2,1,0:T(8,128)(2,1)S(1)}, bf16[4,2,48,384]{3,2,1,0:T(8,128)(2,1)S(1)}, u32[]{:S(2)}, u32[]{:S(2)}) collective-permute-start(bf16[4,2,48,384]{3,2,1,0:T(8,128)(2,1)S(1)} %all-to-all-done.1.refs_0_), channel_id=1, source_target_pairs={{0,4},{2,6},{4,0},{6,2},{1,5},{3,7},{5,1},{7,3},{8,12},{10,14},{12... | collective-permute-start | bytes 884744 | tf_op jit(solution)/shard_map/ppermute | solution.py:756
  30.4 13.7 %collective-permute-start.2 = (bf16[4,2,48,384]{3,2,1,0:T(8,128)(2,1)S(1)}, bf16[4,2,48,384]{3,2,1,0:T(8,128)(2,1)S(1)}, u32[]{:S(2)}, u32[]{:S(2)}) collective-permute-start(bf16[4,2,48,384]{3,2,1,0:T(8,128)(2,1)S(1)} %all-to-all-done.1.refs_0_), channel_id=1, source_target_pairs={{0,2},{2,0},{4,6},{6,4},{1,3},{3,1},{5,7},{7,5},{8,10},{10,8},{12,... | collective-permute-start | bytes 884744 | tf_op jit(solution)/shard_map/ppermute | solution.py:756
  65.9 3.3 %collective-permute-start.17 = (bf16[2,4,2,48,384]{4,3,2,1,0:T(8,128)(2,1)S(1)}, bf16[2,4,2,48,384]{4,3,2,1,0:T(8,128)(2,1)S(1)}, u32[]{:S(2)}, u32[]{:S(2)}) collective-permute-start(bf16[2,4,2,48,384]{4,3,2,1,0:T(8,128)(2,1)S(1)} %get-tuple-element.103), channel_id=1, source_target_pairs={{0,1},{1,0},{2,3},{3,2},{4,5},{5,4},{6,7},{7,6},{8,9},{9,8},{10,11... | collective-permute-start | bytes 1769480 | tf_op jit(solution)/shard_map/ppermute | solution.py:747
  67.9 18.2 %collective-permute-start.16 = (bf16[4,2,48,384]{3,2,1,0:T(8,128)(2,1)S(1)}, bf16[4,2,48,384]{3,2,1,0:T(8,128)(2,1)S(1)}, u32[]{:S(2)}, u32[]{:S(2)}) collective-permute-start(bf16[4,2,48,384]{3,2,1,0:T(8,128)(2,1)S(1)} %get-tuple-element.101), channel_id=1, source_target_pairs={{0,2},{2,0},{4,6},{6,4},{1,3},{3,1},{5,7},{7,5},{8,10},{10,8},{12,... | collective-permute-start | bytes 884744 | tf_op jit(solution)/shard_map/ppermute | solution.py:756
  69.3 16.8 %collective-permute-start.18 = (bf16[4,2,48,384]{3,2,1,0:T(8,128)(2,1)S(1)}, bf16[4,2,48,384]{3,2,1,0:T(8,128)(2,1)S(1)}, u32[]{:S(2)}, u32[]{:S(2)}) collective-permute-start(bf16[4,2,48,384]{3,2,1,0:T(8,128)(2,1)S(1)} %get-tuple-element.104), channel_id=1, source_target_pairs={{0,4},{2,6},{4,0},{6,2},{1,5},{3,7},{5,1},{7,3},{8,12},{10,14},{12... | collective-permute-start | bytes 884744 | tf_op jit(solution)/shard_map/ppermute | solution.py:756
  70.5 15.6 %collective-permute-start.19 = (bf16[4,2,48,384]{3,2,1,0:T(8,128)(2,1)S(1)}, bf16[4,2,48,384]{3,2,1,0:T(8,128)(2,1)S(1)}, u32[]{:S(2)}, u32[]{:S(2)}) collective-permute-start(bf16[4,2,48,384]{3,2,1,0:T(8,128)(2,1)S(1)} %get-tuple-element.105), channel_id=1, source_target_pairs={{0,6},{2,4},{4,2},{6,0},{1,7},{3,5},{5,3},{7,1},{8,14},{10,12},{12... | collective-permute-start | bytes 884744 | tf_op jit(solution)/shard_map/ppermute | solution.py:756
  86.1 5.9 %collective-permute-start.20 = (bf16[17,48,384]{2,1,0:T(8,128)(2,1)S(1)}, bf16[17,48,384]{2,1,0:T(8,128)(2,1)S(1)}, u32[]{:S(2)}, u32[]{:S(2)}) collective-permute-start(bf16[17,48,384]{2,1,0:T(8,128)(2,1)S(1)} %get-tuple-element.107), channel_id=1, source_target_pairs={{0,1},{1,0},{2,3},{3,2},{4,5},{5,4},{6,7},{7,6},{8,9},{9,8},{10,11... | collective-permute-start | bytes 1880072 | tf_op jit(solution)/shard_map/ppermute | solution.py:747
  87.1 16.7 %all-to-all-start.2 = ((bf16[4,2,48,384]{3,2,1,0:T(8,128)(2,1)}), bf16[4,2,48,384]{3,2,1,0:T(8,128)(2,1)S(1)}, u32[]{:S(2)}, u32[]{:S(2)}) async-start(bf16[4,2,48,384]{3,2,1,0:T(8,128)(2,1)} %sum_late.1), calls=%async_computation.2 | async-start | bytes 589824 | tf_op jit(solution)/shard_map/all_to_all | solution.py:751
  92.8 10.2 %collective-permute-start.21 = (bf16[200,384]{1,0:T(8,128)(2,1)S(1)}, bf16[200,384]{1,0:T(8,128)(2,1)S(1)}, u32[]{:S(2)}, u32[]{:S(2)}) collective-permute-start(bf16[200,384]{1,0:T(8,128)(2,1)S(1)} %get-tuple-element.115), channel_id=1, source_target_pairs={{0,2},{2,0},{4,6},{6,4},{1,3},{3,1},{5,7},{7,5},{8,10},{10,8},{12,... | collective-permute-start | bytes 460808 | tf_op jit(solution)/shard_map/ppermute | solution.py:756
  94.0 9.1 %collective-permute-start.22 = (bf16[200,384]{1,0:T(8,128)(2,1)S(1)}, bf16[200,384]{1,0:T(8,128)(2,1)S(1)}, u32[]{:S(2)}, u32[]{:S(2)}) collective-permute-start(bf16[200,384]{1,0:T(8,128)(2,1)S(1)} %get-tuple-element.116), channel_id=1, source_target_pairs={{0,4},{2,6},{4,0},{6,2},{1,5},{3,7},{5,1},{7,3},{8,12},{10,14},{12... | collective-permute-start | bytes 460808 | tf_op jit(solution)/shard_map/ppermute | solution.py:756
  94.8 8.3 %collective-permute-start.23 = (bf16[200,384]{1,0:T(8,128)(2,1)S(1)}, bf16[200,384]{1,0:T(8,128)(2,1)S(1)}, u32[]{:S(2)}, u32[]{:S(2)}) collective-permute-start(bf16[200,384]{1,0:T(8,128)(2,1)S(1)} %get-tuple-element.117), channel_id=1, source_target_pairs={{0,6},{2,4},{4,2},{6,0},{1,7},{3,5},{5,3},{7,1},{8,14},{10,12},{12... | collective-permute-start | bytes 460808 | tf_op jit(solution)/shard_map/ppermute | solution.py:756
  103.8 14.0 %all-to-all-start.3 = ((bf16[4,56,384]{2,1,0:T(8,128)(2,1)}), bf16[4,56,384]{2,1,0:T(8,128)(2,1)S(1)}, u32[]{:S(2)}, u32[]{:S(2)}) async-start(bf16[4,56,384]{2,1,0:T(8,128)(2,1)} %join.1), calls=%async_computation.3 | async-start | bytes 344064 | tf_op jit(solution)/shard_map/all_to_all | solution.py:751
  (12 other events, 122.3 us)

commit v11 on v10

--- a/solution.py
+++ b/solution.py
@@ -65,6 +65,10 @@
     return grad_in, jnp.concatenate([gain_grad, shift_grad], axis=0)
 
 
+def grown(step, total, part):
+    return jnp.where(step == 0, part, total + part)
+
+
 def slab_at(owner):
     return (owner % INNER) * OUTER + owner // INNER
 
@@ -189,7 +193,7 @@
         scratch_shapes=[pltpu.VMEM((2, INNER, OUTER, 48, D), BF)],
         compiler_params=pltpu.CompilerParams(vmem_limit_bytes=VMEM_LIMIT),
         cost_estimate=pl.CostEstimate(
-            flops=rows * D * (8 * D + 16 * S), bytes_accessed=16 << 20, transcendentals=rows * 6 * S
+            flops=rows * D * (2 * D + 4 * S), bytes_accessed=4 << 20, transcendentals=0
         ),
         name="attn_forward",
     )(place, own_mask, other_mask, in_hbm(tokens), in_hbm(norm_params), *slabs)
@@ -212,9 +216,6 @@
 
     @pl.when(step == 0)
     def _():
-        up_grad_ref[...] = jnp.zeros_like(up_grad_ref)
-        down_grad_ref[...] = jnp.zeros_like(down_grad_ref)
-        norm_grad_ref[...] = jnp.zeros_like(norm_grad_ref)
         for number, ref in enumerate(slab_refs):
             side, apart = divmod(number, INNER)
             for outer in range(OUTER):
@@ -239,11 +240,11 @@
         total = total + nn(act, down)
         term = nt(pre_grad, up)
         back = term if back is None else back + term
-        down_grad_ref[side] += tn(act, cot)
-        up_grad_ref[side] += tn(rows, pre_grad)
+        down_grad_ref[side] = grown(step, down_grad_ref[side], tn(act, cot))
+        up_grad_ref[side] = grown(step, up_grad_ref[side], tn(rows, pre_grad))
     out_ref[...] = total
     grad_in, norm_part = norm_backward(back, normed, inverse_std, norm_ref[2:3, :])
-    norm_grad_ref[...] += norm_part
+    norm_grad_ref[...] = grown(step, norm_grad_ref[...], norm_part)
     grad_ref[...] = cot.astype(F32) + grad_in
 
     @pl.when(step == pl.num_programs(0) - 1)
@@ -304,16 +305,10 @@
 ):
     step = pl.program_id(0)
 
-    @pl.when(step == 0)
-    def _():
-        cross_ref[...] = jnp.zeros_like(cross_ref)
-        column_ref[...] = jnp.zeros_like(column_ref)
-        wo_grad_ref[...] = jnp.zeros_like(wo_grad_ref)
-
     normed, _ = normalize(x_ref[...].astype(F32))
     low_grad = grad_ref[...].astype(BF)
     head_out = out_ref[...]
-    wo_grad_ref[...] += tn(head_out, low_grad)
+    wo_grad_ref[...] = grown(step, wo_grad_ref[...], tn(head_out, low_grad))
     whole_grad = nt(low_grad, wo_ref[...]).astype(BF)
     first, second = lane_halves()
     first_wide, second_wide = first.astype(F32), second.astype(F32)
@@ -353,8 +348,9 @@
         dqkv_ref[here, key_lanes] = jnp.transpose(key_grad).astype(BF)
         dqkv_ref[here, value_lanes] = jnp.transpose(value_grad).astype(BF)
     dqkv = dqkv_ref[...]
-    cross_ref[...] += tn(normed.astype(BF), dqkv)
-    column_ref[...] += jnp.sum(dqkv.astype(F32), axis=0, keepdims=True)
+    cross_ref[...] = grown(step, cross_ref[...], tn(normed.astype(BF), dqkv))
+    columns = jnp.sum(dqkv.astype(F32), axis=0, keepdims=True)
+    column_ref[...] = grown(step, column_ref[...], columns)
 
     @pl.when(step == pl.num_programs(0) - 1)
     def _():
@@ -477,19 +473,11 @@
             out_ref[copy, group] = slab
 
 
-def pack(weights, first, groups):
-    _, count, edge, _ = weights.shape
+def pack(weights):
+    groups, count, edge, _ = weights.shape
     shape = (OUTER, groups, edge, count * edge)
     return pl.pallas_call(
         pack_kernel,
-        grid=(1,),
-        in_specs=[
-            pl.BlockSpec(
-                (pl.Element(groups), pl.Element(count), pl.Element(edge), pl.Element(edge)),
-                lambda i: (first, 0, 0, 0),
-            )
-        ],
-        out_specs=pl.BlockSpec(shape, lambda i: (0, 0, 0, 0)),
         out_shape=jax.ShapeDtypeStruct(shape, BF),
         compiler_params=pltpu.CompilerParams(vmem_limit_bytes=SMALL_VMEM),
         name="pack",
@@ -761,12 +749,13 @@
 
 
 def gather_slabs(weights, small):
-    early = to_all(pack(weights, 0, 1), "outer")[:, 0]
-    early, late = lax.optimization_barrier((early, pack(weights, 1, 2)))
-    late = to_all(late, "outer")
+    column = to_all(pack(weights), "outer")
+    early = column[:, 0]
+    column, early = lax.optimization_barrier((column, early))
     early = from_all(early)
-    early[1], late, small = lax.optimization_barrier((early[1], late, small))
-    return early, from_all(late), small
+    late = from_all(column[:, 1:])
+    early[-1], small = lax.optimization_barrier((early[-1], small))
+    return early, late, small
 
 
 def gather_blocks(local):

time: 125 us -> 127 us (1.016)
  blocking collectives: 0 us -> 18.9 us
  starting transfers between devices: 36.1 us -> 25.3 us
  waiting for transfers between devices: 14 us -> 10.3 us
  Pallas kernels: 73.2 us -> 70.1 us
    all_to_all x0 -> x1, blocking collectives: none -> 18.9 us  [to_all(): return lax.all_to_all(values, axis, 0, 0)]
    all_to_all x4 -> x2, starting transfers between devices: 19.7 us -> 8.22 us  [to_all(): return lax.all_to_all(values, axis, 0, 0)]
    all_to_all x4 -> x2, waiting for transfers between devices: 4.49 us -> 0.01 us  [to_all(): return lax.all_to_all(values, axis, 0, 0)]
    pallas_call x2 -> x1, Pallas kernels: 3.52 us -> 1.21 us  [pack(): pl.pallas_call(pack_kernel, out_shape=jax.ShapeDtypeStruct(shape, BF), co...]
    ppermute x12, waiting for transfers between devices: 3.41 us -> 5.13 us  [swap_heads(): return lax.ppermute(values, 'head', [(0, 1), (1, 0)])]
  transfers between devices with their start and end apart: 28 -> 26, of which waited for: 10 -> 11; matrix products, arithmetic and copies ran while one was open for 0% -> 1% of each run, Pallas kernels for 37% -> 34%
where the time goes in v11:
time: 127 us; the launch traced here: 126 us
  Pallas kernels  70.1 us (55%)
  starting transfers between devices  25.3 us (20%)
  blocking collectives  18.9 us (15%)
  waiting for transfers between devices  10.3 us (8%)
    all_to_all x1, blocking collectives, to_all(): return lax.all_to_all(values, axis, 0, 0)  18.9 us
    pallas_call x1, Pallas kernels, mlp(): pl.pallas_call(mlp_kernel, grid=(rows // TILE,), in_specs=[pl.BlockSpec(m...  18.8 us
    pallas_call x2, Pallas kernels, shampoo(): pl.pallas_call(lambda *refs: shampoo_kernel(scale, bool(norms), *refs), g...  15.5 us
    ppermute x12, starting transfers between devices, across(): return lax.ppermute(values, 'inner', pairs)  14.8 us
    pallas_call x1, Pallas kernels, attn_backward(): pl.pallas_call(attn_backward_kernel, grid=(rows // TILE,), in_specs=[smem...  14 us
    pallas_call x1, Pallas kernels, attn_forward(): pl.pallas_call(attn_forward_kernel, grid=(rows // TILE,), in_specs=[smem]...  11.3 us
    all_to_all x2, starting transfers between devices, to_all(): return lax.all_to_all(values, axis, 0, 0)  8.22 us
    pallas_call x1, Pallas kernels, input_gradient(): pl.pallas_call(input_grad_kernel, grid=(rows // INPUT_TILE,), in_specs=[t...  6.63 us
  transfers between devices with their start and end apart: 26, of which 11 were waited for; matrix products, arithmetic and copies ran while one was open for 1% of the time, Pallas kernels for 34%

profile of v11, /device:TPU:0, one launch (start us, length us, event | category | flops | bytes accessed | tf_op | source)
XLA Modules:
  0.0 126.2 jit_solution(2753178838273670539)
XLA Ops:
  0.7 1.2 pack.1
  1.9 18.9 %all_to_all.15 = bf16[4,3,48,384]{3,2,1,0:T(8,128)(2,1)S(1)} all-to-all(bf16[4,3,48,384]{3,2,1,0:T(8,128)(2,1)S(1)} %pack.1), channel_id=1, replica_groups=mesh['outer'=4,'inner'=4,'head'=2] {'outer'}, dimensions={0} | all-to-all | bytes 884736 | tf_op jit(solution)/shard_map/all_to_all | solution.py:739
  20.7 1.6 %collective-permute-start.6 = (bf16[4,48,384]{2,1,0:T(8,128)(2,1)S(1)}, bf16[4,48,384]{2,1,0:T(8,128)(2,1)S(1)}, u32[]{:S(2)}, u32[]{:S(2)}) collective-permute-start(bf16[4,48,384]{2,1,0:T(8,128)(2,1)S(1)} %slice_bitcast_fusion.refs_0_), channel_id=1, source_target_pairs={{0,4},{2,6},{4,0},{6,2},{1,5},{3,7},{5,1},{7,3},{8,12},{10,14},{12... | collective-permute-start | bytes 442376 | tf_op jit(solution)/shard_map/ppermute | solution.py:744
  22.3 1.4 %collective-permute-start = (bf16[4,48,384]{2,1,0:T(8,128)(2,1)S(1)}, bf16[4,48,384]{2,1,0:T(8,128)(2,1)S(1)}, u32[]{:S(2)}, u32[]{:S(2)}) collective-permute-start(bf16[4,48,384]{2,1,0:T(8,128)(2,1)S(1)} %slice_bitcast_fusion.refs_0_), channel_id=1, source_target_pairs={{0,6},{2,4},{4,2},{6,0},{1,7},{3,5},{5,3},{7,1},{8,14},{10,12},{12... | collective-permute-start | bytes 442376 | tf_op jit(solution)/shard_map/ppermute | solution.py:744
  24.3 3.9 %collective-permute-done.6.refs_2_ = bf16[4,48,384]{2,1,0:T(8,128)(2,1)S(1)} collective-permute-done((bf16[4,48,384]{2,1,0:T(8,128)(2,1)S(1)}, bf16[4,48,384]{2,1,0:T(8,128)(2,1)S(1)}, u32[]{:S(2)}, u32[]{:S(2)}) %collective-permute-start.6) | collective-permute-done | bytes 147488 | tf_op jit(solution)/shard_map/ppermute | solution.py:744
  28.2 0.8 copy.22.own_mask_ref
  29.5 0.8 collective-permute-done.1.other_mask_ref
  30.3 3.4 %collective-permute-start.4 = (bf16[4,2,48,384]{3,2,1,0:T(8,128)(2,1)S(1)}, bf16[4,2,48,384]{3,2,1,0:T(8,128)(2,1)S(1)}, u32[]{:S(2)}, u32[]{:S(2)}) collective-permute-start(bf16[4,2,48,384]{3,2,1,0:T(8,128)(2,1)S(1)} %slice.7.refs_0_), channel_id=1, source_target_pairs={{0,6},{2,4},{4,2},{6,0},{1,7},{3,5},{5,3},{7,1},{8,14},{10,12},{12... | collective-permute-start | bytes 884744 | tf_op jit(solution)/shard_map/ppermute | solution.py:744
  34.9 0.9 collective-permute-done.8.refs_5_
  36.0 11.3 %attn_forward.1 = (bf16[6,3,512,256]{3,2,1,0:T(8,128)(2,1)}, bf16[1536,1152]{1,0:T(8,128)(2,1)}, bf16[1536,384]{1,0:T(8,128)(2,1)}, f32[1536,384]{1,0:T(8,128)},...) custom-call(s32[14]{0:T(128)S(1)} %pad_add_fusion.place_ref, s32[12,3]{1,0:T(8,128)S(1)} %copy.22.own_mask_ref, ...), custom_call_target="tpu_custom_call" | custom-call | flops 1056964608 | bytes 4194304 | tf_op jit(solution)/shard_map/attn_forward/pallas_call | solution.py:173
  48.3 1.1 collective-permute-done.12.refs_5_
  50.2 18.8 %mlp.1 = (f32[1536,384]{1,0:T(8,128)}, f32[1536,384]{1,0:T(8,128)}, f32[2,384]{1,0:T(2,128)S(1)}, bf16[2,4,2,48,384]{4,3,2,1,0:T(8,128)(2,1)S(1)}, bf16[2,4,2,48...) custom-call(s32[14]{0:T(128)S(1)} %pad_add_fusion.place_ref, ...), custom_call_target="tpu_custom_call" | custom-call | flops 10871635968 | bytes 20971520 | tf_op jit(solution)/shard_map/mlp/pallas_call | solution.py:269
  69.6 1.5 %collective-permute-done.15.received_ref = bf16[2,4,2,48,384]{4,3,2,1,0:T(8,128)(2,1)S(1)} collective-permute-done((bf16[2,4,2,48,384]{4,3,2,1,0:T(8,128)(2,1)S(1)}, bf16[2,4,2,48,384]{4,3,2,1,0:T(8,128)(2,1)S(1)}, u32[]{:S(2)}, u32[]{:S(2)}) %collective-permute-start.15) | collective-permute-done | bytes 589856 | tf_op jit(solution)/shard_map/ppermute | solution.py:735
  71.2 1.6 %collective-permute-start.16 = (bf16[4,2,48,384]{3,2,1,0:T(8,128)(2,1)S(1)}, bf16[4,2,48,384]{3,2,1,0:T(8,128)(2,1)S(1)}, u32[]{:S(2)}, u32[]{:S(2)}) collective-permute-start(bf16[4,2,48,384]{3,2,1,0:T(8,128)(2,1)S(1)} %get-tuple-element.99), channel_id=1, source_target_pairs={{0,2},{2,0},{4,6},{6,4},{1,3},{3,1},{5,7},{7,5},{8,10},{10,8},{12,... | collective-permute-start | bytes 884744 | tf_op jit(solution)/shard_map/ppermute | solution.py:744
  72.9 1.5 %collective-permute-start.18 = (bf16[4,2,48,384]{3,2,1,0:T(8,128)(2,1)S(1)}, bf16[4,2,48,384]{3,2,1,0:T(8,128)(2,1)S(1)}, u32[]{:S(2)}, u32[]{:S(2)}) collective-permute-start(bf16[4,2,48,384]{3,2,1,0:T(8,128)(2,1)S(1)} %get-tuple-element.102), channel_id=1, source_target_pairs={{0,4},{2,6},{4,0},{6,2},{1,5},{3,7},{5,1},{7,3},{8,12},{10,14},{12... | collective-permute-start | bytes 884744 | tf_op jit(solution)/shard_map/ppermute | solution.py:744
  75.1 14.0 %attn_backward.1 = (bf16[1536,1152]{1,0:T(8,128)(2,1)}, bf16[16,48,384]{2,1,0:T(8,128)(2,1)S(1)}, bf16[17,48,384]{2,1,0:T(8,128)(2,1)S(1)}, f32[4,384]{1,0:T(4,128)S(1)}) custom-call(s32[14]{0:T(128)S(1)} %pad_add_fusion.place_ref, s32[12,3]{1,0:T(8,128)S(1)} %copy.22.own_mask_ref, s32[12,3]{1,0:T(8,128)S(1)} %collective-permute-done.1.other_mask_ref, ...), custom_call_target="tpu_custom_call" | custom-call | flops 7096762368 | bytes 20971520 | tf_op jit(solution)/shard_map/attn_backward/pallas_call | solution.py:391
  89.2 0.9 sum_late.1
  90.0 3.5 %all-to-all-start.1 = ((bf16[4,2,48,384]{3,2,1,0:T(8,128)(2,1)}), bf16[4,2,48,384]{3,2,1,0:T(8,128)(2,1)S(1)}, u32[]{:S(2)}, u32[]{:S(2)}) async-start(bf16[4,2,48,384]{3,2,1,0:T(8,128)(2,1)} %sum_late.1), calls=%async_computation.1 | async-start | bytes 589824 | tf_op jit(solution)/shard_map/all_to_all | solution.py:739
  94.3 1.5 %collective-permute-start.21 = (bf16[200,384]{1,0:T(8,128)(2,1)S(1)}, bf16[200,384]{1,0:T(8,128)(2,1)S(1)}, u32[]{:S(2)}, u32[]{:S(2)}) collective-permute-start(bf16[200,384]{1,0:T(8,128)(2,1)S(1)} %get-tuple-element.113), channel_id=1, source_target_pairs={{0,2},{2,0},{4,6},{6,4},{1,3},{3,1},{5,7},{7,5},{8,10},{10,8},{12,... | collective-permute-start | bytes 460808 | tf_op jit(solution)/shard_map/ppermute | solution.py:744
  95.7 1.5 %collective-permute-start.22 = (bf16[200,384]{1,0:T(8,128)(2,1)S(1)}, bf16[200,384]{1,0:T(8,128)(2,1)S(1)}, u32[]{:S(2)}, u32[]{:S(2)}) collective-permute-start(bf16[200,384]{1,0:T(8,128)(2,1)S(1)} %get-tuple-element.114), channel_id=1, source_target_pairs={{0,4},{2,6},{4,0},{6,2},{1,5},{3,7},{5,1},{7,3},{8,12},{10,14},{12... | collective-permute-start | bytes 460808 | tf_op jit(solution)/shard_map/ppermute | solution.py:744
  97.8 6.6 %input_gradient.1 = f32[1536,384]{1,0:T(8,128)} custom-call(bf16[1536,384]{1,0:T(8,128)(2,1)} %x_ref.5, f32[1536,384]{1,0:T(8,128)} %get-tuple-element.90.grad_ref, bf16[1536,1152]{1,0:T(8,128)(2,1)} %get-tuple-element.116.dqkv_ref, f32[4,384]{1,0:T(4,128)} %refs_4_.1, bf16[384,1152]{1,0:T(8,128)(2,1)} %get-tuple-element.95.wqkv_ref), custom_call_target="tpu_custom_call" | custom-call | flops 1358954496 | bytes 10485760 | tf_op jit(solution)/shard_map/input_gradient/pallas_call | solution.py:447
  105.9 4.8 %all-to-all-start.2 = ((bf16[4,56,384]{2,1,0:T(8,128)(2,1)}), bf16[4,56,384]{2,1,0:T(8,128)(2,1)S(1)}, u32[]{:S(2)}, u32[]{:S(2)}) async-start(bf16[4,56,384]{2,1,0:T(8,128)(2,1)} %join.1), calls=%async_computation.2 | async-start | bytes 344064 | tf_op jit(solution)/shard_map/all_to_all | solution.py:739
  110.7 9.0 %shampoo.2 = (f32[3,8,48,48]{3,2,1,0:T(8,128)}, f32[3,8,48,48]{3,2,1,0:T(8,128)}, f32[3,8,48,48]{3,2,1,0:T(8,128)}, f32[3,8,48,48]{3,2,1,0:T(8,128)}) custom-call(bf16[4,2,48,384]{3,2,1,0:T(8,128)(2,1)S(1)} %all-to-all-done.1.refs_0_, f32[3,8,48,48]{3,2,1,0:T(8,128)S(1)} %bitcast.13, f32[3,8,48,48]{3,2,1,0:T(8,128)S(1)} %bitcast.16, ...), custom_call_target="tpu_custom_call" | custom-call | flops 6442450944 | bytes 4194304 | tf_op jit(solution)/shard_map/shampoo/pallas_call | solution.py:710
  119.6 6.6 %shampoo.3 = (f32[3,8,48,48]{3,2,1,0:T(8,128)}, f32[3,8,48,48]{3,2,1,0:T(8,128)}, f32[3,8,48,48]{3,2,1,0:T(8,128)}, f32[3,8,48,48]{3,2,1,0:T(8,128)}, f32[4,384]...) custom-call(bf16[4,1,56,384]{3,2,1,0:T(8,128)(2,1)S(1)} %bitcast.15,, ...), custom_call_target="tpu_custom_call", output_to_operand_aliasing={{0}: (6, {}), {1}: (7, {}), {2}: (8, {}), {3}: (9, {})} | custom-call | flops 3221225472 | bytes 4194304 | tf_op jit(solution)/shard_map/shampoo/pallas_call | solution.py:710
  (59 shorter events, 8.7 us)
Async XLA Ops:
  20.7 7.4 %collective-permute-start.6 = (bf16[4,48,384]{2,1,0:T(8,128)(2,1)S(1)}, bf16[4,48,384]{2,1,0:T(8,128)(2,1)S(1)}, u32[]{:S(2)}, u32[]{:S(2)}) collective-permute-start(bf16[4,48,384]{2,1,0:T(8,128)(2,1)S(1)} %slice_bitcast_fusion.refs_0_), channel_id=1, source_target_pairs={{0,4},{2,6},{4,0},{6,2},{1,5},{3,7},{5,1},{7,3},{8,12},{10,14},{12... | collective-permute-start | bytes 442376 | tf_op jit(solution)/shard_map/ppermute | solution.py:744
  22.3 11.3 %collective-permute-start.7 = (bf16[4,48,384]{2,1,0:T(8,128)(2,1)S(1)}, bf16[4,48,384]{2,1,0:T(8,128)(2,1)S(1)}, u32[]{:S(2)}, u32[]{:S(2)}) collective-permute-start(bf16[4,48,384]{2,1,0:T(8,128)(2,1)S(1)} %slice_bitcast_fusion.refs_0_), channel_id=1, source_target_pairs={{0,1},{1,0},{2,3},{3,2},{4,5},{5,4},{6,7},{7,6},{8,9},{9,8},{10,11... | collective-permute-start | bytes 442376 | tf_op jit(solution)/shard_map/ppermute | solution.py:735
  22.3 11.3 %collective-permute-start = (bf16[4,48,384]{2,1,0:T(8,128)(2,1)S(1)}, bf16[4,48,384]{2,1,0:T(8,128)(2,1)S(1)}, u32[]{:S(2)}, u32[]{:S(2)}) collective-permute-start(bf16[4,48,384]{2,1,0:T(8,128)(2,1)S(1)} %slice_bitcast_fusion.refs_0_), channel_id=1, source_target_pairs={{0,6},{2,4},{4,2},{6,0},{1,7},{3,5},{5,3},{7,1},{8,14},{10,12},{12... | collective-permute-start | bytes 442376 | tf_op jit(solution)/shard_map/ppermute | solution.py:744
  23.8 10.6 %collective-permute-start.5 = (bf16[4,48,384]{2,1,0:T(8,128)(2,1)S(1)}, bf16[4,48,384]{2,1,0:T(8,128)(2,1)S(1)}, u32[]{:S(2)}, u32[]{:S(2)}) collective-permute-start(bf16[4,48,384]{2,1,0:T(8,128)(2,1)S(1)} %slice_bitcast_fusion.refs_0_), channel_id=1, source_target_pairs={{0,2},{2,0},{4,6},{6,4},{1,3},{3,1},{5,7},{7,5},{8,10},{10,8},{12,... | collective-permute-start | bytes 442376 | tf_op jit(solution)/shard_map/ppermute | solution.py:744
  28.2 6.2 %collective-permute-start.9 = (bf16[4,48,384]{2,1,0:T(8,128)(2,1)S(1)}, bf16[4,48,384]{2,1,0:T(8,128)(2,1)S(1)}, u32[]{:S(2)}, u32[]{:S(2)}) collective-permute-start(bf16[4,48,384]{2,1,0:T(8,128)(2,1)S(1)} %collective-permute-done.6.refs_2_), channel_id=1, source_target_pairs={{0,1},{1,0},{2,3},{3,2},{4,5},{5,4},{6,7},{7,6},{8,9},{9,8},{10,11... | collective-permute-start | bytes 442376 | tf_op jit(solution)/shard_map/ppermute | solution.py:735
  30.3 16.9 %collective-permute-start.4 = (bf16[4,2,48,384]{3,2,1,0:T(8,128)(2,1)S(1)}, bf16[4,2,48,384]{3,2,1,0:T(8,128)(2,1)S(1)}, u32[]{:S(2)}, u32[]{:S(2)}) collective-permute-start(bf16[4,2,48,384]{3,2,1,0:T(8,128)(2,1)S(1)} %slice.7.refs_0_), channel_id=1, source_target_pairs={{0,6},{2,4},{4,2},{6,0},{1,7},{3,5},{5,3},{7,1},{8,14},{10,12},{12... | collective-permute-start | bytes 884744 | tf_op jit(solution)/shard_map/ppermute | solution.py:744
  33.7 13.8 %collective-permute-start.3 = (bf16[4,2,48,384]{3,2,1,0:T(8,128)(2,1)S(1)}, bf16[4,2,48,384]{3,2,1,0:T(8,128)(2,1)S(1)}, u32[]{:S(2)}, u32[]{:S(2)}) collective-permute-start(bf16[4,2,48,384]{3,2,1,0:T(8,128)(2,1)S(1)} %slice.7.refs_0_), channel_id=1, source_target_pairs={{0,4},{2,6},{4,0},{6,2},{1,5},{3,7},{5,1},{7,3},{8,12},{10,14},{12... | collective-permute-start | bytes 884744 | tf_op jit(solution)/shard_map/ppermute | solution.py:744
  33.7 14.1 %collective-permute-start.2 = (bf16[4,2,48,384]{3,2,1,0:T(8,128)(2,1)S(1)}, bf16[4,2,48,384]{3,2,1,0:T(8,128)(2,1)S(1)}, u32[]{:S(2)}, u32[]{:S(2)}) collective-permute-start(bf16[4,2,48,384]{3,2,1,0:T(8,128)(2,1)S(1)} %slice.7.refs_0_), channel_id=1, source_target_pairs={{0,2},{2,0},{4,6},{6,4},{1,3},{3,1},{5,7},{7,5},{8,10},{10,8},{12,... | collective-permute-start | bytes 884744 | tf_op jit(solution)/shard_map/ppermute | solution.py:744
  34.4 1.6 %collective-permute-start.10 = (bf16[4,48,384]{2,1,0:T(8,128)(2,1)S(1)}, bf16[4,48,384]{2,1,0:T(8,128)(2,1)S(1)}, u32[]{:S(2)}, u32[]{:S(2)}) collective-permute-start(bf16[4,48,384]{2,1,0:T(8,128)(2,1)S(1)} %collective-permute-done.refs_3_), channel_id=1, source_target_pairs={{0,1},{1,0},{2,3},{3,2},{4,5},{5,4},{6,7},{7,6},{8,9},{9,8},{10,11... | collective-permute-start | bytes 442376 | tf_op jit(solution)/shard_map/ppermute | solution.py:735
  35.7 12.6 %collective-permute-start.11 = (bf16[4,2,48,384]{3,2,1,0:T(8,128)(2,1)S(1)}, bf16[4,2,48,384]{3,2,1,0:T(8,128)(2,1)S(1)}, u32[]{:S(2)}, u32[]{:S(2)}) collective-permute-start(bf16[4,2,48,384]{3,2,1,0:T(8,128)(2,1)S(1)} %slice.7.refs_0_), channel_id=1, source_target_pairs={{0,1},{1,0},{2,3},{3,2},{4,5},{5,4},{6,7},{7,6},{8,9},{9,8},{10,11... | collective-permute-start | bytes 884744 | tf_op jit(solution)/shard_map/ppermute | solution.py:735
  47.8 1.6 %collective-permute-start.12 = (bf16[4,2,48,384]{3,2,1,0:T(8,128)(2,1)S(1)}, bf16[4,2,48,384]{3,2,1,0:T(8,128)(2,1)S(1)}, u32[]{:S(2)}, u32[]{:S(2)}) collective-permute-start(bf16[4,2,48,384]{3,2,1,0:T(8,128)(2,1)S(1)} %collective-permute-done.2.refs_1_), channel_id=1, source_target_pairs={{0,1},{1,0},{2,3},{3,2},{4,5},{5,4},{6,7},{7,6},{8,9},{9,8},{10,11... | collective-permute-start | bytes 884744 | tf_op jit(solution)/shard_map/ppermute | solution.py:735
  47.8 2.0 %collective-permute-start.13 = (bf16[4,2,48,384]{3,2,1,0:T(8,128)(2,1)S(1)}, bf16[4,2,48,384]{3,2,1,0:T(8,128)(2,1)S(1)}, u32[]{:S(2)}, u32[]{:S(2)}) collective-permute-start(bf16[4,2,48,384]{3,2,1,0:T(8,128)(2,1)S(1)} %collective-permute-done.3.refs_2_), channel_id=1, source_target_pairs={{0,1},{1,0},{2,3},{3,2},{4,5},{5,4},{6,7},{7,6},{8,9},{9,8},{10,11... | collective-permute-start | bytes 884744 | tf_op jit(solution)/shard_map/ppermute | solution.py:735
  48.3 1.9 %collective-permute-start.14 = (bf16[4,2,48,384]{3,2,1,0:T(8,128)(2,1)S(1)}, bf16[4,2,48,384]{3,2,1,0:T(8,128)(2,1)S(1)}, u32[]{:S(2)}, u32[]{:S(2)}) collective-permute-start(bf16[4,2,48,384]{3,2,1,0:T(8,128)(2,1)S(1)} %collective-permute-done.4.refs_3_), channel_id=1, source_target_pairs={{0,1},{1,0},{2,3},{3,2},{4,5},{5,4},{6,7},{7,6},{8,9},{9,8},{10,11... | collective-permute-start | bytes 884744 | tf_op jit(solution)/shard_map/ppermute | solution.py:735
  69.1 2.0 %collective-permute-start.15 = (bf16[2,4,2,48,384]{4,3,2,1,0:T(8,128)(2,1)S(1)}, bf16[2,4,2,48,384]{4,3,2,1,0:T(8,128)(2,1)S(1)}, u32[]{:S(2)}, u32[]{:S(2)}) collective-permute-start(bf16[2,4,2,48,384]{4,3,2,1,0:T(8,128)(2,1)S(1)} %get-tuple-element.86), channel_id=1, source_target_pairs={{0,1},{1,0},{2,3},{3,2},{4,5},{5,4},{6,7},{7,6},{8,9},{9,8},{10,11... | collective-permute-start | bytes 1769480 | tf_op jit(solution)/shard_map/ppermute | solution.py:735
  69.2 3.6 %collective-permute-start.17 = (bf16[2,4,2,48,384]{4,3,2,1,0:T(8,128)(2,1)S(1)}, bf16[2,4,2,48,384]{4,3,2,1,0:T(8,128)(2,1)S(1)}, u32[]{:S(2)}, u32[]{:S(2)}) collective-permute-start(bf16[2,4,2,48,384]{4,3,2,1,0:T(8,128)(2,1)S(1)} %get-tuple-element.101), channel_id=1, source_target_pairs={{0,1},{1,0},{2,3},{3,2},{4,5},{5,4},{6,7},{7,6},{8,9},{9,8},{10,11... | collective-permute-start | bytes 1769480 | tf_op jit(solution)/shard_map/ppermute | solution.py:735
  71.2 17.8 %collective-permute-start.16 = (bf16[4,2,48,384]{3,2,1,0:T(8,128)(2,1)S(1)}, bf16[4,2,48,384]{3,2,1,0:T(8,128)(2,1)S(1)}, u32[]{:S(2)}, u32[]{:S(2)}) collective-permute-start(bf16[4,2,48,384]{3,2,1,0:T(8,128)(2,1)S(1)} %get-tuple-element.99), channel_id=1, source_target_pairs={{0,2},{2,0},{4,6},{6,4},{1,3},{3,1},{5,7},{7,5},{8,10},{10,8},{12,... | collective-permute-start | bytes 884744 | tf_op jit(solution)/shard_map/ppermute | solution.py:744
  72.9 16.1 %collective-permute-start.18 = (bf16[4,2,48,384]{3,2,1,0:T(8,128)(2,1)S(1)}, bf16[4,2,48,384]{3,2,1,0:T(8,128)(2,1)S(1)}, u32[]{:S(2)}, u32[]{:S(2)}) collective-permute-start(bf16[4,2,48,384]{3,2,1,0:T(8,128)(2,1)S(1)} %get-tuple-element.102), channel_id=1, source_target_pairs={{0,4},{2,6},{4,0},{6,2},{1,5},{3,7},{5,1},{7,3},{8,12},{10,14},{12... | collective-permute-start | bytes 884744 | tf_op jit(solution)/shard_map/ppermute | solution.py:744
  74.5 14.6 %collective-permute-start.19 = (bf16[4,2,48,384]{3,2,1,0:T(8,128)(2,1)S(1)}, bf16[4,2,48,384]{3,2,1,0:T(8,128)(2,1)S(1)}, u32[]{:S(2)}, u32[]{:S(2)}) collective-permute-start(bf16[4,2,48,384]{3,2,1,0:T(8,128)(2,1)S(1)} %get-tuple-element.103), channel_id=1, source_target_pairs={{0,6},{2,4},{4,2},{6,0},{1,7},{3,5},{5,3},{7,1},{8,14},{10,12},{12... | collective-permute-start | bytes 884744 | tf_op jit(solution)/shard_map/ppermute | solution.py:744
  89.1 4.4 %collective-permute-start.20 = (bf16[17,48,384]{2,1,0:T(8,128)(2,1)S(1)}, bf16[17,48,384]{2,1,0:T(8,128)(2,1)S(1)}, u32[]{:S(2)}, u32[]{:S(2)}) collective-permute-start(bf16[17,48,384]{2,1,0:T(8,128)(2,1)S(1)} %get-tuple-element.105), channel_id=1, source_target_pairs={{0,1},{1,0},{2,3},{3,2},{4,5},{5,4},{6,7},{7,6},{8,9},{9,8},{10,11... | collective-permute-start | bytes 1880072 | tf_op jit(solution)/shard_map/ppermute | solution.py:735
  90.0 15.8 %all-to-all-start.1 = ((bf16[4,2,48,384]{3,2,1,0:T(8,128)(2,1)}), bf16[4,2,48,384]{3,2,1,0:T(8,128)(2,1)S(1)}, u32[]{:S(2)}, u32[]{:S(2)}) async-start(bf16[4,2,48,384]{3,2,1,0:T(8,128)(2,1)} %sum_late.1), calls=%async_computation.1 | async-start | bytes 589824 | tf_op jit(solution)/shard_map/all_to_all | solution.py:739
  94.3 10.2 %collective-permute-start.21 = (bf16[200,384]{1,0:T(8,128)(2,1)S(1)}, bf16[200,384]{1,0:T(8,128)(2,1)S(1)}, u32[]{:S(2)}, u32[]{:S(2)}) collective-permute-start(bf16[200,384]{1,0:T(8,128)(2,1)S(1)} %get-tuple-element.113), channel_id=1, source_target_pairs={{0,2},{2,0},{4,6},{6,4},{1,3},{3,1},{5,7},{7,5},{8,10},{10,8},{12,... | collective-permute-start | bytes 460808 | tf_op jit(solution)/shard_map/ppermute | solution.py:744
  95.7 9.4 %collective-permute-start.22 = (bf16[200,384]{1,0:T(8,128)(2,1)S(1)}, bf16[200,384]{1,0:T(8,128)(2,1)S(1)}, u32[]{:S(2)}, u32[]{:S(2)}) collective-permute-start(bf16[200,384]{1,0:T(8,128)(2,1)S(1)} %get-tuple-element.114), channel_id=1, source_target_pairs={{0,4},{2,6},{4,0},{6,2},{1,5},{3,7},{5,1},{7,3},{8,12},{10,14},{12... | collective-permute-start | bytes 460808 | tf_op jit(solution)/shard_map/ppermute | solution.py:744
  97.2 7.9 %collective-permute-start.23 = (bf16[200,384]{1,0:T(8,128)(2,1)S(1)}, bf16[200,384]{1,0:T(8,128)(2,1)S(1)}, u32[]{:S(2)}, u32[]{:S(2)}) collective-permute-start(bf16[200,384]{1,0:T(8,128)(2,1)S(1)} %get-tuple-element.115), channel_id=1, source_target_pairs={{0,6},{2,4},{4,2},{6,0},{1,7},{3,5},{5,3},{7,1},{8,14},{10,12},{12... | collective-permute-start | bytes 460808 | tf_op jit(solution)/shard_map/ppermute | solution.py:744
  105.9 13.8 %all-to-all-start.2 = ((bf16[4,56,384]{2,1,0:T(8,128)(2,1)}), bf16[4,56,384]{2,1,0:T(8,128)(2,1)S(1)}, u32[]{:S(2)}, u32[]{:S(2)}) async-start(bf16[4,56,384]{2,1,0:T(8,128)(2,1)} %join.1), calls=%async_computation.2 | async-start | bytes 344064 | tf_op jit(solution)/shard_map/all_to_all | solution.py:739
  (9 other events, 105.6 us)

commit v12 on v10

--- a/solution.py
+++ b/solution.py
@@ -65,6 +65,10 @@
     return grad_in, jnp.concatenate([gain_grad, shift_grad], axis=0)
 
 
+def grown(step, total, part):
+    return jnp.where(step == 0, part, total + part)
+
+
 def slab_at(owner):
     return (owner % INNER) * OUTER + owner // INNER
 
@@ -94,7 +98,7 @@
     place_ref, own_mask_ref, other_mask_ref, x_ref, norm_ref, *refs
 ):
     slab_refs, refs = refs[: 2 * INNER], refs[2 * INNER :]
-    prob_ref, qkv_ref, out_ref, middle_ref, wqkv_ref, wo_ref, held_ref = refs
+    prob_ref, qkv_ref, out_ref, middle_ref, rows_ref, wqkv_ref, wo_ref, held_ref = refs
     step = pl.program_id(0)
 
     @pl.when(step == 0)
@@ -157,7 +161,10 @@
         head_out = nn(prob[:S], values * first) + nn(prob[S:], values * second)
         mask = mask_lanes(place_ref, own_mask_ref, other_mask_ref, IMAGES * step + task[0], task[1])
         out_ref[here, lanes] = (head_out * mask).astype(BF)
-    middle_ref[...] = x + nn(out_ref[...], wo_ref[...])
+    middle = x + nn(out_ref[...], wo_ref[...])
+    middle_ref[...] = middle
+    normed, _ = normalize(middle)
+    rows_ref[...] = (normed * norm_ref[2:3, :] + norm_ref[3:4, :]).astype(BF)
 
 
 def attn_forward(place, own_mask, other_mask, tokens, norm_params, slabs):
@@ -175,6 +182,7 @@
             pl.BlockSpec((TILE, 3 * D), lambda i: (i, 0)),
             tile,
             tile,
+            tile,
             pl.BlockSpec((D, 3 * D), lambda i: (0, 0)),
             pl.BlockSpec((D, D), lambda i: (0, 0)),
         ],
@@ -183,6 +191,7 @@
             pltpu.HBM((rows, 3 * D), BF),
             pltpu.HBM((rows, D), BF),
             pltpu.HBM((rows, D), F32),
+            pltpu.HBM((rows, D), BF),
             pltpu.HBM((D, 3 * D), BF),
             pltpu.HBM((D, D), BF),
         ],
@@ -195,7 +204,7 @@
     )(place, own_mask, other_mask, in_hbm(tokens), in_hbm(norm_params), *slabs)
 
 
-def mlp_kernel(place_ref, middle_ref, cot_ref, norm_ref, *refs):
+def mlp_kernel(place_ref, middle_ref, rows_ref, cot_ref, norm_ref, *refs):
     slab_refs, refs = refs[: 2 * INNER], refs[2 * INNER :]
     out_ref, grad_ref, norm_grad_ref, *refs = refs
     own_refs, sent_refs, refs = refs[:2], refs[2:4], refs[4:]
@@ -212,9 +221,6 @@
 
     @pl.when(step == 0)
     def _():
-        up_grad_ref[...] = jnp.zeros_like(up_grad_ref)
-        down_grad_ref[...] = jnp.zeros_like(down_grad_ref)
-        norm_grad_ref[...] = jnp.zeros_like(norm_grad_ref)
         for number, ref in enumerate(slab_refs):
             side, apart = divmod(number, INNER)
             for outer in range(OUTER):
@@ -224,8 +230,7 @@
 
     middle = middle_ref[...]
     normed, inverse_std = normalize(middle)
-    rows = (normed * norm_ref[2:3, :] + norm_ref[3:4, :]).astype(BF)
-    cot = cot_ref[...]
+    rows, cot = rows_ref[...], cot_ref[...]
     total = middle
     back = None
     for side in range(2):
@@ -239,11 +244,11 @@
         total = total + nn(act, down)
         term = nt(pre_grad, up)
         back = term if back is None else back + term
-        down_grad_ref[side] += tn(act, cot)
-        up_grad_ref[side] += tn(rows, pre_grad)
+        down_grad_ref[side] = grown(step, down_grad_ref[side], tn(act, cot))
+        up_grad_ref[side] = grown(step, up_grad_ref[side], tn(rows, pre_grad))
     out_ref[...] = total
     grad_in, norm_part = norm_backward(back, normed, inverse_std, norm_ref[2:3, :])
-    norm_grad_ref[...] += norm_part
+    norm_grad_ref[...] = grown(step, norm_grad_ref[...], norm_part)
     grad_ref[...] = cot.astype(F32) + grad_in
 
     @pl.when(step == pl.num_programs(0) - 1)
@@ -259,7 +264,7 @@
                     ref[apart % 2, outer, 1] = down.astype(BF)
 
 
-def mlp(place, middle, cotangent, norm_params, slabs):
+def mlp(place, middle, second_rows, cotangent, norm_params, slabs):
     rows = middle.shape[0]
     slab = pl.BlockSpec((OUTER, 2, 48, D), lambda i: (0, 0, 0, 0))
     grads = (INNER // 2, OUTER, 2, 48, D)
@@ -270,6 +275,7 @@
         grid=(rows // TILE,),
         in_specs=[
             pl.BlockSpec(memory_space=pltpu.SMEM),
+            tile,
             tile,
             tile,
             pl.BlockSpec((4, D), lambda i: (0, 0)),
@@ -293,7 +299,7 @@
             flops=12 * rows * D * MLP, bytes_accessed=20 << 20, transcendentals=2 * rows * MLP
         ),
         name="mlp",
-    )(place, in_hbm(middle), in_hbm(cotangent), in_hbm(norm_params), *slabs)
+    )(place, *map(in_hbm, (middle, second_rows, cotangent, norm_params)), *slabs)
 
 
 def attn_backward_kernel(
@@ -304,16 +310,10 @@
 ):
     step = pl.program_id(0)
 
-    @pl.when(step == 0)
-    def _():
-        cross_ref[...] = jnp.zeros_like(cross_ref)
-        column_ref[...] = jnp.zeros_like(column_ref)
-        wo_grad_ref[...] = jnp.zeros_like(wo_grad_ref)
-
     normed, _ = normalize(x_ref[...].astype(F32))
     low_grad = grad_ref[...].astype(BF)
     head_out = out_ref[...]
-    wo_grad_ref[...] += tn(head_out, low_grad)
+    wo_grad_ref[...] = grown(step, wo_grad_ref[...], tn(head_out, low_grad))
     whole_grad = nt(low_grad, wo_ref[...]).astype(BF)
     first, second = lane_halves()
     first_wide, second_wide = first.astype(F32), second.astype(F32)
@@ -353,8 +353,9 @@
         dqkv_ref[here, key_lanes] = jnp.transpose(key_grad).astype(BF)
         dqkv_ref[here, value_lanes] = jnp.transpose(value_grad).astype(BF)
     dqkv = dqkv_ref[...]
-    cross_ref[...] += tn(normed.astype(BF), dqkv)
-    column_ref[...] += jnp.sum(dqkv.astype(F32), axis=0, keepdims=True)
+    cross_ref[...] = grown(step, cross_ref[...], tn(normed.astype(BF), dqkv))
+    columns = jnp.sum(dqkv.astype(F32), axis=0, keepdims=True)
+    column_ref[...] = grown(step, column_ref[...], columns)
 
     @pl.when(step == pl.num_programs(0) - 1)
     def _():
@@ -693,7 +694,8 @@
             power_ref[slot] = product(powers[slot], rights[slot])
 
     advance(True)
-    lax.fori_loop(0, ITERS - 2, lambda _, carry: advance(False) or carry, 0)
+    for _ in range(ITERS - 2):
+        advance(False)
     rights = [spread(split((5.0 * identity - power_ref[slot]) * 0.25)) for slot in slots]
     for slot in slots:
         root_ref[slot] = product(split(root_ref[slot]), rights[slot])
@@ -811,12 +813,14 @@
     early, late = list(early), list(late)
     masks = (head_mask, other_mask)
     early += [swap_heads(piece) for piece in early]
-    prob, qkv, out, middle, wqkv, wo = attn_forward(
+    prob, qkv, out, middle, second_rows, wqkv, wo = attn_forward(
         place, *masks, tokens, norm_params, early
     )
     late[1:], middle = lax.optimization_barrier((late[1:], middle))
     late += [swap_heads(piece) for piece in late]
-    block_out, middle_grad, norm_two, *late_sums = mlp(place, middle, cotangent, norm_params, late)
+    block_out, middle_grad, norm_two, *late_sums = mlp(
+        place, middle, second_rows, cotangent, norm_params, late
+    )
     own_late, late_received = late_sums[:2], [swap_heads(sent) for sent in late_sums[2:]]
     if whole_slabs:
         far = add_late(own_late[1], late_received[1])

time: 125 us -> 122 us (0.976)
  Pallas kernels: 73.2 us -> 71.1 us
    pallas_call x2, Pallas kernels: 15.5 us -> 13.8 us  [shampoo(): pl.pallas_call(lambda *refs: shampoo_kernel(scale, bool(norms), *refs), g...]
where the time goes in v12:
time: 122 us
  Pallas kernels  71.1 us (58%)
  starting transfers between devices  36.1 us (30%)
  waiting for transfers between devices  13.3 us (11%)
    all_to_all x4, starting transfers between devices, to_all(): return lax.all_to_all(values, axis, 0, 0)  19.7 us
    pallas_call x1, Pallas kernels, mlp(): pl.pallas_call(mlp_kernel, grid=(rows // TILE,), in_specs=[pl.BlockSpec(m...  18.3 us
    ppermute x12, starting transfers between devices, across(): return lax.ppermute(values, 'inner', pairs)  14.2 us
    pallas_call x1, Pallas kernels, attn_backward(): pl.pallas_call(attn_backward_kernel, grid=(rows // TILE,), in_specs=[smem...  14.2 us
    pallas_call x2, Pallas kernels, shampoo(): pl.pallas_call(lambda *refs: shampoo_kernel(scale, bool(norms), *refs), g...  13.8 us
    pallas_call x1, Pallas kernels, attn_forward(): pl.pallas_call(attn_forward_kernel, grid=(rows // TILE,), in_specs=[smem]...  12 us
    pallas_call x1, Pallas kernels, input_gradient(): pl.pallas_call(input_grad_kernel, grid=(rows // INPUT_TILE,), in_specs=[t...  6.62 us
    ppermute x12, waiting for transfers between devices, across(): return lax.ppermute(values, 'inner', pairs)  5.39 us
  transfers between devices with their start and end apart: 28, of which 10 were waited for; matrix products, arithmetic and copies ran while one was open for 0% of the time, Pallas kernels for 37%

profile of v12, /device:TPU:0, one launch (start us, length us, event | category | flops | bytes accessed | tf_op | source)
XLA Modules:
  0.0 121.5 jit_solution(13326899159768140767)
XLA Ops:
  0.7 1.7 %pack.2 = bf16[4,1,48,384]{3,2,1,0:T(8,128)(2,1)} custom-call(f32[3,8,48,48]{3,2,1,0:T(8,128)} %bitcast.11), custom_call_target="tpu_custom_call" | custom-call | tf_op jit(solution)/shard_map/pack/pallas_call | solution.py:484
  2.4 6.3 %all-to-all-start = ((bf16[4,1,48,384]{3,2,1,0:T(8,128)(2,1)}), bf16[4,1,48,384]{3,2,1,0:T(8,128)(2,1)S(1)}, u32[]{:S(2)}, u32[]{:S(2)}) async-start(bf16[4,1,48,384]{3,2,1,0:T(8,128)(2,1)} %pack.2), calls=%async_computation | async-start | bytes 294912 | tf_op jit(solution)/shard_map/all_to_all | solution.py:753
  8.7 1.8 %pack.3 = bf16[4,2,48,384]{3,2,1,0:T(8,128)(2,1)} custom-call(f32[3,8,48,48]{3,2,1,0:T(8,128)} %bitcast.12), custom_call_target="tpu_custom_call" | custom-call | tf_op jit(solution)/shard_map/pack/pallas_call | solution.py:484
  10.5 4.4 %all-to-all-done = bf16[4,1,48,384]{3,2,1,0:T(8,128)(2,1)S(1)} async-done(((bf16[4,1,48,384]{3,2,1,0:T(8,128)(2,1)}), bf16[4,1,48,384]{3,2,1,0:T(8,128)(2,1)S(1)}, u32[]{:S(2)}, u32[]{:S(2)}) %all-to-all-start) | async-done | bytes 147488 | tf_op jit(solution)/shard_map/all_to_all | solution.py:753
  14.9 3.5 %all-to-all-start.1 = ((bf16[4,2,48,384]{3,2,1,0:T(8,128)(2,1)}), bf16[4,2,48,384]{3,2,1,0:T(8,128)(2,1)S(1)}, u32[]{:S(2)}, u32[]{:S(2)}) async-start(bf16[4,2,48,384]{3,2,1,0:T(8,128)(2,1)} %pack.3), calls=%async_computation.1 | async-start | bytes 589824 | tf_op jit(solution)/shard_map/all_to_all | solution.py:753
  18.4 2.5 %collective-permute-start.6 = (bf16[4,48,384]{2,1,0:T(8,128)(2,1)S(1)}, bf16[4,48,384]{2,1,0:T(8,128)(2,1)S(1)}, u32[]{:S(2)}, u32[]{:S(2)}) collective-permute-start(bf16[4,48,384]{2,1,0:T(8,128)(2,1)S(1)} %bitcast.16), channel_id=1, source_target_pairs={{0,6},{2,4},{4,2},{6,0},{1,7},{3,5},{5,3},{7,1},{8,14},{10,12},{12... | collective-permute-start | bytes 442376 | tf_op jit(solution)/shard_map/ppermute | solution.py:758
  22.6 3.4 %collective-permute-done.6.refs_3_ = bf16[4,48,384]{2,1,0:T(8,128)(2,1)S(1)} collective-permute-done((bf16[4,48,384]{2,1,0:T(8,128)(2,1)S(1)}, bf16[4,48,384]{2,1,0:T(8,128)(2,1)S(1)}, u32[]{:S(2)}, u32[]{:S(2)}) %collective-permute-start.6) | collective-permute-done | bytes 147488 | tf_op jit(solution)/shard_map/ppermute | solution.py:758
  27.5 2.4 %collective-permute-start.4 = (bf16[4,2,48,384]{3,2,1,0:T(8,128)(2,1)S(1)}, bf16[4,2,48,384]{3,2,1,0:T(8,128)(2,1)S(1)}, u32[]{:S(2)}, u32[]{:S(2)}) collective-permute-start(bf16[4,2,48,384]{3,2,1,0:T(8,128)(2,1)S(1)} %all-to-all-done.1.refs_0_), channel_id=1, source_target_pairs={{0,6},{2,4},{4,2},{6,0},{1,7},{3,5},{5,3},{7,1},{8,14},{10,12},{12... | collective-permute-start | bytes 884744 | tf_op jit(solution)/shard_map/ppermute | solution.py:758
  31.0 12.0 %attn_forward.1 = (bf16[6,3,512,256]{3,2,1,0:T(8,128)(2,1)}, bf16[1536,1152]{1,0:T(8,128)(2,1)}, bf16[1536,384]{1,0:T(8,128)(2,1)}, f32[1536,384]{1,0:T(8,128)},...) custom-call(s32[14]{0:T(128)S(1)} %pad_add_fusion.place_ref, ...), custom_call_target="tpu_custom_call" | custom-call | flops 4227858432 | bytes 16777216 | tf_op jit(solution)/shard_map/attn_forward/pallas_call | solution.py:176
  43.1 1.0 collective-permute-done.3.refs_2_
  44.6 1.1 collective-permute-done.12.refs_5_
  46.5 18.3 %mlp.1 = (f32[1536,384]{1,0:T(8,128)}, f32[1536,384]{1,0:T(8,128)}, f32[2,384]{1,0:T(2,128)S(1)}, bf16[2,4,2,48,384]{4,3,2,1,0:T(8,128)(2,1)S(1)}, bf16[2,4,2,48...) custom-call(s32[14]{0:T(128)S(1)} %pad_add_fusion.place_ref, ...), custom_call_target="tpu_custom_call" | custom-call | flops 10871635968 | bytes 20971520 | tf_op jit(solution)/shard_map/mlp/pallas_call | solution.py:273
  65.4 1.5 %collective-permute-done.15.received_ref = bf16[2,4,2,48,384]{4,3,2,1,0:T(8,128)(2,1)S(1)} collective-permute-done((bf16[2,4,2,48,384]{4,3,2,1,0:T(8,128)(2,1)S(1)}, bf16[2,4,2,48,384]{4,3,2,1,0:T(8,128)(2,1)S(1)}, u32[]{:S(2)}, u32[]{:S(2)}) %collective-permute-start.15) | collective-permute-done | bytes 589856 | tf_op jit(solution)/shard_map/ppermute | solution.py:749
  67.0 1.3 %collective-permute-start.16 = (bf16[4,2,48,384]{3,2,1,0:T(8,128)(2,1)S(1)}, bf16[4,2,48,384]{3,2,1,0:T(8,128)(2,1)S(1)}, u32[]{:S(2)}, u32[]{:S(2)}) collective-permute-start(bf16[4,2,48,384]{3,2,1,0:T(8,128)(2,1)S(1)} %get-tuple-element.103), channel_id=1, source_target_pairs={{0,2},{2,0},{4,6},{6,4},{1,3},{3,1},{5,7},{7,5},{8,10},{10,8},{12,... | collective-permute-start | bytes 884744 | tf_op jit(solution)/shard_map/ppermute | solution.py:758
  68.4 1.1 collective-permute-start.18
  69.6 1.2 collective-permute-start.19
  70.8 14.2 %attn_backward.1 = (bf16[1536,1152]{1,0:T(8,128)(2,1)}, bf16[16,48,384]{2,1,0:T(8,128)(2,1)S(1)}, bf16[17,48,384]{2,1,0:T(8,128)(2,1)S(1)}, f32[4,384]{1,0:T(4,128)S(1)}) custom-call(s32[14]{0:T(128)S(1)} %pad_add_fusion.place_ref, s32[12,3]{1,0:T(8,128)S(1)} %copy.26.own_mask_ref, s32[12,3]{1,0:T(8,128)S(1)} %collective-permute-done.1.other_mask_ref, ...), custom_call_target="tpu_custom_call" | custom-call | flops 7096762368 | bytes 20971520 | tf_op jit(solution)/shard_map/attn_backward/pallas_call | solution.py:396
  85.9 4.9 %all-to-all-start.2 = ((bf16[4,2,48,384]{3,2,1,0:T(8,128)(2,1)}), bf16[4,2,48,384]{3,2,1,0:T(8,128)(2,1)S(1)}, u32[]{:S(2)}, u32[]{:S(2)}) async-start(bf16[4,2,48,384]{3,2,1,0:T(8,128)(2,1)} %sum_late.1), calls=%async_computation.2 | async-start | bytes 589824 | tf_op jit(solution)/shard_map/all_to_all | solution.py:753
  91.6 1.2 collective-permute-start.21
  93.6 1.6 %collective-permute-start.23 = (bf16[200,384]{1,0:T(8,128)(2,1)S(1)}, bf16[200,384]{1,0:T(8,128)(2,1)S(1)}, u32[]{:S(2)}, u32[]{:S(2)}) collective-permute-start(bf16[200,384]{1,0:T(8,128)(2,1)S(1)} %get-tuple-element.119), channel_id=1, source_target_pairs={{0,6},{2,4},{4,2},{6,0},{1,7},{3,5},{5,3},{7,1},{8,14},{10,12},{12... | collective-permute-start | bytes 460808 | tf_op jit(solution)/shard_map/ppermute | solution.py:758
  95.2 6.6 %input_gradient.1 = f32[1536,384]{1,0:T(8,128)} custom-call(bf16[1536,384]{1,0:T(8,128)(2,1)} %x_ref.5, f32[1536,384]{1,0:T(8,128)} %get-tuple-element.94.grad_ref, bf16[1536,1152]{1,0:T(8,128)(2,1)} %get-tuple-element.120.dqkv_ref, f32[4,384]{1,0:T(4,128)} %refs_4_.1, bf16[384,1152]{1,0:T(8,128)(2,1)} %get-tuple-element.99.wqkv_ref), custom_call_target="tpu_custom_call" | custom-call | flops 1358954496 | bytes 10485760 | tf_op jit(solution)/shard_map/input_gradient/pallas_call | solution.py:452
  102.7 5.0 %all-to-all-start.3 = ((bf16[4,56,384]{2,1,0:T(8,128)(2,1)}), bf16[4,56,384]{2,1,0:T(8,128)(2,1)S(1)}, u32[]{:S(2)}, u32[]{:S(2)}) async-start(bf16[4,56,384]{2,1,0:T(8,128)(2,1)} %join.1), calls=%async_computation.3 | async-start | bytes 344064 | tf_op jit(solution)/shard_map/all_to_all | solution.py:753
  107.7 8.0 %shampoo.2 = (f32[3,8,48,48]{3,2,1,0:T(8,128)}, f32[3,8,48,48]{3,2,1,0:T(8,128)}, f32[3,8,48,48]{3,2,1,0:T(8,128)}, f32[3,8,48,48]{3,2,1,0:T(8,128)}) custom-call(bf16[4,2,48,384]{3,2,1,0:T(8,128)(2,1)S(1)} %all-to-all-done.2.refs_0_, f32[3,8,48,48]{3,2,1,0:T(8,128)S(1)} %bitcast.13, f32[3,8,48,48]{3,2,1,0:T(8,128)S(1)} %bitcast.21, ...), custom_call_target="tpu_custom_call" | custom-call | flops 6442450944 | bytes 4194304 | tf_op jit(solution)/shard_map/shampoo/pallas_call | solution.py:724
  115.7 5.8 %shampoo.3 = (f32[3,8,48,48]{3,2,1,0:T(8,128)}, f32[3,8,48,48]{3,2,1,0:T(8,128)}, f32[3,8,48,48]{3,2,1,0:T(8,128)}, f32[3,8,48,48]{3,2,1,0:T(8,128)}, f32[4,384]...) custom-call(bf16[4,1,56,384]{3,2,1,0:T(8,128)(2,1)S(1)} %bitcast.15,, ...), custom_call_target="tpu_custom_call", output_to_operand_aliasing={{0}: (6, {}), {1}: (7, {}), {2}: (8, {}), {3}: (9, {})} | custom-call | flops 3221225472 | bytes 4194304 | tf_op jit(solution)/shard_map/shampoo/pallas_call | solution.py:724
  (63 shorter events, 9.9 us)
Async XLA Ops:
  2.4 12.6 %all-to-all-start = ((bf16[4,1,48,384]{3,2,1,0:T(8,128)(2,1)}), bf16[4,1,48,384]{3,2,1,0:T(8,128)(2,1)S(1)}, u32[]{:S(2)}, u32[]{:S(2)}) async-start(bf16[4,1,48,384]{3,2,1,0:T(8,128)(2,1)} %pack.2), calls=%async_computation | async-start | bytes 294912 | tf_op jit(solution)/shard_map/all_to_all | solution.py:753
  14.9 12.0 %all-to-all-start.1 = ((bf16[4,2,48,384]{3,2,1,0:T(8,128)(2,1)}), bf16[4,2,48,384]{3,2,1,0:T(8,128)(2,1)S(1)}, u32[]{:S(2)}, u32[]{:S(2)}) async-start(bf16[4,2,48,384]{3,2,1,0:T(8,128)(2,1)} %pack.3), calls=%async_computation.1 | async-start | bytes 589824 | tf_op jit(solution)/shard_map/all_to_all | solution.py:753
  18.4 7.6 %collective-permute-start.6 = (bf16[4,48,384]{2,1,0:T(8,128)(2,1)S(1)}, bf16[4,48,384]{2,1,0:T(8,128)(2,1)S(1)}, u32[]{:S(2)}, u32[]{:S(2)}) collective-permute-start(bf16[4,48,384]{2,1,0:T(8,128)(2,1)S(1)} %bitcast.16), channel_id=1, source_target_pairs={{0,6},{2,4},{4,2},{6,0},{1,7},{3,5},{5,3},{7,1},{8,14},{10,12},{12... | collective-permute-start | bytes 442376 | tf_op jit(solution)/shard_map/ppermute | solution.py:758
  20.9 6.0 %collective-permute-start.5 = (bf16[4,48,384]{2,1,0:T(8,128)(2,1)S(1)}, bf16[4,48,384]{2,1,0:T(8,128)(2,1)S(1)}, u32[]{:S(2)}, u32[]{:S(2)}) collective-permute-start(bf16[4,48,384]{2,1,0:T(8,128)(2,1)S(1)} %bitcast.17), channel_id=1, source_target_pairs={{0,4},{2,6},{4,0},{6,2},{1,5},{3,7},{5,1},{7,3},{8,12},{10,14},{12... | collective-permute-start | bytes 442376 | tf_op jit(solution)/shard_map/ppermute | solution.py:758
  21.4 5.5 %collective-permute-start = (bf16[4,48,384]{2,1,0:T(8,128)(2,1)S(1)}, bf16[4,48,384]{2,1,0:T(8,128)(2,1)S(1)}, u32[]{:S(2)}, u32[]{:S(2)}) collective-permute-start(bf16[4,48,384]{2,1,0:T(8,128)(2,1)S(1)} %bitcast.18), channel_id=1, source_target_pairs={{0,2},{2,0},{4,6},{6,4},{1,3},{3,1},{5,7},{7,5},{8,10},{10,8},{12,... | collective-permute-start | bytes 442376 | tf_op jit(solution)/shard_map/ppermute | solution.py:758
  22.0 4.8 %collective-permute-start.1 = (s32[12,3]{1,0:T(8,128)S(1)}, s32[12,3]{1,0:T(8,128)S(1)}, u32[]{:S(2)}, u32[]{:S(2)}) collective-permute-start(s32[12,3]{1,0:T(8,128)S(1)} %copy.26.own_mask_ref), channel_id=1, source_target_pairs={{0,1},{1,0},{2,3},{3,2},{4,5},{5,4},{6,7},{7,6},{8,9},{9,8},{10,11... | collective-permute-start | bytes 440 | tf_op jit(solution)/shard_map/ppermute | solution.py:749
  22.1 5.4 %collective-permute-start.7 = (bf16[4,48,384]{2,1,0:T(8,128)(2,1)S(1)}, bf16[4,48,384]{2,1,0:T(8,128)(2,1)S(1)}, u32[]{:S(2)}, u32[]{:S(2)}) collective-permute-start(bf16[4,48,384]{2,1,0:T(8,128)(2,1)S(1)} %bitcast.19), channel_id=1, source_target_pairs={{0,1},{1,0},{2,3},{3,2},{4,5},{5,4},{6,7},{7,6},{8,9},{9,8},{10,11... | collective-permute-start | bytes 442376 | tf_op jit(solution)/shard_map/ppermute | solution.py:749
  26.0 3.9 %collective-permute-start.10 = (bf16[4,48,384]{2,1,0:T(8,128)(2,1)S(1)}, bf16[4,48,384]{2,1,0:T(8,128)(2,1)S(1)}, u32[]{:S(2)}, u32[]{:S(2)}) collective-permute-start(bf16[4,48,384]{2,1,0:T(8,128)(2,1)S(1)} %collective-permute-done.6.refs_3_), channel_id=1, source_target_pairs={{0,1},{1,0},{2,3},{3,2},{4,5},{5,4},{6,7},{7,6},{8,9},{9,8},{10,11... | collective-permute-start | bytes 442376 | tf_op jit(solution)/shard_map/ppermute | solution.py:749
  26.8 3.6 %collective-permute-start.9 = (bf16[4,48,384]{2,1,0:T(8,128)(2,1)S(1)}, bf16[4,48,384]{2,1,0:T(8,128)(2,1)S(1)}, u32[]{:S(2)}, u32[]{:S(2)}) collective-permute-start(bf16[4,48,384]{2,1,0:T(8,128)(2,1)S(1)} %collective-permute-done.5.refs_2_), channel_id=1, source_target_pairs={{0,1},{1,0},{2,3},{3,2},{4,5},{5,4},{6,7},{7,6},{8,9},{9,8},{10,11... | collective-permute-start | bytes 442376 | tf_op jit(solution)/shard_map/ppermute | solution.py:749
  26.9 4.1 %collective-permute-start.8 = (bf16[4,48,384]{2,1,0:T(8,128)(2,1)S(1)}, bf16[4,48,384]{2,1,0:T(8,128)(2,1)S(1)}, u32[]{:S(2)}, u32[]{:S(2)}) collective-permute-start(bf16[4,48,384]{2,1,0:T(8,128)(2,1)S(1)} %collective-permute-done.refs_1_), channel_id=1, source_target_pairs={{0,1},{1,0},{2,3},{3,2},{4,5},{5,4},{6,7},{7,6},{8,9},{9,8},{10,11... | collective-permute-start | bytes 442376 | tf_op jit(solution)/shard_map/ppermute | solution.py:749
  27.4 17.2 %collective-permute-start.11 = (bf16[4,2,48,384]{3,2,1,0:T(8,128)(2,1)S(1)}, bf16[4,2,48,384]{3,2,1,0:T(8,128)(2,1)S(1)}, u32[]{:S(2)}, u32[]{:S(2)}) collective-permute-start(bf16[4,2,48,384]{3,2,1,0:T(8,128)(2,1)S(1)} %all-to-all-done.1.refs_0_), channel_id=1, source_target_pairs={{0,1},{1,0},{2,3},{3,2},{4,5},{5,4},{6,7},{7,6},{8,9},{9,8},{10,11... | collective-permute-start | bytes 884744 | tf_op jit(solution)/shard_map/ppermute | solution.py:749
  27.5 15.5 %collective-permute-start.4 = (bf16[4,2,48,384]{3,2,1,0:T(8,128)(2,1)S(1)}, bf16[4,2,48,384]{3,2,1,0:T(8,128)(2,1)S(1)}, u32[]{:S(2)}, u32[]{:S(2)}) collective-permute-start(bf16[4,2,48,384]{3,2,1,0:T(8,128)(2,1)S(1)} %all-to-all-done.1.refs_0_), channel_id=1, source_target_pairs={{0,6},{2,4},{4,2},{6,0},{1,7},{3,5},{5,3},{7,1},{8,14},{10,12},{12... | collective-permute-start | bytes 884744 | tf_op jit(solution)/shard_map/ppermute | solution.py:758
  29.9 14.2 %collective-permute-start.3 = (bf16[4,2,48,384]{3,2,1,0:T(8,128)(2,1)S(1)}, bf16[4,2,48,384]{3,2,1,0:T(8,128)(2,1)S(1)}, u32[]{:S(2)}, u32[]{:S(2)}) collective-permute-start(bf16[4,2,48,384]{3,2,1,0:T(8,128)(2,1)S(1)} %all-to-all-done.1.refs_0_), channel_id=1, source_target_pairs={{0,4},{2,6},{4,0},{6,2},{1,5},{3,7},{5,1},{7,3},{8,12},{10,14},{12... | collective-permute-start | bytes 884744 | tf_op jit(solution)/shard_map/ppermute | solution.py:758
  30.4 13.7 %collective-permute-start.2 = (bf16[4,2,48,384]{3,2,1,0:T(8,128)(2,1)S(1)}, bf16[4,2,48,384]{3,2,1,0:T(8,128)(2,1)S(1)}, u32[]{:S(2)}, u32[]{:S(2)}) collective-permute-start(bf16[4,2,48,384]{3,2,1,0:T(8,128)(2,1)S(1)} %all-to-all-done.1.refs_0_), channel_id=1, source_target_pairs={{0,2},{2,0},{4,6},{6,4},{1,3},{3,1},{5,7},{7,5},{8,10},{10,8},{12,... | collective-permute-start | bytes 884744 | tf_op jit(solution)/shard_map/ppermute | solution.py:758
  65.0 3.3 %collective-permute-start.17 = (bf16[2,4,2,48,384]{4,3,2,1,0:T(8,128)(2,1)S(1)}, bf16[2,4,2,48,384]{4,3,2,1,0:T(8,128)(2,1)S(1)}, u32[]{:S(2)}, u32[]{:S(2)}) collective-permute-start(bf16[2,4,2,48,384]{4,3,2,1,0:T(8,128)(2,1)S(1)} %get-tuple-element.105), channel_id=1, source_target_pairs={{0,1},{1,0},{2,3},{3,2},{4,5},{5,4},{6,7},{7,6},{8,9},{9,8},{10,11... | collective-permute-start | bytes 1769480 | tf_op jit(solution)/shard_map/ppermute | solution.py:749
  67.0 17.9 %collective-permute-start.16 = (bf16[4,2,48,384]{3,2,1,0:T(8,128)(2,1)S(1)}, bf16[4,2,48,384]{3,2,1,0:T(8,128)(2,1)S(1)}, u32[]{:S(2)}, u32[]{:S(2)}) collective-permute-start(bf16[4,2,48,384]{3,2,1,0:T(8,128)(2,1)S(1)} %get-tuple-element.103), channel_id=1, source_target_pairs={{0,2},{2,0},{4,6},{6,4},{1,3},{3,1},{5,7},{7,5},{8,10},{10,8},{12,... | collective-permute-start | bytes 884744 | tf_op jit(solution)/shard_map/ppermute | solution.py:758
  68.4 16.5 %collective-permute-start.18 = (bf16[4,2,48,384]{3,2,1,0:T(8,128)(2,1)S(1)}, bf16[4,2,48,384]{3,2,1,0:T(8,128)(2,1)S(1)}, u32[]{:S(2)}, u32[]{:S(2)}) collective-permute-start(bf16[4,2,48,384]{3,2,1,0:T(8,128)(2,1)S(1)} %get-tuple-element.106), channel_id=1, source_target_pairs={{0,4},{2,6},{4,0},{6,2},{1,5},{3,7},{5,1},{7,3},{8,12},{10,14},{12... | collective-permute-start | bytes 884744 | tf_op jit(solution)/shard_map/ppermute | solution.py:758
  69.6 15.4 %collective-permute-start.19 = (bf16[4,2,48,384]{3,2,1,0:T(8,128)(2,1)S(1)}, bf16[4,2,48,384]{3,2,1,0:T(8,128)(2,1)S(1)}, u32[]{:S(2)}, u32[]{:S(2)}) collective-permute-start(bf16[4,2,48,384]{3,2,1,0:T(8,128)(2,1)S(1)} %get-tuple-element.107), channel_id=1, source_target_pairs={{0,6},{2,4},{4,2},{6,0},{1,7},{3,5},{5,3},{7,1},{8,14},{10,12},{12... | collective-permute-start | bytes 884744 | tf_op jit(solution)/shard_map/ppermute | solution.py:758
  85.0 5.9 %collective-permute-start.20 = (bf16[17,48,384]{2,1,0:T(8,128)(2,1)S(1)}, bf16[17,48,384]{2,1,0:T(8,128)(2,1)S(1)}, u32[]{:S(2)}, u32[]{:S(2)}) collective-permute-start(bf16[17,48,384]{2,1,0:T(8,128)(2,1)S(1)} %get-tuple-element.109), channel_id=1, source_target_pairs={{0,1},{1,0},{2,3},{3,2},{4,5},{5,4},{6,7},{7,6},{8,9},{9,8},{10,11... | collective-permute-start | bytes 1880072 | tf_op jit(solution)/shard_map/ppermute | solution.py:749
  85.9 16.7 %all-to-all-start.2 = ((bf16[4,2,48,384]{3,2,1,0:T(8,128)(2,1)}), bf16[4,2,48,384]{3,2,1,0:T(8,128)(2,1)S(1)}, u32[]{:S(2)}, u32[]{:S(2)}) async-start(bf16[4,2,48,384]{3,2,1,0:T(8,128)(2,1)} %sum_late.1), calls=%async_computation.2 | async-start | bytes 589824 | tf_op jit(solution)/shard_map/all_to_all | solution.py:753
  91.6 10.2 %collective-permute-start.21 = (bf16[200,384]{1,0:T(8,128)(2,1)S(1)}, bf16[200,384]{1,0:T(8,128)(2,1)S(1)}, u32[]{:S(2)}, u32[]{:S(2)}) collective-permute-start(bf16[200,384]{1,0:T(8,128)(2,1)S(1)} %get-tuple-element.117), channel_id=1, source_target_pairs={{0,2},{2,0},{4,6},{6,4},{1,3},{3,1},{5,7},{7,5},{8,10},{10,8},{12,... | collective-permute-start | bytes 460808 | tf_op jit(solution)/shard_map/ppermute | solution.py:758
  92.8 9.1 %collective-permute-start.22 = (bf16[200,384]{1,0:T(8,128)(2,1)S(1)}, bf16[200,384]{1,0:T(8,128)(2,1)S(1)}, u32[]{:S(2)}, u32[]{:S(2)}) collective-permute-start(bf16[200,384]{1,0:T(8,128)(2,1)S(1)} %get-tuple-element.118), channel_id=1, source_target_pairs={{0,4},{2,6},{4,0},{6,2},{1,5},{3,7},{5,1},{7,3},{8,12},{10,14},{12... | collective-permute-start | bytes 460808 | tf_op jit(solution)/shard_map/ppermute | solution.py:758
  93.6 8.3 %collective-permute-start.23 = (bf16[200,384]{1,0:T(8,128)(2,1)S(1)}, bf16[200,384]{1,0:T(8,128)(2,1)S(1)}, u32[]{:S(2)}, u32[]{:S(2)}) collective-permute-start(bf16[200,384]{1,0:T(8,128)(2,1)S(1)} %get-tuple-element.119), channel_id=1, source_target_pairs={{0,6},{2,4},{4,2},{6,0},{1,7},{3,5},{5,3},{7,1},{8,14},{10,12},{12... | collective-permute-start | bytes 460808 | tf_op jit(solution)/shard_map/ppermute | solution.py:758
  102.7 13.0 %all-to-all-start.3 = ((bf16[4,56,384]{2,1,0:T(8,128)(2,1)}), bf16[4,56,384]{2,1,0:T(8,128)(2,1)S(1)}, u32[]{:S(2)}, u32[]{:S(2)}) async-start(bf16[4,56,384]{2,1,0:T(8,128)(2,1)} %join.1), calls=%async_computation.3 | async-start | bytes 344064 | tf_op jit(solution)/shard_map/all_to_all | solution.py:753
  (12 other events, 120.4 us)

commit v13 on v12

--- a/solution.py
+++ b/solution.py
@@ -190,8 +190,8 @@
             pltpu.HBM((images, PAIRS, 2 * S, S), BF),
             pltpu.HBM((rows, 3 * D), BF),
             pltpu.HBM((rows, D), BF),
-            pltpu.HBM((rows, D), F32),
-            pltpu.HBM((rows, D), BF),
+            jax.ShapeDtypeStruct((rows, D), F32),
+            jax.ShapeDtypeStruct((rows, D), BF),
             pltpu.HBM((D, 3 * D), BF),
             pltpu.HBM((D, D), BF),
         ],
@@ -299,7 +299,7 @@
             flops=12 * rows * D * MLP, bytes_accessed=20 << 20, transcendentals=2 * rows * MLP
         ),
         name="mlp",
-    )(place, *map(in_hbm, (middle, second_rows, cotangent, norm_params)), *slabs)
+    )(place, middle, second_rows, *map(in_hbm, (cotangent, norm_params)), *slabs)
 
 
 def attn_backward_kernel(
@@ -434,7 +434,7 @@
         name="attn_backward",
     )(
         place, own_mask, other_mask,
-        *map(in_hbm, (tokens, grad, prob, qkv, out, norm_params, later_norms, wqkv, wo)),
+        in_hbm(tokens), in_hbm(grad), *map(in_hbm, (prob, qkv, out, norm_params, later_norms)), in_hbm(wqkv), in_hbm(wo),
     )
 
 
@@ -466,7 +466,7 @@
             flops=rows * D * 6 * D, bytes_accessed=10 << 20, transcendentals=0
         ),
         name="input_gradient",
-    )(*map(in_hbm, (tokens, grad, dqkv, norm_params, wqkv)))
+    )(in_hbm(tokens), in_hbm(grad), in_hbm(dqkv), in_hbm(norm_params), in_hbm(wqkv))
 
 
 def pack_kernel(weight_ref, out_ref):
@@ -763,7 +763,9 @@
 
 
 def gather_slabs(weights, small):
-    early = to_all(pack(weights, 0, 1), "outer")[:, 0]
+    _, count, edge, _ = weights.shape
+    early = weights[0].astype(BF).transpose(1, 0, 2).reshape(1, edge, count * edge)
+    early = to_all(jnp.broadcast_to(early, (OUTER, edge, count * edge)), "outer")
     early, late = lax.optimization_barrier((early, pack(weights, 1, 2)))
     late = to_all(late, "outer")
     early = from_all(early)

time: 122 us -> 122 us (level)
  Pallas kernels: 71.1 us -> 69 us
  local copies, waits for them, and re-layouts: 0.14 us -> 1.92 us
    pallas_call x2 -> x1, Pallas kernels: 3.52 us -> 1.83 us  [pack(): pl.pallas_call(pack_kernel, grid=(1,), in_specs=[pl.BlockSpec((pl.Element...]
where the time goes in v13:
time: 122 us
  Pallas kernels  69 us (57%)
  starting transfers between devices  36.1 us (30%)
  waiting for transfers between devices  13.7 us (11%)
  local copies, waits for them, and re-layouts  1.92 us (2%)
    all_to_all x4, starting transfers between devices, to_all(): return lax.all_to_all(values, axis, 0, 0)  19.7 us
    pallas_call x1, Pallas kernels, mlp(): pl.pallas_call(mlp_kernel, grid=(rows // TILE,), in_specs=[pl.BlockSpec(m...  18.3 us
    ppermute x12, starting transfers between devices, across(): return lax.ppermute(values, 'inner', pairs)  14.2 us
    pallas_call x1, Pallas kernels, attn_backward(): pl.pallas_call(attn_backward_kernel, grid=(rows // TILE,), in_specs=[smem...  14.2 us
    pallas_call x2, Pallas kernels, shampoo(): pl.pallas_call(lambda *refs: shampoo_kernel(scale, bool(norms), *refs), g...  13.8 us
    pallas_call x1, Pallas kernels, attn_forward(): pl.pallas_call(attn_forward_kernel, grid=(rows // TILE,), in_specs=[smem]...  11.6 us
    pallas_call x1, Pallas kernels, input_gradient(): pl.pallas_call(input_grad_kernel, grid=(rows // INPUT_TILE,), in_specs=[t...  6.62 us
    ppermute x12, waiting for transfers between devices, across(): return lax.ppermute(values, 'inner', pairs)  5.77 us
  transfers between devices with their start and end apart: 28, of which 10 were waited for; matrix products, arithmetic and copies ran while one was open for 0% of the time, Pallas kernels for 37%

profile of v13, /device:TPU:0, one launch (start us, length us, event | category | flops | bytes accessed | tf_op | source)
XLA Modules:
  0.0 121.6 jit_solution(6723894737536166671)
XLA Ops:
  0.7 1.0 fusion
  2.5 6.3 %all-to-all-start = ((bf16[4,48,384]{2,1,0:T(8,128)(2,1)}), bf16[4,48,384]{2,1,0:T(8,128)(2,1)S(1)}, u32[]{:S(2)}, u32[]{:S(2)}) async-start(bf16[4,48,384]{2,1,0:T(8,128)(2,1)} %broadcast_in_dim.23), calls=%async_computation | async-start | bytes 294912 | tf_op jit(solution)/shard_map/all_to_all | solution.py:753
  8.8 1.8 %pack.1 = bf16[4,2,48,384]{3,2,1,0:T(8,128)(2,1)} custom-call(f32[3,8,48,48]{3,2,1,0:T(8,128)} %bitcast.14), custom_call_target="tpu_custom_call" | custom-call | tf_op jit(solution)/shard_map/pack/pallas_call | solution.py:484
  10.6 4.4 %all-to-all-done.refs_0_ = bf16[4,48,384]{2,1,0:T(8,128)(2,1)S(1)} async-done(((bf16[4,48,384]{2,1,0:T(8,128)(2,1)}), bf16[4,48,384]{2,1,0:T(8,128)(2,1)S(1)}, u32[]{:S(2)}, u32[]{:S(2)}) %all-to-all-start) | async-done | bytes 147488 | tf_op jit(solution)/shard_map/all_to_all | solution.py:753
  15.0 3.5 %all-to-all-start.1 = ((bf16[4,2,48,384]{3,2,1,0:T(8,128)(2,1)}), bf16[4,2,48,384]{3,2,1,0:T(8,128)(2,1)S(1)}, u32[]{:S(2)}, u32[]{:S(2)}) async-start(bf16[4,2,48,384]{3,2,1,0:T(8,128)(2,1)} %pack.1), calls=%async_computation.1 | async-start | bytes 589824 | tf_op jit(solution)/shard_map/all_to_all | solution.py:753
  18.5 2.5 %collective-permute-start.6 = (bf16[4,48,384]{2,1,0:T(8,128)(2,1)S(1)}, bf16[4,48,384]{2,1,0:T(8,128)(2,1)S(1)}, u32[]{:S(2)}, u32[]{:S(2)}) collective-permute-start(bf16[4,48,384]{2,1,0:T(8,128)(2,1)S(1)} %all-to-all-done.refs_0_), channel_id=1, source_target_pairs={{0,6},{2,4},{4,2},{6,0},{1,7},{3,5},{5,3},{7,1},{8,14},{10,12},{12... | collective-permute-start | bytes 442376 | tf_op jit(solution)/shard_map/ppermute | solution.py:758
  22.7 3.4 %collective-permute-done.6.refs_3_ = bf16[4,48,384]{2,1,0:T(8,128)(2,1)S(1)} collective-permute-done((bf16[4,48,384]{2,1,0:T(8,128)(2,1)S(1)}, bf16[4,48,384]{2,1,0:T(8,128)(2,1)S(1)}, u32[]{:S(2)}, u32[]{:S(2)}) %collective-permute-start.6) | collective-permute-done | bytes 147488 | tf_op jit(solution)/shard_map/ppermute | solution.py:758
  27.6 2.4 %collective-permute-start.4 = (bf16[4,2,48,384]{3,2,1,0:T(8,128)(2,1)S(1)}, bf16[4,2,48,384]{3,2,1,0:T(8,128)(2,1)S(1)}, u32[]{:S(2)}, u32[]{:S(2)}) collective-permute-start(bf16[4,2,48,384]{3,2,1,0:T(8,128)(2,1)S(1)} %all-to-all-done.1.refs_0_), channel_id=1, source_target_pairs={{0,6},{2,4},{4,2},{6,0},{1,7},{3,5},{5,3},{7,1},{8,14},{10,12},{12... | collective-permute-start | bytes 884744 | tf_op jit(solution)/shard_map/ppermute | solution.py:758
  31.1 11.6 %attn_forward.1 = (bf16[6,3,512,256]{3,2,1,0:T(8,128)(2,1)}, bf16[1536,1152]{1,0:T(8,128)(2,1)}, bf16[1536,384]{1,0:T(8,128)(2,1)}, f32[1536,384]{1,0:T(8,128)S(...) custom-call(s32[14]{0:T(128)S(1)} %pad_add_fusion.place_ref, ...), custom_call_target="tpu_custom_call" | custom-call | flops 4227858432 | bytes 16777216 | tf_op jit(solution)/shard_map/attn_forward/pallas_call | solution.py:176
  42.8 1.4 %collective-permute-done.3.refs_2_ = bf16[4,2,48,384]{3,2,1,0:T(8,128)(2,1)S(1)} collective-permute-done((bf16[4,2,48,384]{3,2,1,0:T(8,128)(2,1)S(1)}, bf16[4,2,48,384]{3,2,1,0:T(8,128)(2,1)S(1)}, u32[]{:S(2)}, u32[]{:S(2)}) %collective-permute-start.3) | collective-permute-done | bytes 294944 | tf_op jit(solution)/shard_map/ppermute | solution.py:758
  44.7 1.1 collective-permute-done.12.refs_5_
  46.6 18.3 %mlp.1 = (f32[1536,384]{1,0:T(8,128)}, f32[1536,384]{1,0:T(8,128)}, f32[2,384]{1,0:T(2,128)S(1)}, bf16[2,4,2,48,384]{4,3,2,1,0:T(8,128)(2,1)S(1)}, bf16[2,4,2,48...) custom-call(s32[14]{0:T(128)S(1)} %pad_add_fusion.place_ref, ...), custom_call_target="tpu_custom_call" | custom-call | flops 10871635968 | bytes 20971520 | tf_op jit(solution)/shard_map/mlp/pallas_call | solution.py:273
  65.4 1.5 %collective-permute-done.15.received_ref = bf16[2,4,2,48,384]{4,3,2,1,0:T(8,128)(2,1)S(1)} collective-permute-done((bf16[2,4,2,48,384]{4,3,2,1,0:T(8,128)(2,1)S(1)}, bf16[2,4,2,48,384]{4,3,2,1,0:T(8,128)(2,1)S(1)}, u32[]{:S(2)}, u32[]{:S(2)}) %collective-permute-start.15) | collective-permute-done | bytes 589856 | tf_op jit(solution)/shard_map/ppermute | solution.py:749
  67.0 1.3 %collective-permute-start.16 = (bf16[4,2,48,384]{3,2,1,0:T(8,128)(2,1)S(1)}, bf16[4,2,48,384]{3,2,1,0:T(8,128)(2,1)S(1)}, u32[]{:S(2)}, u32[]{:S(2)}) collective-permute-start(bf16[4,2,48,384]{3,2,1,0:T(8,128)(2,1)S(1)} %get-tuple-element.103), channel_id=1, source_target_pairs={{0,2},{2,0},{4,6},{6,4},{1,3},{3,1},{5,7},{7,5},{8,10},{10,8},{12,... | collective-permute-start | bytes 884744 | tf_op jit(solution)/shard_map/ppermute | solution.py:758
  68.5 1.1 collective-permute-start.18
  69.6 1.2 collective-permute-start.19
  70.8 14.2 %attn_backward.1 = (bf16[1536,1152]{1,0:T(8,128)(2,1)}, bf16[16,48,384]{2,1,0:T(8,128)(2,1)S(1)}, bf16[17,48,384]{2,1,0:T(8,128)(2,1)S(1)}, f32[4,384]{1,0:T(4,128)S(1)}) custom-call(s32[14]{0:T(128)S(1)} %pad_add_fusion.place_ref, s32[12,3]{1,0:T(8,128)S(1)} %copy.26.own_mask_ref, s32[12,3]{1,0:T(8,128)S(1)} %collective-permute-done.1.other_mask_ref, ...), custom_call_target="tpu_custom_call" | custom-call | flops 7096762368 | bytes 20971520 | tf_op jit(solution)/shard_map/attn_backward/pallas_call | solution.py:396
  86.0 4.9 %all-to-all-start.2 = ((bf16[4,2,48,384]{3,2,1,0:T(8,128)(2,1)}), bf16[4,2,48,384]{3,2,1,0:T(8,128)(2,1)S(1)}, u32[]{:S(2)}, u32[]{:S(2)}) async-start(bf16[4,2,48,384]{3,2,1,0:T(8,128)(2,1)} %sum_late.1), calls=%async_computation.2 | async-start | bytes 589824 | tf_op jit(solution)/shard_map/all_to_all | solution.py:753
  91.7 1.2 collective-permute-start.21
  93.7 1.6 %collective-permute-start.23 = (bf16[200,384]{1,0:T(8,128)(2,1)S(1)}, bf16[200,384]{1,0:T(8,128)(2,1)S(1)}, u32[]{:S(2)}, u32[]{:S(2)}) collective-permute-start(bf16[200,384]{1,0:T(8,128)(2,1)S(1)} %get-tuple-element.119), channel_id=1, source_target_pairs={{0,6},{2,4},{4,2},{6,0},{1,7},{3,5},{5,3},{7,1},{8,14},{10,12},{12... | collective-permute-start | bytes 460808 | tf_op jit(solution)/shard_map/ppermute | solution.py:758
  95.2 6.6 %input_gradient.1 = f32[1536,384]{1,0:T(8,128)} custom-call(bf16[1536,384]{1,0:T(8,128)(2,1)} %x_ref.5, f32[1536,384]{1,0:T(8,128)} %get-tuple-element.94.grad_ref, bf16[1536,1152]{1,0:T(8,128)(2,1)} %get-tuple-element.120.dqkv_ref, f32[4,384]{1,0:T(4,128)} %refs_4_.1, bf16[384,1152]{1,0:T(8,128)(2,1)} %get-tuple-element.99.wqkv_ref), custom_call_target="tpu_custom_call" | custom-call | flops 1358954496 | bytes 10485760 | tf_op jit(solution)/shard_map/input_gradient/pallas_call | solution.py:452
  102.7 5.0 %all-to-all-start.3 = ((bf16[4,56,384]{2,1,0:T(8,128)(2,1)}), bf16[4,56,384]{2,1,0:T(8,128)(2,1)S(1)}, u32[]{:S(2)}, u32[]{:S(2)}) async-start(bf16[4,56,384]{2,1,0:T(8,128)(2,1)} %join.1), calls=%async_computation.3 | async-start | bytes 344064 | tf_op jit(solution)/shard_map/all_to_all | solution.py:753
  107.7 8.0 %shampoo.2 = (f32[3,8,48,48]{3,2,1,0:T(8,128)}, f32[3,8,48,48]{3,2,1,0:T(8,128)}, f32[3,8,48,48]{3,2,1,0:T(8,128)}, f32[3,8,48,48]{3,2,1,0:T(8,128)}) custom-call(bf16[4,2,48,384]{3,2,1,0:T(8,128)(2,1)S(1)} %all-to-all-done.2.refs_0_, f32[3,8,48,48]{3,2,1,0:T(8,128)S(1)} %bitcast.15, f32[3,8,48,48]{3,2,1,0:T(8,128)S(1)} %bitcast.18, ...), custom_call_target="tpu_custom_call" | custom-call | flops 6442450944 | bytes 4194304 | tf_op jit(solution)/shard_map/shampoo/pallas_call | solution.py:724
  115.7 5.8 %shampoo.3 = (f32[3,8,48,48]{3,2,1,0:T(8,128)}, f32[3,8,48,48]{3,2,1,0:T(8,128)}, f32[3,8,48,48]{3,2,1,0:T(8,128)}, f32[3,8,48,48]{3,2,1,0:T(8,128)}, f32[4,384]...) custom-call(bf16[4,1,56,384]{3,2,1,0:T(8,128)(2,1)S(1)} %bitcast.17,, ...), custom_call_target="tpu_custom_call", output_to_operand_aliasing={{0}: (6, {}), {1}: (7, {}), {2}: (8, {}), {3}: (9, {})} | custom-call | flops 3221225472 | bytes 4194304 | tf_op jit(solution)/shard_map/shampoo/pallas_call | solution.py:724
  (66 shorter events, 10.8 us)
Async XLA Ops:
  2.5 12.6 %all-to-all-start = ((bf16[4,48,384]{2,1,0:T(8,128)(2,1)}), bf16[4,48,384]{2,1,0:T(8,128)(2,1)S(1)}, u32[]{:S(2)}, u32[]{:S(2)}) async-start(bf16[4,48,384]{2,1,0:T(8,128)(2,1)} %broadcast_in_dim.23), calls=%async_computation | async-start | bytes 294912 | tf_op jit(solution)/shard_map/all_to_all | solution.py:753
  15.0 12.0 %all-to-all-start.1 = ((bf16[4,2,48,384]{3,2,1,0:T(8,128)(2,1)}), bf16[4,2,48,384]{3,2,1,0:T(8,128)(2,1)S(1)}, u32[]{:S(2)}, u32[]{:S(2)}) async-start(bf16[4,2,48,384]{3,2,1,0:T(8,128)(2,1)} %pack.1), calls=%async_computation.1 | async-start | bytes 589824 | tf_op jit(solution)/shard_map/all_to_all | solution.py:753
  18.5 7.6 %collective-permute-start.6 = (bf16[4,48,384]{2,1,0:T(8,128)(2,1)S(1)}, bf16[4,48,384]{2,1,0:T(8,128)(2,1)S(1)}, u32[]{:S(2)}, u32[]{:S(2)}) collective-permute-start(bf16[4,48,384]{2,1,0:T(8,128)(2,1)S(1)} %all-to-all-done.refs_0_), channel_id=1, source_target_pairs={{0,6},{2,4},{4,2},{6,0},{1,7},{3,5},{5,3},{7,1},{8,14},{10,12},{12... | collective-permute-start | bytes 442376 | tf_op jit(solution)/shard_map/ppermute | solution.py:758
  21.0 6.0 %collective-permute-start.5 = (bf16[4,48,384]{2,1,0:T(8,128)(2,1)S(1)}, bf16[4,48,384]{2,1,0:T(8,128)(2,1)S(1)}, u32[]{:S(2)}, u32[]{:S(2)}) collective-permute-start(bf16[4,48,384]{2,1,0:T(8,128)(2,1)S(1)} %all-to-all-done.refs_0_), channel_id=1, source_target_pairs={{0,4},{2,6},{4,0},{6,2},{1,5},{3,7},{5,1},{7,3},{8,12},{10,14},{12... | collective-permute-start | bytes 442376 | tf_op jit(solution)/shard_map/ppermute | solution.py:758
  21.5 5.5 %collective-permute-start = (bf16[4,48,384]{2,1,0:T(8,128)(2,1)S(1)}, bf16[4,48,384]{2,1,0:T(8,128)(2,1)S(1)}, u32[]{:S(2)}, u32[]{:S(2)}) collective-permute-start(bf16[4,48,384]{2,1,0:T(8,128)(2,1)S(1)} %all-to-all-done.refs_0_), channel_id=1, source_target_pairs={{0,2},{2,0},{4,6},{6,4},{1,3},{3,1},{5,7},{7,5},{8,10},{10,8},{12,... | collective-permute-start | bytes 442376 | tf_op jit(solution)/shard_map/ppermute | solution.py:758
  22.1 4.8 %collective-permute-start.1 = (s32[12,3]{1,0:T(8,128)S(1)}, s32[12,3]{1,0:T(8,128)S(1)}, u32[]{:S(2)}, u32[]{:S(2)}) collective-permute-start(s32[12,3]{1,0:T(8,128)S(1)} %copy.26.own_mask_ref), channel_id=1, source_target_pairs={{0,1},{1,0},{2,3},{3,2},{4,5},{5,4},{6,7},{7,6},{8,9},{9,8},{10,11... | collective-permute-start | bytes 440 | tf_op jit(solution)/shard_map/ppermute | solution.py:749
  22.2 5.4 %collective-permute-start.7 = (bf16[4,48,384]{2,1,0:T(8,128)(2,1)S(1)}, bf16[4,48,384]{2,1,0:T(8,128)(2,1)S(1)}, u32[]{:S(2)}, u32[]{:S(2)}) collective-permute-start(bf16[4,48,384]{2,1,0:T(8,128)(2,1)S(1)} %all-to-all-done.refs_0_), channel_id=1, source_target_pairs={{0,1},{1,0},{2,3},{3,2},{4,5},{5,4},{6,7},{7,6},{8,9},{9,8},{10,11... | collective-permute-start | bytes 442376 | tf_op jit(solution)/shard_map/ppermute | solution.py:749
  26.1 3.9 %collective-permute-start.10 = (bf16[4,48,384]{2,1,0:T(8,128)(2,1)S(1)}, bf16[4,48,384]{2,1,0:T(8,128)(2,1)S(1)}, u32[]{:S(2)}, u32[]{:S(2)}) collective-permute-start(bf16[4,48,384]{2,1,0:T(8,128)(2,1)S(1)} %collective-permute-done.6.refs_3_), channel_id=1, source_target_pairs={{0,1},{1,0},{2,3},{3,2},{4,5},{5,4},{6,7},{7,6},{8,9},{9,8},{10,11... | collective-permute-start | bytes 442376 | tf_op jit(solution)/shard_map/ppermute | solution.py:749
  26.9 3.6 %collective-permute-start.9 = (bf16[4,48,384]{2,1,0:T(8,128)(2,1)S(1)}, bf16[4,48,384]{2,1,0:T(8,128)(2,1)S(1)}, u32[]{:S(2)}, u32[]{:S(2)}) collective-permute-start(bf16[4,48,384]{2,1,0:T(8,128)(2,1)S(1)} %collective-permute-done.5.refs_2_), channel_id=1, source_target_pairs={{0,1},{1,0},{2,3},{3,2},{4,5},{5,4},{6,7},{7,6},{8,9},{9,8},{10,11... | collective-permute-start | bytes 442376 | tf_op jit(solution)/shard_map/ppermute | solution.py:749
  27.0 4.1 %collective-permute-start.8 = (bf16[4,48,384]{2,1,0:T(8,128)(2,1)S(1)}, bf16[4,48,384]{2,1,0:T(8,128)(2,1)S(1)}, u32[]{:S(2)}, u32[]{:S(2)}) collective-permute-start(bf16[4,48,384]{2,1,0:T(8,128)(2,1)S(1)} %collective-permute-done.refs_1_), channel_id=1, source_target_pairs={{0,1},{1,0},{2,3},{3,2},{4,5},{5,4},{6,7},{7,6},{8,9},{9,8},{10,11... | collective-permute-start | bytes 442376 | tf_op jit(solution)/shard_map/ppermute | solution.py:749
  27.5 17.2 %collective-permute-start.11 = (bf16[4,2,48,384]{3,2,1,0:T(8,128)(2,1)S(1)}, bf16[4,2,48,384]{3,2,1,0:T(8,128)(2,1)S(1)}, u32[]{:S(2)}, u32[]{:S(2)}) collective-permute-start(bf16[4,2,48,384]{3,2,1,0:T(8,128)(2,1)S(1)} %all-to-all-done.1.refs_0_), channel_id=1, source_target_pairs={{0,1},{1,0},{2,3},{3,2},{4,5},{5,4},{6,7},{7,6},{8,9},{9,8},{10,11... | collective-permute-start | bytes 884744 | tf_op jit(solution)/shard_map/ppermute | solution.py:749
  27.6 15.1 %collective-permute-start.4 = (bf16[4,2,48,384]{3,2,1,0:T(8,128)(2,1)S(1)}, bf16[4,2,48,384]{3,2,1,0:T(8,128)(2,1)S(1)}, u32[]{:S(2)}, u32[]{:S(2)}) collective-permute-start(bf16[4,2,48,384]{3,2,1,0:T(8,128)(2,1)S(1)} %all-to-all-done.1.refs_0_), channel_id=1, source_target_pairs={{0,6},{2,4},{4,2},{6,0},{1,7},{3,5},{5,3},{7,1},{8,14},{10,12},{12... | collective-permute-start | bytes 884744 | tf_op jit(solution)/shard_map/ppermute | solution.py:758
  30.0 14.2 %collective-permute-start.3 = (bf16[4,2,48,384]{3,2,1,0:T(8,128)(2,1)S(1)}, bf16[4,2,48,384]{3,2,1,0:T(8,128)(2,1)S(1)}, u32[]{:S(2)}, u32[]{:S(2)}) collective-permute-start(bf16[4,2,48,384]{3,2,1,0:T(8,128)(2,1)S(1)} %all-to-all-done.1.refs_0_), channel_id=1, source_target_pairs={{0,4},{2,6},{4,0},{6,2},{1,5},{3,7},{5,1},{7,3},{8,12},{10,14},{12... | collective-permute-start | bytes 884744 | tf_op jit(solution)/shard_map/ppermute | solution.py:758
  30.5 13.7 %collective-permute-start.2 = (bf16[4,2,48,384]{3,2,1,0:T(8,128)(2,1)S(1)}, bf16[4,2,48,384]{3,2,1,0:T(8,128)(2,1)S(1)}, u32[]{:S(2)}, u32[]{:S(2)}) collective-permute-start(bf16[4,2,48,384]{3,2,1,0:T(8,128)(2,1)S(1)} %all-to-all-done.1.refs_0_), channel_id=1, source_target_pairs={{0,2},{2,0},{4,6},{6,4},{1,3},{3,1},{5,7},{7,5},{8,10},{10,8},{12,... | collective-permute-start | bytes 884744 | tf_op jit(solution)/shard_map/ppermute | solution.py:758
  65.0 3.3 %collective-permute-start.17 = (bf16[2,4,2,48,384]{4,3,2,1,0:T(8,128)(2,1)S(1)}, bf16[2,4,2,48,384]{4,3,2,1,0:T(8,128)(2,1)S(1)}, u32[]{:S(2)}, u32[]{:S(2)}) collective-permute-start(bf16[2,4,2,48,384]{4,3,2,1,0:T(8,128)(2,1)S(1)} %get-tuple-element.105), channel_id=1, source_target_pairs={{0,1},{1,0},{2,3},{3,2},{4,5},{5,4},{6,7},{7,6},{8,9},{9,8},{10,11... | collective-permute-start | bytes 1769480 | tf_op jit(solution)/shard_map/ppermute | solution.py:749
  67.0 17.9 %collective-permute-start.16 = (bf16[4,2,48,384]{3,2,1,0:T(8,128)(2,1)S(1)}, bf16[4,2,48,384]{3,2,1,0:T(8,128)(2,1)S(1)}, u32[]{:S(2)}, u32[]{:S(2)}) collective-permute-start(bf16[4,2,48,384]{3,2,1,0:T(8,128)(2,1)S(1)} %get-tuple-element.103), channel_id=1, source_target_pairs={{0,2},{2,0},{4,6},{6,4},{1,3},{3,1},{5,7},{7,5},{8,10},{10,8},{12,... | collective-permute-start | bytes 884744 | tf_op jit(solution)/shard_map/ppermute | solution.py:758
  68.5 16.5 %collective-permute-start.18 = (bf16[4,2,48,384]{3,2,1,0:T(8,128)(2,1)S(1)}, bf16[4,2,48,384]{3,2,1,0:T(8,128)(2,1)S(1)}, u32[]{:S(2)}, u32[]{:S(2)}) collective-permute-start(bf16[4,2,48,384]{3,2,1,0:T(8,128)(2,1)S(1)} %get-tuple-element.106), channel_id=1, source_target_pairs={{0,4},{2,6},{4,0},{6,2},{1,5},{3,7},{5,1},{7,3},{8,12},{10,14},{12... | collective-permute-start | bytes 884744 | tf_op jit(solution)/shard_map/ppermute | solution.py:758
  69.6 15.4 %collective-permute-start.19 = (bf16[4,2,48,384]{3,2,1,0:T(8,128)(2,1)S(1)}, bf16[4,2,48,384]{3,2,1,0:T(8,128)(2,1)S(1)}, u32[]{:S(2)}, u32[]{:S(2)}) collective-permute-start(bf16[4,2,48,384]{3,2,1,0:T(8,128)(2,1)S(1)} %get-tuple-element.107), channel_id=1, source_target_pairs={{0,6},{2,4},{4,2},{6,0},{1,7},{3,5},{5,3},{7,1},{8,14},{10,12},{12... | collective-permute-start | bytes 884744 | tf_op jit(solution)/shard_map/ppermute | solution.py:758
  85.0 5.9 %collective-permute-start.20 = (bf16[17,48,384]{2,1,0:T(8,128)(2,1)S(1)}, bf16[17,48,384]{2,1,0:T(8,128)(2,1)S(1)}, u32[]{:S(2)}, u32[]{:S(2)}) collective-permute-start(bf16[17,48,384]{2,1,0:T(8,128)(2,1)S(1)} %get-tuple-element.109), channel_id=1, source_target_pairs={{0,1},{1,0},{2,3},{3,2},{4,5},{5,4},{6,7},{7,6},{8,9},{9,8},{10,11... | collective-permute-start | bytes 1880072 | tf_op jit(solution)/shard_map/ppermute | solution.py:749
  86.0 16.7 %all-to-all-start.2 = ((bf16[4,2,48,384]{3,2,1,0:T(8,128)(2,1)}), bf16[4,2,48,384]{3,2,1,0:T(8,128)(2,1)S(1)}, u32[]{:S(2)}, u32[]{:S(2)}) async-start(bf16[4,2,48,384]{3,2,1,0:T(8,128)(2,1)} %sum_late.1), calls=%async_computation.2 | async-start | bytes 589824 | tf_op jit(solution)/shard_map/all_to_all | solution.py:753
  91.7 10.2 %collective-permute-start.21 = (bf16[200,384]{1,0:T(8,128)(2,1)S(1)}, bf16[200,384]{1,0:T(8,128)(2,1)S(1)}, u32[]{:S(2)}, u32[]{:S(2)}) collective-permute-start(bf16[200,384]{1,0:T(8,128)(2,1)S(1)} %get-tuple-element.117), channel_id=1, source_target_pairs={{0,2},{2,0},{4,6},{6,4},{1,3},{3,1},{5,7},{7,5},{8,10},{10,8},{12,... | collective-permute-start | bytes 460808 | tf_op jit(solution)/shard_map/ppermute | solution.py:758
  92.8 9.1 %collective-permute-start.22 = (bf16[200,384]{1,0:T(8,128)(2,1)S(1)}, bf16[200,384]{1,0:T(8,128)(2,1)S(1)}, u32[]{:S(2)}, u32[]{:S(2)}) collective-permute-start(bf16[200,384]{1,0:T(8,128)(2,1)S(1)} %get-tuple-element.118), channel_id=1, source_target_pairs={{0,4},{2,6},{4,0},{6,2},{1,5},{3,7},{5,1},{7,3},{8,12},{10,14},{12... | collective-permute-start | bytes 460808 | tf_op jit(solution)/shard_map/ppermute | solution.py:758
  93.7 8.3 %collective-permute-start.23 = (bf16[200,384]{1,0:T(8,128)(2,1)S(1)}, bf16[200,384]{1,0:T(8,128)(2,1)S(1)}, u32[]{:S(2)}, u32[]{:S(2)}) collective-permute-start(bf16[200,384]{1,0:T(8,128)(2,1)S(1)} %get-tuple-element.119), channel_id=1, source_target_pairs={{0,6},{2,4},{4,2},{6,0},{1,7},{3,5},{5,3},{7,1},{8,14},{10,12},{12... | collective-permute-start | bytes 460808 | tf_op jit(solution)/shard_map/ppermute | solution.py:758
  102.7 13.0 %all-to-all-start.3 = ((bf16[4,56,384]{2,1,0:T(8,128)(2,1)}), bf16[4,56,384]{2,1,0:T(8,128)(2,1)S(1)}, u32[]{:S(2)}, u32[]{:S(2)}) async-start(bf16[4,56,384]{2,1,0:T(8,128)(2,1)} %join.1), calls=%async_computation.3 | async-start | bytes 344064 | tf_op jit(solution)/shard_map/all_to_all | solution.py:753
  (12 other events, 120.5 us)

commit v14 on v13

--- a/solution.py
+++ b/solution.py
@@ -201,7 +201,7 @@
             flops=rows * D * (8 * D + 16 * S), bytes_accessed=16 << 20, transcendentals=rows * 6 * S
         ),
         name="attn_forward",
-    )(place, own_mask, other_mask, in_hbm(tokens), in_hbm(norm_params), *slabs)
+    )(place, own_mask, other_mask, tokens, in_hbm(norm_params), *slabs)
 
 
 def mlp_kernel(place_ref, middle_ref, rows_ref, cot_ref, norm_ref, *refs):
@@ -299,7 +299,7 @@
             flops=12 * rows * D * MLP, bytes_accessed=20 << 20, transcendentals=2 * rows * MLP
         ),
         name="mlp",
-    )(place, middle, second_rows, *map(in_hbm, (cotangent, norm_params)), *slabs)
+    )(place, middle, second_rows, cotangent, in_hbm(norm_params), *slabs)
 
 
 def attn_backward_kernel(
@@ -434,7 +434,7 @@
         name="attn_backward",
     )(
         place, own_mask, other_mask,
-        in_hbm(tokens), in_hbm(grad), *map(in_hbm, (prob, qkv, out, norm_params, later_norms)), in_hbm(wqkv), in_hbm(wo),
+        tokens, in_hbm(grad), prob, qkv, out, in_hbm(norm_params), in_hbm(later_norms), wqkv, wo,
     )
 
 
@@ -763,9 +763,7 @@
 
 
 def gather_slabs(weights, small):
-    _, count, edge, _ = weights.shape
-    early = weights[0].astype(BF).transpose(1, 0, 2).reshape(1, edge, count * edge)
-    early = to_all(jnp.broadcast_to(early, (OUTER, edge, count * edge)), "outer")
+    early = to_all(pack(weights, 0, 1), "outer")[:, 0]
     early, late = lax.optimization_barrier((early, pack(weights, 1, 2)))
     late = to_all(late, "outer")
     early = from_all(early)

time: 122 us -> 121 us (level)
  local copies, waits for them, and re-layouts: 1.92 us -> 0.17 us
    pallas_call x1 -> x2, Pallas kernels: 1.83 us -> 3.61 us  [pack(): pl.pallas_call(pack_kernel, grid=(1,), in_specs=[pl.BlockSpec((pl.Element...]
where the time goes in v14:
time: 121 us; the launch traced here: 120 us
  Pallas kernels  70 us (58%)
  starting transfers between devices  36.2 us (30%)
  waiting for transfers between devices  13.1 us (11%)
    all_to_all x4, starting transfers between devices, to_all(): return lax.all_to_all(values, axis, 0, 0)  19.7 us
    pallas_call x1, Pallas kernels, mlp(): pl.pallas_call(mlp_kernel, grid=(rows // TILE,), in_specs=[pl.BlockSpec(m...  18.1 us
    ppermute x12, starting transfers between devices, across(): return lax.ppermute(values, 'inner', pairs)  14.2 us
    pallas_call x2, Pallas kernels, shampoo(): pl.pallas_call(lambda *refs: shampoo_kernel(scale, bool(norms), *refs), g...  13.8 us
    pallas_call x1, Pallas kernels, attn_backward(): pl.pallas_call(attn_backward_kernel, grid=(rows // TILE,), in_specs=[smem...  13.1 us
    pallas_call x1, Pallas kernels, attn_forward(): pl.pallas_call(attn_forward_kernel, grid=(rows // TILE,), in_specs=[smem]...  12.2 us
    pallas_call x1, Pallas kernels, input_gradient(): pl.pallas_call(input_grad_kernel, grid=(rows // INPUT_TILE,), in_specs=[t...  6.62 us
    ppermute x12, waiting for transfers between devices, across(): return lax.ppermute(values, 'inner', pairs)  5.16 us
  transfers between devices with their start and end apart: 28, of which 10 were waited for; matrix products, arithmetic and copies ran while one was open for 0% of the time, Pallas kernels for 37%

profile of v14, /device:TPU:0, one launch (start us, length us, event | category | flops | bytes accessed | tf_op | source)
XLA Modules:
  0.0 120.4 jit_solution(5085194522496587710)
XLA Ops:
  0.7 1.8 %pack.2 = bf16[4,1,48,384]{3,2,1,0:T(8,128)(2,1)} custom-call(f32[3,8,48,48]{3,2,1,0:T(8,128)} %bitcast.11), custom_call_target="tpu_custom_call" | custom-call | tf_op jit(solution)/shard_map/pack/pallas_call | solution.py:484
  2.5 6.3 %all-to-all-start = ((bf16[4,1,48,384]{3,2,1,0:T(8,128)(2,1)}), bf16[4,1,48,384]{3,2,1,0:T(8,128)(2,1)S(1)}, u32[]{:S(2)}, u32[]{:S(2)}) async-start(bf16[4,1,48,384]{3,2,1,0:T(8,128)(2,1)} %pack.2), calls=%async_computation | async-start | bytes 294912 | tf_op jit(solution)/shard_map/all_to_all | solution.py:753
  8.8 1.8 %pack.3 = bf16[4,2,48,384]{3,2,1,0:T(8,128)(2,1)} custom-call(f32[3,8,48,48]{3,2,1,0:T(8,128)} %bitcast.12), custom_call_target="tpu_custom_call" | custom-call | tf_op jit(solution)/shard_map/pack/pallas_call | solution.py:484
  10.6 4.4 %all-to-all-done = bf16[4,1,48,384]{3,2,1,0:T(8,128)(2,1)S(1)} async-done(((bf16[4,1,48,384]{3,2,1,0:T(8,128)(2,1)}), bf16[4,1,48,384]{3,2,1,0:T(8,128)(2,1)S(1)}, u32[]{:S(2)}, u32[]{:S(2)}) %all-to-all-start) | async-done | bytes 147488 | tf_op jit(solution)/shard_map/all_to_all | solution.py:753
  15.0 3.5 %all-to-all-start.1 = ((bf16[4,2,48,384]{3,2,1,0:T(8,128)(2,1)}), bf16[4,2,48,384]{3,2,1,0:T(8,128)(2,1)S(1)}, u32[]{:S(2)}, u32[]{:S(2)}) async-start(bf16[4,2,48,384]{3,2,1,0:T(8,128)(2,1)} %pack.3), calls=%async_computation.1 | async-start | bytes 589824 | tf_op jit(solution)/shard_map/all_to_all | solution.py:753
  18.5 2.5 %collective-permute-start.6 = (bf16[4,48,384]{2,1,0:T(8,128)(2,1)S(1)}, bf16[4,48,384]{2,1,0:T(8,128)(2,1)S(1)}, u32[]{:S(2)}, u32[]{:S(2)}) collective-permute-start(bf16[4,48,384]{2,1,0:T(8,128)(2,1)S(1)} %bitcast.16), channel_id=1, source_target_pairs={{0,6},{2,4},{4,2},{6,0},{1,7},{3,5},{5,3},{7,1},{8,14},{10,12},{12... | collective-permute-start | bytes 442376 | tf_op jit(solution)/shard_map/ppermute | solution.py:758
  22.7 3.4 %collective-permute-done.6.refs_3_ = bf16[4,48,384]{2,1,0:T(8,128)(2,1)S(1)} collective-permute-done((bf16[4,48,384]{2,1,0:T(8,128)(2,1)S(1)}, bf16[4,48,384]{2,1,0:T(8,128)(2,1)S(1)}, u32[]{:S(2)}, u32[]{:S(2)}) %collective-permute-start.6) | collective-permute-done | bytes 147488 | tf_op jit(solution)/shard_map/ppermute | solution.py:758
  27.6 2.4 %collective-permute-start.4 = (bf16[4,2,48,384]{3,2,1,0:T(8,128)(2,1)S(1)}, bf16[4,2,48,384]{3,2,1,0:T(8,128)(2,1)S(1)}, u32[]{:S(2)}, u32[]{:S(2)}) collective-permute-start(bf16[4,2,48,384]{3,2,1,0:T(8,128)(2,1)S(1)} %all-to-all-done.1.refs_0_), channel_id=1, source_target_pairs={{0,6},{2,4},{4,2},{6,0},{1,7},{3,5},{5,3},{7,1},{8,14},{10,12},{12... | collective-permute-start | bytes 884744 | tf_op jit(solution)/shard_map/ppermute | solution.py:758
  31.1 12.2 %attn_forward.1 = (bf16[6,3,512,256]{3,2,1,0:T(8,128)(2,1)}, bf16[1536,1152]{1,0:T(8,128)(2,1)}, bf16[1536,384]{1,0:T(8,128)(2,1)}, f32[1536,384]{1,0:T(8,128)S(...) custom-call(s32[14]{0:T(128)S(1)} %pad_add_fusion.place_ref, ...), custom_call_target="tpu_custom_call" | custom-call | flops 4227858432 | bytes 16777216 | tf_op jit(solution)/shard_map/attn_forward/pallas_call | solution.py:176
  44.7 1.1 collective-permute-done.12.refs_5_
  46.6 18.1 %mlp.1 = (f32[1536,384]{1,0:T(8,128)}, f32[1536,384]{1,0:T(8,128)}, f32[2,384]{1,0:T(2,128)S(1)}, bf16[2,4,2,48,384]{4,3,2,1,0:T(8,128)(2,1)S(1)}, bf16[2,4,2,48...) custom-call(s32[14]{0:T(128)S(1)} %pad_add_fusion.place_ref, ...), custom_call_target="tpu_custom_call" | custom-call | flops 10871635968 | bytes 20971520 | tf_op jit(solution)/shard_map/mlp/pallas_call | solution.py:273
  65.3 1.5 %collective-permute-done.15.received_ref = bf16[2,4,2,48,384]{4,3,2,1,0:T(8,128)(2,1)S(1)} collective-permute-done((bf16[2,4,2,48,384]{4,3,2,1,0:T(8,128)(2,1)S(1)}, bf16[2,4,2,48,384]{4,3,2,1,0:T(8,128)(2,1)S(1)}, u32[]{:S(2)}, u32[]{:S(2)}) %collective-permute-start.15) | collective-permute-done | bytes 589856 | tf_op jit(solution)/shard_map/ppermute | solution.py:749
  66.9 1.3 %collective-permute-start.16 = (bf16[4,2,48,384]{3,2,1,0:T(8,128)(2,1)S(1)}, bf16[4,2,48,384]{3,2,1,0:T(8,128)(2,1)S(1)}, u32[]{:S(2)}, u32[]{:S(2)}) collective-permute-start(bf16[4,2,48,384]{3,2,1,0:T(8,128)(2,1)S(1)} %get-tuple-element.103), channel_id=1, source_target_pairs={{0,2},{2,0},{4,6},{6,4},{1,3},{3,1},{5,7},{7,5},{8,10},{10,8},{12,... | collective-permute-start | bytes 884744 | tf_op jit(solution)/shard_map/ppermute | solution.py:758
  68.4 1.1 collective-permute-start.18
  69.5 1.2 collective-permute-start.19
  70.8 13.1 %attn_backward.1 = (bf16[1536,1152]{1,0:T(8,128)(2,1)}, bf16[16,48,384]{2,1,0:T(8,128)(2,1)S(1)}, bf16[17,48,384]{2,1,0:T(8,128)(2,1)}, f32[4,384]{1,0:T(4,128)S(1)}) custom-call(s32[14]{0:T(128)S(1)} %pad_add_fusion.place_ref, s32[12,3]{1,0:T(8,128)S(1)} %copy.26.own_mask_ref, s32[12,3]{1,0:T(8,128)S(1)} %collective-permute-done.1.other_mask_ref, ...), custom_call_target="tpu_custom_call" | custom-call | flops 7096762368 | bytes 20971520 | tf_op jit(solution)/shard_map/attn_backward/pallas_call | solution.py:396
  84.0 0.9 sum_late.1
  84.8 4.9 %all-to-all-start.2 = ((bf16[4,2,48,384]{3,2,1,0:T(8,128)(2,1)}), bf16[4,2,48,384]{3,2,1,0:T(8,128)(2,1)S(1)}, u32[]{:S(2)}, u32[]{:S(2)}) async-start(bf16[4,2,48,384]{3,2,1,0:T(8,128)(2,1)} %sum_late.1), calls=%async_computation.2 | async-start | bytes 589824 | tf_op jit(solution)/shard_map/all_to_all | solution.py:753
  90.5 1.2 collective-permute-start.21
  92.5 1.6 %collective-permute-start.23 = (bf16[200,384]{1,0:T(8,128)(2,1)S(1)}, bf16[200,384]{1,0:T(8,128)(2,1)S(1)}, u32[]{:S(2)}, u32[]{:S(2)}) collective-permute-start(bf16[200,384]{1,0:T(8,128)(2,1)S(1)} %get-tuple-element.119), channel_id=1, source_target_pairs={{0,6},{2,4},{4,2},{6,0},{1,7},{3,5},{5,3},{7,1},{8,14},{10,12},{12... | collective-permute-start | bytes 460808 | tf_op jit(solution)/shard_map/ppermute | solution.py:758
  94.1 6.6 %input_gradient.1 = f32[1536,384]{1,0:T(8,128)} custom-call(bf16[1536,384]{1,0:T(8,128)(2,1)} %x_ref.5, f32[1536,384]{1,0:T(8,128)} %get-tuple-element.94.grad_ref, bf16[1536,1152]{1,0:T(8,128)(2,1)} %get-tuple-element.120.dqkv_ref, f32[4,384]{1,0:T(4,128)} %refs_4_.1, bf16[384,1152]{1,0:T(8,128)(2,1)} %get-tuple-element.99.wqkv_ref), custom_call_target="tpu_custom_call" | custom-call | flops 1358954496 | bytes 10485760 | tf_op jit(solution)/shard_map/input_gradient/pallas_call | solution.py:452
  101.6 5.0 %all-to-all-start.3 = ((bf16[4,56,384]{2,1,0:T(8,128)(2,1)}), bf16[4,56,384]{2,1,0:T(8,128)(2,1)S(1)}, u32[]{:S(2)}, u32[]{:S(2)}) async-start(bf16[4,56,384]{2,1,0:T(8,128)(2,1)} %join.1), calls=%async_computation.3 | async-start | bytes 344064 | tf_op jit(solution)/shard_map/all_to_all | solution.py:753
  106.6 8.0 %shampoo.2 = (f32[3,8,48,48]{3,2,1,0:T(8,128)}, f32[3,8,48,48]{3,2,1,0:T(8,128)}, f32[3,8,48,48]{3,2,1,0:T(8,128)}, f32[3,8,48,48]{3,2,1,0:T(8,128)}) custom-call(bf16[4,2,48,384]{3,2,1,0:T(8,128)(2,1)S(1)} %all-to-all-done.2.refs_0_, f32[3,8,48,48]{3,2,1,0:T(8,128)S(1)} %bitcast.13, f32[3,8,48,48]{3,2,1,0:T(8,128)S(1)} %bitcast.21, ...), custom_call_target="tpu_custom_call" | custom-call | flops 6442450944 | bytes 4194304 | tf_op jit(solution)/shard_map/shampoo/pallas_call | solution.py:724
  114.6 5.8 %shampoo.3 = (f32[3,8,48,48]{3,2,1,0:T(8,128)}, f32[3,8,48,48]{3,2,1,0:T(8,128)}, f32[3,8,48,48]{3,2,1,0:T(8,128)}, f32[3,8,48,48]{3,2,1,0:T(8,128)}, f32[4,384]...) custom-call(bf16[4,1,56,384]{3,2,1,0:T(8,128)(2,1)S(1)} %bitcast.15,, ...), custom_call_target="tpu_custom_call", output_to_operand_aliasing={{0}: (6, {}), {1}: (7, {}), {2}: (8, {}), {3}: (9, {})} | custom-call | flops 3221225472 | bytes 4194304 | tf_op jit(solution)/shard_map/shampoo/pallas_call | solution.py:724
  (80 shorter events, 10.0 us)
Async XLA Ops:
  2.5 12.6 %all-to-all-start = ((bf16[4,1,48,384]{3,2,1,0:T(8,128)(2,1)}), bf16[4,1,48,384]{3,2,1,0:T(8,128)(2,1)S(1)}, u32[]{:S(2)}, u32[]{:S(2)}) async-start(bf16[4,1,48,384]{3,2,1,0:T(8,128)(2,1)} %pack.2), calls=%async_computation | async-start | bytes 294912 | tf_op jit(solution)/shard_map/all_to_all | solution.py:753
  15.0 12.0 %all-to-all-start.1 = ((bf16[4,2,48,384]{3,2,1,0:T(8,128)(2,1)}), bf16[4,2,48,384]{3,2,1,0:T(8,128)(2,1)S(1)}, u32[]{:S(2)}, u32[]{:S(2)}) async-start(bf16[4,2,48,384]{3,2,1,0:T(8,128)(2,1)} %pack.3), calls=%async_computation.1 | async-start | bytes 589824 | tf_op jit(solution)/shard_map/all_to_all | solution.py:753
  18.5 7.6 %collective-permute-start.6 = (bf16[4,48,384]{2,1,0:T(8,128)(2,1)S(1)}, bf16[4,48,384]{2,1,0:T(8,128)(2,1)S(1)}, u32[]{:S(2)}, u32[]{:S(2)}) collective-permute-start(bf16[4,48,384]{2,1,0:T(8,128)(2,1)S(1)} %bitcast.16), channel_id=1, source_target_pairs={{0,6},{2,4},{4,2},{6,0},{1,7},{3,5},{5,3},{7,1},{8,14},{10,12},{12... | collective-permute-start | bytes 442376 | tf_op jit(solution)/shard_map/ppermute | solution.py:758
  21.0 6.0 %collective-permute-start.5 = (bf16[4,48,384]{2,1,0:T(8,128)(2,1)S(1)}, bf16[4,48,384]{2,1,0:T(8,128)(2,1)S(1)}, u32[]{:S(2)}, u32[]{:S(2)}) collective-permute-start(bf16[4,48,384]{2,1,0:T(8,128)(2,1)S(1)} %bitcast.17), channel_id=1, source_target_pairs={{0,4},{2,6},{4,0},{6,2},{1,5},{3,7},{5,1},{7,3},{8,12},{10,14},{12... | collective-permute-start | bytes 442376 | tf_op jit(solution)/shard_map/ppermute | solution.py:758
  21.5 5.5 %collective-permute-start = (bf16[4,48,384]{2,1,0:T(8,128)(2,1)S(1)}, bf16[4,48,384]{2,1,0:T(8,128)(2,1)}, u32[]{:S(2)}, u32[]{:S(2)}) collective-permute-start(bf16[4,48,384]{2,1,0:T(8,128)(2,1)S(1)} %bitcast.18), channel_id=1, source_target_pairs={{0,2},{2,0},{4,6},{6,4},{1,3},{3,1},{5,7},{7,5},{8,10},{10,8},{12,... | collective-permute-start | bytes 442376 | tf_op jit(solution)/shard_map/ppermute | solution.py:758
  22.1 4.8 %collective-permute-start.1 = (s32[12,3]{1,0:T(8,128)S(1)}, s32[12,3]{1,0:T(8,128)S(1)}, u32[]{:S(2)}, u32[]{:S(2)}) collective-permute-start(s32[12,3]{1,0:T(8,128)S(1)} %copy.26.own_mask_ref), channel_id=1, source_target_pairs={{0,1},{1,0},{2,3},{3,2},{4,5},{5,4},{6,7},{7,6},{8,9},{9,8},{10,11... | collective-permute-start | bytes 440 | tf_op jit(solution)/shard_map/ppermute | solution.py:749
  22.2 5.4 %collective-permute-start.7 = (bf16[4,48,384]{2,1,0:T(8,128)(2,1)S(1)}, bf16[4,48,384]{2,1,0:T(8,128)(2,1)}, u32[]{:S(2)}, u32[]{:S(2)}) collective-permute-start(bf16[4,48,384]{2,1,0:T(8,128)(2,1)S(1)} %bitcast.19), channel_id=1, source_target_pairs={{0,1},{1,0},{2,3},{3,2},{4,5},{5,4},{6,7},{7,6},{8,9},{9,8},{10,11... | collective-permute-start | bytes 442376 | tf_op jit(solution)/shard_map/ppermute | solution.py:749
  26.1 3.9 %collective-permute-start.10 = (bf16[4,48,384]{2,1,0:T(8,128)(2,1)S(1)}, bf16[4,48,384]{2,1,0:T(8,128)(2,1)}, u32[]{:S(2)}, u32[]{:S(2)}) collective-permute-start(bf16[4,48,384]{2,1,0:T(8,128)(2,1)S(1)} %collective-permute-done.6.refs_3_), channel_id=1, source_target_pairs={{0,1},{1,0},{2,3},{3,2},{4,5},{5,4},{6,7},{7,6},{8,9},{9,8},{10,11... | collective-permute-start | bytes 442376 | tf_op jit(solution)/shard_map/ppermute | solution.py:749
  26.9 3.6 %collective-permute-start.9 = (bf16[4,48,384]{2,1,0:T(8,128)(2,1)S(1)}, bf16[4,48,384]{2,1,0:T(8,128)(2,1)}, u32[]{:S(2)}, u32[]{:S(2)}) collective-permute-start(bf16[4,48,384]{2,1,0:T(8,128)(2,1)S(1)} %collective-permute-done.5.refs_2_), channel_id=1, source_target_pairs={{0,1},{1,0},{2,3},{3,2},{4,5},{5,4},{6,7},{7,6},{8,9},{9,8},{10,11... | collective-permute-start | bytes 442376 | tf_op jit(solution)/shard_map/ppermute | solution.py:749
  27.0 4.1 %collective-permute-start.8 = (bf16[4,48,384]{2,1,0:T(8,128)(2,1)}, bf16[4,48,384]{2,1,0:T(8,128)(2,1)S(1)}, u32[]{:S(2)}, u32[]{:S(2)}) collective-permute-start(bf16[4,48,384]{2,1,0:T(8,128)(2,1)} %collective-permute-done.refs_1_), channel_id=1, source_target_pairs={{0,1},{1,0},{2,3},{3,2},{4,5},{5,4},{6,7},{7,6},{8,9},{9,8},{10,11... | collective-permute-start | bytes 442376 | tf_op jit(solution)/shard_map/ppermute | solution.py:749
  27.5 17.2 %collective-permute-start.11 = (bf16[4,2,48,384]{3,2,1,0:T(8,128)(2,1)S(1)}, bf16[4,2,48,384]{3,2,1,0:T(8,128)(2,1)S(1)}, u32[]{:S(2)}, u32[]{:S(2)}) collective-permute-start(bf16[4,2,48,384]{3,2,1,0:T(8,128)(2,1)S(1)} %all-to-all-done.1.refs_0_), channel_id=1, source_target_pairs={{0,1},{1,0},{2,3},{3,2},{4,5},{5,4},{6,7},{7,6},{8,9},{9,8},{10,11... | collective-permute-start | bytes 884744 | tf_op jit(solution)/shard_map/ppermute | solution.py:749
  27.6 15.7 %collective-permute-start.4 = (bf16[4,2,48,384]{3,2,1,0:T(8,128)(2,1)S(1)}, bf16[4,2,48,384]{3,2,1,0:T(8,128)(2,1)S(1)}, u32[]{:S(2)}, u32[]{:S(2)}) collective-permute-start(bf16[4,2,48,384]{3,2,1,0:T(8,128)(2,1)S(1)} %all-to-all-done.1.refs_0_), channel_id=1, source_target_pairs={{0,6},{2,4},{4,2},{6,0},{1,7},{3,5},{5,3},{7,1},{8,14},{10,12},{12... | collective-permute-start | bytes 884744 | tf_op jit(solution)/shard_map/ppermute | solution.py:758
  30.0 14.2 %collective-permute-start.3 = (bf16[4,2,48,384]{3,2,1,0:T(8,128)(2,1)S(1)}, bf16[4,2,48,384]{3,2,1,0:T(8,128)(2,1)S(1)}, u32[]{:S(2)}, u32[]{:S(2)}) collective-permute-start(bf16[4,2,48,384]{3,2,1,0:T(8,128)(2,1)S(1)} %all-to-all-done.1.refs_0_), channel_id=1, source_target_pairs={{0,4},{2,6},{4,0},{6,2},{1,5},{3,7},{5,1},{7,3},{8,12},{10,14},{12... | collective-permute-start | bytes 884744 | tf_op jit(solution)/shard_map/ppermute | solution.py:758
  30.5 13.7 %collective-permute-start.2 = (bf16[4,2,48,384]{3,2,1,0:T(8,128)(2,1)S(1)}, bf16[4,2,48,384]{3,2,1,0:T(8,128)(2,1)S(1)}, u32[]{:S(2)}, u32[]{:S(2)}) collective-permute-start(bf16[4,2,48,384]{3,2,1,0:T(8,128)(2,1)S(1)} %all-to-all-done.1.refs_0_), channel_id=1, source_target_pairs={{0,2},{2,0},{4,6},{6,4},{1,3},{3,1},{5,7},{7,5},{8,10},{10,8},{12,... | collective-permute-start | bytes 884744 | tf_op jit(solution)/shard_map/ppermute | solution.py:758
  64.9 3.3 %collective-permute-start.17 = (bf16[2,4,2,48,384]{4,3,2,1,0:T(8,128)(2,1)S(1)}, bf16[2,4,2,48,384]{4,3,2,1,0:T(8,128)(2,1)S(1)}, u32[]{:S(2)}, u32[]{:S(2)}) collective-permute-start(bf16[2,4,2,48,384]{4,3,2,1,0:T(8,128)(2,1)S(1)} %get-tuple-element.105), channel_id=1, source_target_pairs={{0,1},{1,0},{2,3},{3,2},{4,5},{5,4},{6,7},{7,6},{8,9},{9,8},{10,11... | collective-permute-start | bytes 1769480 | tf_op jit(solution)/shard_map/ppermute | solution.py:749
  66.9 16.9 %collective-permute-start.16 = (bf16[4,2,48,384]{3,2,1,0:T(8,128)(2,1)S(1)}, bf16[4,2,48,384]{3,2,1,0:T(8,128)(2,1)S(1)}, u32[]{:S(2)}, u32[]{:S(2)}) collective-permute-start(bf16[4,2,48,384]{3,2,1,0:T(8,128)(2,1)S(1)} %get-tuple-element.103), channel_id=1, source_target_pairs={{0,2},{2,0},{4,6},{6,4},{1,3},{3,1},{5,7},{7,5},{8,10},{10,8},{12,... | collective-permute-start | bytes 884744 | tf_op jit(solution)/shard_map/ppermute | solution.py:758
  68.4 15.5 %collective-permute-start.18 = (bf16[4,2,48,384]{3,2,1,0:T(8,128)(2,1)S(1)}, bf16[4,2,48,384]{3,2,1,0:T(8,128)(2,1)S(1)}, u32[]{:S(2)}, u32[]{:S(2)}) collective-permute-start(bf16[4,2,48,384]{3,2,1,0:T(8,128)(2,1)S(1)} %get-tuple-element.106), channel_id=1, source_target_pairs={{0,4},{2,6},{4,0},{6,2},{1,5},{3,7},{5,1},{7,3},{8,12},{10,14},{12... | collective-permute-start | bytes 884744 | tf_op jit(solution)/shard_map/ppermute | solution.py:758
  69.5 14.3 %collective-permute-start.19 = (bf16[4,2,48,384]{3,2,1,0:T(8,128)(2,1)S(1)}, bf16[4,2,48,384]{3,2,1,0:T(8,128)(2,1)S(1)}, u32[]{:S(2)}, u32[]{:S(2)}) collective-permute-start(bf16[4,2,48,384]{3,2,1,0:T(8,128)(2,1)S(1)} %get-tuple-element.107), channel_id=1, source_target_pairs={{0,6},{2,4},{4,2},{6,0},{1,7},{3,5},{5,3},{7,1},{8,14},{10,12},{12... | collective-permute-start | bytes 884744 | tf_op jit(solution)/shard_map/ppermute | solution.py:758
  83.9 5.9 %collective-permute-start.20 = (bf16[17,48,384]{2,1,0:T(8,128)(2,1)}, bf16[17,48,384]{2,1,0:T(8,128)(2,1)S(1)}, u32[]{:S(2)}, u32[]{:S(2)}) collective-permute-start(bf16[17,48,384]{2,1,0:T(8,128)(2,1)} %get-tuple-element.109), channel_id=1, source_target_pairs={{0,1},{1,0},{2,3},{3,2},{4,5},{5,4},{6,7},{7,6},{8,9},{9,8},{10,11... | collective-permute-start | bytes 1880072 | tf_op jit(solution)/shard_map/ppermute | solution.py:749
  84.8 16.7 %all-to-all-start.2 = ((bf16[4,2,48,384]{3,2,1,0:T(8,128)(2,1)}), bf16[4,2,48,384]{3,2,1,0:T(8,128)(2,1)S(1)}, u32[]{:S(2)}, u32[]{:S(2)}) async-start(bf16[4,2,48,384]{3,2,1,0:T(8,128)(2,1)} %sum_late.1), calls=%async_computation.2 | async-start | bytes 589824 | tf_op jit(solution)/shard_map/all_to_all | solution.py:753
  90.5 10.2 %collective-permute-start.21 = (bf16[200,384]{1,0:T(8,128)(2,1)S(1)}, bf16[200,384]{1,0:T(8,128)(2,1)S(1)}, u32[]{:S(2)}, u32[]{:S(2)}) collective-permute-start(bf16[200,384]{1,0:T(8,128)(2,1)S(1)} %get-tuple-element.117), channel_id=1, source_target_pairs={{0,2},{2,0},{4,6},{6,4},{1,3},{3,1},{5,7},{7,5},{8,10},{10,8},{12,... | collective-permute-start | bytes 460808 | tf_op jit(solution)/shard_map/ppermute | solution.py:758
  91.7 9.1 %collective-permute-start.22 = (bf16[200,384]{1,0:T(8,128)(2,1)S(1)}, bf16[200,384]{1,0:T(8,128)(2,1)S(1)}, u32[]{:S(2)}, u32[]{:S(2)}) collective-permute-start(bf16[200,384]{1,0:T(8,128)(2,1)S(1)} %get-tuple-element.118), channel_id=1, source_target_pairs={{0,4},{2,6},{4,0},{6,2},{1,5},{3,7},{5,1},{7,3},{8,12},{10,14},{12... | collective-permute-start | bytes 460808 | tf_op jit(solution)/shard_map/ppermute | solution.py:758
  92.5 8.3 %collective-permute-start.23 = (bf16[200,384]{1,0:T(8,128)(2,1)S(1)}, bf16[200,384]{1,0:T(8,128)(2,1)S(1)}, u32[]{:S(2)}, u32[]{:S(2)}) collective-permute-start(bf16[200,384]{1,0:T(8,128)(2,1)S(1)} %get-tuple-element.119), channel_id=1, source_target_pairs={{0,6},{2,4},{4,2},{6,0},{1,7},{3,5},{5,3},{7,1},{8,14},{10,12},{12... | collective-permute-start | bytes 460808 | tf_op jit(solution)/shard_map/ppermute | solution.py:758
  101.6 13.0 %all-to-all-start.3 = ((bf16[4,56,384]{2,1,0:T(8,128)(2,1)}), bf16[4,56,384]{2,1,0:T(8,128)(2,1)S(1)}, u32[]{:S(2)}, u32[]{:S(2)}) async-start(bf16[4,56,384]{2,1,0:T(8,128)(2,1)} %join.1), calls=%async_computation.3 | async-start | bytes 344064 | tf_op jit(solution)/shard_map/all_to_all | solution.py:753
  (20 other events, 265.9 us)

commit v15 on v14

--- a/solution.py
+++ b/solution.py
@@ -816,8 +816,11 @@
     prob, qkv, out, middle, second_rows, wqkv, wo = attn_forward(
         place, *masks, tokens, norm_params, early
     )
-    late[1:], middle = lax.optimization_barrier((late[1:], middle))
-    late += [swap_heads(piece) for piece in late]
+    late[1], late[3], middle = lax.optimization_barrier((late[1], late[3], middle))
+    others = [swap_heads(late[0]), swap_heads(late[1]), None, swap_heads(late[3])]
+    late[2], others[1], others[3] = lax.optimization_barrier((late[2], others[1], others[3]))
+    others[2] = swap_heads(late[2])
+    late += others
     block_out, middle_grad, norm_two, *late_sums = mlp(
         place, middle, second_rows, cotangent, norm_params, late
     )

time: 121 us -> 122 us (level)
  transfers between devices with their start and end apart: 28 -> 28, of which waited for: 10 -> 11; matrix products, arithmetic and copies ran while one was open for 0% -> 0% of each run, Pallas kernels for 37% -> 37%
where the time goes in v15:
time: 122 us; the launch traced here: 121 us
  Pallas kernels  70.1 us (57%)
  starting transfers between devices  36.2 us (30%)
  waiting for transfers between devices  14.1 us (12%)
    all_to_all x4, starting transfers between devices, to_all(): return lax.all_to_all(values, axis, 0, 0)  19.6 us
    pallas_call x1, Pallas kernels, mlp(): pl.pallas_call(mlp_kernel, grid=(rows // TILE,), in_specs=[pl.BlockSpec(m...  18.1 us
    ppermute x12, starting transfers between devices, across(): return lax.ppermute(values, 'inner', pairs)  14.2 us
    pallas_call x2, Pallas kernels, shampoo(): pl.pallas_call(lambda *refs: shampoo_kernel(scale, bool(norms), *refs), g...  13.8 us
    pallas_call x1, Pallas kernels, attn_backward(): pl.pallas_call(attn_backward_kernel, grid=(rows // TILE,), in_specs=[smem...  13.1 us
    pallas_call x1, Pallas kernels, attn_forward(): pl.pallas_call(attn_forward_kernel, grid=(rows // TILE,), in_specs=[smem]...  12.2 us
    pallas_call x1, Pallas kernels, input_gradient(): pl.pallas_call(input_grad_kernel, grid=(rows // INPUT_TILE,), in_specs=[t...  6.63 us
    ppermute x12, waiting for transfers between devices, across(): return lax.ppermute(values, 'inner', pairs)  5.21 us
  transfers between devices with their start and end apart: 28, of which 11 were waited for; matrix products, arithmetic and copies ran while one was open for 0% of the time, Pallas kernels for 37%

profile of v15, /device:TPU:0, one launch (start us, length us, event | category | flops | bytes accessed | tf_op | source)
XLA Modules:
  0.0 121.5 jit_solution(986458967980204578)
XLA Ops:
  0.7 1.8 %pack.2 = bf16[4,1,48,384]{3,2,1,0:T(8,128)(2,1)} custom-call(f32[3,8,48,48]{3,2,1,0:T(8,128)} %bitcast.11), custom_call_target="tpu_custom_call" | custom-call | tf_op jit(solution)/shard_map/pack/pallas_call | solution.py:484
  2.5 6.3 %all-to-all-start = ((bf16[4,1,48,384]{3,2,1,0:T(8,128)(2,1)}), bf16[4,1,48,384]{3,2,1,0:T(8,128)(2,1)S(1)}, u32[]{:S(2)}, u32[]{:S(2)}) async-start(bf16[4,1,48,384]{3,2,1,0:T(8,128)(2,1)} %pack.2), calls=%async_computation | async-start | bytes 294912 | tf_op jit(solution)/shard_map/all_to_all | solution.py:753
  8.8 1.8 %pack.3 = bf16[4,2,48,384]{3,2,1,0:T(8,128)(2,1)} custom-call(f32[3,8,48,48]{3,2,1,0:T(8,128)} %bitcast.12), custom_call_target="tpu_custom_call" | custom-call | tf_op jit(solution)/shard_map/pack/pallas_call | solution.py:484
  10.6 4.4 %all-to-all-done = bf16[4,1,48,384]{3,2,1,0:T(8,128)(2,1)S(1)} async-done(((bf16[4,1,48,384]{3,2,1,0:T(8,128)(2,1)}), bf16[4,1,48,384]{3,2,1,0:T(8,128)(2,1)S(1)}, u32[]{:S(2)}, u32[]{:S(2)}) %all-to-all-start) | async-done | bytes 147488 | tf_op jit(solution)/shard_map/all_to_all | solution.py:753
  15.0 3.5 %all-to-all-start.1 = ((bf16[4,2,48,384]{3,2,1,0:T(8,128)(2,1)}), bf16[4,2,48,384]{3,2,1,0:T(8,128)(2,1)S(1)}, u32[]{:S(2)}, u32[]{:S(2)}) async-start(bf16[4,2,48,384]{3,2,1,0:T(8,128)(2,1)} %pack.3), calls=%async_computation.1 | async-start | bytes 589824 | tf_op jit(solution)/shard_map/all_to_all | solution.py:753
  18.5 2.5 %collective-permute-start.5 = (bf16[4,48,384]{2,1,0:T(8,128)(2,1)S(1)}, bf16[4,48,384]{2,1,0:T(8,128)(2,1)S(1)}, u32[]{:S(2)}, u32[]{:S(2)}) collective-permute-start(bf16[4,48,384]{2,1,0:T(8,128)(2,1)S(1)} %bitcast.16), channel_id=1, source_target_pairs={{0,6},{2,4},{4,2},{6,0},{1,7},{3,5},{5,3},{7,1},{8,14},{10,12},{12... | collective-permute-start | bytes 442376 | tf_op jit(solution)/shard_map/ppermute | solution.py:758
  22.7 3.4 %collective-permute-done.5.refs_3_ = bf16[4,48,384]{2,1,0:T(8,128)(2,1)S(1)} collective-permute-done((bf16[4,48,384]{2,1,0:T(8,128)(2,1)S(1)}, bf16[4,48,384]{2,1,0:T(8,128)(2,1)S(1)}, u32[]{:S(2)}, u32[]{:S(2)}) %collective-permute-start.5) | collective-permute-done | bytes 147488 | tf_op jit(solution)/shard_map/ppermute | solution.py:758
  27.5 1.3 %collective-permute-start.10 = (bf16[4,2,48,384]{3,2,1,0:T(8,128)(2,1)S(1)}, bf16[4,2,48,384]{3,2,1,0:T(8,128)(2,1)S(1)}, u32[]{:S(2)}, u32[]{:S(2)}) collective-permute-start(bf16[4,2,48,384]{3,2,1,0:T(8,128)(2,1)S(1)} %all-to-all-done.1.refs_0_), channel_id=1, source_target_pairs={{0,4},{2,6},{4,0},{6,2},{1,5},{3,7},{5,1},{7,3},{8,12},{10,14},{12... | collective-permute-start | bytes 884744 | tf_op jit(solution)/shard_map/ppermute | solution.py:758
  28.8 1.4 %collective-permute-start.3 = (bf16[4,2,48,384]{3,2,1,0:T(8,128)(2,1)S(1)}, bf16[4,2,48,384]{3,2,1,0:T(8,128)(2,1)S(1)}, u32[]{:S(2)}, u32[]{:S(2)}) collective-permute-start(bf16[4,2,48,384]{3,2,1,0:T(8,128)(2,1)S(1)} %all-to-all-done.1.refs_0_), channel_id=1, source_target_pairs={{0,6},{2,4},{4,2},{6,0},{1,7},{3,5},{5,3},{7,1},{8,14},{10,12},{12... | collective-permute-start | bytes 884744 | tf_op jit(solution)/shard_map/ppermute | solution.py:758
  31.0 12.2 %attn_forward.1 = (bf16[6,3,512,256]{3,2,1,0:T(8,128)(2,1)}, bf16[1536,1152]{1,0:T(8,128)(2,1)}, bf16[1536,384]{1,0:T(8,128)(2,1)}, f32[1536,384]{1,0:T(8,128)S(...) custom-call(s32[14]{0:T(128)S(1)} %pad_add_fusion.place_ref, ...), custom_call_target="tpu_custom_call" | custom-call | flops 4227858432 | bytes 16777216 | tf_op jit(solution)/shard_map/attn_forward/pallas_call | solution.py:176
  44.6 1.1 collective-permute-done.11.refs_5_
  46.5 1.2 collective-permute-done.14.refs_6_
  47.7 18.1 %mlp.1 = (f32[1536,384]{1,0:T(8,128)}, f32[1536,384]{1,0:T(8,128)}, f32[2,384]{1,0:T(2,128)S(1)}, bf16[2,4,2,48,384]{4,3,2,1,0:T(8,128)(2,1)S(1)}, bf16[2,4,2,48...) custom-call(s32[14]{0:T(128)S(1)} %pad_add_fusion.place_ref, ...), custom_call_target="tpu_custom_call" | custom-call | flops 10871635968 | bytes 20971520 | tf_op jit(solution)/shard_map/mlp/pallas_call | solution.py:273
  66.3 1.5 %collective-permute-done.15.received_ref = bf16[2,4,2,48,384]{4,3,2,1,0:T(8,128)(2,1)S(1)} collective-permute-done((bf16[2,4,2,48,384]{4,3,2,1,0:T(8,128)(2,1)S(1)}, bf16[2,4,2,48,384]{4,3,2,1,0:T(8,128)(2,1)S(1)}, u32[]{:S(2)}, u32[]{:S(2)}) %collective-permute-start.15) | collective-permute-done | bytes 589856 | tf_op jit(solution)/shard_map/ppermute | solution.py:749
  68.0 1.5 %collective-permute-start.16 = (bf16[4,2,48,384]{3,2,1,0:T(8,128)(2,1)S(1)}, bf16[4,2,48,384]{3,2,1,0:T(8,128)(2,1)S(1)}, u32[]{:S(2)}, u32[]{:S(2)}) collective-permute-start(bf16[4,2,48,384]{3,2,1,0:T(8,128)(2,1)S(1)} %get-tuple-element.107), channel_id=1, source_target_pairs={{0,2},{2,0},{4,6},{6,4},{1,3},{3,1},{5,7},{7,5},{8,10},{10,8},{12,... | collective-permute-start | bytes 884744 | tf_op jit(solution)/shard_map/ppermute | solution.py:758
  69.6 1.6 %collective-permute-start.18 = (bf16[4,2,48,384]{3,2,1,0:T(8,128)(2,1)S(1)}, bf16[4,2,48,384]{3,2,1,0:T(8,128)(2,1)S(1)}, u32[]{:S(2)}, u32[]{:S(2)}) collective-permute-start(bf16[4,2,48,384]{3,2,1,0:T(8,128)(2,1)S(1)} %get-tuple-element.110), channel_id=1, source_target_pairs={{0,4},{2,6},{4,0},{6,2},{1,5},{3,7},{5,1},{7,3},{8,12},{10,14},{12... | collective-permute-start | bytes 884744 | tf_op jit(solution)/shard_map/ppermute | solution.py:758
  71.8 13.1 %attn_backward.1 = (bf16[1536,1152]{1,0:T(8,128)(2,1)}, bf16[16,48,384]{2,1,0:T(8,128)(2,1)S(1)}, bf16[17,48,384]{2,1,0:T(8,128)(2,1)}, f32[4,384]{1,0:T(4,128)S(1)}) custom-call(s32[14]{0:T(128)S(1)} %pad_add_fusion.place_ref, s32[12,3]{1,0:T(8,128)S(1)} %copy.26.own_mask_ref, s32[12,3]{1,0:T(8,128)S(1)} %collective-permute-done.1.other_mask_ref, ...), custom_call_target="tpu_custom_call" | custom-call | flops 7096762368 | bytes 20971520 | tf_op jit(solution)/shard_map/attn_backward/pallas_call | solution.py:396
  85.9 4.9 %all-to-all-start.2 = ((bf16[4,2,48,384]{3,2,1,0:T(8,128)(2,1)}), bf16[4,2,48,384]{3,2,1,0:T(8,128)(2,1)S(1)}, u32[]{:S(2)}, u32[]{:S(2)}) async-start(bf16[4,2,48,384]{3,2,1,0:T(8,128)(2,1)} %sum_late.1), calls=%async_computation.2 | async-start | bytes 589824 | tf_op jit(solution)/shard_map/all_to_all | solution.py:753
  91.5 1.3 %collective-permute-start.21 = (bf16[200,384]{1,0:T(8,128)(2,1)S(1)}, bf16[200,384]{1,0:T(8,128)(2,1)S(1)}, u32[]{:S(2)}, u32[]{:S(2)}) collective-permute-start(bf16[200,384]{1,0:T(8,128)(2,1)S(1)} %get-tuple-element.121), channel_id=1, source_target_pairs={{0,2},{2,0},{4,6},{6,4},{1,3},{3,1},{5,7},{7,5},{8,10},{10,8},{12,... | collective-permute-start | bytes 460808 | tf_op jit(solution)/shard_map/ppermute | solution.py:758
  93.5 1.6 %collective-permute-start.23 = (bf16[200,384]{1,0:T(8,128)(2,1)S(1)}, bf16[200,384]{1,0:T(8,128)(2,1)S(1)}, u32[]{:S(2)}, u32[]{:S(2)}) collective-permute-start(bf16[200,384]{1,0:T(8,128)(2,1)S(1)} %get-tuple-element.123), channel_id=1, source_target_pairs={{0,6},{2,4},{4,2},{6,0},{1,7},{3,5},{5,3},{7,1},{8,14},{10,12},{12... | collective-permute-start | bytes 460808 | tf_op jit(solution)/shard_map/ppermute | solution.py:758
  95.1 6.6 %input_gradient.1 = f32[1536,384]{1,0:T(8,128)} custom-call(bf16[1536,384]{1,0:T(8,128)(2,1)} %x_ref.5, f32[1536,384]{1,0:T(8,128)} %get-tuple-element.98.grad_ref, bf16[1536,1152]{1,0:T(8,128)(2,1)} %get-tuple-element.124.dqkv_ref, f32[4,384]{1,0:T(4,128)} %refs_4_.1, bf16[384,1152]{1,0:T(8,128)(2,1)} %get-tuple-element.103.wqkv_ref), custom_call_target="tpu_custom_call" | custom-call | flops 1358954496 | bytes 10485760 | tf_op jit(solution)/shard_map/input_gradient/pallas_call | solution.py:452
  102.7 4.9 %all-to-all-start.3 = ((bf16[4,56,384]{2,1,0:T(8,128)(2,1)}), bf16[4,56,384]{2,1,0:T(8,128)(2,1)S(1)}, u32[]{:S(2)}, u32[]{:S(2)}) async-start(bf16[4,56,384]{2,1,0:T(8,128)(2,1)} %join.1), calls=%async_computation.3 | async-start | bytes 344064 | tf_op jit(solution)/shard_map/all_to_all | solution.py:753
  107.6 8.0 %shampoo.2 = (f32[3,8,48,48]{3,2,1,0:T(8,128)}, f32[3,8,48,48]{3,2,1,0:T(8,128)}, f32[3,8,48,48]{3,2,1,0:T(8,128)}, f32[3,8,48,48]{3,2,1,0:T(8,128)}) custom-call(bf16[4,2,48,384]{3,2,1,0:T(8,128)(2,1)S(1)} %all-to-all-done.2.refs_0_, f32[3,8,48,48]{3,2,1,0:T(8,128)S(1)} %bitcast.13, f32[3,8,48,48]{3,2,1,0:T(8,128)S(1)} %bitcast.21, ...), custom_call_target="tpu_custom_call" | custom-call | flops 6442450944 | bytes 4194304 | tf_op jit(solution)/shard_map/shampoo/pallas_call | solution.py:724
  115.7 5.8 %shampoo.3 = (f32[3,8,48,48]{3,2,1,0:T(8,128)}, f32[3,8,48,48]{3,2,1,0:T(8,128)}, f32[3,8,48,48]{3,2,1,0:T(8,128)}, f32[3,8,48,48]{3,2,1,0:T(8,128)}, f32[4,384]...) custom-call(bf16[4,1,56,384]{3,2,1,0:T(8,128)(2,1)S(1)} %bitcast.15,, ...), custom_call_target="tpu_custom_call", output_to_operand_aliasing={{0}: (6, {}), {1}: (7, {}), {2}: (8, {}), {3}: (9, {})} | custom-call | flops 3221225472 | bytes 4194304 | tf_op jit(solution)/shard_map/shampoo/pallas_call | solution.py:724
  (80 shorter events, 10.9 us)
Async XLA Ops:
  2.5 12.6 %all-to-all-start = ((bf16[4,1,48,384]{3,2,1,0:T(8,128)(2,1)}), bf16[4,1,48,384]{3,2,1,0:T(8,128)(2,1)S(1)}, u32[]{:S(2)}, u32[]{:S(2)}) async-start(bf16[4,1,48,384]{3,2,1,0:T(8,128)(2,1)} %pack.2), calls=%async_computation | async-start | bytes 294912 | tf_op jit(solution)/shard_map/all_to_all | solution.py:753
  15.0 12.0 %all-to-all-start.1 = ((bf16[4,2,48,384]{3,2,1,0:T(8,128)(2,1)}), bf16[4,2,48,384]{3,2,1,0:T(8,128)(2,1)S(1)}, u32[]{:S(2)}, u32[]{:S(2)}) async-start(bf16[4,2,48,384]{3,2,1,0:T(8,128)(2,1)} %pack.3), calls=%async_computation.1 | async-start | bytes 589824 | tf_op jit(solution)/shard_map/all_to_all | solution.py:753
  18.5 7.6 %collective-permute-start.5 = (bf16[4,48,384]{2,1,0:T(8,128)(2,1)S(1)}, bf16[4,48,384]{2,1,0:T(8,128)(2,1)S(1)}, u32[]{:S(2)}, u32[]{:S(2)}) collective-permute-start(bf16[4,48,384]{2,1,0:T(8,128)(2,1)S(1)} %bitcast.16), channel_id=1, source_target_pairs={{0,6},{2,4},{4,2},{6,0},{1,7},{3,5},{5,3},{7,1},{8,14},{10,12},{12... | collective-permute-start | bytes 442376 | tf_op jit(solution)/shard_map/ppermute | solution.py:758
  21.0 6.0 %collective-permute-start.4 = (bf16[4,48,384]{2,1,0:T(8,128)(2,1)S(1)}, bf16[4,48,384]{2,1,0:T(8,128)(2,1)S(1)}, u32[]{:S(2)}, u32[]{:S(2)}) collective-permute-start(bf16[4,48,384]{2,1,0:T(8,128)(2,1)S(1)} %bitcast.17), channel_id=1, source_target_pairs={{0,4},{2,6},{4,0},{6,2},{1,5},{3,7},{5,1},{7,3},{8,12},{10,14},{12... | collective-permute-start | bytes 442376 | tf_op jit(solution)/shard_map/ppermute | solution.py:758
  21.5 5.5 %collective-permute-start = (bf16[4,48,384]{2,1,0:T(8,128)(2,1)S(1)}, bf16[4,48,384]{2,1,0:T(8,128)(2,1)}, u32[]{:S(2)}, u32[]{:S(2)}) collective-permute-start(bf16[4,48,384]{2,1,0:T(8,128)(2,1)S(1)} %bitcast.18), channel_id=1, source_target_pairs={{0,2},{2,0},{4,6},{6,4},{1,3},{3,1},{5,7},{7,5},{8,10},{10,8},{12,... | collective-permute-start | bytes 442376 | tf_op jit(solution)/shard_map/ppermute | solution.py:758
  22.1 4.8 %collective-permute-start.1 = (s32[12,3]{1,0:T(8,128)S(1)}, s32[12,3]{1,0:T(8,128)S(1)}, u32[]{:S(2)}, u32[]{:S(2)}) collective-permute-start(s32[12,3]{1,0:T(8,128)S(1)} %copy.26.own_mask_ref), channel_id=1, source_target_pairs={{0,1},{1,0},{2,3},{3,2},{4,5},{5,4},{6,7},{7,6},{8,9},{9,8},{10,11... | collective-permute-start | bytes 440 | tf_op jit(solution)/shard_map/ppermute | solution.py:749
  22.2 6.6 %collective-permute-start.6 = (bf16[4,48,384]{2,1,0:T(8,128)(2,1)S(1)}, bf16[4,48,384]{2,1,0:T(8,128)(2,1)}, u32[]{:S(2)}, u32[]{:S(2)}) collective-permute-start(bf16[4,48,384]{2,1,0:T(8,128)(2,1)S(1)} %bitcast.19), channel_id=1, source_target_pairs={{0,1},{1,0},{2,3},{3,2},{4,5},{5,4},{6,7},{7,6},{8,9},{9,8},{10,11... | collective-permute-start | bytes 442376 | tf_op jit(solution)/shard_map/ppermute | solution.py:749
  26.1 4.1 %collective-permute-start.9 = (bf16[4,48,384]{2,1,0:T(8,128)(2,1)S(1)}, bf16[4,48,384]{2,1,0:T(8,128)(2,1)}, u32[]{:S(2)}, u32[]{:S(2)}) collective-permute-start(bf16[4,48,384]{2,1,0:T(8,128)(2,1)S(1)} %collective-permute-done.5.refs_3_), channel_id=1, source_target_pairs={{0,1},{1,0},{2,3},{3,2},{4,5},{5,4},{6,7},{7,6},{8,9},{9,8},{10,11... | collective-permute-start | bytes 442376 | tf_op jit(solution)/shard_map/ppermute | solution.py:749
  26.9 4.1 %collective-permute-start.8 = (bf16[4,48,384]{2,1,0:T(8,128)(2,1)S(1)}, bf16[4,48,384]{2,1,0:T(8,128)(2,1)}, u32[]{:S(2)}, u32[]{:S(2)}) collective-permute-start(bf16[4,48,384]{2,1,0:T(8,128)(2,1)S(1)} %collective-permute-done.4.refs_2_), channel_id=1, source_target_pairs={{0,1},{1,0},{2,3},{3,2},{4,5},{5,4},{6,7},{7,6},{8,9},{9,8},{10,11... | collective-permute-start | bytes 442376 | tf_op jit(solution)/shard_map/ppermute | solution.py:749
  27.0 4.0 %collective-permute-start.7 = (bf16[4,48,384]{2,1,0:T(8,128)(2,1)}, bf16[4,48,384]{2,1,0:T(8,128)(2,1)S(1)}, u32[]{:S(2)}, u32[]{:S(2)}) collective-permute-start(bf16[4,48,384]{2,1,0:T(8,128)(2,1)} %collective-permute-done.refs_1_), channel_id=1, source_target_pairs={{0,1},{1,0},{2,3},{3,2},{4,5},{5,4},{6,7},{7,6},{8,9},{9,8},{10,11... | collective-permute-start | bytes 442376 | tf_op jit(solution)/shard_map/ppermute | solution.py:749
  27.5 17.1 %collective-permute-start.10 = (bf16[4,2,48,384]{3,2,1,0:T(8,128)(2,1)S(1)}, bf16[4,2,48,384]{3,2,1,0:T(8,128)(2,1)S(1)}, u32[]{:S(2)}, u32[]{:S(2)}) collective-permute-start(bf16[4,2,48,384]{3,2,1,0:T(8,128)(2,1)S(1)} %all-to-all-done.1.refs_0_), channel_id=1, source_target_pairs={{0,4},{2,6},{4,0},{6,2},{1,5},{3,7},{5,1},{7,3},{8,12},{10,14},{12... | collective-permute-start | bytes 884744 | tf_op jit(solution)/shard_map/ppermute | solution.py:758
  28.8 14.5 %collective-permute-start.3 = (bf16[4,2,48,384]{3,2,1,0:T(8,128)(2,1)S(1)}, bf16[4,2,48,384]{3,2,1,0:T(8,128)(2,1)S(1)}, u32[]{:S(2)}, u32[]{:S(2)}) collective-permute-start(bf16[4,2,48,384]{3,2,1,0:T(8,128)(2,1)S(1)} %all-to-all-done.1.refs_0_), channel_id=1, source_target_pairs={{0,6},{2,4},{4,2},{6,0},{1,7},{3,5},{5,3},{7,1},{8,14},{10,12},{12... | collective-permute-start | bytes 884744 | tf_op jit(solution)/shard_map/ppermute | solution.py:758
  30.3 13.8 %collective-permute-start.2 = (bf16[4,2,48,384]{3,2,1,0:T(8,128)(2,1)S(1)}, bf16[4,2,48,384]{3,2,1,0:T(8,128)(2,1)S(1)}, u32[]{:S(2)}, u32[]{:S(2)}) collective-permute-start(bf16[4,2,48,384]{3,2,1,0:T(8,128)(2,1)S(1)} %all-to-all-done.1.refs_0_), channel_id=1, source_target_pairs={{0,2},{2,0},{4,6},{6,4},{1,3},{3,1},{5,7},{7,5},{8,10},{10,8},{12,... | collective-permute-start | bytes 884744 | tf_op jit(solution)/shard_map/ppermute | solution.py:758
  65.8 2.1 %collective-permute-start.15 = (bf16[2,4,2,48,384]{4,3,2,1,0:T(8,128)(2,1)S(1)}, bf16[2,4,2,48,384]{4,3,2,1,0:T(8,128)(2,1)S(1)}, u32[]{:S(2)}, u32[]{:S(2)}) collective-permute-start(bf16[2,4,2,48,384]{4,3,2,1,0:T(8,128)(2,1)S(1)} %get-tuple-element.94), channel_id=1, source_target_pairs={{0,1},{1,0},{2,3},{3,2},{4,5},{5,4},{6,7},{7,6},{8,9},{9,8},{10,11... | collective-permute-start | bytes 1769480 | tf_op jit(solution)/shard_map/ppermute | solution.py:749
  66.0 3.5 %collective-permute-start.17 = (bf16[2,4,2,48,384]{4,3,2,1,0:T(8,128)(2,1)S(1)}, bf16[2,4,2,48,384]{4,3,2,1,0:T(8,128)(2,1)S(1)}, u32[]{:S(2)}, u32[]{:S(2)}) collective-permute-start(bf16[2,4,2,48,384]{4,3,2,1,0:T(8,128)(2,1)S(1)} %get-tuple-element.109), channel_id=1, source_target_pairs={{0,1},{1,0},{2,3},{3,2},{4,5},{5,4},{6,7},{7,6},{8,9},{9,8},{10,11... | collective-permute-start | bytes 1769480 | tf_op jit(solution)/shard_map/ppermute | solution.py:749
  68.0 16.9 %collective-permute-start.16 = (bf16[4,2,48,384]{3,2,1,0:T(8,128)(2,1)S(1)}, bf16[4,2,48,384]{3,2,1,0:T(8,128)(2,1)S(1)}, u32[]{:S(2)}, u32[]{:S(2)}) collective-permute-start(bf16[4,2,48,384]{3,2,1,0:T(8,128)(2,1)S(1)} %get-tuple-element.107), channel_id=1, source_target_pairs={{0,2},{2,0},{4,6},{6,4},{1,3},{3,1},{5,7},{7,5},{8,10},{10,8},{12,... | collective-permute-start | bytes 884744 | tf_op jit(solution)/shard_map/ppermute | solution.py:758
  69.6 15.3 %collective-permute-start.18 = (bf16[4,2,48,384]{3,2,1,0:T(8,128)(2,1)S(1)}, bf16[4,2,48,384]{3,2,1,0:T(8,128)(2,1)S(1)}, u32[]{:S(2)}, u32[]{:S(2)}) collective-permute-start(bf16[4,2,48,384]{3,2,1,0:T(8,128)(2,1)S(1)} %get-tuple-element.110), channel_id=1, source_target_pairs={{0,4},{2,6},{4,0},{6,2},{1,5},{3,7},{5,1},{7,3},{8,12},{10,14},{12... | collective-permute-start | bytes 884744 | tf_op jit(solution)/shard_map/ppermute | solution.py:758
  71.2 13.7 %collective-permute-start.19 = (bf16[4,2,48,384]{3,2,1,0:T(8,128)(2,1)S(1)}, bf16[4,2,48,384]{3,2,1,0:T(8,128)(2,1)S(1)}, u32[]{:S(2)}, u32[]{:S(2)}) collective-permute-start(bf16[4,2,48,384]{3,2,1,0:T(8,128)(2,1)S(1)} %get-tuple-element.111), channel_id=1, source_target_pairs={{0,6},{2,4},{4,2},{6,0},{1,7},{3,5},{5,3},{7,1},{8,14},{10,12},{12... | collective-permute-start | bytes 884744 | tf_op jit(solution)/shard_map/ppermute | solution.py:758
  84.9 5.9 %collective-permute-start.20 = (bf16[17,48,384]{2,1,0:T(8,128)(2,1)}, bf16[17,48,384]{2,1,0:T(8,128)(2,1)S(1)}, u32[]{:S(2)}, u32[]{:S(2)}) collective-permute-start(bf16[17,48,384]{2,1,0:T(8,128)(2,1)} %get-tuple-element.113), channel_id=1, source_target_pairs={{0,1},{1,0},{2,3},{3,2},{4,5},{5,4},{6,7},{7,6},{8,9},{9,8},{10,11... | collective-permute-start | bytes 1880072 | tf_op jit(solution)/shard_map/ppermute | solution.py:749
  85.9 16.8 %all-to-all-start.2 = ((bf16[4,2,48,384]{3,2,1,0:T(8,128)(2,1)}), bf16[4,2,48,384]{3,2,1,0:T(8,128)(2,1)S(1)}, u32[]{:S(2)}, u32[]{:S(2)}) async-start(bf16[4,2,48,384]{3,2,1,0:T(8,128)(2,1)} %sum_late.1), calls=%async_computation.2 | async-start | bytes 589824 | tf_op jit(solution)/shard_map/all_to_all | solution.py:753
  91.5 10.2 %collective-permute-start.21 = (bf16[200,384]{1,0:T(8,128)(2,1)S(1)}, bf16[200,384]{1,0:T(8,128)(2,1)S(1)}, u32[]{:S(2)}, u32[]{:S(2)}) collective-permute-start(bf16[200,384]{1,0:T(8,128)(2,1)S(1)} %get-tuple-element.121), channel_id=1, source_target_pairs={{0,2},{2,0},{4,6},{6,4},{1,3},{3,1},{5,7},{7,5},{8,10},{10,8},{12,... | collective-permute-start | bytes 460808 | tf_op jit(solution)/shard_map/ppermute | solution.py:758
  92.8 9.1 %collective-permute-start.22 = (bf16[200,384]{1,0:T(8,128)(2,1)S(1)}, bf16[200,384]{1,0:T(8,128)(2,1)S(1)}, u32[]{:S(2)}, u32[]{:S(2)}) collective-permute-start(bf16[200,384]{1,0:T(8,128)(2,1)S(1)} %get-tuple-element.122), channel_id=1, source_target_pairs={{0,4},{2,6},{4,0},{6,2},{1,5},{3,7},{5,1},{7,3},{8,12},{10,14},{12... | collective-permute-start | bytes 460808 | tf_op jit(solution)/shard_map/ppermute | solution.py:758
  93.5 8.4 %collective-permute-start.23 = (bf16[200,384]{1,0:T(8,128)(2,1)S(1)}, bf16[200,384]{1,0:T(8,128)(2,1)S(1)}, u32[]{:S(2)}, u32[]{:S(2)}) collective-permute-start(bf16[200,384]{1,0:T(8,128)(2,1)S(1)} %get-tuple-element.123), channel_id=1, source_target_pairs={{0,6},{2,4},{4,2},{6,0},{1,7},{3,5},{5,3},{7,1},{8,14},{10,12},{12... | collective-permute-start | bytes 460808 | tf_op jit(solution)/shard_map/ppermute | solution.py:758
  102.7 12.9 %all-to-all-start.3 = ((bf16[4,56,384]{2,1,0:T(8,128)(2,1)}), bf16[4,56,384]{2,1,0:T(8,128)(2,1)S(1)}, u32[]{:S(2)}, u32[]{:S(2)}) async-start(bf16[4,56,384]{2,1,0:T(8,128)(2,1)} %join.1), calls=%async_computation.3 | async-start | bytes 344064 | tf_op jit(solution)/shard_map/all_to_all | solution.py:753
  (20 other events, 266.5 us)

commit v16 on v14

--- a/solution.py
+++ b/solution.py
@@ -27,7 +27,7 @@
 DENSITY_FACTOR = 0.3989422804014327
 BF = jnp.bfloat16
 F32 = jnp.float32
-VMEM_LIMIT = 40 << 20
+VMEM_LIMIT = 28 << 20
 SMALL_VMEM = 8 << 20
 SHAMPOO_VMEM = 24 << 20
 
@@ -284,7 +284,7 @@
         out_specs=[tile, tile, pl.BlockSpec((2, D), lambda i: (0, 0)), *[grad] * 4],
         out_shape=[
             jax.ShapeDtypeStruct((rows, D), F32),
-            pltpu.HBM((rows, D), F32),
+            jax.ShapeDtypeStruct((rows, D), F32),
             jax.ShapeDtypeStruct((2, D), F32),
             *[jax.ShapeDtypeStruct(grads, BF)] * 4,
         ],
@@ -434,7 +434,7 @@
         name="attn_backward",
     )(
         place, own_mask, other_mask,
-        tokens, in_hbm(grad), prob, qkv, out, in_hbm(norm_params), in_hbm(later_norms), wqkv, wo,
+        tokens, grad, prob, qkv, out, in_hbm(norm_params), in_hbm(later_norms), wqkv, wo,
     )
 
 

time: 121 us -> 123 us (1.017)
  local copies, waits for them, and re-layouts: 0.17 us -> 2.12 us
    unnamed x33 -> x45, local copies, waits for them, and re-layouts: 0.17 us -> 2.12 us
  transfers between devices with their start and end apart: 28 -> 28, of which waited for: 10 -> 10; matrix products, arithmetic and copies ran while one was open for 0% -> 0% of each run, Pallas kernels for 37% -> 35%
where the time goes in v16:
time: 123 us; the launch traced here: 122 us
  Pallas kernels  68.9 us (56%)
  starting transfers between devices  36.2 us (29%)
  waiting for transfers between devices  13.8 us (11%)
  local copies, waits for them, and re-layouts  2.12 us (2%)
    all_to_all x4, starting transfers between devices, to_all(): return lax.all_to_all(values, axis, 0, 0)  19.7 us
    pallas_call x1, Pallas kernels, mlp(): pl.pallas_call(mlp_kernel, grid=(rows // TILE,), in_specs=[pl.BlockSpec(m...  18 us
    ppermute x12, starting transfers between devices, across(): return lax.ppermute(values, 'inner', pairs)  14.2 us
    pallas_call x2, Pallas kernels, shampoo(): pl.pallas_call(lambda *refs: shampoo_kernel(scale, bool(norms), *refs), g...  13.8 us
    pallas_call x1, Pallas kernels, attn_backward(): pl.pallas_call(attn_backward_kernel, grid=(rows // TILE,), in_specs=[smem...  12.8 us
    pallas_call x1, Pallas kernels, attn_forward(): pl.pallas_call(attn_forward_kernel, grid=(rows // TILE,), in_specs=[smem]...  11.4 us
    pallas_call x1, Pallas kernels, input_gradient(): pl.pallas_call(input_grad_kernel, grid=(rows // INPUT_TILE,), in_specs=[t...  6.62 us
    ppermute x12, waiting for transfers between devices, across(): return lax.ppermute(values, 'inner', pairs)  5.96 us
  transfers between devices with their start and end apart: 28, of which 10 were waited for; matrix products, arithmetic and copies ran while one was open for 0% of the time, Pallas kernels for 35%

profile of v16, /device:TPU:0, one launch (start us, length us, event | category | flops | bytes accessed | tf_op | source)
XLA Modules:
  0.0 122.1 jit_solution(5237242318397984996)
XLA Ops:
  0.7 1.8 %pack.2 = bf16[4,1,48,384]{3,2,1,0:T(8,128)(2,1)} custom-call(f32[3,8,48,48]{3,2,1,0:T(8,128)} %bitcast.11), custom_call_target="tpu_custom_call" | custom-call | tf_op jit(solution)/shard_map/pack/pallas_call | solution.py:484
  2.5 6.3 %all-to-all-start = ((bf16[4,1,48,384]{3,2,1,0:T(8,128)(2,1)}), bf16[4,1,48,384]{3,2,1,0:T(8,128)(2,1)S(1)}, u32[]{:S(2)}, u32[]{:S(2)}) async-start(bf16[4,1,48,384]{3,2,1,0:T(8,128)(2,1)} %pack.2), calls=%async_computation | async-start | bytes 294912 | tf_op jit(solution)/shard_map/all_to_all | solution.py:753
  8.8 1.8 %pack.3 = bf16[4,2,48,384]{3,2,1,0:T(8,128)(2,1)} custom-call(f32[3,8,48,48]{3,2,1,0:T(8,128)} %bitcast.12), custom_call_target="tpu_custom_call" | custom-call | tf_op jit(solution)/shard_map/pack/pallas_call | solution.py:484
  10.6 4.4 %all-to-all-done = bf16[4,1,48,384]{3,2,1,0:T(8,128)(2,1)S(1)} async-done(((bf16[4,1,48,384]{3,2,1,0:T(8,128)(2,1)}), bf16[4,1,48,384]{3,2,1,0:T(8,128)(2,1)S(1)}, u32[]{:S(2)}, u32[]{:S(2)}) %all-to-all-start) | async-done | bytes 147488 | tf_op jit(solution)/shard_map/all_to_all | solution.py:753
  15.0 3.5 %all-to-all-start.1 = ((bf16[4,2,48,384]{3,2,1,0:T(8,128)(2,1)}), bf16[4,2,48,384]{3,2,1,0:T(8,128)(2,1)S(1)}, u32[]{:S(2)}, u32[]{:S(2)}) async-start(bf16[4,2,48,384]{3,2,1,0:T(8,128)(2,1)} %pack.3), calls=%async_computation.1 | async-start | bytes 589824 | tf_op jit(solution)/shard_map/all_to_all | solution.py:753
  18.5 2.5 %collective-permute-start.6 = (bf16[4,48,384]{2,1,0:T(8,128)(2,1)S(1)}, bf16[4,48,384]{2,1,0:T(8,128)(2,1)S(1)}, u32[]{:S(2)}, u32[]{:S(2)}) collective-permute-start(bf16[4,48,384]{2,1,0:T(8,128)(2,1)S(1)} %bitcast.16), channel_id=1, source_target_pairs={{0,6},{2,4},{4,2},{6,0},{1,7},{3,5},{5,3},{7,1},{8,14},{10,12},{12... | collective-permute-start | bytes 442376 | tf_op jit(solution)/shard_map/ppermute | solution.py:758
  22.7 3.4 %collective-permute-done.6.refs_3_ = bf16[4,48,384]{2,1,0:T(8,128)(2,1)S(1)} collective-permute-done((bf16[4,48,384]{2,1,0:T(8,128)(2,1)S(1)}, bf16[4,48,384]{2,1,0:T(8,128)(2,1)S(1)}, u32[]{:S(2)}, u32[]{:S(2)}) %collective-permute-start.6) | collective-permute-done | bytes 147488 | tf_op jit(solution)/shard_map/ppermute | solution.py:758
  27.6 2.4 %collective-permute-start.4 = (bf16[4,2,48,384]{3,2,1,0:T(8,128)(2,1)S(1)}, bf16[4,2,48,384]{3,2,1,0:T(8,128)(2,1)S(1)}, u32[]{:S(2)}, u32[]{:S(2)}) collective-permute-start(bf16[4,2,48,384]{3,2,1,0:T(8,128)(2,1)S(1)} %all-to-all-done.1.refs_0_), channel_id=1, source_target_pairs={{0,6},{2,4},{4,2},{6,0},{1,7},{3,5},{5,3},{7,1},{8,14},{10,12},{12... | collective-permute-start | bytes 884744 | tf_op jit(solution)/shard_map/ppermute | solution.py:758
  31.1 11.4 %attn_forward.1 = (bf16[6,3,512,256]{3,2,1,0:T(8,128)(2,1)}, bf16[1536,1152]{1,0:T(8,128)(2,1)}, bf16[1536,384]{1,0:T(8,128)(2,1)}, f32[1536,384]{1,0:T(8,128)S(...) custom-call(s32[14]{0:T(128)S(1)} %pad_add_fusion.place_ref, ...), custom_call_target="tpu_custom_call" | custom-call | flops 4227858432 | bytes 16777216 | tf_op jit(solution)/shard_map/attn_forward/pallas_call | solution.py:176
  42.6 1.6 %collective-permute-done.3.refs_2_ = bf16[4,2,48,384]{3,2,1,0:T(8,128)(2,1)S(1)} collective-permute-done((bf16[4,2,48,384]{3,2,1,0:T(8,128)(2,1)S(1)}, bf16[4,2,48,384]{3,2,1,0:T(8,128)(2,1)S(1)}, u32[]{:S(2)}, u32[]{:S(2)}) %collective-permute-start.3) | collective-permute-done | bytes 294944 | tf_op jit(solution)/shard_map/ppermute | solution.py:758
  46.6 1.3 %copy-done.9 = bf16[1536,384]{1,0:T(8,128)(2,1)S(1)} copy-done((bf16[1536,384]{1,0:T(8,128)(2,1)S(1)}, bf16[1536,384]{1,0:T(8,128)(2,1)}, u32[]{:S(2)}) %copy-start.9) | copy-done | bytes 1179672
  47.9 18.0 %mlp.1 = (f32[1536,384]{1,0:T(8,128)}, f32[1536,384]{1,0:T(8,128)S(1)}, f32[2,384]{1,0:T(2,128)S(1)}, bf16[2,4,2,48,384]{4,3,2,1,0:T(8,128)(2,1)S(1)}, bf16[2,4,...) custom-call(s32[14]{0:T(128)S(1)} %pad_add_fusion.place_ref, ...), custom_call_target="tpu_custom_call" | custom-call | flops 10871635968 | bytes 20971520 | tf_op jit(solution)/shard_map/mlp/pallas_call | solution.py:273
  66.5 1.5 %collective-permute-done.15.received_ref = bf16[2,4,2,48,384]{4,3,2,1,0:T(8,128)(2,1)S(1)} collective-permute-done((bf16[2,4,2,48,384]{4,3,2,1,0:T(8,128)(2,1)S(1)}, bf16[2,4,2,48,384]{4,3,2,1,0:T(8,128)(2,1)S(1)}, u32[]{:S(2)}, u32[]{:S(2)}) %collective-permute-start.15) | collective-permute-done | bytes 589856 | tf_op jit(solution)/shard_map/ppermute | solution.py:749
  68.2 1.3 %collective-permute-start.16 = (bf16[4,2,48,384]{3,2,1,0:T(8,128)(2,1)S(1)}, bf16[4,2,48,384]{3,2,1,0:T(8,128)(2,1)S(1)}, u32[]{:S(2)}, u32[]{:S(2)}) collective-permute-start(bf16[4,2,48,384]{3,2,1,0:T(8,128)(2,1)S(1)} %get-tuple-element.103), channel_id=1, source_target_pairs={{0,2},{2,0},{4,6},{6,4},{1,3},{3,1},{5,7},{7,5},{8,10},{10,8},{12,... | collective-permute-start | bytes 884744 | tf_op jit(solution)/shard_map/ppermute | solution.py:758
  69.6 1.1 collective-permute-start.18
  70.8 1.2 collective-permute-start.19
  72.0 12.8 %attn_backward.1 = (bf16[1536,1152]{1,0:T(8,128)(2,1)}, bf16[16,48,384]{2,1,0:T(8,128)(2,1)S(1)}, bf16[17,48,384]{2,1,0:T(8,128)(2,1)}, f32[4,384]{1,0:T(4,128)S(1)}) custom-call(s32[14]{0:T(128)S(1)} %copy-done.7, s32[12,3]{1,0:T(8,128)S(1)} %copy.26.own_mask_ref, s32[12,3]{1,0:T(8,128)S(1)} %copy-done.13, bf16[1536,384]{1,0:T(8,128)(2,1)S(1)} %copy-done.3, ...), custom_call_target="tpu_custom_call" | custom-call | flops 7096762368 | bytes 20971520 | tf_op jit(solution)/shard_map/attn_backward/pallas_call | solution.py:396
  85.8 4.9 %all-to-all-start.2 = ((bf16[4,2,48,384]{3,2,1,0:T(8,128)(2,1)}), bf16[4,2,48,384]{3,2,1,0:T(8,128)(2,1)S(1)}, u32[]{:S(2)}, u32[]{:S(2)}) async-start(bf16[4,2,48,384]{3,2,1,0:T(8,128)(2,1)} %sum_late.1), calls=%async_computation.2 | async-start | bytes 589824 | tf_op jit(solution)/shard_map/all_to_all | solution.py:753
  92.2 1.2 collective-permute-start.21
  94.2 1.5 %collective-permute-start.23 = (bf16[200,384]{1,0:T(8,128)(2,1)S(1)}, bf16[200,384]{1,0:T(8,128)(2,1)S(1)}, u32[]{:S(2)}, u32[]{:S(2)}) collective-permute-start(bf16[200,384]{1,0:T(8,128)(2,1)S(1)} %get-tuple-element.119), channel_id=1, source_target_pairs={{0,6},{2,4},{4,2},{6,0},{1,7},{3,5},{5,3},{7,1},{8,14},{10,12},{12... | collective-permute-start | bytes 460808 | tf_op jit(solution)/shard_map/ppermute | solution.py:758
  95.7 6.6 %input_gradient.1 = f32[1536,384]{1,0:T(8,128)} custom-call(bf16[1536,384]{1,0:T(8,128)(2,1)} %x_ref.5, f32[1536,384]{1,0:T(8,128)} %copy-done.1, bf16[1536,1152]{1,0:T(8,128)(2,1)} %get-tuple-element.120.dqkv_ref, f32[4,384]{1,0:T(4,128)} %refs_4_.1, bf16[384,1152]{1,0:T(8,128)(2,1)} %get-tuple-element.99.wqkv_ref), custom_call_target="tpu_custom_call" | custom-call | flops 1358954496 | bytes 10485760 | tf_op jit(solution)/shard_map/input_gradient/pallas_call | solution.py:452
  103.2 5.0 %all-to-all-start.3 = ((bf16[4,56,384]{2,1,0:T(8,128)(2,1)}), bf16[4,56,384]{2,1,0:T(8,128)(2,1)S(1)}, u32[]{:S(2)}, u32[]{:S(2)}) async-start(bf16[4,56,384]{2,1,0:T(8,128)(2,1)} %join.1), calls=%async_computation.3 | async-start | bytes 344064 | tf_op jit(solution)/shard_map/all_to_all | solution.py:753
  108.2 8.0 %shampoo.2 = (f32[3,8,48,48]{3,2,1,0:T(8,128)}, f32[3,8,48,48]{3,2,1,0:T(8,128)}, f32[3,8,48,48]{3,2,1,0:T(8,128)}, f32[3,8,48,48]{3,2,1,0:T(8,128)}) custom-call(bf16[4,2,48,384]{3,2,1,0:T(8,128)(2,1)S(1)} %all-to-all-done.2.refs_0_, f32[3,8,48,48]{3,2,1,0:T(8,128)S(1)} %bitcast.13, f32[3,8,48,48]{3,2,1,0:T(8,128)S(1)} %bitcast.21, ...), custom_call_target="tpu_custom_call" | custom-call | flops 6442450944 | bytes 4194304 | tf_op jit(solution)/shard_map/shampoo/pallas_call | solution.py:724
  116.2 5.8 %shampoo.3 = (f32[3,8,48,48]{3,2,1,0:T(8,128)}, f32[3,8,48,48]{3,2,1,0:T(8,128)}, f32[3,8,48,48]{3,2,1,0:T(8,128)}, f32[3,8,48,48]{3,2,1,0:T(8,128)}, f32[4,384]...) custom-call(bf16[4,1,56,384]{3,2,1,0:T(8,128)(2,1)S(1)} %bitcast.15,, ...), custom_call_target="tpu_custom_call", output_to_operand_aliasing={{0}: (6, {}), {1}: (7, {}), {2}: (8, {}), {3}: (9, {})} | custom-call | flops 3221225472 | bytes 4194304 | tf_op jit(solution)/shard_map/shampoo/pallas_call | solution.py:724
  (91 shorter events, 11.8 us)
Async XLA Ops:
  2.5 12.6 %all-to-all-start = ((bf16[4,1,48,384]{3,2,1,0:T(8,128)(2,1)}), bf16[4,1,48,384]{3,2,1,0:T(8,128)(2,1)S(1)}, u32[]{:S(2)}, u32[]{:S(2)}) async-start(bf16[4,1,48,384]{3,2,1,0:T(8,128)(2,1)} %pack.2), calls=%async_computation | async-start | bytes 294912 | tf_op jit(solution)/shard_map/all_to_all | solution.py:753
  15.0 12.0 %all-to-all-start.1 = ((bf16[4,2,48,384]{3,2,1,0:T(8,128)(2,1)}), bf16[4,2,48,384]{3,2,1,0:T(8,128)(2,1)S(1)}, u32[]{:S(2)}, u32[]{:S(2)}) async-start(bf16[4,2,48,384]{3,2,1,0:T(8,128)(2,1)} %pack.3), calls=%async_computation.1 | async-start | bytes 589824 | tf_op jit(solution)/shard_map/all_to_all | solution.py:753
  18.5 7.6 %collective-permute-start.6 = (bf16[4,48,384]{2,1,0:T(8,128)(2,1)S(1)}, bf16[4,48,384]{2,1,0:T(8,128)(2,1)S(1)}, u32[]{:S(2)}, u32[]{:S(2)}) collective-permute-start(bf16[4,48,384]{2,1,0:T(8,128)(2,1)S(1)} %bitcast.16), channel_id=1, source_target_pairs={{0,6},{2,4},{4,2},{6,0},{1,7},{3,5},{5,3},{7,1},{8,14},{10,12},{12... | collective-permute-start | bytes 442376 | tf_op jit(solution)/shard_map/ppermute | solution.py:758
  21.0 6.0 %collective-permute-start.5 = (bf16[4,48,384]{2,1,0:T(8,128)(2,1)S(1)}, bf16[4,48,384]{2,1,0:T(8,128)(2,1)S(1)}, u32[]{:S(2)}, u32[]{:S(2)}) collective-permute-start(bf16[4,48,384]{2,1,0:T(8,128)(2,1)S(1)} %bitcast.17), channel_id=1, source_target_pairs={{0,4},{2,6},{4,0},{6,2},{1,5},{3,7},{5,1},{7,3},{8,12},{10,14},{12... | collective-permute-start | bytes 442376 | tf_op jit(solution)/shard_map/ppermute | solution.py:758
  21.5 5.5 %collective-permute-start = (bf16[4,48,384]{2,1,0:T(8,128)(2,1)S(1)}, bf16[4,48,384]{2,1,0:T(8,128)(2,1)S(1)}, u32[]{:S(2)}, u32[]{:S(2)}) collective-permute-start(bf16[4,48,384]{2,1,0:T(8,128)(2,1)S(1)} %bitcast.18), channel_id=1, source_target_pairs={{0,2},{2,0},{4,6},{6,4},{1,3},{3,1},{5,7},{7,5},{8,10},{10,8},{12,... | collective-permute-start | bytes 442376 | tf_op jit(solution)/shard_map/ppermute | solution.py:758
  22.1 4.8 %collective-permute-start.1 = (s32[12,3]{1,0:T(8,128)S(1)}, s32[12,3]{1,0:T(8,128)S(1)}, u32[]{:S(2)}, u32[]{:S(2)}) collective-permute-start(s32[12,3]{1,0:T(8,128)S(1)} %copy.26.own_mask_ref), channel_id=1, source_target_pairs={{0,1},{1,0},{2,3},{3,2},{4,5},{5,4},{6,7},{7,6},{8,9},{9,8},{10,11... | collective-permute-start | bytes 440 | tf_op jit(solution)/shard_map/ppermute | solution.py:749
  22.2 5.4 %collective-permute-start.7 = (bf16[4,48,384]{2,1,0:T(8,128)(2,1)S(1)}, bf16[4,48,384]{2,1,0:T(8,128)(2,1)S(1)}, u32[]{:S(2)}, u32[]{:S(2)}) collective-permute-start(bf16[4,48,384]{2,1,0:T(8,128)(2,1)S(1)} %bitcast.19), channel_id=1, source_target_pairs={{0,1},{1,0},{2,3},{3,2},{4,5},{5,4},{6,7},{7,6},{8,9},{9,8},{10,11... | collective-permute-start | bytes 442376 | tf_op jit(solution)/shard_map/ppermute | solution.py:749
  26.1 3.9 %collective-permute-start.10 = (bf16[4,48,384]{2,1,0:T(8,128)(2,1)S(1)}, bf16[4,48,384]{2,1,0:T(8,128)(2,1)S(1)}, u32[]{:S(2)}, u32[]{:S(2)}) collective-permute-start(bf16[4,48,384]{2,1,0:T(8,128)(2,1)S(1)} %collective-permute-done.6.refs_3_), channel_id=1, source_target_pairs={{0,1},{1,0},{2,3},{3,2},{4,5},{5,4},{6,7},{7,6},{8,9},{9,8},{10,11... | collective-permute-start | bytes 442376 | tf_op jit(solution)/shard_map/ppermute | solution.py:749
  26.9 3.6 %collective-permute-start.9 = (bf16[4,48,384]{2,1,0:T(8,128)(2,1)S(1)}, bf16[4,48,384]{2,1,0:T(8,128)(2,1)S(1)}, u32[]{:S(2)}, u32[]{:S(2)}) collective-permute-start(bf16[4,48,384]{2,1,0:T(8,128)(2,1)S(1)} %collective-permute-done.5.refs_2_), channel_id=1, source_target_pairs={{0,1},{1,0},{2,3},{3,2},{4,5},{5,4},{6,7},{7,6},{8,9},{9,8},{10,11... | collective-permute-start | bytes 442376 | tf_op jit(solution)/shard_map/ppermute | solution.py:749
  27.0 4.1 %collective-permute-start.8 = (bf16[4,48,384]{2,1,0:T(8,128)(2,1)S(1)}, bf16[4,48,384]{2,1,0:T(8,128)(2,1)S(1)}, u32[]{:S(2)}, u32[]{:S(2)}) collective-permute-start(bf16[4,48,384]{2,1,0:T(8,128)(2,1)S(1)} %collective-permute-done.refs_1_), channel_id=1, source_target_pairs={{0,1},{1,0},{2,3},{3,2},{4,5},{5,4},{6,7},{7,6},{8,9},{9,8},{10,11... | collective-permute-start | bytes 442376 | tf_op jit(solution)/shard_map/ppermute | solution.py:749
  27.5 17.2 %collective-permute-start.11 = (bf16[4,2,48,384]{3,2,1,0:T(8,128)(2,1)S(1)}, bf16[4,2,48,384]{3,2,1,0:T(8,128)(2,1)S(1)}, u32[]{:S(2)}, u32[]{:S(2)}) collective-permute-start(bf16[4,2,48,384]{3,2,1,0:T(8,128)(2,1)S(1)} %all-to-all-done.1.refs_0_), channel_id=1, source_target_pairs={{0,1},{1,0},{2,3},{3,2},{4,5},{5,4},{6,7},{7,6},{8,9},{9,8},{10,11... | collective-permute-start | bytes 884744 | tf_op jit(solution)/shard_map/ppermute | solution.py:749
  27.6 15.0 %collective-permute-start.4 = (bf16[4,2,48,384]{3,2,1,0:T(8,128)(2,1)S(1)}, bf16[4,2,48,384]{3,2,1,0:T(8,128)(2,1)S(1)}, u32[]{:S(2)}, u32[]{:S(2)}) collective-permute-start(bf16[4,2,48,384]{3,2,1,0:T(8,128)(2,1)S(1)} %all-to-all-done.1.refs_0_), channel_id=1, source_target_pairs={{0,6},{2,4},{4,2},{6,0},{1,7},{3,5},{5,3},{7,1},{8,14},{10,12},{12... | collective-permute-start | bytes 884744 | tf_op jit(solution)/shard_map/ppermute | solution.py:758
  30.0 14.2 %collective-permute-start.3 = (bf16[4,2,48,384]{3,2,1,0:T(8,128)(2,1)S(1)}, bf16[4,2,48,384]{3,2,1,0:T(8,128)(2,1)S(1)}, u32[]{:S(2)}, u32[]{:S(2)}) collective-permute-start(bf16[4,2,48,384]{3,2,1,0:T(8,128)(2,1)S(1)} %all-to-all-done.1.refs_0_), channel_id=1, source_target_pairs={{0,4},{2,6},{4,0},{6,2},{1,5},{3,7},{5,1},{7,3},{8,12},{10,14},{12... | collective-permute-start | bytes 884744 | tf_op jit(solution)/shard_map/ppermute | solution.py:758
  30.5 13.7 %collective-permute-start.2 = (bf16[4,2,48,384]{3,2,1,0:T(8,128)(2,1)S(1)}, bf16[4,2,48,384]{3,2,1,0:T(8,128)(2,1)S(1)}, u32[]{:S(2)}, u32[]{:S(2)}) collective-permute-start(bf16[4,2,48,384]{3,2,1,0:T(8,128)(2,1)S(1)} %all-to-all-done.1.refs_0_), channel_id=1, source_target_pairs={{0,2},{2,0},{4,6},{6,4},{1,3},{3,1},{5,7},{7,5},{8,10},{10,8},{12,... | collective-permute-start | bytes 884744 | tf_op jit(solution)/shard_map/ppermute | solution.py:758
  66.2 3.3 %collective-permute-start.17 = (bf16[2,4,2,48,384]{4,3,2,1,0:T(8,128)(2,1)S(1)}, bf16[2,4,2,48,384]{4,3,2,1,0:T(8,128)(2,1)S(1)}, u32[]{:S(2)}, u32[]{:S(2)}) collective-permute-start(bf16[2,4,2,48,384]{4,3,2,1,0:T(8,128)(2,1)S(1)} %get-tuple-element.105), channel_id=1, source_target_pairs={{0,1},{1,0},{2,3},{3,2},{4,5},{5,4},{6,7},{7,6},{8,9},{9,8},{10,11... | collective-permute-start | bytes 1769480 | tf_op jit(solution)/shard_map/ppermute | solution.py:749
  68.2 16.7 %collective-permute-start.16 = (bf16[4,2,48,384]{3,2,1,0:T(8,128)(2,1)S(1)}, bf16[4,2,48,384]{3,2,1,0:T(8,128)(2,1)S(1)}, u32[]{:S(2)}, u32[]{:S(2)}) collective-permute-start(bf16[4,2,48,384]{3,2,1,0:T(8,128)(2,1)S(1)} %get-tuple-element.103), channel_id=1, source_target_pairs={{0,2},{2,0},{4,6},{6,4},{1,3},{3,1},{5,7},{7,5},{8,10},{10,8},{12,... | collective-permute-start | bytes 884744 | tf_op jit(solution)/shard_map/ppermute | solution.py:758
  69.6 15.2 %collective-permute-start.18 = (bf16[4,2,48,384]{3,2,1,0:T(8,128)(2,1)S(1)}, bf16[4,2,48,384]{3,2,1,0:T(8,128)(2,1)S(1)}, u32[]{:S(2)}, u32[]{:S(2)}) collective-permute-start(bf16[4,2,48,384]{3,2,1,0:T(8,128)(2,1)S(1)} %get-tuple-element.106), channel_id=1, source_target_pairs={{0,4},{2,6},{4,0},{6,2},{1,5},{3,7},{5,1},{7,3},{8,12},{10,14},{12... | collective-permute-start | bytes 884744 | tf_op jit(solution)/shard_map/ppermute | solution.py:758
  70.8 14.1 %collective-permute-start.19 = (bf16[4,2,48,384]{3,2,1,0:T(8,128)(2,1)S(1)}, bf16[4,2,48,384]{3,2,1,0:T(8,128)(2,1)S(1)}, u32[]{:S(2)}, u32[]{:S(2)}) collective-permute-start(bf16[4,2,48,384]{3,2,1,0:T(8,128)(2,1)S(1)} %get-tuple-element.107), channel_id=1, source_target_pairs={{0,6},{2,4},{4,2},{6,0},{1,7},{3,5},{5,3},{7,1},{8,14},{10,12},{12... | collective-permute-start | bytes 884744 | tf_op jit(solution)/shard_map/ppermute | solution.py:758
  84.9 5.9 %collective-permute-start.20 = (bf16[17,48,384]{2,1,0:T(8,128)(2,1)}, bf16[17,48,384]{2,1,0:T(8,128)(2,1)S(1)}, u32[]{:S(2)}, u32[]{:S(2)}) collective-permute-start(bf16[17,48,384]{2,1,0:T(8,128)(2,1)} %get-tuple-element.109), channel_id=1, source_target_pairs={{0,1},{1,0},{2,3},{3,2},{4,5},{5,4},{6,7},{7,6},{8,9},{9,8},{10,11... | collective-permute-start | bytes 1880072 | tf_op jit(solution)/shard_map/ppermute | solution.py:749
  85.8 17.4 %all-to-all-start.2 = ((bf16[4,2,48,384]{3,2,1,0:T(8,128)(2,1)}), bf16[4,2,48,384]{3,2,1,0:T(8,128)(2,1)S(1)}, u32[]{:S(2)}, u32[]{:S(2)}) async-start(bf16[4,2,48,384]{3,2,1,0:T(8,128)(2,1)} %sum_late.1), calls=%async_computation.2 | async-start | bytes 589824 | tf_op jit(solution)/shard_map/all_to_all | solution.py:753
  92.2 10.2 %collective-permute-start.21 = (bf16[200,384]{1,0:T(8,128)(2,1)S(1)}, bf16[200,384]{1,0:T(8,128)(2,1)S(1)}, u32[]{:S(2)}, u32[]{:S(2)}) collective-permute-start(bf16[200,384]{1,0:T(8,128)(2,1)S(1)} %get-tuple-element.117), channel_id=1, source_target_pairs={{0,2},{2,0},{4,6},{6,4},{1,3},{3,1},{5,7},{7,5},{8,10},{10,8},{12,... | collective-permute-start | bytes 460808 | tf_op jit(solution)/shard_map/ppermute | solution.py:758
  93.3 9.1 %collective-permute-start.22 = (bf16[200,384]{1,0:T(8,128)(2,1)S(1)}, bf16[200,384]{1,0:T(8,128)(2,1)S(1)}, u32[]{:S(2)}, u32[]{:S(2)}) collective-permute-start(bf16[200,384]{1,0:T(8,128)(2,1)S(1)} %get-tuple-element.118), channel_id=1, source_target_pairs={{0,4},{2,6},{4,0},{6,2},{1,5},{3,7},{5,1},{7,3},{8,12},{10,14},{12... | collective-permute-start | bytes 460808 | tf_op jit(solution)/shard_map/ppermute | solution.py:758
  94.2 8.3 %collective-permute-start.23 = (bf16[200,384]{1,0:T(8,128)(2,1)S(1)}, bf16[200,384]{1,0:T(8,128)(2,1)S(1)}, u32[]{:S(2)}, u32[]{:S(2)}) collective-permute-start(bf16[200,384]{1,0:T(8,128)(2,1)S(1)} %get-tuple-element.119), channel_id=1, source_target_pairs={{0,6},{2,4},{4,2},{6,0},{1,7},{3,5},{5,3},{7,1},{8,14},{10,12},{12... | collective-permute-start | bytes 460808 | tf_op jit(solution)/shard_map/ppermute | solution.py:758
  103.2 13.0 %all-to-all-start.3 = ((bf16[4,56,384]{2,1,0:T(8,128)(2,1)}), bf16[4,56,384]{2,1,0:T(8,128)(2,1)S(1)}, u32[]{:S(2)}, u32[]{:S(2)}) async-start(bf16[4,56,384]{2,1,0:T(8,128)(2,1)} %join.1), calls=%async_computation.3 | async-start | bytes 344064 | tf_op jit(solution)/shard_map/all_to_all | solution.py:753
  (26 other events, 314.6 us)

commit v17 on v14

--- a/solution.py
+++ b/solution.py
@@ -478,6 +478,23 @@
             out_ref[copy, group] = slab
 
 
+def pack_early_kernel(weight_ref, out_ref):
+    blocks = [weight_ref[0, block] for block in range(weight_ref.shape[1])]
+    slab = jnp.concatenate(blocks, axis=1).astype(BF)
+    for copy in range(OUTER):
+        out_ref[copy] = slab
+
+
+def pack_early(weights):
+    _, count, edge, _ = weights.shape
+    return pl.pallas_call(
+        pack_early_kernel,
+        out_shape=jax.ShapeDtypeStruct((OUTER, edge, count * edge), BF),
+        compiler_params=pltpu.CompilerParams(vmem_limit_bytes=SMALL_VMEM),
+        name="pack_early",
+    )(in_hbm(weights))
+
+
 def pack(weights, first, groups):
     _, count, edge, _ = weights.shape
     shape = (OUTER, groups, edge, count * edge)
@@ -763,7 +780,7 @@
 
 
 def gather_slabs(weights, small):
-    early = to_all(pack(weights, 0, 1), "outer")[:, 0]
+    early = to_all(pack_early(weights), "outer")
     early, late = lax.optimization_barrier((early, pack(weights, 1, 2)))
     late = to_all(late, "outer")
     early = from_all(early)

time: 121 us -> 121 us (level)
    pallas_call x0 -> x1, Pallas kernels: none -> 1.92 us  [pack_early(): pl.pallas_call(pack_early_kernel, out_shape=jax.ShapeDtypeStruct((OUTER,...]
    pallas_call x2 -> x1, Pallas kernels: 3.61 us -> 1.83 us  [pack(): pl.pallas_call(pack_kernel, grid=(1,), in_specs=[pl.BlockSpec((pl.Element...]
where the time goes in v17:
time: 121 us
  Pallas kernels  70.1 us (58%)
  starting transfers between devices  36.2 us (30%)
  waiting for transfers between devices  13.1 us (11%)
    all_to_all x4, starting transfers between devices, to_all(): return lax.all_to_all(values, axis, 0, 0)  19.7 us
    pallas_call x1, Pallas kernels, mlp(): pl.pallas_call(mlp_kernel, grid=(rows // TILE,), in_specs=[pl.BlockSpec(m...  18.1 us
    ppermute x12, starting transfers between devices, across(): return lax.ppermute(values, 'inner', pairs)  14.2 us
    pallas_call x2, Pallas kernels, shampoo(): pl.pallas_call(lambda *refs: shampoo_kernel(scale, bool(norms), *refs), g...  13.8 us
    pallas_call x1, Pallas kernels, attn_backward(): pl.pallas_call(attn_backward_kernel, grid=(rows // TILE,), in_specs=[smem...  13.1 us
    pallas_call x1, Pallas kernels, attn_forward(): pl.pallas_call(attn_forward_kernel, grid=(rows // TILE,), in_specs=[smem]...  12.2 us
    pallas_call x1, Pallas kernels, input_gradient(): pl.pallas_call(input_grad_kernel, grid=(rows // INPUT_TILE,), in_specs=[t...  6.62 us
    ppermute x12, waiting for transfers between devices, across(): return lax.ppermute(values, 'inner', pairs)  5.19 us
  transfers between devices with their start and end apart: 28, of which 10 were waited for; matrix products, arithmetic and copies ran while one was open for 0% of the time, Pallas kernels for 37%

profile of v17, /device:TPU:0, one launch (start us, length us, event | category | flops | bytes accessed | tf_op | source)
XLA Modules:
  0.0 120.6 jit_solution(16959922480043551173)
XLA Ops:
  0.7 1.9 %pack_early.1 = bf16[4,48,384]{2,1,0:T(8,128)(2,1)} custom-call(f32[3,8,48,48]{3,2,1,0:T(8,128)} %bitcast.10), custom_call_target="tpu_custom_call" | custom-call | tf_op jit(solution)/shard_map/pack_early/pallas_call | solution.py:490
  2.6 6.3 %all-to-all-start = ((bf16[4,48,384]{2,1,0:T(8,128)(2,1)}), bf16[4,48,384]{2,1,0:T(8,128)(2,1)S(1)}, u32[]{:S(2)}, u32[]{:S(2)}) async-start(bf16[4,48,384]{2,1,0:T(8,128)(2,1)} %pack_early.1), calls=%async_computation | async-start | bytes 294912 | tf_op jit(solution)/shard_map/all_to_all | solution.py:770
  8.9 1.8 %pack.1 = bf16[4,2,48,384]{3,2,1,0:T(8,128)(2,1)} custom-call(f32[3,8,48,48]{3,2,1,0:T(8,128)} %bitcast.11), custom_call_target="tpu_custom_call" | custom-call | tf_op jit(solution)/shard_map/pack/pallas_call | solution.py:501
  10.7 4.4 %all-to-all-done.refs_0_ = bf16[4,48,384]{2,1,0:T(8,128)(2,1)S(1)} async-done(((bf16[4,48,384]{2,1,0:T(8,128)(2,1)}), bf16[4,48,384]{2,1,0:T(8,128)(2,1)S(1)}, u32[]{:S(2)}, u32[]{:S(2)}) %all-to-all-start) | async-done | bytes 147488 | tf_op jit(solution)/shard_map/all_to_all | solution.py:770
  15.2 3.5 %all-to-all-start.1 = ((bf16[4,2,48,384]{3,2,1,0:T(8,128)(2,1)}), bf16[4,2,48,384]{3,2,1,0:T(8,128)(2,1)S(1)}, u32[]{:S(2)}, u32[]{:S(2)}) async-start(bf16[4,2,48,384]{3,2,1,0:T(8,128)(2,1)} %pack.1), calls=%async_computation.1 | async-start | bytes 589824 | tf_op jit(solution)/shard_map/all_to_all | solution.py:770
  18.6 2.5 %collective-permute-start.6 = (bf16[4,48,384]{2,1,0:T(8,128)(2,1)S(1)}, bf16[4,48,384]{2,1,0:T(8,128)(2,1)S(1)}, u32[]{:S(2)}, u32[]{:S(2)}) collective-permute-start(bf16[4,48,384]{2,1,0:T(8,128)(2,1)S(1)} %all-to-all-done.refs_0_), channel_id=1, source_target_pairs={{0,6},{2,4},{4,2},{6,0},{1,7},{3,5},{5,3},{7,1},{8,14},{10,12},{12... | collective-permute-start | bytes 442376 | tf_op jit(solution)/shard_map/ppermute | solution.py:775
  22.9 3.4 %collective-permute-done.6.refs_3_ = bf16[4,48,384]{2,1,0:T(8,128)(2,1)S(1)} collective-permute-done((bf16[4,48,384]{2,1,0:T(8,128)(2,1)S(1)}, bf16[4,48,384]{2,1,0:T(8,128)(2,1)S(1)}, u32[]{:S(2)}, u32[]{:S(2)}) %collective-permute-start.6) | collective-permute-done | bytes 147488 | tf_op jit(solution)/shard_map/ppermute | solution.py:775
  27.8 2.4 %collective-permute-start.4 = (bf16[4,2,48,384]{3,2,1,0:T(8,128)(2,1)S(1)}, bf16[4,2,48,384]{3,2,1,0:T(8,128)(2,1)S(1)}, u32[]{:S(2)}, u32[]{:S(2)}) collective-permute-start(bf16[4,2,48,384]{3,2,1,0:T(8,128)(2,1)S(1)} %all-to-all-done.1.refs_0_), channel_id=1, source_target_pairs={{0,6},{2,4},{4,2},{6,0},{1,7},{3,5},{5,3},{7,1},{8,14},{10,12},{12... | collective-permute-start | bytes 884744 | tf_op jit(solution)/shard_map/ppermute | solution.py:775
  31.3 12.2 %attn_forward.1 = (bf16[6,3,512,256]{3,2,1,0:T(8,128)(2,1)}, bf16[1536,1152]{1,0:T(8,128)(2,1)}, bf16[1536,384]{1,0:T(8,128)(2,1)}, f32[1536,384]{1,0:T(8,128)S(...) custom-call(s32[14]{0:T(128)S(1)} %pad_add_fusion.place_ref, ...), custom_call_target="tpu_custom_call" | custom-call | flops 4227858432 | bytes 16777216 | tf_op jit(solution)/shard_map/attn_forward/pallas_call | solution.py:176
  44.9 1.1 collective-permute-done.12.refs_5_
  46.8 18.1 %mlp.1 = (f32[1536,384]{1,0:T(8,128)}, f32[1536,384]{1,0:T(8,128)}, f32[2,384]{1,0:T(2,128)S(1)}, bf16[2,4,2,48,384]{4,3,2,1,0:T(8,128)(2,1)S(1)}, bf16[2,4,2,48...) custom-call(s32[14]{0:T(128)S(1)} %pad_add_fusion.place_ref, ...), custom_call_target="tpu_custom_call" | custom-call | flops 10871635968 | bytes 20971520 | tf_op jit(solution)/shard_map/mlp/pallas_call | solution.py:273
  65.4 1.5 %collective-permute-done.15.received_ref = bf16[2,4,2,48,384]{4,3,2,1,0:T(8,128)(2,1)S(1)} collective-permute-done((bf16[2,4,2,48,384]{4,3,2,1,0:T(8,128)(2,1)S(1)}, bf16[2,4,2,48,384]{4,3,2,1,0:T(8,128)(2,1)S(1)}, u32[]{:S(2)}, u32[]{:S(2)}) %collective-permute-start.15) | collective-permute-done | bytes 589856 | tf_op jit(solution)/shard_map/ppermute | solution.py:766
  67.1 1.3 %collective-permute-start.16 = (bf16[4,2,48,384]{3,2,1,0:T(8,128)(2,1)S(1)}, bf16[4,2,48,384]{3,2,1,0:T(8,128)(2,1)S(1)}, u32[]{:S(2)}, u32[]{:S(2)}) collective-permute-start(bf16[4,2,48,384]{3,2,1,0:T(8,128)(2,1)S(1)} %get-tuple-element.103), channel_id=1, source_target_pairs={{0,2},{2,0},{4,6},{6,4},{1,3},{3,1},{5,7},{7,5},{8,10},{10,8},{12,... | collective-permute-start | bytes 884744 | tf_op jit(solution)/shard_map/ppermute | solution.py:775
  68.5 1.1 collective-permute-start.18
  69.7 1.2 collective-permute-start.19
  70.9 13.1 %attn_backward.1 = (bf16[1536,1152]{1,0:T(8,128)(2,1)}, bf16[16,48,384]{2,1,0:T(8,128)(2,1)S(1)}, bf16[17,48,384]{2,1,0:T(8,128)(2,1)}, f32[4,384]{1,0:T(4,128)S(1)}) custom-call(s32[14]{0:T(128)S(1)} %pad_add_fusion.place_ref, s32[12,3]{1,0:T(8,128)S(1)} %copy.22.own_mask_ref, s32[12,3]{1,0:T(8,128)S(1)} %collective-permute-done.1.other_mask_ref, ...), custom_call_target="tpu_custom_call" | custom-call | flops 7096762368 | bytes 20971520 | tf_op jit(solution)/shard_map/attn_backward/pallas_call | solution.py:396
  84.1 0.9 sum_late.1
  85.0 4.9 %all-to-all-start.2 = ((bf16[4,2,48,384]{3,2,1,0:T(8,128)(2,1)}), bf16[4,2,48,384]{3,2,1,0:T(8,128)(2,1)S(1)}, u32[]{:S(2)}, u32[]{:S(2)}) async-start(bf16[4,2,48,384]{3,2,1,0:T(8,128)(2,1)} %sum_late.1), calls=%async_computation.2 | async-start | bytes 589824 | tf_op jit(solution)/shard_map/all_to_all | solution.py:770
  90.6 1.2 collective-permute-start.21
  92.6 1.6 %collective-permute-start.23 = (bf16[200,384]{1,0:T(8,128)(2,1)S(1)}, bf16[200,384]{1,0:T(8,128)(2,1)S(1)}, u32[]{:S(2)}, u32[]{:S(2)}) collective-permute-start(bf16[200,384]{1,0:T(8,128)(2,1)S(1)} %get-tuple-element.119), channel_id=1, source_target_pairs={{0,6},{2,4},{4,2},{6,0},{1,7},{3,5},{5,3},{7,1},{8,14},{10,12},{12... | collective-permute-start | bytes 460808 | tf_op jit(solution)/shard_map/ppermute | solution.py:775
  94.2 6.6 %input_gradient.1 = f32[1536,384]{1,0:T(8,128)} custom-call(bf16[1536,384]{1,0:T(8,128)(2,1)} %x_ref.5, f32[1536,384]{1,0:T(8,128)} %get-tuple-element.94.grad_ref, bf16[1536,1152]{1,0:T(8,128)(2,1)} %get-tuple-element.120.dqkv_ref, f32[4,384]{1,0:T(4,128)} %refs_4_.1, bf16[384,1152]{1,0:T(8,128)(2,1)} %get-tuple-element.99.wqkv_ref), custom_call_target="tpu_custom_call" | custom-call | flops 1358954496 | bytes 10485760 | tf_op jit(solution)/shard_map/input_gradient/pallas_call | solution.py:452
  101.7 5.0 %all-to-all-start.3 = ((bf16[4,56,384]{2,1,0:T(8,128)(2,1)}), bf16[4,56,384]{2,1,0:T(8,128)(2,1)S(1)}, u32[]{:S(2)}, u32[]{:S(2)}) async-start(bf16[4,56,384]{2,1,0:T(8,128)(2,1)} %join.1), calls=%async_computation.3 | async-start | bytes 344064 | tf_op jit(solution)/shard_map/all_to_all | solution.py:770
  106.7 8.0 %shampoo.2 = (f32[3,8,48,48]{3,2,1,0:T(8,128)}, f32[3,8,48,48]{3,2,1,0:T(8,128)}, f32[3,8,48,48]{3,2,1,0:T(8,128)}, f32[3,8,48,48]{3,2,1,0:T(8,128)}) custom-call(bf16[4,2,48,384]{3,2,1,0:T(8,128)(2,1)S(1)} %all-to-all-done.2.refs_0_, f32[3,8,48,48]{3,2,1,0:T(8,128)S(1)} %bitcast.12, f32[3,8,48,48]{3,2,1,0:T(8,128)S(1)} %bitcast.15, ...), custom_call_target="tpu_custom_call" | custom-call | flops 6442450944 | bytes 4194304 | tf_op jit(solution)/shard_map/shampoo/pallas_call | solution.py:741
  114.7 5.8 %shampoo.3 = (f32[3,8,48,48]{3,2,1,0:T(8,128)}, f32[3,8,48,48]{3,2,1,0:T(8,128)}, f32[3,8,48,48]{3,2,1,0:T(8,128)}, f32[3,8,48,48]{3,2,1,0:T(8,128)}, f32[4,384]...) custom-call(bf16[4,1,56,384]{3,2,1,0:T(8,128)(2,1)S(1)} %bitcast.14,, ...), custom_call_target="tpu_custom_call", output_to_operand_aliasing={{0}: (6, {}), {1}: (7, {}), {2}: (8, {}), {3}: (9, {})} | custom-call | flops 3221225472 | bytes 4194304 | tf_op jit(solution)/shard_map/shampoo/pallas_call | solution.py:741
  (80 shorter events, 10.0 us)
Async XLA Ops:
  2.6 12.6 %all-to-all-start = ((bf16[4,48,384]{2,1,0:T(8,128)(2,1)}), bf16[4,48,384]{2,1,0:T(8,128)(2,1)S(1)}, u32[]{:S(2)}, u32[]{:S(2)}) async-start(bf16[4,48,384]{2,1,0:T(8,128)(2,1)} %pack_early.1), calls=%async_computation | async-start | bytes 294912 | tf_op jit(solution)/shard_map/all_to_all | solution.py:770
  15.2 12.0 %all-to-all-start.1 = ((bf16[4,2,48,384]{3,2,1,0:T(8,128)(2,1)}), bf16[4,2,48,384]{3,2,1,0:T(8,128)(2,1)S(1)}, u32[]{:S(2)}, u32[]{:S(2)}) async-start(bf16[4,2,48,384]{3,2,1,0:T(8,128)(2,1)} %pack.1), calls=%async_computation.1 | async-start | bytes 589824 | tf_op jit(solution)/shard_map/all_to_all | solution.py:770
  18.6 7.6 %collective-permute-start.6 = (bf16[4,48,384]{2,1,0:T(8,128)(2,1)S(1)}, bf16[4,48,384]{2,1,0:T(8,128)(2,1)S(1)}, u32[]{:S(2)}, u32[]{:S(2)}) collective-permute-start(bf16[4,48,384]{2,1,0:T(8,128)(2,1)S(1)} %all-to-all-done.refs_0_), channel_id=1, source_target_pairs={{0,6},{2,4},{4,2},{6,0},{1,7},{3,5},{5,3},{7,1},{8,14},{10,12},{12... | collective-permute-start | bytes 442376 | tf_op jit(solution)/shard_map/ppermute | solution.py:775
  21.1 6.0 %collective-permute-start.5 = (bf16[4,48,384]{2,1,0:T(8,128)(2,1)S(1)}, bf16[4,48,384]{2,1,0:T(8,128)(2,1)S(1)}, u32[]{:S(2)}, u32[]{:S(2)}) collective-permute-start(bf16[4,48,384]{2,1,0:T(8,128)(2,1)S(1)} %all-to-all-done.refs_0_), channel_id=1, source_target_pairs={{0,4},{2,6},{4,0},{6,2},{1,5},{3,7},{5,1},{7,3},{8,12},{10,14},{12... | collective-permute-start | bytes 442376 | tf_op jit(solution)/shard_map/ppermute | solution.py:775
  21.6 5.5 %collective-permute-start = (bf16[4,48,384]{2,1,0:T(8,128)(2,1)S(1)}, bf16[4,48,384]{2,1,0:T(8,128)(2,1)}, u32[]{:S(2)}, u32[]{:S(2)}) collective-permute-start(bf16[4,48,384]{2,1,0:T(8,128)(2,1)S(1)} %all-to-all-done.refs_0_), channel_id=1, source_target_pairs={{0,2},{2,0},{4,6},{6,4},{1,3},{3,1},{5,7},{7,5},{8,10},{10,8},{12,... | collective-permute-start | bytes 442376 | tf_op jit(solution)/shard_map/ppermute | solution.py:775
  22.3 4.8 %collective-permute-start.1 = (s32[12,3]{1,0:T(8,128)S(1)}, s32[12,3]{1,0:T(8,128)S(1)}, u32[]{:S(2)}, u32[]{:S(2)}) collective-permute-start(s32[12,3]{1,0:T(8,128)S(1)} %copy.22.own_mask_ref), channel_id=1, source_target_pairs={{0,1},{1,0},{2,3},{3,2},{4,5},{5,4},{6,7},{7,6},{8,9},{9,8},{10,11... | collective-permute-start | bytes 440 | tf_op jit(solution)/shard_map/ppermute | solution.py:766
  22.4 5.4 %collective-permute-start.7 = (bf16[4,48,384]{2,1,0:T(8,128)(2,1)S(1)}, bf16[4,48,384]{2,1,0:T(8,128)(2,1)}, u32[]{:S(2)}, u32[]{:S(2)}) collective-permute-start(bf16[4,48,384]{2,1,0:T(8,128)(2,1)S(1)} %all-to-all-done.refs_0_), channel_id=1, source_target_pairs={{0,1},{1,0},{2,3},{3,2},{4,5},{5,4},{6,7},{7,6},{8,9},{9,8},{10,11... | collective-permute-start | bytes 442376 | tf_op jit(solution)/shard_map/ppermute | solution.py:766
  26.2 3.9 %collective-permute-start.10 = (bf16[4,48,384]{2,1,0:T(8,128)(2,1)S(1)}, bf16[4,48,384]{2,1,0:T(8,128)(2,1)}, u32[]{:S(2)}, u32[]{:S(2)}) collective-permute-start(bf16[4,48,384]{2,1,0:T(8,128)(2,1)S(1)} %collective-permute-done.6.refs_3_), channel_id=1, source_target_pairs={{0,1},{1,0},{2,3},{3,2},{4,5},{5,4},{6,7},{7,6},{8,9},{9,8},{10,11... | collective-permute-start | bytes 442376 | tf_op jit(solution)/shard_map/ppermute | solution.py:766
  27.1 3.6 %collective-permute-start.9 = (bf16[4,48,384]{2,1,0:T(8,128)(2,1)S(1)}, bf16[4,48,384]{2,1,0:T(8,128)(2,1)}, u32[]{:S(2)}, u32[]{:S(2)}) collective-permute-start(bf16[4,48,384]{2,1,0:T(8,128)(2,1)S(1)} %collective-permute-done.5.refs_2_), channel_id=1, source_target_pairs={{0,1},{1,0},{2,3},{3,2},{4,5},{5,4},{6,7},{7,6},{8,9},{9,8},{10,11... | collective-permute-start | bytes 442376 | tf_op jit(solution)/shard_map/ppermute | solution.py:766
  27.2 4.1 %collective-permute-start.8 = (bf16[4,48,384]{2,1,0:T(8,128)(2,1)}, bf16[4,48,384]{2,1,0:T(8,128)(2,1)S(1)}, u32[]{:S(2)}, u32[]{:S(2)}) collective-permute-start(bf16[4,48,384]{2,1,0:T(8,128)(2,1)} %collective-permute-done.refs_1_), channel_id=1, source_target_pairs={{0,1},{1,0},{2,3},{3,2},{4,5},{5,4},{6,7},{7,6},{8,9},{9,8},{10,11... | collective-permute-start | bytes 442376 | tf_op jit(solution)/shard_map/ppermute | solution.py:766
  27.7 17.2 %collective-permute-start.11 = (bf16[4,2,48,384]{3,2,1,0:T(8,128)(2,1)S(1)}, bf16[4,2,48,384]{3,2,1,0:T(8,128)(2,1)S(1)}, u32[]{:S(2)}, u32[]{:S(2)}) collective-permute-start(bf16[4,2,48,384]{3,2,1,0:T(8,128)(2,1)S(1)} %all-to-all-done.1.refs_0_), channel_id=1, source_target_pairs={{0,1},{1,0},{2,3},{3,2},{4,5},{5,4},{6,7},{7,6},{8,9},{9,8},{10,11... | collective-permute-start | bytes 884744 | tf_op jit(solution)/shard_map/ppermute | solution.py:766
  27.8 15.7 %collective-permute-start.4 = (bf16[4,2,48,384]{3,2,1,0:T(8,128)(2,1)S(1)}, bf16[4,2,48,384]{3,2,1,0:T(8,128)(2,1)S(1)}, u32[]{:S(2)}, u32[]{:S(2)}) collective-permute-start(bf16[4,2,48,384]{3,2,1,0:T(8,128)(2,1)S(1)} %all-to-all-done.1.refs_0_), channel_id=1, source_target_pairs={{0,6},{2,4},{4,2},{6,0},{1,7},{3,5},{5,3},{7,1},{8,14},{10,12},{12... | collective-permute-start | bytes 884744 | tf_op jit(solution)/shard_map/ppermute | solution.py:775
  30.1 14.2 %collective-permute-start.3 = (bf16[4,2,48,384]{3,2,1,0:T(8,128)(2,1)S(1)}, bf16[4,2,48,384]{3,2,1,0:T(8,128)(2,1)S(1)}, u32[]{:S(2)}, u32[]{:S(2)}) collective-permute-start(bf16[4,2,48,384]{3,2,1,0:T(8,128)(2,1)S(1)} %all-to-all-done.1.refs_0_), channel_id=1, source_target_pairs={{0,4},{2,6},{4,0},{6,2},{1,5},{3,7},{5,1},{7,3},{8,12},{10,14},{12... | collective-permute-start | bytes 884744 | tf_op jit(solution)/shard_map/ppermute | solution.py:775
  30.6 13.7 %collective-permute-start.2 = (bf16[4,2,48,384]{3,2,1,0:T(8,128)(2,1)S(1)}, bf16[4,2,48,384]{3,2,1,0:T(8,128)(2,1)S(1)}, u32[]{:S(2)}, u32[]{:S(2)}) collective-permute-start(bf16[4,2,48,384]{3,2,1,0:T(8,128)(2,1)S(1)} %all-to-all-done.1.refs_0_), channel_id=1, source_target_pairs={{0,2},{2,0},{4,6},{6,4},{1,3},{3,1},{5,7},{7,5},{8,10},{10,8},{12,... | collective-permute-start | bytes 884744 | tf_op jit(solution)/shard_map/ppermute | solution.py:775
  65.1 3.3 %collective-permute-start.17 = (bf16[2,4,2,48,384]{4,3,2,1,0:T(8,128)(2,1)S(1)}, bf16[2,4,2,48,384]{4,3,2,1,0:T(8,128)(2,1)S(1)}, u32[]{:S(2)}, u32[]{:S(2)}) collective-permute-start(bf16[2,4,2,48,384]{4,3,2,1,0:T(8,128)(2,1)S(1)} %get-tuple-element.105), channel_id=1, source_target_pairs={{0,1},{1,0},{2,3},{3,2},{4,5},{5,4},{6,7},{7,6},{8,9},{9,8},{10,11... | collective-permute-start | bytes 1769480 | tf_op jit(solution)/shard_map/ppermute | solution.py:766
  67.1 16.9 %collective-permute-start.16 = (bf16[4,2,48,384]{3,2,1,0:T(8,128)(2,1)S(1)}, bf16[4,2,48,384]{3,2,1,0:T(8,128)(2,1)S(1)}, u32[]{:S(2)}, u32[]{:S(2)}) collective-permute-start(bf16[4,2,48,384]{3,2,1,0:T(8,128)(2,1)S(1)} %get-tuple-element.103), channel_id=1, source_target_pairs={{0,2},{2,0},{4,6},{6,4},{1,3},{3,1},{5,7},{7,5},{8,10},{10,8},{12,... | collective-permute-start | bytes 884744 | tf_op jit(solution)/shard_map/ppermute | solution.py:775
  68.5 15.5 %collective-permute-start.18 = (bf16[4,2,48,384]{3,2,1,0:T(8,128)(2,1)S(1)}, bf16[4,2,48,384]{3,2,1,0:T(8,128)(2,1)S(1)}, u32[]{:S(2)}, u32[]{:S(2)}) collective-permute-start(bf16[4,2,48,384]{3,2,1,0:T(8,128)(2,1)S(1)} %get-tuple-element.106), channel_id=1, source_target_pairs={{0,4},{2,6},{4,0},{6,2},{1,5},{3,7},{5,1},{7,3},{8,12},{10,14},{12... | collective-permute-start | bytes 884744 | tf_op jit(solution)/shard_map/ppermute | solution.py:775
  69.7 14.3 %collective-permute-start.19 = (bf16[4,2,48,384]{3,2,1,0:T(8,128)(2,1)S(1)}, bf16[4,2,48,384]{3,2,1,0:T(8,128)(2,1)S(1)}, u32[]{:S(2)}, u32[]{:S(2)}) collective-permute-start(bf16[4,2,48,384]{3,2,1,0:T(8,128)(2,1)S(1)} %get-tuple-element.107), channel_id=1, source_target_pairs={{0,6},{2,4},{4,2},{6,0},{1,7},{3,5},{5,3},{7,1},{8,14},{10,12},{12... | collective-permute-start | bytes 884744 | tf_op jit(solution)/shard_map/ppermute | solution.py:775
  84.0 5.9 %collective-permute-start.20 = (bf16[17,48,384]{2,1,0:T(8,128)(2,1)}, bf16[17,48,384]{2,1,0:T(8,128)(2,1)S(1)}, u32[]{:S(2)}, u32[]{:S(2)}) collective-permute-start(bf16[17,48,384]{2,1,0:T(8,128)(2,1)} %get-tuple-element.109), channel_id=1, source_target_pairs={{0,1},{1,0},{2,3},{3,2},{4,5},{5,4},{6,7},{7,6},{8,9},{9,8},{10,11... | collective-permute-start | bytes 1880072 | tf_op jit(solution)/shard_map/ppermute | solution.py:766
  85.0 16.7 %all-to-all-start.2 = ((bf16[4,2,48,384]{3,2,1,0:T(8,128)(2,1)}), bf16[4,2,48,384]{3,2,1,0:T(8,128)(2,1)S(1)}, u32[]{:S(2)}, u32[]{:S(2)}) async-start(bf16[4,2,48,384]{3,2,1,0:T(8,128)(2,1)} %sum_late.1), calls=%async_computation.2 | async-start | bytes 589824 | tf_op jit(solution)/shard_map/all_to_all | solution.py:770
  90.6 10.2 %collective-permute-start.21 = (bf16[200,384]{1,0:T(8,128)(2,1)S(1)}, bf16[200,384]{1,0:T(8,128)(2,1)S(1)}, u32[]{:S(2)}, u32[]{:S(2)}) collective-permute-start(bf16[200,384]{1,0:T(8,128)(2,1)S(1)} %get-tuple-element.117), channel_id=1, source_target_pairs={{0,2},{2,0},{4,6},{6,4},{1,3},{3,1},{5,7},{7,5},{8,10},{10,8},{12,... | collective-permute-start | bytes 460808 | tf_op jit(solution)/shard_map/ppermute | solution.py:775
  91.8 9.1 %collective-permute-start.22 = (bf16[200,384]{1,0:T(8,128)(2,1)S(1)}, bf16[200,384]{1,0:T(8,128)(2,1)S(1)}, u32[]{:S(2)}, u32[]{:S(2)}) collective-permute-start(bf16[200,384]{1,0:T(8,128)(2,1)S(1)} %get-tuple-element.118), channel_id=1, source_target_pairs={{0,4},{2,6},{4,0},{6,2},{1,5},{3,7},{5,1},{7,3},{8,12},{10,14},{12... | collective-permute-start | bytes 460808 | tf_op jit(solution)/shard_map/ppermute | solution.py:775
  92.6 8.3 %collective-permute-start.23 = (bf16[200,384]{1,0:T(8,128)(2,1)S(1)}, bf16[200,384]{1,0:T(8,128)(2,1)S(1)}, u32[]{:S(2)}, u32[]{:S(2)}) collective-permute-start(bf16[200,384]{1,0:T(8,128)(2,1)S(1)} %get-tuple-element.119), channel_id=1, source_target_pairs={{0,6},{2,4},{4,2},{6,0},{1,7},{3,5},{5,3},{7,1},{8,14},{10,12},{12... | collective-permute-start | bytes 460808 | tf_op jit(solution)/shard_map/ppermute | solution.py:775
  101.7 13.0 %all-to-all-start.3 = ((bf16[4,56,384]{2,1,0:T(8,128)(2,1)}), bf16[4,56,384]{2,1,0:T(8,128)(2,1)S(1)}, u32[]{:S(2)}, u32[]{:S(2)}) async-start(bf16[4,56,384]{2,1,0:T(8,128)(2,1)} %join.1), calls=%async_computation.3 | async-start | bytes 344064 | tf_op jit(solution)/shard_map/all_to_all | solution.py:770
  (20 other events, 266.3 us)

commit v18 on v14

--- a/solution.py
+++ b/solution.py
@@ -596,9 +596,9 @@
 
 def two_products(left, middle, right):
     right_high, right_low = right
-    both = cut_rows(nn(stack(left[0], middle[0], left[1], middle[1]), right_high), 4)
-    high = cut_rows(nn(stack(left[0], middle[0]), right_low), 2)
-    return both[0] + (both[2] + high[0]), both[1] + (both[3] + high[1])
+    both = cut_rows(nn(stack(middle[0], middle[1], left[0], left[1]), right_high), 4)
+    high = cut_rows(nn(stack(middle[0], left[0]), right_low), 2)
+    return both[2] + (both[3] + high[1]), both[0] + (both[1] + high[0])
 
 
 def update_norms(scale, total, param_ref, state_ref, grad_ref, new_state_ref, new_ref):

time: 121 us -> 121 us (level)
  no operation moved by 1% of the time
where the time goes in v18:
time: 121 us; the launch traced here: 120 us
  Pallas kernels  70 us (58%)
  starting transfers between devices  36.2 us (30%)
  waiting for transfers between devices  13.1 us (11%)
    all_to_all x4, starting transfers between devices, to_all(): return lax.all_to_all(values, axis, 0, 0)  19.7 us
    pallas_call x1, Pallas kernels, mlp(): pl.pallas_call(mlp_kernel, grid=(rows // TILE,), in_specs=[pl.BlockSpec(m...  18.1 us
    ppermute x12, starting transfers between devices, across(): return lax.ppermute(values, 'inner', pairs)  14.2 us
    pallas_call x2, Pallas kernels, shampoo(): pl.pallas_call(lambda *refs: shampoo_kernel(scale, bool(norms), *refs), g...  13.8 us
    pallas_call x1, Pallas kernels, attn_backward(): pl.pallas_call(attn_backward_kernel, grid=(rows // TILE,), in_specs=[smem...  13.1 us
    pallas_call x1, Pallas kernels, attn_forward(): pl.pallas_call(attn_forward_kernel, grid=(rows // TILE,), in_specs=[smem]...  12.2 us
    pallas_call x1, Pallas kernels, input_gradient(): pl.pallas_call(input_grad_kernel, grid=(rows // INPUT_TILE,), in_specs=[t...  6.62 us
    ppermute x12, waiting for transfers between devices, across(): return lax.ppermute(values, 'inner', pairs)  5.16 us
  transfers between devices with their start and end apart: 28, of which 10 were waited for; matrix products, arithmetic and copies ran while one was open for 0% of the time, Pallas kernels for 37%

profile of v18, /device:TPU:0, one launch (start us, length us, event | category | flops | bytes accessed | tf_op | source)
XLA Modules:
  0.0 120.4 jit_solution(4262709294638664809)
XLA Ops:
  0.7 1.8 %pack.2 = bf16[4,1,48,384]{3,2,1,0:T(8,128)(2,1)} custom-call(f32[3,8,48,48]{3,2,1,0:T(8,128)} %bitcast.11), custom_call_target="tpu_custom_call" | custom-call | tf_op jit(solution)/shard_map/pack/pallas_call | solution.py:484
  2.5 6.3 %all-to-all-start = ((bf16[4,1,48,384]{3,2,1,0:T(8,128)(2,1)}), bf16[4,1,48,384]{3,2,1,0:T(8,128)(2,1)S(1)}, u32[]{:S(2)}, u32[]{:S(2)}) async-start(bf16[4,1,48,384]{3,2,1,0:T(8,128)(2,1)} %pack.2), calls=%async_computation | async-start | bytes 294912 | tf_op jit(solution)/shard_map/all_to_all | solution.py:753
  8.8 1.8 %pack.3 = bf16[4,2,48,384]{3,2,1,0:T(8,128)(2,1)} custom-call(f32[3,8,48,48]{3,2,1,0:T(8,128)} %bitcast.12), custom_call_target="tpu_custom_call" | custom-call | tf_op jit(solution)/shard_map/pack/pallas_call | solution.py:484
  10.6 4.4 %all-to-all-done = bf16[4,1,48,384]{3,2,1,0:T(8,128)(2,1)S(1)} async-done(((bf16[4,1,48,384]{3,2,1,0:T(8,128)(2,1)}), bf16[4,1,48,384]{3,2,1,0:T(8,128)(2,1)S(1)}, u32[]{:S(2)}, u32[]{:S(2)}) %all-to-all-start) | async-done | bytes 147488 | tf_op jit(solution)/shard_map/all_to_all | solution.py:753
  15.0 3.5 %all-to-all-start.1 = ((bf16[4,2,48,384]{3,2,1,0:T(8,128)(2,1)}), bf16[4,2,48,384]{3,2,1,0:T(8,128)(2,1)S(1)}, u32[]{:S(2)}, u32[]{:S(2)}) async-start(bf16[4,2,48,384]{3,2,1,0:T(8,128)(2,1)} %pack.3), calls=%async_computation.1 | async-start | bytes 589824 | tf_op jit(solution)/shard_map/all_to_all | solution.py:753
  18.5 2.5 %collective-permute-start.6 = (bf16[4,48,384]{2,1,0:T(8,128)(2,1)S(1)}, bf16[4,48,384]{2,1,0:T(8,128)(2,1)S(1)}, u32[]{:S(2)}, u32[]{:S(2)}) collective-permute-start(bf16[4,48,384]{2,1,0:T(8,128)(2,1)S(1)} %bitcast.16), channel_id=1, source_target_pairs={{0,6},{2,4},{4,2},{6,0},{1,7},{3,5},{5,3},{7,1},{8,14},{10,12},{12... | collective-permute-start | bytes 442376 | tf_op jit(solution)/shard_map/ppermute | solution.py:758
  22.7 3.4 %collective-permute-done.6.refs_3_ = bf16[4,48,384]{2,1,0:T(8,128)(2,1)S(1)} collective-permute-done((bf16[4,48,384]{2,1,0:T(8,128)(2,1)S(1)}, bf16[4,48,384]{2,1,0:T(8,128)(2,1)S(1)}, u32[]{:S(2)}, u32[]{:S(2)}) %collective-permute-start.6) | collective-permute-done | bytes 147488 | tf_op jit(solution)/shard_map/ppermute | solution.py:758
  27.6 2.4 %collective-permute-start.4 = (bf16[4,2,48,384]{3,2,1,0:T(8,128)(2,1)S(1)}, bf16[4,2,48,384]{3,2,1,0:T(8,128)(2,1)S(1)}, u32[]{:S(2)}, u32[]{:S(2)}) collective-permute-start(bf16[4,2,48,384]{3,2,1,0:T(8,128)(2,1)S(1)} %all-to-all-done.1.refs_0_), channel_id=1, source_target_pairs={{0,6},{2,4},{4,2},{6,0},{1,7},{3,5},{5,3},{7,1},{8,14},{10,12},{12... | collective-permute-start | bytes 884744 | tf_op jit(solution)/shard_map/ppermute | solution.py:758
  31.1 12.2 %attn_forward.1 = (bf16[6,3,512,256]{3,2,1,0:T(8,128)(2,1)}, bf16[1536,1152]{1,0:T(8,128)(2,1)}, bf16[1536,384]{1,0:T(8,128)(2,1)}, f32[1536,384]{1,0:T(8,128)S(...) custom-call(s32[14]{0:T(128)S(1)} %pad_add_fusion.place_ref, ...), custom_call_target="tpu_custom_call" | custom-call | flops 4227858432 | bytes 16777216 | tf_op jit(solution)/shard_map/attn_forward/pallas_call | solution.py:176
  44.7 1.1 collective-permute-done.12.refs_5_
  46.6 18.1 %mlp.1 = (f32[1536,384]{1,0:T(8,128)}, f32[1536,384]{1,0:T(8,128)}, f32[2,384]{1,0:T(2,128)S(1)}, bf16[2,4,2,48,384]{4,3,2,1,0:T(8,128)(2,1)S(1)}, bf16[2,4,2,48...) custom-call(s32[14]{0:T(128)S(1)} %pad_add_fusion.place_ref, ...), custom_call_target="tpu_custom_call" | custom-call | flops 10871635968 | bytes 20971520 | tf_op jit(solution)/shard_map/mlp/pallas_call | solution.py:273
  65.3 1.5 %collective-permute-done.15.received_ref = bf16[2,4,2,48,384]{4,3,2,1,0:T(8,128)(2,1)S(1)} collective-permute-done((bf16[2,4,2,48,384]{4,3,2,1,0:T(8,128)(2,1)S(1)}, bf16[2,4,2,48,384]{4,3,2,1,0:T(8,128)(2,1)S(1)}, u32[]{:S(2)}, u32[]{:S(2)}) %collective-permute-start.15) | collective-permute-done | bytes 589856 | tf_op jit(solution)/shard_map/ppermute | solution.py:749
  66.9 1.3 %collective-permute-start.16 = (bf16[4,2,48,384]{3,2,1,0:T(8,128)(2,1)S(1)}, bf16[4,2,48,384]{3,2,1,0:T(8,128)(2,1)S(1)}, u32[]{:S(2)}, u32[]{:S(2)}) collective-permute-start(bf16[4,2,48,384]{3,2,1,0:T(8,128)(2,1)S(1)} %get-tuple-element.103), channel_id=1, source_target_pairs={{0,2},{2,0},{4,6},{6,4},{1,3},{3,1},{5,7},{7,5},{8,10},{10,8},{12,... | collective-permute-start | bytes 884744 | tf_op jit(solution)/shard_map/ppermute | solution.py:758
  68.4 1.1 collective-permute-start.18
  69.5 1.2 collective-permute-start.19
  70.8 13.1 %attn_backward.1 = (bf16[1536,1152]{1,0:T(8,128)(2,1)}, bf16[16,48,384]{2,1,0:T(8,128)(2,1)S(1)}, bf16[17,48,384]{2,1,0:T(8,128)(2,1)}, f32[4,384]{1,0:T(4,128)S(1)}) custom-call(s32[14]{0:T(128)S(1)} %pad_add_fusion.place_ref, s32[12,3]{1,0:T(8,128)S(1)} %copy.26.own_mask_ref, s32[12,3]{1,0:T(8,128)S(1)} %collective-permute-done.1.other_mask_ref, ...), custom_call_target="tpu_custom_call" | custom-call | flops 7096762368 | bytes 20971520 | tf_op jit(solution)/shard_map/attn_backward/pallas_call | solution.py:396
  84.0 0.9 sum_late.1
  84.8 4.9 %all-to-all-start.2 = ((bf16[4,2,48,384]{3,2,1,0:T(8,128)(2,1)}), bf16[4,2,48,384]{3,2,1,0:T(8,128)(2,1)S(1)}, u32[]{:S(2)}, u32[]{:S(2)}) async-start(bf16[4,2,48,384]{3,2,1,0:T(8,128)(2,1)} %sum_late.1), calls=%async_computation.2 | async-start | bytes 589824 | tf_op jit(solution)/shard_map/all_to_all | solution.py:753
  90.5 1.2 collective-permute-start.21
  92.5 1.6 %collective-permute-start.23 = (bf16[200,384]{1,0:T(8,128)(2,1)S(1)}, bf16[200,384]{1,0:T(8,128)(2,1)S(1)}, u32[]{:S(2)}, u32[]{:S(2)}) collective-permute-start(bf16[200,384]{1,0:T(8,128)(2,1)S(1)} %get-tuple-element.119), channel_id=1, source_target_pairs={{0,6},{2,4},{4,2},{6,0},{1,7},{3,5},{5,3},{7,1},{8,14},{10,12},{12... | collective-permute-start | bytes 460808 | tf_op jit(solution)/shard_map/ppermute | solution.py:758
  94.1 6.6 %input_gradient.1 = f32[1536,384]{1,0:T(8,128)} custom-call(bf16[1536,384]{1,0:T(8,128)(2,1)} %x_ref.5, f32[1536,384]{1,0:T(8,128)} %get-tuple-element.94.grad_ref, bf16[1536,1152]{1,0:T(8,128)(2,1)} %get-tuple-element.120.dqkv_ref, f32[4,384]{1,0:T(4,128)} %refs_4_.1, bf16[384,1152]{1,0:T(8,128)(2,1)} %get-tuple-element.99.wqkv_ref), custom_call_target="tpu_custom_call" | custom-call | flops 1358954496 | bytes 10485760 | tf_op jit(solution)/shard_map/input_gradient/pallas_call | solution.py:452
  101.6 5.0 %all-to-all-start.3 = ((bf16[4,56,384]{2,1,0:T(8,128)(2,1)}), bf16[4,56,384]{2,1,0:T(8,128)(2,1)S(1)}, u32[]{:S(2)}, u32[]{:S(2)}) async-start(bf16[4,56,384]{2,1,0:T(8,128)(2,1)} %join.1), calls=%async_computation.3 | async-start | bytes 344064 | tf_op jit(solution)/shard_map/all_to_all | solution.py:753
  106.6 8.0 %shampoo.2 = (f32[3,8,48,48]{3,2,1,0:T(8,128)}, f32[3,8,48,48]{3,2,1,0:T(8,128)}, f32[3,8,48,48]{3,2,1,0:T(8,128)}, f32[3,8,48,48]{3,2,1,0:T(8,128)}) custom-call(bf16[4,2,48,384]{3,2,1,0:T(8,128)(2,1)S(1)} %all-to-all-done.2.refs_0_, f32[3,8,48,48]{3,2,1,0:T(8,128)S(1)} %bitcast.13, f32[3,8,48,48]{3,2,1,0:T(8,128)S(1)} %bitcast.21, ...), custom_call_target="tpu_custom_call" | custom-call | flops 6442450944 | bytes 4194304 | tf_op jit(solution)/shard_map/shampoo/pallas_call | solution.py:724
  114.6 5.8 %shampoo.3 = (f32[3,8,48,48]{3,2,1,0:T(8,128)}, f32[3,8,48,48]{3,2,1,0:T(8,128)}, f32[3,8,48,48]{3,2,1,0:T(8,128)}, f32[3,8,48,48]{3,2,1,0:T(8,128)}, f32[4,384]...) custom-call(bf16[4,1,56,384]{3,2,1,0:T(8,128)(2,1)S(1)} %bitcast.15,, ...), custom_call_target="tpu_custom_call", output_to_operand_aliasing={{0}: (6, {}), {1}: (7, {}), {2}: (8, {}), {3}: (9, {})} | custom-call | flops 3221225472 | bytes 4194304 | tf_op jit(solution)/shard_map/shampoo/pallas_call | solution.py:724
  (80 shorter events, 10.0 us)
Async XLA Ops:
  2.5 12.6 %all-to-all-start = ((bf16[4,1,48,384]{3,2,1,0:T(8,128)(2,1)}), bf16[4,1,48,384]{3,2,1,0:T(8,128)(2,1)S(1)}, u32[]{:S(2)}, u32[]{:S(2)}) async-start(bf16[4,1,48,384]{3,2,1,0:T(8,128)(2,1)} %pack.2), calls=%async_computation | async-start | bytes 294912 | tf_op jit(solution)/shard_map/all_to_all | solution.py:753
  15.0 12.0 %all-to-all-start.1 = ((bf16[4,2,48,384]{3,2,1,0:T(8,128)(2,1)}), bf16[4,2,48,384]{3,2,1,0:T(8,128)(2,1)S(1)}, u32[]{:S(2)}, u32[]{:S(2)}) async-start(bf16[4,2,48,384]{3,2,1,0:T(8,128)(2,1)} %pack.3), calls=%async_computation.1 | async-start | bytes 589824 | tf_op jit(solution)/shard_map/all_to_all | solution.py:753
  18.5 7.6 %collective-permute-start.6 = (bf16[4,48,384]{2,1,0:T(8,128)(2,1)S(1)}, bf16[4,48,384]{2,1,0:T(8,128)(2,1)S(1)}, u32[]{:S(2)}, u32[]{:S(2)}) collective-permute-start(bf16[4,48,384]{2,1,0:T(8,128)(2,1)S(1)} %bitcast.16), channel_id=1, source_target_pairs={{0,6},{2,4},{4,2},{6,0},{1,7},{3,5},{5,3},{7,1},{8,14},{10,12},{12... | collective-permute-start | bytes 442376 | tf_op jit(solution)/shard_map/ppermute | solution.py:758
  21.0 6.0 %collective-permute-start.5 = (bf16[4,48,384]{2,1,0:T(8,128)(2,1)S(1)}, bf16[4,48,384]{2,1,0:T(8,128)(2,1)S(1)}, u32[]{:S(2)}, u32[]{:S(2)}) collective-permute-start(bf16[4,48,384]{2,1,0:T(8,128)(2,1)S(1)} %bitcast.17), channel_id=1, source_target_pairs={{0,4},{2,6},{4,0},{6,2},{1,5},{3,7},{5,1},{7,3},{8,12},{10,14},{12... | collective-permute-start | bytes 442376 | tf_op jit(solution)/shard_map/ppermute | solution.py:758
  21.5 5.5 %collective-permute-start = (bf16[4,48,384]{2,1,0:T(8,128)(2,1)S(1)}, bf16[4,48,384]{2,1,0:T(8,128)(2,1)}, u32[]{:S(2)}, u32[]{:S(2)}) collective-permute-start(bf16[4,48,384]{2,1,0:T(8,128)(2,1)S(1)} %bitcast.18), channel_id=1, source_target_pairs={{0,2},{2,0},{4,6},{6,4},{1,3},{3,1},{5,7},{7,5},{8,10},{10,8},{12,... | collective-permute-start | bytes 442376 | tf_op jit(solution)/shard_map/ppermute | solution.py:758
  22.1 4.8 %collective-permute-start.1 = (s32[12,3]{1,0:T(8,128)S(1)}, s32[12,3]{1,0:T(8,128)S(1)}, u32[]{:S(2)}, u32[]{:S(2)}) collective-permute-start(s32[12,3]{1,0:T(8,128)S(1)} %copy.26.own_mask_ref), channel_id=1, source_target_pairs={{0,1},{1,0},{2,3},{3,2},{4,5},{5,4},{6,7},{7,6},{8,9},{9,8},{10,11... | collective-permute-start | bytes 440 | tf_op jit(solution)/shard_map/ppermute | solution.py:749
  22.2 5.4 %collective-permute-start.7 = (bf16[4,48,384]{2,1,0:T(8,128)(2,1)S(1)}, bf16[4,48,384]{2,1,0:T(8,128)(2,1)}, u32[]{:S(2)}, u32[]{:S(2)}) collective-permute-start(bf16[4,48,384]{2,1,0:T(8,128)(2,1)S(1)} %bitcast.19), channel_id=1, source_target_pairs={{0,1},{1,0},{2,3},{3,2},{4,5},{5,4},{6,7},{7,6},{8,9},{9,8},{10,11... | collective-permute-start | bytes 442376 | tf_op jit(solution)/shard_map/ppermute | solution.py:749
  26.1 3.9 %collective-permute-start.10 = (bf16[4,48,384]{2,1,0:T(8,128)(2,1)S(1)}, bf16[4,48,384]{2,1,0:T(8,128)(2,1)}, u32[]{:S(2)}, u32[]{:S(2)}) collective-permute-start(bf16[4,48,384]{2,1,0:T(8,128)(2,1)S(1)} %collective-permute-done.6.refs_3_), channel_id=1, source_target_pairs={{0,1},{1,0},{2,3},{3,2},{4,5},{5,4},{6,7},{7,6},{8,9},{9,8},{10,11... | collective-permute-start | bytes 442376 | tf_op jit(solution)/shard_map/ppermute | solution.py:749
  26.9 3.6 %collective-permute-start.9 = (bf16[4,48,384]{2,1,0:T(8,128)(2,1)S(1)}, bf16[4,48,384]{2,1,0:T(8,128)(2,1)}, u32[]{:S(2)}, u32[]{:S(2)}) collective-permute-start(bf16[4,48,384]{2,1,0:T(8,128)(2,1)S(1)} %collective-permute-done.5.refs_2_), channel_id=1, source_target_pairs={{0,1},{1,0},{2,3},{3,2},{4,5},{5,4},{6,7},{7,6},{8,9},{9,8},{10,11... | collective-permute-start | bytes 442376 | tf_op jit(solution)/shard_map/ppermute | solution.py:749
  27.0 4.1 %collective-permute-start.8 = (bf16[4,48,384]{2,1,0:T(8,128)(2,1)}, bf16[4,48,384]{2,1,0:T(8,128)(2,1)S(1)}, u32[]{:S(2)}, u32[]{:S(2)}) collective-permute-start(bf16[4,48,384]{2,1,0:T(8,128)(2,1)} %collective-permute-done.refs_1_), channel_id=1, source_target_pairs={{0,1},{1,0},{2,3},{3,2},{4,5},{5,4},{6,7},{7,6},{8,9},{9,8},{10,11... | collective-permute-start | bytes 442376 | tf_op jit(solution)/shard_map/ppermute | solution.py:749
  27.5 17.2 %collective-permute-start.11 = (bf16[4,2,48,384]{3,2,1,0:T(8,128)(2,1)S(1)}, bf16[4,2,48,384]{3,2,1,0:T(8,128)(2,1)S(1)}, u32[]{:S(2)}, u32[]{:S(2)}) collective-permute-start(bf16[4,2,48,384]{3,2,1,0:T(8,128)(2,1)S(1)} %all-to-all-done.1.refs_0_), channel_id=1, source_target_pairs={{0,1},{1,0},{2,3},{3,2},{4,5},{5,4},{6,7},{7,6},{8,9},{9,8},{10,11... | collective-permute-start | bytes 884744 | tf_op jit(solution)/shard_map/ppermute | solution.py:749
  27.6 15.7 %collective-permute-start.4 = (bf16[4,2,48,384]{3,2,1,0:T(8,128)(2,1)S(1)}, bf16[4,2,48,384]{3,2,1,0:T(8,128)(2,1)S(1)}, u32[]{:S(2)}, u32[]{:S(2)}) collective-permute-start(bf16[4,2,48,384]{3,2,1,0:T(8,128)(2,1)S(1)} %all-to-all-done.1.refs_0_), channel_id=1, source_target_pairs={{0,6},{2,4},{4,2},{6,0},{1,7},{3,5},{5,3},{7,1},{8,14},{10,12},{12... | collective-permute-start | bytes 884744 | tf_op jit(solution)/shard_map/ppermute | solution.py:758
  30.0 14.2 %collective-permute-start.3 = (bf16[4,2,48,384]{3,2,1,0:T(8,128)(2,1)S(1)}, bf16[4,2,48,384]{3,2,1,0:T(8,128)(2,1)S(1)}, u32[]{:S(2)}, u32[]{:S(2)}) collective-permute-start(bf16[4,2,48,384]{3,2,1,0:T(8,128)(2,1)S(1)} %all-to-all-done.1.refs_0_), channel_id=1, source_target_pairs={{0,4},{2,6},{4,0},{6,2},{1,5},{3,7},{5,1},{7,3},{8,12},{10,14},{12... | collective-permute-start | bytes 884744 | tf_op jit(solution)/shard_map/ppermute | solution.py:758
  30.5 13.7 %collective-permute-start.2 = (bf16[4,2,48,384]{3,2,1,0:T(8,128)(2,1)S(1)}, bf16[4,2,48,384]{3,2,1,0:T(8,128)(2,1)S(1)}, u32[]{:S(2)}, u32[]{:S(2)}) collective-permute-start(bf16[4,2,48,384]{3,2,1,0:T(8,128)(2,1)S(1)} %all-to-all-done.1.refs_0_), channel_id=1, source_target_pairs={{0,2},{2,0},{4,6},{6,4},{1,3},{3,1},{5,7},{7,5},{8,10},{10,8},{12,... | collective-permute-start | bytes 884744 | tf_op jit(solution)/shard_map/ppermute | solution.py:758
  64.9 3.3 %collective-permute-start.17 = (bf16[2,4,2,48,384]{4,3,2,1,0:T(8,128)(2,1)S(1)}, bf16[2,4,2,48,384]{4,3,2,1,0:T(8,128)(2,1)S(1)}, u32[]{:S(2)}, u32[]{:S(2)}) collective-permute-start(bf16[2,4,2,48,384]{4,3,2,1,0:T(8,128)(2,1)S(1)} %get-tuple-element.105), channel_id=1, source_target_pairs={{0,1},{1,0},{2,3},{3,2},{4,5},{5,4},{6,7},{7,6},{8,9},{9,8},{10,11... | collective-permute-start | bytes 1769480 | tf_op jit(solution)/shard_map/ppermute | solution.py:749
  66.9 16.9 %collective-permute-start.16 = (bf16[4,2,48,384]{3,2,1,0:T(8,128)(2,1)S(1)}, bf16[4,2,48,384]{3,2,1,0:T(8,128)(2,1)S(1)}, u32[]{:S(2)}, u32[]{:S(2)}) collective-permute-start(bf16[4,2,48,384]{3,2,1,0:T(8,128)(2,1)S(1)} %get-tuple-element.103), channel_id=1, source_target_pairs={{0,2},{2,0},{4,6},{6,4},{1,3},{3,1},{5,7},{7,5},{8,10},{10,8},{12,... | collective-permute-start | bytes 884744 | tf_op jit(solution)/shard_map/ppermute | solution.py:758
  68.4 15.5 %collective-permute-start.18 = (bf16[4,2,48,384]{3,2,1,0:T(8,128)(2,1)S(1)}, bf16[4,2,48,384]{3,2,1,0:T(8,128)(2,1)S(1)}, u32[]{:S(2)}, u32[]{:S(2)}) collective-permute-start(bf16[4,2,48,384]{3,2,1,0:T(8,128)(2,1)S(1)} %get-tuple-element.106), channel_id=1, source_target_pairs={{0,4},{2,6},{4,0},{6,2},{1,5},{3,7},{5,1},{7,3},{8,12},{10,14},{12... | collective-permute-start | bytes 884744 | tf_op jit(solution)/shard_map/ppermute | solution.py:758
  69.5 14.3 %collective-permute-start.19 = (bf16[4,2,48,384]{3,2,1,0:T(8,128)(2,1)S(1)}, bf16[4,2,48,384]{3,2,1,0:T(8,128)(2,1)S(1)}, u32[]{:S(2)}, u32[]{:S(2)}) collective-permute-start(bf16[4,2,48,384]{3,2,1,0:T(8,128)(2,1)S(1)} %get-tuple-element.107), channel_id=1, source_target_pairs={{0,6},{2,4},{4,2},{6,0},{1,7},{3,5},{5,3},{7,1},{8,14},{10,12},{12... | collective-permute-start | bytes 884744 | tf_op jit(solution)/shard_map/ppermute | solution.py:758
  83.9 5.9 %collective-permute-start.20 = (bf16[17,48,384]{2,1,0:T(8,128)(2,1)}, bf16[17,48,384]{2,1,0:T(8,128)(2,1)S(1)}, u32[]{:S(2)}, u32[]{:S(2)}) collective-permute-start(bf16[17,48,384]{2,1,0:T(8,128)(2,1)} %get-tuple-element.109), channel_id=1, source_target_pairs={{0,1},{1,0},{2,3},{3,2},{4,5},{5,4},{6,7},{7,6},{8,9},{9,8},{10,11... | collective-permute-start | bytes 1880072 | tf_op jit(solution)/shard_map/ppermute | solution.py:749
  84.8 16.7 %all-to-all-start.2 = ((bf16[4,2,48,384]{3,2,1,0:T(8,128)(2,1)}), bf16[4,2,48,384]{3,2,1,0:T(8,128)(2,1)S(1)}, u32[]{:S(2)}, u32[]{:S(2)}) async-start(bf16[4,2,48,384]{3,2,1,0:T(8,128)(2,1)} %sum_late.1), calls=%async_computation.2 | async-start | bytes 589824 | tf_op jit(solution)/shard_map/all_to_all | solution.py:753
  90.5 10.2 %collective-permute-start.21 = (bf16[200,384]{1,0:T(8,128)(2,1)S(1)}, bf16[200,384]{1,0:T(8,128)(2,1)S(1)}, u32[]{:S(2)}, u32[]{:S(2)}) collective-permute-start(bf16[200,384]{1,0:T(8,128)(2,1)S(1)} %get-tuple-element.117), channel_id=1, source_target_pairs={{0,2},{2,0},{4,6},{6,4},{1,3},{3,1},{5,7},{7,5},{8,10},{10,8},{12,... | collective-permute-start | bytes 460808 | tf_op jit(solution)/shard_map/ppermute | solution.py:758
  91.7 9.1 %collective-permute-start.22 = (bf16[200,384]{1,0:T(8,128)(2,1)S(1)}, bf16[200,384]{1,0:T(8,128)(2,1)S(1)}, u32[]{:S(2)}, u32[]{:S(2)}) collective-permute-start(bf16[200,384]{1,0:T(8,128)(2,1)S(1)} %get-tuple-element.118), channel_id=1, source_target_pairs={{0,4},{2,6},{4,0},{6,2},{1,5},{3,7},{5,1},{7,3},{8,12},{10,14},{12... | collective-permute-start | bytes 460808 | tf_op jit(solution)/shard_map/ppermute | solution.py:758
  92.5 8.3 %collective-permute-start.23 = (bf16[200,384]{1,0:T(8,128)(2,1)S(1)}, bf16[200,384]{1,0:T(8,128)(2,1)S(1)}, u32[]{:S(2)}, u32[]{:S(2)}) collective-permute-start(bf16[200,384]{1,0:T(8,128)(2,1)S(1)} %get-tuple-element.119), channel_id=1, source_target_pairs={{0,6},{2,4},{4,2},{6,0},{1,7},{3,5},{5,3},{7,1},{8,14},{10,12},{12... | collective-permute-start | bytes 460808 | tf_op jit(solution)/shard_map/ppermute | solution.py:758
  101.6 13.1 %all-to-all-start.3 = ((bf16[4,56,384]{2,1,0:T(8,128)(2,1)}), bf16[4,56,384]{2,1,0:T(8,128)(2,1)S(1)}, u32[]{:S(2)}, u32[]{:S(2)}) async-start(bf16[4,56,384]{2,1,0:T(8,128)(2,1)} %join.1), calls=%async_computation.3 | async-start | bytes 344064 | tf_op jit(solution)/shard_map/all_to_all | solution.py:753
  (20 other events, 266.0 us)
